TPU v7x, 128 devices: a whole 4x4x4 slice. The times are simulated.
128 devices in a mesh: req: 4 (over z_hi, core), frames: 32 (over z_lo, y, x).
Axes of the slice: x: 4, y: 4, z: 4 (z_hi: 2, z_lo: 2; z = z_hi * 2 + z_lo), core: 2. Of those that a mesh axis runs over, the one named last changes fastest.
Arguments:
- tokens: bfloat16 [8192, 1536], P(('req', 'frames')), parts along dimension 0, may hold values from -6 to 6
- queries: bfloat16 [8192, 1536], P(('req', 'frames')), parts along dimension 0, may hold values from -8 to 8
- keys: bfloat16 [8192, 1536], P(('req', 'frames')), parts along dimension 0, may hold values from -8 to 8
- values: bfloat16 [8192, 1536], P(('req', 'frames')), parts along dimension 0, may hold values from -6.5 to 6.5
- branch_gate: float32 [1536], replicated, may hold values from 0.5 to 2
- output_weight: bfloat16 [1536, 1536], replicated, may hold values from -0.15625 to 0.15625
- head_scale: float32 [1536], replicated, may hold values from -0.5 to 0.5
- head_shift: float32 [1536], replicated, may hold values from -3 to 3
- head_weight: bfloat16 [1536, 64], replicated, may hold values from -0.15625 to 0.15625
- noise_level: float32 [4], P('req'), parts along dimension 0, may hold values from 0.2 to 0.8
- noisy_latent: float32 [256, 4, 512], P(('req', 'frames')), parts along dimension 0, may hold values from -6 to 6
- input_kernel: bfloat16 [3, 3, 3, 16, 384], replicated, may hold values from -0.3125 to 0.3125
- first_gain: float32 [384], replicated, may hold values from 0.1 to 1.9
- middle_kernel: bfloat16 [3, 3, 3, 384, 384], replicated, may hold values from -0.0625 to 0.0625
- second_gain: float32 [384], replicated, may hold values from 0.1 to 1.9
- final_kernel: bfloat16 [3, 3, 3, 384, 384], replicated, may hold values from -0.0625 to 0.0625
Outputs:
- layer_output: bfloat16 [8192, 1536], P(('req', 'frames')), parts along dimension 0
- decoded: bfloat16 [256, 4, 32, 384], P(('req', 'frames')), parts along dimension 0
There are 4 independent parts, one for each index of `req`. A program takes and returns all parts, laid end to end along the dimension named above; an argument that names none is the same for every part. Nothing has to cross between parts.
All inputs are finite; a program needn't handle non-finite values.
Results may differ from a plain program's by a relative error of at most 0.012.
Values may be sent and summed in bfloat16 or wider, within the bound.
A program may use at most 128 MiB of HBM per device.

v0:
```python
import math

import jax
import jax.numpy as jnp
from jax import lax
from jax.sharding import PartitionSpec as P

HEAD_DIM = 128
HEADS = 12
LAT_C = 16
PATCH = 2
TOK_H = 2
TOK_W = 16


def shifted(x, axis, by):
    peers = lax.axis_size(axis)
    pairs = [(i, i + by) for i in range(peers) if 0 <= i + by < peers]
    return lax.ppermute(x, axis, pairs)


def split_heads(matrix, head_count):
    return matrix.reshape(matrix.shape[0], head_count, HEAD_DIM)


def empty_state(head_count, row_count):
    return (
        jnp.full((head_count, row_count), -1e30, jnp.float32),
        jnp.zeros((head_count, row_count), jnp.float32),
        jnp.zeros((row_count, head_count, HEAD_DIM), jnp.float32),
    )


def absorb_block(running, query_heads, key_heads, value_heads):
    row_peak, row_total, summed = running
    scores = jnp.einsum(
        "qhd,khd->hqk", query_heads, key_heads, preferred_element_type=jnp.float32
    ) * (1.0 / math.sqrt(HEAD_DIM))
    new_peak = jnp.maximum(row_peak, jnp.max(scores, axis=-1))
    factor = jnp.exp(row_peak - new_peak)
    weights = jnp.exp(scores - new_peak[:, :, None])
    row_total = jnp.sum(weights, axis=-1)
    summed = summed * factor.T[:, :, None] + jnp.einsum(
        "hqk,khd->qhd",
        weights.astype(jnp.bfloat16),
        value_heads,
        preferred_element_type=jnp.float32,
    )
    return (new_peak, row_total, summed)


def layer_norm(layer_output, head_scale, head_shift):
    values_f = layer_output.astype(jnp.float32)
    centre = jnp.mean(values_f, axis=-1, keepdims=True)
    spread = jnp.mean((values_f - centre) ** 2, axis=-1, keepdims=True)
    normed = (values_f - centre) * lax.rsqrt(spread + 1e-06) * (1.0 + head_scale) + head_shift
    return normed.astype(jnp.bfloat16)


def to_latent(velocity, noisy_latent, noise_level):
    frame_count = velocity.shape[0] // (TOK_H * TOK_W)
    grid = velocity.reshape(frame_count, TOK_H, TOK_W, PATCH, PATCH, LAT_C)
    grid = grid.transpose(0, 1, 3, 2, 4, 5).reshape(
        frame_count, PATCH * TOK_H, PATCH * TOK_W, LAT_C
    )
    base_latent = noisy_latent.reshape(frame_count, PATCH * TOK_H, PATCH * TOK_W, LAT_C)
    return (base_latent - noise_level[0] * grid).astype(jnp.bfloat16)


def spatial_conv(extended, kernel):
    result = lax.conv_general_dilated(
        extended[None],
        kernel,
        (1, 1, 1),
        ((0, 0), (1, 1), (1, 1)),
        dimension_numbers=("NDHWC", "DHWIO", "NDHWC"),
        preferred_element_type=jnp.float32,
    )
    return result[0]


def causal_conv(activ, kernel):
    frame_tail = shifted(activ[-2:], "frames", 1)
    return spatial_conv(jnp.concatenate([frame_tail, activ], axis=0), kernel)


def norm_silu(activ, gain):
    values_f = activ.astype(jnp.float32)
    scaled = (
        values_f * lax.rsqrt(jnp.mean(values_f * values_f, axis=-1, keepdims=True) + 1e-06) * gain
    )
    return jax.nn.silu(scaled).astype(jnp.bfloat16)


def body(
    tokens,
    queries,
    keys,
    values,
    branch_gate,
    output_weight,
    head_scale,
    head_shift,
    head_weight,
    noise_level,
    noisy_latent,
    input_kernel,
    first_gain,
    middle_kernel,
    second_gain,
    final_kernel,
):
    rows_here = queries.shape[0]
    full_width = HEADS * HEAD_DIM
    query_heads = split_heads(queries, HEADS)
    row_peak, row_total, summed = absorb_block(
        empty_state(HEADS, rows_here),
        query_heads,
        split_heads(lax.all_gather(keys, "frames", axis=0, tiled=True), HEADS),
        split_heads(lax.all_gather(values, "frames", axis=0, tiled=True), HEADS),
    )
    attended = (
        (summed / row_total.T[:, :, None]).reshape(rows_here, full_width).astype(jnp.bfloat16)
    )
    projected = jnp.dot(attended, output_weight, preferred_element_type=jnp.float32)
    layer_output = (tokens.astype(jnp.float32) + branch_gate * projected).astype(jnp.bfloat16)
    normed = layer_norm(layer_output, head_scale, head_shift)
    velocity = jnp.dot(normed, head_weight, preferred_element_type=jnp.float32)
    clean = to_latent(velocity, noisy_latent, noise_level)
    feature = causal_conv(clean, input_kernel).astype(jnp.bfloat16)
    first_act = norm_silu(feature, first_gain)
    middle = causal_conv(first_act, middle_kernel)
    second_act = norm_silu(middle, second_gain)
    decoded = (feature.astype(jnp.float32) + causal_conv(second_act, final_kernel)).astype(
        jnp.bfloat16
    )
    return (layer_output, decoded)


def solution(mesh):
    in_specs = (
        P(("req", "frames"), None),
        P(("req", "frames"), None),
        P(("req", "frames"), None),
        P(("req", "frames"), None),
        P(),
        P(),
        P(),
        P(),
        P(),
        P("req"),
        P(("req", "frames"), None, None),
        P(),
        P(),
        P(),
        P(),
        P(),
    )
    out_specs = (P(("req", "frames"), None), P(("req", "frames"), None, None, None))
    return jax.shard_map(body, mesh=mesh, in_specs=in_specs, out_specs=out_specs, check_vma=False)
```

profile of v0, /device:TPU:96, one launch (start us, length us, event | category | flops | bytes accessed | tf_op | source)
XLA Modules:
  0.0 409.7 jit_solution(832212411237137039)
XLA Ops:
  7.2 0.7 all-gather.3.cloned.1.call-update
  8.0 0.7 all-gather.5.cloned.1.call-update
  8.7 0.8 reshape.68
  10.1 0.7 broadcast_add_fusion
  10.8 161.0 %all-gather.3.cloned.1.call-done = bf16[2048,1536]{1,0:T(8,128)(2,1)} async-done(((bf16[64,1536]{1,0:T(8,128)(2,1)}), bf16[2048,1536]{1,0:T(8,128)(2,1)}) %all-gather.3.cloned.1.call-update) | async-done | bytes 6291472 | tf_op jit(solution)/shard_map/all_gather | solution.py:119
  171.8 8.6 %copy.37 = bf16[2048,1536]{0,1:T(8,128)(2,1)} copy(bf16[2048,1536]{1,0:T(8,128)(2,1)} %all-gather.3.cloned.1.call-done) | data formatting | bytes 12582912 | tf_op jit(solution)/shard_map/all_gather | solution.py:119
  180.4 4.1 multiply_reduce_fusion
  184.5 2.6 copy-done.1
  187.1 1.2 fusion
  188.2 147.5 %all-gather.5.cloned.1.call-done = bf16[2048,1536]{1,0:T(8,128)(2,1)} async-done(((bf16[64,1536]{1,0:T(8,128)(2,1)}), bf16[2048,1536]{1,0:T(8,128)(2,1)}) %all-gather.5.cloned.1.call-update) | async-done | bytes 6291472 | tf_op jit(solution)/shard_map/all_gather | solution.py:120
  335.7 8.7 %copy.40 = bf16[2048,1536]{0,1:T(8,128)(2,1)} copy(bf16[2048,1536]{1,0:T(8,128)(2,1)} %all-gather.5.cloned.1.call-done) | data formatting | bytes 12582912 | tf_op jit(solution)/shard_map/all_gather | solution.py:120
  344.4 7.1 %fusion.23 = bf16[12,8,8,128]{3,2,1,0:T(8,128)(2,1)S(1)} fusion(bf16[2048,12,128]{0,2,1:T(8,128)(2,1)} %bitcast.84, f32[12,64,2048]{2,1,0:T(8,128)} %copy-done.1, f32[12,64]{1,0:T(8,128)S(1)} %get-tuple-element.7, f32[64,12]{0,1:T(8,128)S(1)} %bitcast.97, f32[64,12]{0,1:T(8,128)S(1)} %get-tuple-element.6), kind=kOutput, calls=%fused_computation.22 | convolution fusion | flops 407666688 | bytes 12788736 | tf_op jit(solution)/shard_map/hqk,khd->qhd/dot_general | solution.py:43
  351.6 1.0 convert_reduce_fusion
  353.5 3.4 collective-permute-start
  356.9 7.0 %collective-permute-done = bf16[2,4,32,16]{3,2,1,0:T(8,128)(2,1)S(1)} collective-permute-done((bf16[2,4,32,16]{3,2,1,0:T(8,128)(2,1)S(1)}, bf16[2,4,32,16]{3,2,1,0:T(8,128)(2,1)S(1)}, u32[]{:S(2)}, u32[]{:S(2)}) %collective-permute-start) | collective-permute-done | bytes 8224 | tf_op jit(solution)/shard_map/ppermute | solution.py:19
  364.1 1.0 fusion.13
  365.4 0.3 fusion.50
  365.7 2.1 collective-permute-start.1
  367.8 9.7 %collective-permute-done.1 = bf16[2,4,32,384]{3,1,2,0:T(4,128)(2,1)S(1)} collective-permute-done((bf16[2,4,32,384]{3,1,2,0:T(4,128)(2,1)S(1)}, bf16[2,4,32,384]{3,1,2,0:T(4,128)(2,1)S(1)}, u32[]{:S(2)}, u32[]{:S(2)}) %collective-permute-start.1) | collective-permute-done | bytes 196640 | tf_op jit(solution)/shard_map/ppermute | solution.py:19
  378.1 7.0 %convolution_select_fusion.2 = f32[2,4,8,5,384]{4,2,3,1,0:T(8,128)S(1)} fusion(bf16[3,3,3,384,384]{4,3,2,1,0:T(8,128)(2,1)} %param.29, bf16[4,4,1,7,2,384]{5,3,4,1,0,2:T(8,128)(2,1)S(1)} %slice.8, bf16[4,4,1,8,5,384]{5,3,4,1,0,2:T(8,128)(2,1)S(1)} %copy.49, pred[8,5]{0,1:T(8,128)(4,1)S(1)} %copy-done.10), kind=kOutput, calls=%fused_computation.15 | convolution fusion | flops 2125553664 | bytes 9117736 | tf_op jit(solution)/shard_map/conv_general_dilated | solution.py:71
  385.8 1.9 collective-permute-start.2
  387.7 9.9 %collective-permute-done.2 = bf16[2,4,32,384]{3,1,2,0:T(4,128)(2,1)S(1)} collective-permute-done((bf16[2,4,32,384]{3,1,2,0:T(4,128)(2,1)S(1)}, bf16[2,4,32,384]{3,1,2,0:T(4,128)(2,1)S(1)}, u32[]{:S(2)}, u32[]{:S(2)}) %collective-permute-start.2) | collective-permute-done | bytes 196640 | tf_op jit(solution)/shard_map/ppermute | solution.py:19
  398.2 3.7 convolution_select_fusion.1
  402.1 0.7 copy.54
  (63 shorter events, 3.3 us)
Async XLA Ops:
  7.2 356.9 %copy-start = (bf16[3,3,3,16,384]{4,3,2,1,0:T(8,128)(2,1)S(1)}, bf16[3,3,3,16,384]{4,3,2,1,0:T(8,128)(2,1)}, u32[]{:S(2)}) copy-start(bf16[3,3,3,16,384]{4,3,2,1,0:T(8,128)(2,1)} %param.27) | copy-start | bytes 995332
  7.2 164.6 %all-gather.3.cloned.1.call-start = ((), (), s32[]{:S(2)}) async-start(), calls=%async_computation | async-start | bytes 6488064 | tf_op jit(solution)/shard_map/all_gather | solution.py:119
  7.9 327.8 %all-gather.5.cloned.1.call-start = ((), (), s32[]{:S(2)}) async-start(), calls=%async_computation.1 | async-start | bytes 6488064 | tf_op jit(solution)/shard_map/all_gather | solution.py:120
  10.8 169.6 %copy-start.3 = (bf16[64,1536]{1,0:T(8,128)(2,1)S(1)}, bf16[64,1536]{1,0:T(8,128)(2,1)}, u32[]{:S(2)}) copy-start(bf16[64,1536]{1,0:T(8,128)(2,1)} %param.17) | copy-start | bytes 589828
  184.5 2.6 copy-start.1
  335.7 15.9 %slice-start = ((s8[4718592]{0:T(1024)(128)(4,1)}), s8[524288]{0:T(1024)(128)(4,1)S(1)}, s32[]{:S(2)}) async-start(s8[4718592]{0:T(1024)(128)(4,1)} %bitcast.85), calls=%async_computation.2 | async-start | bytes 1048576
  344.4 7.2 %slice-start.1 = ((s8[4718592]{0:T(1024)(128)(4,1)}), s8[4194304]{0:T(1024)(128)(4,1)S(1)}, s32[]{:S(2)}) async-start(s8[4718592]{0:T(1024)(128)(4,1)} %bitcast.85), calls=%async_computation.3 | async-start | bytes 8388608
  344.4 7.2 %copy-start.4 = (bf16[64,1536]{1,0:T(8,128)(2,1)S(1)}, bf16[64,1536]{1,0:T(8,128)(2,1)}, u32[]{:S(2)}) copy-start(bf16[64,1536]{1,0:T(8,128)(2,1)} %param.16) | copy-start | bytes 589828
  344.4 7.2 %copy-start.5 = (f32[1536]{0:T(1024)S(1)}, f32[1536]{0:T(1024)}, u32[]{:S(2)}) copy-start(f32[1536]{0:T(1024)} %param.20) | copy-start | bytes 18436
  344.4 8.5 %copy-start.8 = (bf16[1536,64]{0,1:T(8,128)(2,1)S(1)}, bf16[1536,64]{0,1:T(8,128)(2,1)}, u32[]{:S(2)}) copy-start(bf16[1536,64]{0,1:T(8,128)(2,1)} %param.24) | copy-start | bytes 589828
  344.4 8.5 %copy-start.9 = (f32[1536]{0:T(1024)S(1)}, f32[1536]{0:T(1024)}, u32[]{:S(2)}) copy-start(f32[1536]{0:T(1024)} %param.23) | copy-start | bytes 18436
  351.6 12.5 %copy-start.10 = (pred[8,5]{0,1:T(8,128)(4,1)S(1)}, pred[8,5]{0,1:T(8,128)(4,1)}, u32[]{:S(2)}) copy-start(pred[8,5]{0,1:T(8,128)(4,1)} %constant.43) | copy-start | bytes 124
  351.6 13.8 %copy-start.6 = (f32[384]{0:T(512)S(1)}, f32[384]{0:T(512)}, u32[]{:S(2)}) copy-start(f32[384]{0:T(512)} %param.28) | copy-start | bytes 4612
  352.7 32.5 %copy-start.2 = (bf16[64,1536]{1,0:T(8,128)(2,1)}, bf16[64,1536]{1,0:T(8,128)(2,1)S(1)}, u32[]{:S(2)}) copy-start(bf16[64,1536]{1,0:T(8,128)(2,1)S(1)} %get-tuple-element.11) | copy-start | bytes 589828
  353.5 10.4 %collective-permute-start = (bf16[2,4,32,16]{3,2,1,0:T(8,128)(2,1)S(1)}, bf16[2,4,32,16]{3,2,1,0:T(8,128)(2,1)S(1)}, u32[]{:S(2)}, u32[]{:S(2)}) collective-permute-start(bf16[2,4,32,16]{3,2,1,0:T(8,128)(2,1)S(1)} %subtract_convert_fusion), channel_id=1, source_target_pairs={{0,1},{1,2},{2,3},{3,4},{4,5},{5,6},{6,7},{7,8},{8,9},{9,10},{10,1... | collective-permute-start | bytes 24584 | tf_op jit(solution)/shard_map/ppermute | solution.py:19
  365.7 11.8 %collective-permute-start.1 = (bf16[2,4,32,384]{3,1,2,0:T(4,128)(2,1)S(1)}, bf16[2,4,32,384]{3,1,2,0:T(4,128)(2,1)S(1)}, u32[]{:S(2)}, u32[]{:S(2)}) collective-permute-start(bf16[2,4,32,384]{3,1,2,0:T(4,128)(2,1)S(1)} %fusion.50), channel_id=1, source_target_pairs={{0,1},{1,2},{2,3},{3,4},{4,5},{5,6},{6,7},{7,8},{8,9},{9,10},{10,1... | collective-permute-start | bytes 589832 | tf_op jit(solution)/shard_map/ppermute | solution.py:19
  378.0 20.2 %slice-start.2 = ((s8[7962624]{0:T(1024)(128)(4,1)}), s8[4194304]{0:T(1024)(128)(4,1)S(1)}, s32[]{:S(2)}) async-start(s8[7962624]{0:T(1024)(128)(4,1)} %bitcast.98), calls=%async_computation.4 | async-start | bytes 8388608
  378.1 7.4 %copy-start.7 = (f32[384]{0:T(512)S(1)}, f32[384]{0:T(512)}, u32[]{:S(2)}) copy-start(f32[384]{0:T(512)} %param.30) | copy-start | bytes 4612
  378.1 20.1 %slice-start.3 = ((s8[7962624]{0:T(1024)(128)(4,1)}), s8[3768320]{0:T(1024)(128)(4,1)S(1)}, s32[]{:S(2)}) async-start(s8[7962624]{0:T(1024)(128)(4,1)} %bitcast.98), calls=%async_computation.5 | async-start | bytes 7536640
  385.8 11.8 %collective-permute-start.2 = (bf16[2,4,32,384]{3,1,2,0:T(4,128)(2,1)S(1)}, bf16[2,4,32,384]{3,1,2,0:T(4,128)(2,1)S(1)}, u32[]{:S(2)}, u32[]{:S(2)}) collective-permute-start(bf16[2,4,32,384]{3,1,2,0:T(4,128)(2,1)S(1)} %fusion.52), channel_id=1, source_target_pairs={{0,1},{1,2},{2,3},{3,4},{4,5},{5,6},{6,7},{7,8},{8,9},{9,10},{10,1... | collective-permute-start | bytes 589832 | tf_op jit(solution)/shard_map/ppermute | solution.py:19
Sparse Core Ops, SparseCore 0:
  9.6 162.1 all-gather.2
  173.5 162.2 all-gather.4
where the time goes:
time: 411 us; the launch traced here: 410 us
  waiting for transfers between devices  336 us (82%)
  matrix products  24.2 us (6%)
  local copies, waits for them, and re-layouts  22.8 us (6%)
  between operations  15.1 us (4%)
  starting transfers between devices  7.51 us (2%)
    all_gather x1, waiting for transfers between devices, body(): lax.all_gather(keys, 'frames', axis=0, tiled=True)  161 us
    all_gather x1, waiting for transfers between devices, body(): lax.all_gather(values, 'frames', axis=0, tiled=True)  147 us
    ppermute x3, waiting for transfers between devices, shifted(): return lax.ppermute(x, axis, pairs)  26.5 us
    conv_general_dilated x3, matrix products, spatial_conv(): lax.conv_general_dilated(extended[None], kernel, (1, 1, 1), ((0, 0), (1,...  11.7 us
    all_gather x1, local copies, waits for them, and re-layouts, body(): lax.all_gather(values, 'frames', axis=0, tiled=True)  8.72 us
    all_gather x1, local copies, waits for them, and re-layouts, body(): lax.all_gather(keys, 'frames', axis=0, tiled=True)  8.58 us
  transfers between devices with their start and end apart: 5, of which 5 were waited for; matrix products, arithmetic and copies ran while one was open for 4% of the time, Pallas kernels for 0%

commit v1 on v0

--- a/solution.py
+++ b/solution.py
@@ -3,10 +3,13 @@
 import jax
 import jax.numpy as jnp
 from jax import lax
+from jax.sharding import Mesh
 from jax.sharding import PartitionSpec as P
 
 HEAD_DIM = 128
 HEADS = 12
+HEAD_GROUPS = 4
+FRAMES = ("blk", "hg")
 LAT_C = 16
 PATCH = 2
 TOK_H = 2
@@ -14,7 +17,7 @@
 
 
 def shifted(x, axis, by):
-    peers = lax.axis_size(axis)
+    peers = lax.psum(1, axis)
     pairs = [(i, i + by) for i in range(peers) if 0 <= i + by < peers]
     return lax.ppermute(x, axis, pairs)
 
@@ -80,7 +83,7 @@
 
 
 def causal_conv(activ, kernel):
-    frame_tail = shifted(activ[-2:], "frames", 1)
+    frame_tail = shifted(activ[-2:], FRAMES, 1)
     return spatial_conv(jnp.concatenate([frame_tail, activ], axis=0), kernel)
 
 
@@ -112,16 +115,26 @@
 ):
     rows_here = queries.shape[0]
     full_width = HEADS * HEAD_DIM
-    query_heads = split_heads(queries, HEADS)
+    group_width = full_width // HEAD_GROUPS
+    group_heads = HEADS // HEAD_GROUPS
+
+    def to_group(matrix):
+        parts = matrix.reshape(rows_here, HEAD_GROUPS, group_width)
+        return lax.all_to_all(parts, "hg", 1, 0, tiled=True).reshape(-1, group_width)
+
+    query_heads = split_heads(to_group(queries), group_heads)
+    key_heads = split_heads(lax.all_gather(to_group(keys), "blk", axis=0, tiled=True), group_heads)
+    value_heads = split_heads(
+        lax.all_gather(to_group(values), "blk", axis=0, tiled=True), group_heads
+    )
+    group_rows = query_heads.shape[0]
     row_peak, row_total, summed = absorb_block(
-        empty_state(HEADS, rows_here),
-        query_heads,
-        split_heads(lax.all_gather(keys, "frames", axis=0, tiled=True), HEADS),
-        split_heads(lax.all_gather(values, "frames", axis=0, tiled=True), HEADS),
+        empty_state(group_heads, group_rows), query_heads, key_heads, value_heads
     )
-    attended = (
-        (summed / row_total.T[:, :, None]).reshape(rows_here, full_width).astype(jnp.bfloat16)
+    group_out = (
+        (summed / row_total.T[:, :, None]).reshape(group_rows, group_width).astype(jnp.bfloat16)
     )
+    attended = lax.all_to_all(group_out, "hg", 0, 1, tiled=True)
     projected = jnp.dot(attended, output_weight, preferred_element_type=jnp.float32)
     layer_output = (tokens.astype(jnp.float32) + branch_gate * projected).astype(jnp.bfloat16)
     normed = layer_norm(layer_output, head_scale, head_shift)
@@ -138,23 +151,29 @@
 
 
 def solution(mesh):
+    devices = mesh.devices
+    blocks = devices.shape[1] // HEAD_GROUPS
+    split_mesh = Mesh(devices.reshape(devices.shape[0], blocks, HEAD_GROUPS), ("req",) + FRAMES)
+    rows = P(("req",) + FRAMES, None)
     in_specs = (
-        P(("req", "frames"), None),
-        P(("req", "frames"), None),
-        P(("req", "frames"), None),
-        P(("req", "frames"), None),
+        rows,
+        rows,
+        rows,
+        rows,
         P(),
         P(),
         P(),
         P(),
         P(),
         P("req"),
-        P(("req", "frames"), None, None),
+        P(("req",) + FRAMES, None, None),
         P(),
         P(),
         P(),
         P(),
         P(),
     )
-    out_specs = (P(("req", "frames"), None), P(("req", "frames"), None, None, None))
-    return jax.shard_map(body, mesh=mesh, in_specs=in_specs, out_specs=out_specs, check_vma=False)
+    out_specs = (rows, P(("req",) + FRAMES, None, None, None))
+    return jax.shard_map(
+        body, mesh=split_mesh, in_specs=in_specs, out_specs=out_specs, check_vma=False
+    )

time: 411 us -> 177 us (0.43)
  waiting for transfers between devices: 336 us -> 90.1 us
  blocking collectives: 0 us -> 19.9 us
  local copies, waits for them, and re-layouts: 22.8 us -> 13.6 us
  starting transfers between devices: 7.51 us -> 14.2 us
    all_gather x2, waiting for transfers between devices: 308 us -> 51.5 us  [the longest x1 34.4 us: body(): lax.all_gather(to_group(values), 'blk', axis=0, tiled=True)]
    all_to_all x0 -> x2, blocking collectives: none -> 19.9 us  [to_group(): lax.all_to_all(parts, 'hg', 1, 0, tiled=True).reshape(-1, group_width)]
    all_gather x2, local copies, waits for them, and re-layouts: 17.3 us -> 3.42 us  [the longest x1 1.71 us: body(): lax.all_gather(to_group(keys), 'blk', axis=0, tiled=True)]
    all_to_all x0 -> x2, waiting for transfers between devices: none -> 11.1 us  [the longest x1 6.32 us: body(): attended = lax.all_to_all(group_out, 'hg', 0, 1, tiled=True)]
    all_to_all x0 -> x2, starting transfers between devices: none -> 7.61 us  [the longest x1 4.25 us: body(): attended = lax.all_to_all(group_out, 'hg', 0, 1, tiled=True)]
  transfers between devices with their start and end apart: 5 -> 7, of which waited for: 5 -> 7; matrix products, arithmetic and copies ran while one was open for 4% -> 4% of each run, Pallas kernels for 0% -> 0%
where the time goes in v1:
time: 177 us
  waiting for transfers between devices  90.1 us (51%)
  matrix products  20.7 us (12%)
  blocking collectives  19.9 us (11%)
  between operations  15.2 us (9%)
  starting transfers between devices  14.2 us (8%)
  local copies, waits for them, and re-layouts  13.6 us (8%)
  other arithmetic  3.01 us (2%)
    all_gather x1, waiting for transfers between devices, body(): lax.all_gather(to_group(values), 'blk', axis=0, tiled=True)  34.4 us
    ppermute x3, waiting for transfers between devices, shifted(): return lax.ppermute(x, axis, pairs)  27.4 us
    all_to_all x2, blocking collectives, to_group(): lax.all_to_all(parts, 'hg', 1, 0, tiled=True).reshape(-1, group_width)  19.9 us
    all_gather x1, waiting for transfers between devices, body(): lax.all_gather(to_group(keys), 'blk', axis=0, tiled=True)  17.1 us
    conv_general_dilated x3, matrix products, spatial_conv(): lax.conv_general_dilated(extended[None], kernel, (1, 1, 1), ((0, 0), (1,...  11.7 us
    ppermute x3, starting transfers between devices, shifted(): return lax.ppermute(x, axis, pairs)  6.5 us
    all_to_all x1, waiting for transfers between devices, body(): attended = lax.all_to_all(group_out, 'hg', 0, 1, tiled=True)  6.32 us
    all_to_all x1, waiting for transfers between devices, to_group(): lax.all_to_all(parts, 'hg', 1, 0, tiled=True).reshape(-1, group_width)  4.82 us
  transfers between devices with their start and end apart: 7, of which 7 were waited for; matrix products, arithmetic and copies ran while one was open for 4% of the time, Pallas kernels for 0%

profile of v1, /device:TPU:96, one launch (start us, length us, event | category | flops | bytes accessed | tf_op | source)
XLA Modules:
  0.0 176.7 jit_solution(7403168685070804316)
XLA Ops:
  8.2 10.5 %all_to_all.61 = bf16[64,4,384]{2,0,1:T(8,128)(2,1)} all-to-all(bf16[64,4,384]{2,0,1:T(8,128)(2,1)S(1)} %bitcast.113), channel_id=1, replica_groups=mesh['req'=4,'blk'=8,'hg'=4] {'hg'}, dimensions={1} | all-to-all | bytes 393216 | tf_op jit(solution)/shard_map/all_to_all | solution.py:123
  19.8 9.4 %all_to_all.62 = bf16[64,4,384]{2,0,1:T(8,128)(2,1)} all-to-all(bf16[64,4,384]{2,0,1:T(8,128)(2,1)S(1)} %bitcast.114), channel_id=1, replica_groups=mesh['req'=4,'blk'=8,'hg'=4] {'hg'}, dimensions={1} | all-to-all | bytes 393216 | tf_op jit(solution)/shard_map/all_to_all | solution.py:123
  29.2 1.6 copy.98
  30.8 3.4 %all-to-all-start = ((bf16[64,4,384]{2,0,1:T(8,128)(2,1)}), bf16[64,4,384]{2,0,1:T(8,128)(2,1)S(1)}, u32[]{:S(2)}, u32[]{:S(2)}) async-start(bf16[64,4,384]{2,0,1:T(8,128)(2,1)} %bitcast.96), calls=%async_computation | async-start | bytes 393216 | tf_op jit(solution)/shard_map/all_to_all | solution.py:123
  35.7 4.8 %all-to-all-done = bf16[64,4,384]{2,0,1:T(8,128)(2,1)S(1)} async-done(((bf16[64,4,384]{2,0,1:T(8,128)(2,1)}), bf16[64,4,384]{2,0,1:T(8,128)(2,1)S(1)}, u32[]{:S(2)}, u32[]{:S(2)}) %all-to-all-start) | async-done | bytes 196640 | tf_op jit(solution)/shard_map/all_to_all | solution.py:123
  40.5 17.1 %all-gather.3.cloned.1.call-done = bf16[2048,384]{1,0:T(8,128)(2,1)} async-done(((bf16[256,384]{1,0:T(8,128)(2,1)}), bf16[2048,384]{1,0:T(8,128)(2,1)}) %all-gather.3.cloned.1.call-update) | async-done | bytes 1572880 | tf_op jit(solution)/shard_map/all_gather | solution.py:126
  57.7 1.7 copy.62
  59.4 1.1 multiply_reduce_fusion
  60.5 2.6 %copy-done.1 = f32[3,256,2048]{2,1,0:T(8,128)} copy-done((f32[3,256,2048]{2,1,0:T(8,128)}, f32[3,256,2048]{2,1,0:T(8,128)S(1)}, u32[]{:S(2)}) %copy-start.1) | copy-done | bytes 6291480
  63.1 1.2 fusion
  64.2 34.4 %all-gather.5.cloned.1.call-done = bf16[2048,384]{1,0:T(8,128)(2,1)} async-done(((bf16[256,384]{1,0:T(8,128)(2,1)}), bf16[2048,384]{1,0:T(8,128)(2,1)}) %all-gather.5.cloned.1.call-update) | async-done | bytes 1572880 | tf_op jit(solution)/shard_map/all_gather | solution.py:128
  98.6 1.7 copy.66
  100.4 4.2 %fusion.20 = bf16[256,3,128]{2,0,1:T(8,128)(2,1)S(1)} fusion(bf16[2048,3,128]{0,2,1:T(8,128)(2,1)S(1)} %bitcast.107, f32[3,256,2048]{2,1,0:T(8,128)} %copy-done.1, f32[3,256]{1,0:T(4,128)S(1)} %get-tuple-element.9, f32[256,3]{0,1:T(4,128)S(1)} %bitcast.120, f32[256,3]{0,1:T(4,128)S(1)} %get-tuple-element.8), kind=kOutput, calls=%fused_computation.21 | convolution fusion | flops 407666688 | bytes 8070144 | tf_op jit(solution)/shard_map/hqk,khd->qhd/dot_general | solution.py:46
  105.7 4.2 %all-to-all-start.3 = ((bf16[4,64,384]{2,1,0:T(8,128)(2,1)}), bf16[4,64,384]{2,1,0:T(8,128)(2,1)S(1)}, u32[]{:S(2)}, u32[]{:S(2)}) async-start(bf16[4,64,384]{2,1,0:T(8,128)(2,1)} %convert_element_type.48), calls=%async_computation.3 | async-start | bytes 393216 | tf_op jit(solution)/shard_map/all_to_all | solution.py:137
  109.9 6.3 %all-to-all-done.3 = bf16[4,64,384]{2,1,0:T(8,128)(2,1)S(1)} async-done(((bf16[4,64,384]{2,1,0:T(8,128)(2,1)}), bf16[4,64,384]{2,1,0:T(8,128)(2,1)S(1)}, u32[]{:S(2)}, u32[]{:S(2)}) %all-to-all-start.3) | async-done | bytes 196640 | tf_op jit(solution)/shard_map/all_to_all | solution.py:137
  116.3 3.4 %convert_reduce_fusion = (f32[64]{0:T(128)S(1)}, bf16[64,1536]{1,0:T(8,128)(2,1)S(1)}) fusion(bf16[64,1536]{1,0:T(8,128)(2,1)S(1)} %bitcast.108, bf16[1536,1536]{1,0:T(8,128)(2,1)} %param.21, f32[1536]{0:T(1024)S(1)} %copy-done.4, bf16[64,1536]{1,0:T(8,128)(2,1)S(1)} %copy-done.3), kind=kOutput, calls=%fused_computation.36 | convolution fusion | flops 302579648 | bytes 5314816 | tf_op jit(solution)/shard_map/dot_general | solution.py:138
  120.5 2.5 %collective-permute-start = (bf16[2,4,32,16]{3,2,1,0:T(8,128)(2,1)S(1)}, bf16[2,4,32,16]{3,2,1,0:T(8,128)(2,1)S(1)}, u32[]{:S(2)}, u32[]{:S(2)}) collective-permute-start(bf16[2,4,32,16]{3,2,1,0:T(8,128)(2,1)S(1)} %subtract_convert_fusion), channel_id=1, source_target_pairs={{0,1},{1,2},{2,3},{3,4},{4,5},{5,6},{6,7},{7,8},{8,9},{9,10},{10,1... | collective-permute-start | bytes 24584 | tf_op jit(solution)/shard_map/ppermute | solution.py:22
  123.0 7.9 %collective-permute-done = bf16[2,4,32,16]{3,2,1,0:T(8,128)(2,1)S(1)} collective-permute-done((bf16[2,4,32,16]{3,2,1,0:T(8,128)(2,1)S(1)}, bf16[2,4,32,16]{3,2,1,0:T(8,128)(2,1)S(1)}, u32[]{:S(2)}, u32[]{:S(2)}) %collective-permute-start) | collective-permute-done | bytes 8224 | tf_op jit(solution)/shard_map/ppermute | solution.py:22
  132.7 2.1 %collective-permute-start.1 = (bf16[2,4,32,384]{3,1,2,0:T(4,128)(2,1)S(1)}, bf16[2,4,32,384]{3,1,2,0:T(4,128)(2,1)S(1)}, u32[]{:S(2)}, u32[]{:S(2)}) collective-permute-start(bf16[2,4,32,384]{3,1,2,0:T(4,128)(2,1)S(1)} %fusion.47), channel_id=1, source_target_pairs={{0,1},{1,2},{2,3},{3,4},{4,5},{5,6},{6,7},{7,8},{8,9},{9,10},{10,1... | collective-permute-start | bytes 589832 | tf_op jit(solution)/shard_map/ppermute | solution.py:22
  134.8 9.7 %collective-permute-done.1 = bf16[2,4,32,384]{3,1,2,0:T(4,128)(2,1)S(1)} collective-permute-done((bf16[2,4,32,384]{3,1,2,0:T(4,128)(2,1)S(1)}, bf16[2,4,32,384]{3,1,2,0:T(4,128)(2,1)S(1)}, u32[]{:S(2)}, u32[]{:S(2)}) %collective-permute-start.1) | collective-permute-done | bytes 196640 | tf_op jit(solution)/shard_map/ppermute | solution.py:22
  145.1 7.0 %convolution_select_fusion.2 = f32[2,4,8,5,384]{4,2,3,1,0:T(8,128)S(1)} fusion(bf16[3,3,3,384,384]{4,3,2,1,0:T(8,128)(2,1)} %param.29, bf16[4,4,1,7,2,384]{5,3,4,1,0,2:T(8,128)(2,1)S(1)} %slice.8, bf16[4,4,1,8,5,384]{5,3,4,1,0,2:T(8,128)(2,1)S(1)} %copy.76, pred[8,5]{0,1:T(8,128)(4,1)S(1)} %copy-done.10), kind=kOutput, calls=%fused_computation.15 | convolution fusion | flops 2125553664 | bytes 9117736 | tf_op jit(solution)/shard_map/conv_general_dilated | solution.py:74
  152.8 1.9 %collective-permute-start.2 = (bf16[2,4,32,384]{3,1,2,0:T(4,128)(2,1)S(1)}, bf16[2,4,32,384]{3,1,2,0:T(4,128)(2,1)S(1)}, u32[]{:S(2)}, u32[]{:S(2)}) collective-permute-start(bf16[2,4,32,384]{3,1,2,0:T(4,128)(2,1)S(1)} %fusion.49), channel_id=1, source_target_pairs={{0,1},{1,2},{2,3},{3,4},{4,5},{5,6},{6,7},{7,8},{8,9},{9,10},{10,1... | collective-permute-start | bytes 589832 | tf_op jit(solution)/shard_map/ppermute | solution.py:22
  154.7 9.9 %collective-permute-done.2 = bf16[2,4,32,384]{3,1,2,0:T(4,128)(2,1)S(1)} collective-permute-done((bf16[2,4,32,384]{3,1,2,0:T(4,128)(2,1)S(1)}, bf16[2,4,32,384]{3,1,2,0:T(4,128)(2,1)S(1)}, u32[]{:S(2)}, u32[]{:S(2)}) %collective-permute-start.2) | collective-permute-done | bytes 196640 | tf_op jit(solution)/shard_map/ppermute | solution.py:22
  165.2 3.7 %convolution_select_fusion.1 = f32[2,4,8,5,384]{4,2,3,1,0:T(8,128)S(1)} fusion(bf16[3,3,3,384,384]{4,3,2,1,0:T(8,128)(2,1)S(1)} %bitcast.122, bf16[4,4,1,7,2,384]{5,3,4,1,0,2:T(8,128)(2,1)S(1)} %slice.10, bf16[4,4,1,8,5,384]{5,3,4,1,0,2:T(8,128)(2,1)S(1)} %copy.79, pred[8,5]{0,1:T(8,128)(4,1)S(1)} %copy-done.10), kind=kOutput, calls=%fused_computation.14 | convolution fusion | flops 2125553664 | bytes 9117736 | tf_op jit(solution)/shard_map/conv_general_dilated | solution.py:74
  (71 shorter events, 9.2 us)
Async XLA Ops:
  7.2 123.9 %copy-start = (bf16[3,3,3,16,384]{4,3,2,1,0:T(8,128)(2,1)S(1)}, bf16[3,3,3,16,384]{4,3,2,1,0:T(8,128)(2,1)}, u32[]{:S(2)}) copy-start(bf16[3,3,3,16,384]{4,3,2,1,0:T(8,128)(2,1)} %param.27) | copy-start | bytes 995332
  7.2 50.5 %all-gather.3.cloned.1.call-start = ((), (), s32[]{:S(2)}) async-start(), calls=%async_computation.4 | async-start | bytes 1769472 | tf_op jit(solution)/shard_map/all_gather | solution.py:126
  18.8 79.9 %all-gather.5.cloned.1.call-start = ((), (), s32[]{:S(2)}) async-start(), calls=%async_computation.5 | async-start | bytes 1769472 | tf_op jit(solution)/shard_map/all_gather | solution.py:128
  30.8 9.7 %all-to-all-start = ((bf16[64,4,384]{2,0,1:T(8,128)(2,1)}), bf16[64,4,384]{2,0,1:T(8,128)(2,1)S(1)}, u32[]{:S(2)}, u32[]{:S(2)}) async-start(bf16[64,4,384]{2,0,1:T(8,128)(2,1)} %bitcast.96), calls=%async_computation | async-start | bytes 393216 | tf_op jit(solution)/shard_map/all_to_all | solution.py:123
  60.4 2.7 %copy-start.1 = (f32[3,256,2048]{2,1,0:T(8,128)}, f32[3,256,2048]{2,1,0:T(8,128)S(1)}, u32[]{:S(2)}) copy-start(f32[3,256,2048]{2,1,0:T(8,128)S(1)} %get-tuple-element.11) | copy-start | bytes 18874372
  100.3 9.6 %copy-start.5 = (f32[1536]{0:T(1024)S(1)}, f32[1536]{0:T(1024)}, u32[]{:S(2)}) copy-start(f32[1536]{0:T(1024)} %param.22) | copy-start | bytes 18436
  100.3 15.9 %copy-start.3 = (bf16[64,1536]{1,0:T(8,128)(2,1)S(1)}, bf16[64,1536]{1,0:T(8,128)(2,1)}, u32[]{:S(2)}) copy-start(bf16[64,1536]{1,0:T(8,128)(2,1)} %param.16) | copy-start | bytes 589828
  100.4 15.9 %copy-start.4 = (f32[1536]{0:T(1024)S(1)}, f32[1536]{0:T(1024)}, u32[]{:S(2)}) copy-start(f32[1536]{0:T(1024)} %param.20) | copy-start | bytes 18436
  104.6 15.3 %copy-start.8 = (bf16[1536,64]{0,1:T(8,128)(2,1)S(1)}, bf16[1536,64]{0,1:T(8,128)(2,1)}, u32[]{:S(2)}) copy-start(bf16[1536,64]{0,1:T(8,128)(2,1)} %param.24) | copy-start | bytes 589828
  104.6 15.3 %copy-start.9 = (f32[1536]{0:T(1024)S(1)}, f32[1536]{0:T(1024)}, u32[]{:S(2)}) copy-start(f32[1536]{0:T(1024)} %param.23) | copy-start | bytes 18436
  104.8 26.3 %copy-start.10 = (pred[8,5]{0,1:T(8,128)(4,1)S(1)}, pred[8,5]{0,1:T(8,128)(4,1)}, u32[]{:S(2)}) copy-start(pred[8,5]{0,1:T(8,128)(4,1)} %constant.43) | copy-start | bytes 124
  105.7 10.6 %all-to-all-start.3 = ((bf16[4,64,384]{2,1,0:T(8,128)(2,1)}), bf16[4,64,384]{2,1,0:T(8,128)(2,1)S(1)}, u32[]{:S(2)}, u32[]{:S(2)}) async-start(bf16[4,64,384]{2,1,0:T(8,128)(2,1)} %convert_element_type.48), calls=%async_computation.3 | async-start | bytes 393216 | tf_op jit(solution)/shard_map/all_to_all | solution.py:137
  119.7 25.4 %copy-start.2 = (bf16[64,1536]{1,0:T(8,128)(2,1)}, bf16[64,1536]{1,0:T(8,128)(2,1)S(1)}, u32[]{:S(2)}) copy-start(bf16[64,1536]{1,0:T(8,128)(2,1)S(1)} %get-tuple-element.13) | copy-start | bytes 589828
  119.7 12.7 %copy-start.6 = (f32[384]{0:T(512)S(1)}, f32[384]{0:T(512)}, u32[]{:S(2)}) copy-start(f32[384]{0:T(512)} %param.28) | copy-start | bytes 4612
  120.5 10.4 %collective-permute-start = (bf16[2,4,32,16]{3,2,1,0:T(8,128)(2,1)S(1)}, bf16[2,4,32,16]{3,2,1,0:T(8,128)(2,1)S(1)}, u32[]{:S(2)}, u32[]{:S(2)}) collective-permute-start(bf16[2,4,32,16]{3,2,1,0:T(8,128)(2,1)S(1)} %subtract_convert_fusion), channel_id=1, source_target_pairs={{0,1},{1,2},{2,3},{3,4},{4,5},{5,6},{6,7},{7,8},{8,9},{9,10},{10,1... | collective-permute-start | bytes 24584 | tf_op jit(solution)/shard_map/ppermute | solution.py:22
  132.7 11.8 %collective-permute-start.1 = (bf16[2,4,32,384]{3,1,2,0:T(4,128)(2,1)S(1)}, bf16[2,4,32,384]{3,1,2,0:T(4,128)(2,1)S(1)}, u32[]{:S(2)}, u32[]{:S(2)}) collective-permute-start(bf16[2,4,32,384]{3,1,2,0:T(4,128)(2,1)S(1)} %fusion.47), channel_id=1, source_target_pairs={{0,1},{1,2},{2,3},{3,4},{4,5},{5,6},{6,7},{7,8},{8,9},{9,10},{10,1... | collective-permute-start | bytes 589832 | tf_op jit(solution)/shard_map/ppermute | solution.py:22
  145.0 20.2 %slice-start = ((s8[7962624]{0:T(1024)(128)(4,1)}), s8[4194304]{0:T(1024)(128)(4,1)S(1)}, s32[]{:S(2)}) async-start(s8[7962624]{0:T(1024)(128)(4,1)} %bitcast.121), calls=%async_computation.6 | async-start | bytes 8388608
  145.1 7.4 %copy-start.7 = (f32[384]{0:T(512)S(1)}, f32[384]{0:T(512)}, u32[]{:S(2)}) copy-start(f32[384]{0:T(512)} %param.30) | copy-start | bytes 4612
  145.1 20.0 %slice-start.1 = ((s8[7962624]{0:T(1024)(128)(4,1)}), s8[3768320]{0:T(1024)(128)(4,1)S(1)}, s32[]{:S(2)}) async-start(s8[7962624]{0:T(1024)(128)(4,1)} %bitcast.121), calls=%async_computation.7 | async-start | bytes 7536640
  152.8 11.8 %collective-permute-start.2 = (bf16[2,4,32,384]{3,1,2,0:T(4,128)(2,1)S(1)}, bf16[2,4,32,384]{3,1,2,0:T(4,128)(2,1)S(1)}, u32[]{:S(2)}, u32[]{:S(2)}) collective-permute-start(bf16[2,4,32,384]{3,1,2,0:T(4,128)(2,1)S(1)} %fusion.49), channel_id=1, source_target_pairs={{0,1},{1,2},{2,3},{3,4},{4,5},{5,6},{6,7},{7,8},{8,9},{9,10},{10,1... | collective-permute-start | bytes 589832 | tf_op jit(solution)/shard_map/ppermute | solution.py:22
Sparse Core Ops, SparseCore 0:
  18.9 38.7 all-gather.2
  59.3 39.2 all-gather.4

commit v2 on v1

--- a/solution.py
+++ b/solution.py
@@ -122,11 +122,19 @@
         parts = matrix.reshape(rows_here, HEAD_GROUPS, group_width)
         return lax.all_to_all(parts, "hg", 1, 0, tiled=True).reshape(-1, group_width)
 
+    def gather_group(matrix):
+        blocks = lax.psum(1, "blk")
+        parts = matrix.reshape(rows_here, -1, HEAD_GROUPS, group_width)
+        parts = jnp.moveaxis(parts, 2, 0)
+        sent = jnp.broadcast_to(parts[None], (blocks,) + parts.shape)
+        sent = sent.reshape((blocks * HEAD_GROUPS,) + parts.shape[1:])
+        got = lax.all_to_all(sent, FRAMES, 0, 0, tiled=True)
+        return got.reshape((-1,) + got.shape[2:])
+
     query_heads = split_heads(to_group(queries), group_heads)
-    key_heads = split_heads(lax.all_gather(to_group(keys), "blk", axis=0, tiled=True), group_heads)
-    value_heads = split_heads(
-        lax.all_gather(to_group(values), "blk", axis=0, tiled=True), group_heads
-    )
+    key_value = gather_group(jnp.stack([keys, values], axis=1))
+    key_heads = split_heads(key_value[:, 0], group_heads)
+    value_heads = split_heads(key_value[:, 1], group_heads)
     group_rows = query_heads.shape[0]
     row_peak, row_total, summed = absorb_block(
         empty_state(group_heads, group_rows), query_heads, key_heads, value_heads

time: 177 us -> 133 us (0.75)
  blocking collectives: 19.9 us -> 0 us
  waiting for transfers between devices: 90.1 us -> 72.2 us
  between operations: 15.2 us -> 1.82 us
  starting transfers between devices: 14.2 us -> 22.3 us
  matrix products: 20.7 us -> 18.6 us
    all_gather x2 -> x0, waiting for transfers between devices: 51.5 us -> none  [the longest x1 34.4 us: body(): lax.all_gather(to_group(values), 'blk', axis=0, tiled=True)]
    all_to_all x0 -> x1, waiting for transfers between devices: none -> 34.4 us  [gather_group(): got = lax.all_to_all(sent, FRAMES, 0, 0, tiled=True)]
    all_to_all x2 -> x0, blocking collectives: 19.9 us -> none  [to_group(): lax.all_to_all(parts, 'hg', 1, 0, tiled=True).reshape(-1, group_width)]
    all_to_all x0 -> x1, starting transfers between devices: none -> 6.7 us  [gather_group(): got = lax.all_to_all(sent, FRAMES, 0, 0, tiled=True)]
    all_gather x2 -> x0, local copies, waits for them, and re-layouts: 3.42 us -> none  [the longest x1 1.71 us: body(): lax.all_gather(to_group(keys), 'blk', axis=0, tiled=True)]
    dot_general x1, matrix products: 4.23 us -> 1.19 us  [absorb_block(): jnp.einsum('hqk,khd->qhd', weights.astype(jnp.bfloat16), value_heads, pre...]
    slice x0 -> x3, local copies, waits for them, and re-layouts: none -> 2.71 us  [the longest x1 1.65 us: body(): value_heads = split_heads(key_value[:, 1], group_heads)]
    unnamed x28 -> x34, local copies, waits for them, and re-layouts: 3.49 us -> 1.21 us
  transfers between devices with their start and end apart: 7 -> 6, of which waited for: 7 -> 6; matrix products, arithmetic and copies ran while one was open for 4% -> 4% of each run, Pallas kernels for 0% -> 0%
where the time goes in v2:
time: 133 us
  waiting for transfers between devices  72.2 us (54%)
  starting transfers between devices  22.3 us (17%)
  matrix products  18.6 us (14%)
  local copies, waits for them, and re-layouts  14.8 us (11%)
  other arithmetic  3.17 us (2%)
  between operations  1.82 us (1%)
    all_to_all x1, waiting for transfers between devices, gather_group(): got = lax.all_to_all(sent, FRAMES, 0, 0, tiled=True)  34.4 us
    ppermute x3, waiting for transfers between devices, shifted(): return lax.ppermute(x, axis, pairs)  27.4 us
    conv_general_dilated x3, matrix products, spatial_conv(): lax.conv_general_dilated(extended[None], kernel, (1, 1, 1), ((0, 0), (1,...  11.7 us
    all_to_all x1, starting transfers between devices, gather_group(): got = lax.all_to_all(sent, FRAMES, 0, 0, tiled=True)  6.7 us
    ppermute x3, starting transfers between devices, shifted(): return lax.ppermute(x, axis, pairs)  6.49 us
    all_to_all x1, waiting for transfers between devices, body(): attended = lax.all_to_all(group_out, 'hg', 0, 1, tiled=True)  6.32 us
    all_to_all x1, starting transfers between devices, body(): attended = lax.all_to_all(group_out, 'hg', 0, 1, tiled=True)  4.79 us
    all_to_all x1, starting transfers between devices, to_group(): lax.all_to_all(parts, 'hg', 1, 0, tiled=True).reshape(-1, group_width)  4.29 us
  transfers between devices with their start and end apart: 6, of which 6 were waited for; matrix products, arithmetic and copies ran while one was open for 4% of the time, Pallas kernels for 0%

profile of v2, /device:TPU:96, one launch (start us, length us, event | category | flops | bytes accessed | tf_op | source)
XLA Modules:
  0.0 132.9 jit_solution(1265672073716070081)
XLA Ops:
  0.6 1.7 %copy.73 = bf16[8,4,8,384]{3,2,0,1:T(8,128)(2,1)} copy(bf16[8,4,8,384]{3,2,1,0:T(8,128)(2,1)} %bitcast.119) | data formatting | bytes 393216 | tf_op jit(solution)/shard_map/reshape | solution.py:122
  2.3 4.3 %all-to-all-start.1 = ((bf16[64,4,384]{2,0,1:T(8,128)(2,1)}), bf16[64,4,384]{2,0,1:T(8,128)(2,1)S(1)}, u32[]{:S(2)}, u32[]{:S(2)}) async-start(bf16[64,4,384]{2,0,1:T(8,128)(2,1)} %bitcast.100), calls=%async_computation.1 | async-start | bytes 393216 | tf_op jit(solution)/shard_map/all_to_all | solution.py:123
  7.6 1.0 stack.9
  8.9 4.0 %all-to-all-done.1 = bf16[64,4,384]{2,0,1:T(8,128)(2,1)S(1)} async-done(((bf16[64,4,384]{2,0,1:T(8,128)(2,1)}), bf16[64,4,384]{2,0,1:T(8,128)(2,1)S(1)}, u32[]{:S(2)}, u32[]{:S(2)}) %all-to-all-start.1) | async-done | bytes 196640 | tf_op jit(solution)/shard_map/all_to_all | solution.py:123
  12.9 2.1 %broadcast_in_dim.13 = bf16[8,4,64,2,384]{4,2,3,1,0:T(8,128)(2,1)} broadcast(bf16[4,64,2,384]{3,1,2,0:T(8,128)(2,1)S(1)} %copy.41), dimensions={1,2,3,4} | broadcast | bytes 3538944 | tf_op jit(solution)/shard_map/broadcast_in_dim | solution.py:129
  15.1 6.7 %all-to-all-start = ((bf16[32,64,2,384]{3,1,2,0:T(8,128)(2,1)}), bf16[32,64,2,384]{3,1,2,0:T(8,128)(2,1)S(1)}, u32[]{:S(2)}, u32[]{:S(2)}) async-start(bf16[32,64,2,384]{3,1,2,0:T(8,128)(2,1)} %bitcast.102), calls=%async_computation | async-start | bytes 6291456 | tf_op jit(solution)/shard_map/all_to_all | solution.py:131
  23.2 1.7 %reshape_reshape.3 = bf16[256,3,128]{2,1,0:T(4,128)(2,1)} reshape(bf16[4,64,1,384]{3,1,0,2:T(8,128)(2,1)} %bitcast.115) | data formatting | bytes 393216 | tf_op jit(solution)/shard_map/reshape;reshape | solution.py:26
  24.9 34.4 %all-to-all-done = bf16[32,64,2,384]{3,1,2,0:T(8,128)(2,1)S(1)} async-done(((bf16[32,64,2,384]{3,1,2,0:T(8,128)(2,1)}), bf16[32,64,2,384]{3,1,2,0:T(8,128)(2,1)S(1)}, u32[]{:S(2)}, u32[]{:S(2)}) %all-to-all-start) | async-done | bytes 3145760 | tf_op jit(solution)/shard_map/all_to_all | solution.py:131
  60.0 1.6 %copy.47 = bf16[2048,1,384]{0,2,1:T(8,128)(2,1)} copy(bf16[2048,1,384]{2,0,1:T(8,128)(2,1)S(1)} %get-tuple-element.7) | data formatting | bytes 3145728 | tf_op jit(solution)/shard_map/slice | solution.py:137
  62.4 2.0 %bitcast_reduce_fusion = (f32[3,256]{1,0:T(4,128)S(1)}, f32[3,2048,256]{2,1,0:T(8,128)S(1)}) fusion(bf16[2048,3,128]{0,2,1:T(8,128)(2,1)S(1)} %bitcast.104, bf16[256,3,128]{2,1,0:T(4,128)(2,1)} %reshape_reshape.3), kind=kOutput, calls=%fused_computation.1 | convolution fusion | flops 405798144 | bytes 8064000 | tf_op jit(solution)/shard_map/qhd,khd->hqk/dot_general | solution.py:39
  64.5 1.0 fusion.1
  65.8 1.2 fusion.21
  68.1 4.8 %all-to-all-start.2 = ((bf16[4,64,384]{2,1,0:T(8,128)(2,1)}), bf16[4,64,384]{2,1,0:T(8,128)(2,1)S(1)}, u32[]{:S(2)}, u32[]{:S(2)}) async-start(bf16[4,64,384]{2,1,0:T(8,128)(2,1)} %convert_element_type.48), calls=%async_computation.2 | async-start | bytes 393216 | tf_op jit(solution)/shard_map/all_to_all | solution.py:145
  72.9 6.3 %all-to-all-done.2 = bf16[4,64,384]{2,1,0:T(8,128)(2,1)S(1)} async-done(((bf16[4,64,384]{2,1,0:T(8,128)(2,1)}), bf16[4,64,384]{2,1,0:T(8,128)(2,1)S(1)}, u32[]{:S(2)}, u32[]{:S(2)}) %all-to-all-start.2) | async-done | bytes 196640 | tf_op jit(solution)/shard_map/all_to_all | solution.py:145
  79.3 3.4 %convert_reduce_fusion = (f32[64]{0:T(128)S(1)}, bf16[64,1536]{1,0:T(8,128)(2,1)S(1)}) fusion(bf16[64,1536]{1,0:T(8,128)(2,1)S(1)} %bitcast.114, bf16[1536,1536]{1,0:T(8,128)(2,1)} %param.21, f32[1536]{0:T(1024)S(1)} %copy-done.7, bf16[64,1536]{1,0:T(8,128)(2,1)S(1)} %copy-done.5), kind=kOutput, calls=%fused_computation.37 | convolution fusion | flops 302579648 | bytes 5314816 | tf_op jit(solution)/shard_map/dot_general | solution.py:146
  83.5 2.5 %collective-permute-start = (bf16[2,4,32,16]{3,2,1,0:T(8,128)(2,1)S(1)}, bf16[2,4,32,16]{3,2,1,0:T(8,128)(2,1)S(1)}, u32[]{:S(2)}, u32[]{:S(2)}) collective-permute-start(bf16[2,4,32,16]{3,2,1,0:T(8,128)(2,1)S(1)} %subtract_convert_fusion), channel_id=1, source_target_pairs={{0,1},{1,2},{2,3},{3,4},{4,5},{5,6},{6,7},{7,8},{8,9},{9,10},{10,1... | collective-permute-start | bytes 24584 | tf_op jit(solution)/shard_map/ppermute | solution.py:22
  86.0 7.9 %collective-permute-done = bf16[2,4,32,16]{3,2,1,0:T(8,128)(2,1)S(1)} collective-permute-done((bf16[2,4,32,16]{3,2,1,0:T(8,128)(2,1)S(1)}, bf16[2,4,32,16]{3,2,1,0:T(8,128)(2,1)S(1)}, u32[]{:S(2)}, u32[]{:S(2)}) %collective-permute-start) | collective-permute-done | bytes 8224 | tf_op jit(solution)/shard_map/ppermute | solution.py:22
  94.1 1.0 fusion.14
  95.8 2.1 %collective-permute-start.1 = (bf16[2,4,32,384]{3,1,2,0:T(4,128)(2,1)S(1)}, bf16[2,4,32,384]{3,1,2,0:T(4,128)(2,1)S(1)}, u32[]{:S(2)}, u32[]{:S(2)}) collective-permute-start(bf16[2,4,32,384]{3,1,2,0:T(4,128)(2,1)S(1)} %fusion.48), channel_id=1, source_target_pairs={{0,1},{1,2},{2,3},{3,4},{4,5},{5,6},{6,7},{7,8},{8,9},{9,10},{10,1... | collective-permute-start | bytes 589832 | tf_op jit(solution)/shard_map/ppermute | solution.py:22
  97.9 9.7 %collective-permute-done.1 = bf16[2,4,32,384]{3,1,2,0:T(4,128)(2,1)S(1)} collective-permute-done((bf16[2,4,32,384]{3,1,2,0:T(4,128)(2,1)S(1)}, bf16[2,4,32,384]{3,1,2,0:T(4,128)(2,1)S(1)}, u32[]{:S(2)}, u32[]{:S(2)}) %collective-permute-start.1) | collective-permute-done | bytes 196640 | tf_op jit(solution)/shard_map/ppermute | solution.py:22
  108.2 7.0 %convolution_select_fusion.2 = f32[2,4,8,5,384]{4,2,3,1,0:T(8,128)S(1)} fusion(bf16[3,3,3,384,384]{4,3,2,1,0:T(8,128)(2,1)} %param.29, bf16[4,4,1,7,2,384]{5,3,4,1,0,2:T(8,128)(2,1)S(1)} %slice.18, bf16[4,4,1,8,5,384]{5,3,4,1,0,2:T(8,128)(2,1)S(1)} %copy.57, pred[8,5]{0,1:T(8,128)(4,1)S(1)} %copy-done.13), kind=kOutput, calls=%fused_computation.16 | convolution fusion | flops 2125553664 | bytes 9117736 | tf_op jit(solution)/shard_map/conv_general_dilated | solution.py:74
  115.8 1.9 %collective-permute-start.2 = (bf16[2,4,32,384]{3,1,2,0:T(4,128)(2,1)S(1)}, bf16[2,4,32,384]{3,1,2,0:T(4,128)(2,1)S(1)}, u32[]{:S(2)}, u32[]{:S(2)}) collective-permute-start(bf16[2,4,32,384]{3,1,2,0:T(4,128)(2,1)S(1)} %fusion.50), channel_id=1, source_target_pairs={{0,1},{1,2},{2,3},{3,4},{4,5},{5,6},{6,7},{7,8},{8,9},{9,10},{10,1... | collective-permute-start | bytes 589832 | tf_op jit(solution)/shard_map/ppermute | solution.py:22
  117.8 9.9 %collective-permute-done.2 = bf16[2,4,32,384]{3,1,2,0:T(4,128)(2,1)S(1)} collective-permute-done((bf16[2,4,32,384]{3,1,2,0:T(4,128)(2,1)S(1)}, bf16[2,4,32,384]{3,1,2,0:T(4,128)(2,1)S(1)}, u32[]{:S(2)}, u32[]{:S(2)}) %collective-permute-start.2) | collective-permute-done | bytes 196640 | tf_op jit(solution)/shard_map/ppermute | solution.py:22
  128.2 3.7 %convolution_select_fusion.1 = f32[2,4,8,5,384]{4,2,3,1,0:T(8,128)S(1)} fusion(bf16[3,3,3,384,384]{4,3,2,1,0:T(8,128)(2,1)S(1)} %bitcast.122, bf16[4,4,1,7,2,384]{5,3,4,1,0,2:T(8,128)(2,1)S(1)} %slice.20, bf16[4,4,1,8,5,384]{5,3,4,1,0,2:T(8,128)(2,1)S(1)} %copy.60, pred[8,5]{0,1:T(8,128)(4,1)S(1)} %copy-done.13), kind=kOutput, calls=%fused_computation.15 | convolution fusion | flops 2125553664 | bytes 9117736 | tf_op jit(solution)/shard_map/conv_general_dilated | solution.py:74
  (76 shorter events, 9.1 us)
Async XLA Ops:
  0.6 93.5 %copy-start = (bf16[3,3,3,16,384]{4,3,2,1,0:T(8,128)(2,1)S(1)}, bf16[3,3,3,16,384]{4,3,2,1,0:T(8,128)(2,1)}, u32[]{:S(2)}) copy-start(bf16[3,3,3,16,384]{4,3,2,1,0:T(8,128)(2,1)} %param.27) | copy-start | bytes 995332
  2.3 10.6 %all-to-all-start.1 = ((bf16[64,4,384]{2,0,1:T(8,128)(2,1)}), bf16[64,4,384]{2,0,1:T(8,128)(2,1)S(1)}, u32[]{:S(2)}, u32[]{:S(2)}) async-start(bf16[64,4,384]{2,0,1:T(8,128)(2,1)} %bitcast.100), calls=%async_computation.1 | async-start | bytes 393216 | tf_op jit(solution)/shard_map/all_to_all | solution.py:123
  8.9 12.9 %copy-start.6 = (f32[2,4,512]{2,1,0:T(4,128)S(1)}, f32[2,4,512]{2,1,0:T(4,128)}, u32[]{:S(2)}) copy-start(f32[2,4,512]{2,1,0:T(4,128)} %param.26) | copy-start | bytes 49156
  12.9 2.1 %copy-start.3 = (bf16[64,4,384]{2,0,1:T(8,128)(2,1)}, bf16[64,4,384]{2,0,1:T(8,128)(2,1)S(1)}, u32[]{:S(2)}) copy-start(bf16[64,4,384]{2,0,1:T(8,128)(2,1)S(1)} %all-to-all-done.1) | copy-start | bytes 589828
  15.1 44.2 %all-to-all-start = ((bf16[32,64,2,384]{3,1,2,0:T(8,128)(2,1)}), bf16[32,64,2,384]{3,1,2,0:T(8,128)(2,1)S(1)}, u32[]{:S(2)}, u32[]{:S(2)}) async-start(bf16[32,64,2,384]{3,1,2,0:T(8,128)(2,1)} %bitcast.102), calls=%async_computation | async-start | bytes 6291456 | tf_op jit(solution)/shard_map/all_to_all | solution.py:131
  64.4 1.4 %copy-start.1 = (bf16[2048,1,384]{0,2,1:T(8,128)(2,1)S(1)}, bf16[2048,1,384]{0,2,1:T(8,128)(2,1)}, u32[]{:S(2)}) copy-start(bf16[2048,1,384]{0,2,1:T(8,128)(2,1)} %copy.47) | copy-start | bytes 4718596
  65.8 7.1 %copy-start.8 = (f32[1536]{0:T(1024)S(1)}, f32[1536]{0:T(1024)}, u32[]{:S(2)}) copy-start(f32[1536]{0:T(1024)} %param.22) | copy-start | bytes 18436
  65.8 13.4 %copy-start.5 = (bf16[64,1536]{1,0:T(8,128)(2,1)S(1)}, bf16[64,1536]{1,0:T(8,128)(2,1)}, u32[]{:S(2)}) copy-start(bf16[64,1536]{1,0:T(8,128)(2,1)} %param.16) | copy-start | bytes 589828
  65.8 13.4 %copy-start.7 = (f32[1536]{0:T(1024)S(1)}, f32[1536]{0:T(1024)}, u32[]{:S(2)}) copy-start(f32[1536]{0:T(1024)} %param.20) | copy-start | bytes 18436
  67.0 15.9 %copy-start.11 = (bf16[1536,64]{0,1:T(8,128)(2,1)S(1)}, bf16[1536,64]{0,1:T(8,128)(2,1)}, u32[]{:S(2)}) copy-start(bf16[1536,64]{0,1:T(8,128)(2,1)} %param.24) | copy-start | bytes 589828
  67.1 15.9 %copy-start.12 = (f32[1536]{0:T(1024)S(1)}, f32[1536]{0:T(1024)}, u32[]{:S(2)}) copy-start(f32[1536]{0:T(1024)} %param.23) | copy-start | bytes 18436
  67.1 16.4 %copy-start.4 = (f32[2,4,32,16]{3,2,1,0:T(8,128)S(1)}, f32[2,4,32,16]{3,2,1,0:T(8,128)}, u32[]{:S(2)}) copy-start(f32[2,4,32,16]{3,2,1,0:T(8,128)} %reshape.79) | copy-start | bytes 49156
  67.3 26.9 %copy-start.13 = (pred[8,5]{0,1:T(8,128)(4,1)S(1)}, pred[8,5]{0,1:T(8,128)(4,1)}, u32[]{:S(2)}) copy-start(pred[8,5]{0,1:T(8,128)(4,1)} %constant.43) | copy-start | bytes 124
  68.1 11.1 %all-to-all-start.2 = ((bf16[4,64,384]{2,1,0:T(8,128)(2,1)}), bf16[4,64,384]{2,1,0:T(8,128)(2,1)S(1)}, u32[]{:S(2)}, u32[]{:S(2)}) async-start(bf16[4,64,384]{2,1,0:T(8,128)(2,1)} %convert_element_type.48), calls=%async_computation.2 | async-start | bytes 393216 | tf_op jit(solution)/shard_map/all_to_all | solution.py:145
  82.7 25.4 %copy-start.2 = (bf16[64,1536]{1,0:T(8,128)(2,1)}, bf16[64,1536]{1,0:T(8,128)(2,1)S(1)}, u32[]{:S(2)}) copy-start(bf16[64,1536]{1,0:T(8,128)(2,1)S(1)} %get-tuple-element.13) | copy-start | bytes 589828
  82.7 12.7 %copy-start.9 = (f32[384]{0:T(512)S(1)}, f32[384]{0:T(512)}, u32[]{:S(2)}) copy-start(f32[384]{0:T(512)} %param.28) | copy-start | bytes 4612
  83.5 10.4 %collective-permute-start = (bf16[2,4,32,16]{3,2,1,0:T(8,128)(2,1)S(1)}, bf16[2,4,32,16]{3,2,1,0:T(8,128)(2,1)S(1)}, u32[]{:S(2)}, u32[]{:S(2)}) collective-permute-start(bf16[2,4,32,16]{3,2,1,0:T(8,128)(2,1)S(1)} %subtract_convert_fusion), channel_id=1, source_target_pairs={{0,1},{1,2},{2,3},{3,4},{4,5},{5,6},{6,7},{7,8},{8,9},{9,10},{10,1... | collective-permute-start | bytes 24584 | tf_op jit(solution)/shard_map/ppermute | solution.py:22
  95.8 11.8 %collective-permute-start.1 = (bf16[2,4,32,384]{3,1,2,0:T(4,128)(2,1)S(1)}, bf16[2,4,32,384]{3,1,2,0:T(4,128)(2,1)S(1)}, u32[]{:S(2)}, u32[]{:S(2)}) collective-permute-start(bf16[2,4,32,384]{3,1,2,0:T(4,128)(2,1)S(1)} %fusion.48), channel_id=1, source_target_pairs={{0,1},{1,2},{2,3},{3,4},{4,5},{5,6},{6,7},{7,8},{8,9},{9,10},{10,1... | collective-permute-start | bytes 589832 | tf_op jit(solution)/shard_map/ppermute | solution.py:22
  108.0 20.2 %slice-start = ((s8[7962624]{0:T(1024)(128)(4,1)}), s8[4194304]{0:T(1024)(128)(4,1)S(1)}, s32[]{:S(2)}) async-start(s8[7962624]{0:T(1024)(128)(4,1)} %bitcast.121), calls=%async_computation.3 | async-start | bytes 8388608
  108.1 7.4 %copy-start.10 = (f32[384]{0:T(512)S(1)}, f32[384]{0:T(512)}, u32[]{:S(2)}) copy-start(f32[384]{0:T(512)} %param.30) | copy-start | bytes 4612
  108.1 20.0 %slice-start.1 = ((s8[7962624]{0:T(1024)(128)(4,1)}), s8[3768320]{0:T(1024)(128)(4,1)S(1)}, s32[]{:S(2)}) async-start(s8[7962624]{0:T(1024)(128)(4,1)} %bitcast.121), calls=%async_computation.4 | async-start | bytes 7536640
  115.8 11.8 %collective-permute-start.2 = (bf16[2,4,32,384]{3,1,2,0:T(4,128)(2,1)S(1)}, bf16[2,4,32,384]{3,1,2,0:T(4,128)(2,1)S(1)}, u32[]{:S(2)}, u32[]{:S(2)}) collective-permute-start(bf16[2,4,32,384]{3,1,2,0:T(4,128)(2,1)S(1)} %fusion.50), channel_id=1, source_target_pairs={{0,1},{1,2},{2,3},{3,4},{4,5},{5,6},{6,7},{7,8},{8,9},{9,10},{10,1... | collective-permute-start | bytes 589832 | tf_op jit(solution)/shard_map/ppermute | solution.py:22

commit v3 on v2

--- a/solution.py
+++ b/solution.py
@@ -1,8 +1,11 @@
+import functools
 import math
 
 import jax
 import jax.numpy as jnp
 from jax import lax
+from jax.experimental import pallas as pl
+from jax.experimental.pallas import tpu as pltpu
 from jax.sharding import Mesh
 from jax.sharding import PartitionSpec as P
 
@@ -14,6 +17,55 @@
 PATCH = 2
 TOK_H = 2
 TOK_W = 16
+
+
+MESH = pl.DeviceIdType.MESH
+
+
+def gather_kernel(blocks, groups, src_ref, out_ref, send_sem, recv_sem):
+    req = lax.axis_index("req")
+    me = lax.axis_index("blk") * groups + lax.axis_index("hg")
+    peers = blocks * groups
+
+    def device(peer):
+        return (req, peer // groups, lax.rem(peer, groups))
+
+    barrier = pltpu.get_barrier_semaphore()
+    for k in range(1, peers):
+        peer = lax.rem(me + k, peers)
+        pl.semaphore_signal(barrier, inc=1, device_id=device(peer), device_id_type=MESH)
+    pl.semaphore_wait(barrier, peers - 1)
+
+    copies = []
+    for k in range(1, peers):
+        peer = lax.rem(me + k, peers)
+        copy = pltpu.make_async_remote_copy(
+            src_ref=src_ref.at[lax.rem(peer, groups)],
+            dst_ref=out_ref.at[me],
+            send_sem=send_sem.at[k],
+            recv_sem=recv_sem.at[k],
+            device_id=device(peer),
+            device_id_type=MESH,
+        )
+        copy.start()
+        copies.append(copy)
+    out_ref[me] = src_ref[lax.rem(me, groups)]
+    for copy in copies:
+        copy.wait_send()
+        copy.wait_recv()
+
+
+def gather_groups(parts, blocks):
+    groups = parts.shape[0]
+    peers = blocks * groups
+    return pl.pallas_call(
+        functools.partial(gather_kernel, blocks, groups),
+        out_shape=jax.ShapeDtypeStruct((peers,) + parts.shape[1:], parts.dtype),
+        in_specs=[pl.BlockSpec(memory_space=pltpu.VMEM)],
+        out_specs=pl.BlockSpec(memory_space=pltpu.VMEM),
+        scratch_shapes=[pltpu.SemaphoreType.DMA((peers,)), pltpu.SemaphoreType.DMA((peers,))],
+        compiler_params=pltpu.CompilerParams(collective_id=0, has_side_effects=True),
+    )(parts)
 
 
 def shifted(x, axis, by):
@@ -123,12 +175,8 @@
         return lax.all_to_all(parts, "hg", 1, 0, tiled=True).reshape(-1, group_width)
 
     def gather_group(matrix):
-        blocks = lax.psum(1, "blk")
         parts = matrix.reshape(rows_here, -1, HEAD_GROUPS, group_width)
-        parts = jnp.moveaxis(parts, 2, 0)
-        sent = jnp.broadcast_to(parts[None], (blocks,) + parts.shape)
-        sent = sent.reshape((blocks * HEAD_GROUPS,) + parts.shape[1:])
-        got = lax.all_to_all(sent, FRAMES, 0, 0, tiled=True)
+        got = gather_groups(jnp.moveaxis(parts, 2, 0), lax.psum(1, "blk"))
         return got.reshape((-1,) + got.shape[2:])
 
     query_heads = split_heads(to_group(queries), group_heads)

time: 133 us -> 161 us (1.21)
  Pallas kernels: 0 us -> 54.8 us
  waiting for transfers between devices: 72.2 us -> 33.7 us
  local copies, waits for them, and re-layouts: 14.8 us -> 32.1 us
  starting transfers between devices: 22.3 us -> 14.2 us
    pallas_call x0 -> x1, Pallas kernels: none -> 54.8 us  [gather_groups(): pl.pallas_call(functools.partial(gather_kernel, blocks, groups), out_shap...]
    all_to_all x1 -> x0, waiting for transfers between devices: 34.4 us -> none  [gather_group(): got = lax.all_to_all(sent, FRAMES, 0, 0, tiled=True)]
    slice x2 -> x1, local copies, waits for them, and re-layouts: 1.07 us -> 8.75 us  [body(): key_heads = split_heads(key_value[:, 0], group_heads)]
    all_to_all x1 -> x0, starting transfers between devices: 6.7 us -> none  [gather_group(): got = lax.all_to_all(sent, FRAMES, 0, 0, tiled=True)]
    slice x1, local copies, waits for them, and re-layouts: 1.65 us -> 8.29 us  [body(): value_heads = split_heads(key_value[:, 1], group_heads)]
    unnamed x34 -> x31, local copies, waits for them, and re-layouts: 1.21 us -> 7.43 us
    all_to_all x1, waiting for transfers between devices: 4.01 us -> 0.01 us  [to_group(): lax.all_to_all(parts, 'hg', 1, 0, tiled=True).reshape(-1, group_width)]
    broadcast_in_dim x1 -> x0, local copies, waits for them, and re-layouts: 2.14 us -> none  [gather_group(): sent = jnp.broadcast_to(parts[None], (blocks,) + parts.shape)]
  transfers between devices with their start and end apart: 6 -> 5, of which waited for: 6 -> 4; matrix products, arithmetic and copies ran while one was open for 4% -> 17% of each run, Pallas kernels for 0% -> 34%
where the time goes in v3:
time: 161 us; the launch traced here: 160 us
  Pallas kernels  54.8 us (34%)
  waiting for transfers between devices  33.7 us (21%)
  local copies, waits for them, and re-layouts  32.1 us (20%)
  matrix products  19 us (12%)
  starting transfers between devices  14.2 us (9%)
  other arithmetic  4.45 us (3%)
  between operations  1.81 us (1%)
    pallas_call x1, Pallas kernels, gather_groups(): pl.pallas_call(functools.partial(gather_kernel, blocks, groups), out_shap...  54.8 us
    ppermute x3, waiting for transfers between devices, shifted(): return lax.ppermute(x, axis, pairs)  27.4 us
    conv_general_dilated x3, matrix products, spatial_conv(): lax.conv_general_dilated(extended[None], kernel, (1, 1, 1), ((0, 0), (1,...  11.7 us
    slice x1, local copies, waits for them, and re-layouts, body(): key_heads = split_heads(key_value[:, 0], group_heads)  8.75 us
    slice x1, local copies, waits for them, and re-layouts, body(): value_heads = split_heads(key_value[:, 1], group_heads)  8.29 us
    unnamed x31, local copies, waits for them, and re-layouts  7.43 us
    ppermute x3, starting transfers between devices, shifted(): return lax.ppermute(x, axis, pairs)  6.5 us
    all_to_all x1, waiting for transfers between devices, body(): attended = lax.all_to_all(group_out, 'hg', 0, 1, tiled=True)  6.27 us
  transfers between devices with their start and end apart: 5, of which 4 were waited for; matrix products, arithmetic and copies ran while one was open for 17% of the time, Pallas kernels for 34%

profile of v3, /device:TPU:96, one launch (start us, length us, event | category | flops | bytes accessed | tf_op | source)
XLA Modules:
  0.0 160.1 jit_solution(10610274038679205907)
XLA Ops:
  0.6 1.7 %copy.53 = bf16[8,4,8,384]{3,2,0,1:T(8,128)(2,1)} copy(bf16[8,4,8,384]{3,2,1,0:T(8,128)(2,1)} %bitcast.116) | data formatting | bytes 393216 | tf_op jit(solution)/shard_map/reshape | solution.py:174
  2.3 4.3 %all-to-all-start = ((bf16[64,4,384]{2,0,1:T(8,128)(2,1)}), bf16[64,4,384]{2,0,1:T(8,128)(2,1)}, u32[]{:S(2)}, u32[]{:S(2)}) async-start(bf16[64,4,384]{2,0,1:T(8,128)(2,1)} %bitcast.99), calls=%async_computation | async-start | bytes 393216 | tf_op jit(solution)/shard_map/all_to_all | solution.py:175
  7.9 1.0 stack.9
  9.2 1.6 maximum_bitcast_fusion.src_ref
  10.8 54.8 %shard_map.167 = bf16[32,64,2,384]{3,2,1,0:T(2,128)(2,1)} custom-call(bf16[4,64,2,384]{3,2,1,0:T(2,128)(2,1)} %maximum_bitcast_fusion.src_ref), custom_call_target="tpu_custom_call" | custom-call | tf_op jit(solution)/shard_map/pallas_call | solution.py:61
  65.6 8.7 %fusion.77 = (bf16[2048,1,384]{2,1,0:T(2,128)(2,1)S(1)}, bf16[2048,1,384]{2,1,0:T(2,128)(2,1)}) fusion(bf16[2048,2,384]{2,1,0:T(2,128)(2,1)} %bitcast.101), kind=kLoop, calls=%fused_computation.97 | loop fusion | bytes 6291456 | tf_op jit(solution)/shard_map/slice | solution.py:184
  74.4 8.3 %copy.26 = bf16[2048,1,384]{0,2,1:T(8,128)(2,1)} copy(bf16[2048,1,384]{2,1,0:T(2,128)(2,1)} %get-tuple-element.5) | data formatting | bytes 3145728 | tf_op jit(solution)/shard_map/slice | solution.py:185
  82.6 6.2 %copy.44 = bf16[2048,1,384]{0,2,1:T(8,128)(2,1)} copy(bf16[2048,1,384]{2,1,0:T(2,128)(2,1)S(1)} %get-tuple-element.4) | data formatting | bytes 3145728
  89.7 1.0 reshape_reshape.3
  90.6 2.5 %bitcast_reduce_fusion = (f32[3,256]{1,0:T(4,128)S(1)}, f32[3,2048,256]{2,1,0:T(8,128)S(1)}) fusion(bf16[2048,3,128]{0,2,1:T(8,128)(2,1)} %bitcast.102, bf16[256,3,128]{2,1,0:T(4,128)(2,1)S(1)} %reshape_reshape.3), kind=kOutput, calls=%fused_computation.1 | convolution fusion | flops 405798144 | bytes 8064000 | tf_op jit(solution)/shard_map/qhd,khd->hqk/dot_general | solution.py:91
  93.1 1.0 fusion.1
  94.5 1.2 fusion.21
  96.8 3.4 %all-to-all-start.1 = ((bf16[4,64,384]{2,1,0:T(8,128)(2,1)}), bf16[4,64,384]{2,1,0:T(8,128)(2,1)S(1)}, u32[]{:S(2)}, u32[]{:S(2)}) async-start(bf16[4,64,384]{2,1,0:T(8,128)(2,1)} %convert_element_type.48), calls=%async_computation.1 | async-start | bytes 393216 | tf_op jit(solution)/shard_map/all_to_all | solution.py:193
  100.2 6.3 %all-to-all-done.1 = bf16[4,64,384]{2,1,0:T(8,128)(2,1)S(1)} async-done(((bf16[4,64,384]{2,1,0:T(8,128)(2,1)}), bf16[4,64,384]{2,1,0:T(8,128)(2,1)S(1)}, u32[]{:S(2)}, u32[]{:S(2)}) %all-to-all-start.1) | async-done | bytes 196640 | tf_op jit(solution)/shard_map/all_to_all | solution.py:193
  106.5 3.4 %convert_reduce_fusion = (f32[64]{0:T(128)S(1)}, bf16[64,1536]{1,0:T(8,128)(2,1)S(1)}) fusion(bf16[64,1536]{1,0:T(8,128)(2,1)S(1)} %bitcast.112, bf16[1536,1536]{1,0:T(8,128)(2,1)} %param.21, f32[1536]{0:T(1024)S(1)} %copy-done.5, bf16[64,1536]{1,0:T(8,128)(2,1)S(1)} %copy-done.3), kind=kOutput, calls=%fused_computation.37 | convolution fusion | flops 302579648 | bytes 5314816 | tf_op jit(solution)/shard_map/dot_general | solution.py:194
  110.7 2.5 %collective-permute-start = (bf16[2,4,32,16]{3,2,1,0:T(8,128)(2,1)S(1)}, bf16[2,4,32,16]{3,2,1,0:T(8,128)(2,1)S(1)}, u32[]{:S(2)}, u32[]{:S(2)}) collective-permute-start(bf16[2,4,32,16]{3,2,1,0:T(8,128)(2,1)S(1)} %subtract_convert_fusion), channel_id=1, source_target_pairs={{0,1},{1,2},{2,3},{3,4},{4,5},{5,6},{6,7},{7,8},{8,9},{9,10},{10,1... | collective-permute-start | bytes 24584 | tf_op jit(solution)/shard_map/ppermute | solution.py:74
  113.2 7.9 %collective-permute-done = bf16[2,4,32,16]{3,2,1,0:T(8,128)(2,1)S(1)} collective-permute-done((bf16[2,4,32,16]{3,2,1,0:T(8,128)(2,1)S(1)}, bf16[2,4,32,16]{3,2,1,0:T(8,128)(2,1)S(1)}, u32[]{:S(2)}, u32[]{:S(2)}) %collective-permute-start) | collective-permute-done | bytes 8224 | tf_op jit(solution)/shard_map/ppermute | solution.py:74
  121.3 1.0 fusion.14
  123.0 2.1 %collective-permute-start.1 = (bf16[2,4,32,384]{3,1,2,0:T(4,128)(2,1)S(1)}, bf16[2,4,32,384]{3,1,2,0:T(4,128)(2,1)S(1)}, u32[]{:S(2)}, u32[]{:S(2)}) collective-permute-start(bf16[2,4,32,384]{3,1,2,0:T(4,128)(2,1)S(1)} %fusion.48), channel_id=1, source_target_pairs={{0,1},{1,2},{2,3},{3,4},{4,5},{5,6},{6,7},{7,8},{8,9},{9,10},{10,1... | collective-permute-start | bytes 589832 | tf_op jit(solution)/shard_map/ppermute | solution.py:74
  125.1 9.7 %collective-permute-done.1 = bf16[2,4,32,384]{3,1,2,0:T(4,128)(2,1)S(1)} collective-permute-done((bf16[2,4,32,384]{3,1,2,0:T(4,128)(2,1)S(1)}, bf16[2,4,32,384]{3,1,2,0:T(4,128)(2,1)S(1)}, u32[]{:S(2)}, u32[]{:S(2)}) %collective-permute-start.1) | collective-permute-done | bytes 196640 | tf_op jit(solution)/shard_map/ppermute | solution.py:74
  135.4 7.1 %convolution_select_fusion.2 = f32[2,4,8,5,384]{4,2,3,1,0:T(8,128)S(1)} fusion(bf16[3,3,3,384,384]{4,3,2,1,0:T(8,128)(2,1)} %param.29, bf16[4,4,1,7,2,384]{5,3,4,1,0,2:T(8,128)(2,1)S(1)} %slice.18, bf16[4,4,1,8,5,384]{5,3,4,1,0,2:T(8,128)(2,1)S(1)} %copy.36, pred[8,5]{0,1:T(8,128)(4,1)S(1)} %copy-done.11), kind=kOutput, calls=%fused_computation.16 | convolution fusion | flops 2125553664 | bytes 9117736 | tf_op jit(solution)/shard_map/conv_general_dilated | solution.py:126
  143.0 1.9 %collective-permute-start.2 = (bf16[2,4,32,384]{3,1,2,0:T(4,128)(2,1)S(1)}, bf16[2,4,32,384]{3,1,2,0:T(4,128)(2,1)S(1)}, u32[]{:S(2)}, u32[]{:S(2)}) collective-permute-start(bf16[2,4,32,384]{3,1,2,0:T(4,128)(2,1)S(1)} %fusion.50), channel_id=1, source_target_pairs={{0,1},{1,2},{2,3},{3,4},{4,5},{5,6},{6,7},{7,8},{8,9},{9,10},{10,1... | collective-permute-start | bytes 589832 | tf_op jit(solution)/shard_map/ppermute | solution.py:74
  145.0 9.9 %collective-permute-done.2 = bf16[2,4,32,384]{3,1,2,0:T(4,128)(2,1)S(1)} collective-permute-done((bf16[2,4,32,384]{3,1,2,0:T(4,128)(2,1)S(1)}, bf16[2,4,32,384]{3,1,2,0:T(4,128)(2,1)S(1)}, u32[]{:S(2)}, u32[]{:S(2)}) %collective-permute-start.2) | collective-permute-done | bytes 196640 | tf_op jit(solution)/shard_map/ppermute | solution.py:74
  155.4 3.7 %convolution_select_fusion.1 = f32[2,4,8,5,384]{4,2,3,1,0:T(8,128)S(1)} fusion(bf16[3,3,3,384,384]{4,3,2,1,0:T(8,128)(2,1)S(1)} %bitcast.119, bf16[4,4,1,7,2,384]{5,3,4,1,0,2:T(8,128)(2,1)S(1)} %slice.20, bf16[4,4,1,8,5,384]{5,3,4,1,0,2:T(8,128)(2,1)S(1)} %copy.39, pred[8,5]{0,1:T(8,128)(4,1)S(1)} %copy-done.11), kind=kOutput, calls=%fused_computation.15 | convolution fusion | flops 2125553664 | bytes 9117736 | tf_op jit(solution)/shard_map/conv_general_dilated | solution.py:126
  (70 shorter events, 7.3 us)
Async XLA Ops:
  0.6 120.7 %copy-start = (bf16[3,3,3,16,384]{4,3,2,1,0:T(8,128)(2,1)S(1)}, bf16[3,3,3,16,384]{4,3,2,1,0:T(8,128)(2,1)}, u32[]{:S(2)}) copy-start(bf16[3,3,3,16,384]{4,3,2,1,0:T(8,128)(2,1)} %param.27) | copy-start | bytes 995332
  2.3 87.3 %all-to-all-start = ((bf16[64,4,384]{2,0,1:T(8,128)(2,1)}), bf16[64,4,384]{2,0,1:T(8,128)(2,1)}, u32[]{:S(2)}, u32[]{:S(2)}) async-start(bf16[64,4,384]{2,0,1:T(8,128)(2,1)} %bitcast.99), calls=%async_computation | async-start | bytes 393216 | tf_op jit(solution)/shard_map/all_to_all | solution.py:175
  74.4 14.5 %copy-start.4 = (f32[2,4,512]{2,1,0:T(4,128)S(1)}, f32[2,4,512]{2,1,0:T(4,128)}, u32[]{:S(2)}) copy-start(f32[2,4,512]{2,1,0:T(4,128)} %param.26) | copy-start | bytes 49156
  93.1 1.4 copy-start.1
  94.5 5.7 %copy-start.6 = (f32[1536]{0:T(1024)S(1)}, f32[1536]{0:T(1024)}, u32[]{:S(2)}) copy-start(f32[1536]{0:T(1024)} %param.22) | copy-start | bytes 18436
  94.5 12.0 %copy-start.3 = (bf16[64,1536]{1,0:T(8,128)(2,1)S(1)}, bf16[64,1536]{1,0:T(8,128)(2,1)}, u32[]{:S(2)}) copy-start(bf16[64,1536]{1,0:T(8,128)(2,1)} %param.16) | copy-start | bytes 589828
  94.5 12.0 %copy-start.5 = (f32[1536]{0:T(1024)S(1)}, f32[1536]{0:T(1024)}, u32[]{:S(2)}) copy-start(f32[1536]{0:T(1024)} %param.20) | copy-start | bytes 18436
  95.7 14.4 %copy-start.9 = (bf16[1536,64]{0,1:T(8,128)(2,1)S(1)}, bf16[1536,64]{0,1:T(8,128)(2,1)}, u32[]{:S(2)}) copy-start(bf16[1536,64]{0,1:T(8,128)(2,1)} %param.24) | copy-start | bytes 589828
  95.7 14.4 %copy-start.10 = (f32[1536]{0:T(1024)S(1)}, f32[1536]{0:T(1024)}, u32[]{:S(2)}) copy-start(f32[1536]{0:T(1024)} %param.23) | copy-start | bytes 18436
  95.9 25.4 %copy-start.11 = (pred[8,5]{0,1:T(8,128)(4,1)S(1)}, pred[8,5]{0,1:T(8,128)(4,1)}, u32[]{:S(2)}) copy-start(pred[8,5]{0,1:T(8,128)(4,1)} %constant.43) | copy-start | bytes 124
  96.8 9.7 %all-to-all-start.1 = ((bf16[4,64,384]{2,1,0:T(8,128)(2,1)}), bf16[4,64,384]{2,1,0:T(8,128)(2,1)S(1)}, u32[]{:S(2)}, u32[]{:S(2)}) async-start(bf16[4,64,384]{2,1,0:T(8,128)(2,1)} %convert_element_type.48), calls=%async_computation.1 | async-start | bytes 393216 | tf_op jit(solution)/shard_map/all_to_all | solution.py:193
  109.9 25.4 %copy-start.2 = (bf16[64,1536]{1,0:T(8,128)(2,1)}, bf16[64,1536]{1,0:T(8,128)(2,1)S(1)}, u32[]{:S(2)}) copy-start(bf16[64,1536]{1,0:T(8,128)(2,1)S(1)} %get-tuple-element.11) | copy-start | bytes 589828
  109.9 12.7 %copy-start.7 = (f32[384]{0:T(512)S(1)}, f32[384]{0:T(512)}, u32[]{:S(2)}) copy-start(f32[384]{0:T(512)} %param.28) | copy-start | bytes 4612
  110.7 10.4 %collective-permute-start = (bf16[2,4,32,16]{3,2,1,0:T(8,128)(2,1)S(1)}, bf16[2,4,32,16]{3,2,1,0:T(8,128)(2,1)S(1)}, u32[]{:S(2)}, u32[]{:S(2)}) collective-permute-start(bf16[2,4,32,16]{3,2,1,0:T(8,128)(2,1)S(1)} %subtract_convert_fusion), channel_id=1, source_target_pairs={{0,1},{1,2},{2,3},{3,4},{4,5},{5,6},{6,7},{7,8},{8,9},{9,10},{10,1... | collective-permute-start | bytes 24584 | tf_op jit(solution)/shard_map/ppermute | solution.py:74
  123.0 11.8 %collective-permute-start.1 = (bf16[2,4,32,384]{3,1,2,0:T(4,128)(2,1)S(1)}, bf16[2,4,32,384]{3,1,2,0:T(4,128)(2,1)S(1)}, u32[]{:S(2)}, u32[]{:S(2)}) collective-permute-start(bf16[2,4,32,384]{3,1,2,0:T(4,128)(2,1)S(1)} %fusion.48), channel_id=1, source_target_pairs={{0,1},{1,2},{2,3},{3,4},{4,5},{5,6},{6,7},{7,8},{8,9},{9,10},{10,1... | collective-permute-start | bytes 589832 | tf_op jit(solution)/shard_map/ppermute | solution.py:74
  135.2 20.2 %slice-start = ((s8[7962624]{0:T(1024)(128)(4,1)}), s8[4194304]{0:T(1024)(128)(4,1)S(1)}, s32[]{:S(2)}) async-start(s8[7962624]{0:T(1024)(128)(4,1)} %bitcast.118), calls=%async_computation.2 | async-start | bytes 8388608
  135.3 7.4 %copy-start.8 = (f32[384]{0:T(512)S(1)}, f32[384]{0:T(512)}, u32[]{:S(2)}) copy-start(f32[384]{0:T(512)} %param.30) | copy-start | bytes 4612
  135.3 20.0 %slice-start.1 = ((s8[7962624]{0:T(1024)(128)(4,1)}), s8[3768320]{0:T(1024)(128)(4,1)S(1)}, s32[]{:S(2)}) async-start(s8[7962624]{0:T(1024)(128)(4,1)} %bitcast.118), calls=%async_computation.3 | async-start | bytes 7536640
  143.0 11.8 %collective-permute-start.2 = (bf16[2,4,32,384]{3,1,2,0:T(4,128)(2,1)S(1)}, bf16[2,4,32,384]{3,1,2,0:T(4,128)(2,1)S(1)}, u32[]{:S(2)}, u32[]{:S(2)}) collective-permute-start(bf16[2,4,32,384]{3,1,2,0:T(4,128)(2,1)S(1)} %fusion.50), channel_id=1, source_target_pairs={{0,1},{1,2},{2,3},{3,4},{4,5},{5,6},{6,7},{7,8},{8,9},{9,10},{10,1... | collective-permute-start | bytes 589832 | tf_op jit(solution)/shard_map/ppermute | solution.py:74

commit v4 on v2

--- a/solution.py
+++ b/solution.py
@@ -131,7 +131,18 @@
         got = lax.all_to_all(sent, FRAMES, 0, 0, tiled=True)
         return got.reshape((-1,) + got.shape[2:])
 
-    query_heads = split_heads(to_group(queries), group_heads)
+    def permute_to_group(matrix):
+        me = lax.axis_index("hg")
+        parts = matrix.reshape(rows_here, HEAD_GROUPS, group_width)
+        received = [lax.dynamic_index_in_dim(parts, me, 1, keepdims=False)]
+        for k in range(1, HEAD_GROUPS):
+            piece = lax.dynamic_index_in_dim(parts, lax.rem(me + HEAD_GROUPS - k, HEAD_GROUPS), 1, False)
+            pairs = [(i, (i + HEAD_GROUPS - k) % HEAD_GROUPS) for i in range(HEAD_GROUPS)]
+            received.append(lax.ppermute(piece, "hg", pairs))
+        twice = jnp.concatenate(received + received, axis=0)
+        return lax.dynamic_slice_in_dim(twice, (HEAD_GROUPS - me) * rows_here, HEAD_GROUPS * rows_here)
+
+    query_heads = split_heads(permute_to_group(queries), group_heads)
     key_value = gather_group(jnp.stack([keys, values], axis=1))
     key_heads = split_heads(key_value[:, 0], group_heads)
     value_heads = split_heads(key_value[:, 1], group_heads)

time: 133 us -> 137 us (1.030)
  local copies, waits for them, and re-layouts: 14.8 us -> 29 us
  waiting for transfers between devices: 72.2 us -> 60.3 us
    all_to_all x1, waiting for transfers between devices: 34.4 us -> 0.01 us  [gather_group(): got = lax.all_to_all(sent, FRAMES, 0, 0, tiled=True)]
    ppermute x0 -> x3, waiting for transfers between devices: none -> 26.6 us  [permute_to_group(): received.append(lax.ppermute(piece, 'hg', pairs))]
    unnamed x34 -> x44, local copies, waits for them, and re-layouts: 1.21 us -> 10.6 us
    dynamic_slice x0 -> x3, local copies, waits for them, and re-layouts: none -> 4.99 us  [the longest x2 3.36 us: permute_to_group(): lax.dynamic_slice_in_dim(twice, (HEAD_GROUPS - me) * rows_here, HEAD_GROU...]
    ppermute x0 -> x3, starting transfers between devices: none -> 4.39 us  [permute_to_group(): received.append(lax.ppermute(piece, 'hg', pairs))]
    all_to_all x1 -> x0, starting transfers between devices: 4.29 us -> none  [to_group(): lax.all_to_all(parts, 'hg', 1, 0, tiled=True).reshape(-1, group_width)]
    all_to_all x1 -> x0, waiting for transfers between devices: 4.01 us -> none  [to_group(): lax.all_to_all(parts, 'hg', 1, 0, tiled=True).reshape(-1, group_width)]
    all_to_all x1, starting transfers between devices: 6.7 us -> 8.69 us  [gather_group(): got = lax.all_to_all(sent, FRAMES, 0, 0, tiled=True)]
  transfers between devices with their start and end apart: 6 -> 8, of which waited for: 6 -> 6; matrix products, arithmetic and copies ran while one was open for 4% -> 13% of each run, Pallas kernels for 0% -> 0%
where the time goes in v4:
time: 137 us; the launch traced here: 136 us
  waiting for transfers between devices  60.3 us (44%)
  local copies, waits for them, and re-layouts  29 us (21%)
  starting transfers between devices  22.9 us (17%)
  matrix products  18.8 us (14%)
  other arithmetic  3.29 us (2%)
  between operations  1.86 us (1%)
    ppermute x3, waiting for transfers between devices, shifted(): return lax.ppermute(x, axis, pairs)  27.4 us
    ppermute x3, waiting for transfers between devices, permute_to_group(): received.append(lax.ppermute(piece, 'hg', pairs))  26.6 us
    conv_general_dilated x3, matrix products, spatial_conv(): lax.conv_general_dilated(extended[None], kernel, (1, 1, 1), ((0, 0), (1,...  11.7 us
    unnamed x44, local copies, waits for them, and re-layouts  10.6 us
    all_to_all x1, starting transfers between devices, gather_group(): got = lax.all_to_all(sent, FRAMES, 0, 0, tiled=True)  8.69 us
    ppermute x3, starting transfers between devices, shifted(): return lax.ppermute(x, axis, pairs)  6.49 us
    all_to_all x1, waiting for transfers between devices, body(): attended = lax.all_to_all(group_out, 'hg', 0, 1, tiled=True)  6.27 us
    ppermute x3, starting transfers between devices, permute_to_group(): received.append(lax.ppermute(piece, 'hg', pairs))  4.39 us
  transfers between devices with their start and end apart: 8, of which 6 were waited for; matrix products, arithmetic and copies ran while one was open for 13% of the time, Pallas kernels for 0%

profile of v4, /device:TPU:96, one launch (start us, length us, event | category | flops | bytes accessed | tf_op | source)
XLA Modules:
  0.0 136.2 jit_solution(12252724096023479901)
XLA Ops:
  3.0 2.2 %broadcast_in_dim.13 = bf16[8,4,64,2,384]{4,2,3,1,0:T(8,128)(2,1)} broadcast(bf16[4,64,2,384]{3,1,2,0:T(8,128)(2,1)S(1)} %copy.60), dimensions={1,2,3,4} | broadcast | bytes 3538944 | tf_op jit(solution)/shard_map/broadcast_in_dim | solution.py:129
  5.2 8.7 %all-to-all-start = ((bf16[32,64,2,384]{3,1,2,0:T(8,128)(2,1)}), bf16[32,64,2,384]{3,1,2,0:T(8,128)(2,1)S(1)}, u32[]{:S(2)}, u32[]{:S(2)}) async-start(bf16[32,64,2,384]{3,1,2,0:T(8,128)(2,1)} %bitcast.87), calls=%async_computation | async-start | bytes 6291456 | tf_op jit(solution)/shard_map/all_to_all | solution.py:131
  13.9 1.7 %reshape.78 = bf16[64,4,384]{2,1,0:T(4,128)(2,1)} reshape(bf16[64,1536]{1,0:T(8,128)(2,1)} %param.17) | data formatting | bytes 393216 | tf_op jit(solution)/shard_map/reshape | solution.py:136
  15.5 1.6 %constant_dynamic-slice_fusion.1 = (bf16[64,1,384]{2,1,0:T(2,128)(2,1)S(1)}, bf16[64,1,384]{2,1,0:T(2,128)(2,1)S(1)}, bf16[64,1,384]{2,1,0:T(2,128)(2,1)S(1)}, bf16[64,1,384]{2,1,0:T(2,128)(2,1)S(1)}) fusion(bf16[64,4,384]{2,1,0:T(4,128)(2,1)} %reshape.78, s32[]{:T(128)S(6)} %select_n.20, s32[]{:T(128)S(6)} %select_n.19, s32[]{:T(128)S(6)} %select_n.18, ...), kind=kLoop, calls=%fused_computation.93 | loop fusion | bytes 393232 | tf_op jit(solution)/shard_map/jit(dynamic_index_in_dim)/dynamic_slice | solution.py:139
  17.8 2.7 %collective-permute-start = (bf16[64,384]{1,0:T(8,128)(2,1)}, bf16[64,384]{1,0:T(8,128)(2,1)S(1)}, u32[]{:S(2)}, u32[]{:S(2)}) collective-permute-start(bf16[64,384]{1,0:T(8,128)(2,1)} %bitcast.85), channel_id=1, source_target_pairs={{0,3},{1,0},{2,1},{3,2},{4,7},{5,4},{6,5},{7,6},{8,11},{9,8},{10,9... | collective-permute-start | bytes 147464 | tf_op jit(solution)/shard_map/ppermute | solution.py:141
  25.5 25.5 %collective-permute-done = bf16[64,384]{1,0:T(8,128)(2,1)S(1)} collective-permute-done((bf16[64,384]{1,0:T(8,128)(2,1)}, bf16[64,384]{1,0:T(8,128)(2,1)S(1)}, u32[]{:S(2)}, u32[]{:S(2)}) %collective-permute-start) | collective-permute-done | bytes 49184 | tf_op jit(solution)/shard_map/ppermute | solution.py:141
  54.1 1.4 %constant_dynamic-update-slice_fusion.3 = bf16[512,384]{1,0:T(8,128)(2,1)} fusion(bf16[512,384]{1,0:T(8,128)(2,1)} %constant_dynamic-update-slice_fusion.4, bf16[64,384]{1,0:T(8,128)(2,1)} %collective-permute-done.2), kind=kLoop, calls=%fused_computation.86 | loop fusion | bytes 98304
  55.5 1.5 %bitcast_dynamic-update-slice_fusion.1 = bf16[512,384]{1,0:T(8,128)(2,1)} fusion(bf16[512,384]{1,0:T(8,128)(2,1)} %constant_dynamic-update-slice_fusion.3, bf16[64,1,384]{2,1,0:T(2,128)(2,1)} %copy-done.2), kind=kLoop, calls=%fused_computation.80 | loop fusion | bytes 147456
  57.6 1.4 %constant_dynamic-update-slice_fusion.1 = bf16[512,384]{1,0:T(8,128)(2,1)} fusion(bf16[512,384]{1,0:T(8,128)(2,1)} %constant_dynamic-update-slice_fusion.2, bf16[64,384]{1,0:T(8,128)(2,1)} %collective-permute-done.1), kind=kLoop, calls=%fused_computation.84 | loop fusion | bytes 98304
  60.5 1.6 %constant_dynamic-slice_fusion = bf16[256,384]{1,0:T(8,128)(2,1)} fusion(bf16[512,384]{1,0:T(8,128)(2,1)} %constant_dynamic-update-slice_fusion, s32[]{:T(128)S(6)} %select_n.21), kind=kLoop, calls=%fused_computation.92 | loop fusion | bytes 393220 | tf_op jit(solution)/shard_map/dynamic_slice | solution.py:143
  62.1 1.7 %copy.59 = bf16[256,384]{0,1:T(8,128)(2,1)} copy(bf16[256,384]{1,0:T(8,128)(2,1)} %constant_dynamic-slice_fusion) | data formatting | bytes 393216 | tf_op jit(solution)/shard_map/dynamic_slice | solution.py:143
  64.5 1.6 %copy.65 = bf16[2048,1,384]{0,2,1:T(8,128)(2,1)} copy(bf16[2048,1,384]{2,0,1:T(8,128)(2,1)S(1)} %get-tuple-element.9) | data formatting | bytes 3145728 | tf_op jit(solution)/shard_map/slice | solution.py:148
  67.0 2.1 %multiply_reduce_fusion = (f32[3,256]{1,0:T(4,128)S(1)}, f32[3,256,2048]{2,1,0:T(8,128)S(1)}) fusion(bf16[256,3,128]{0,2,1:T(8,128)(2,1)} %bitcast.99, bf16[2048,3,128]{0,2,1:T(8,128)(2,1)S(1)} %bitcast.89), kind=kOutput, calls=%fused_computation.1 | convolution fusion | flops 405798144 | bytes 8064000 | tf_op jit(solution)/shard_map/qhd,khd->hqk/dot_general | solution.py:39
  72.9 3.4 %all-to-all-start.1 = ((bf16[4,64,384]{2,1,0:T(8,128)(2,1)}), bf16[4,64,384]{2,1,0:T(8,128)(2,1)S(1)}, u32[]{:S(2)}, u32[]{:S(2)}) async-start(bf16[4,64,384]{2,1,0:T(8,128)(2,1)} %convert_element_type.48), calls=%async_computation.1 | async-start | bytes 393216 | tf_op jit(solution)/shard_map/all_to_all | solution.py:156
  76.3 6.3 %all-to-all-done.1 = bf16[4,64,384]{2,1,0:T(8,128)(2,1)S(1)} async-done(((bf16[4,64,384]{2,1,0:T(8,128)(2,1)}), bf16[4,64,384]{2,1,0:T(8,128)(2,1)S(1)}, u32[]{:S(2)}, u32[]{:S(2)}) %all-to-all-start.1) | async-done | bytes 196640 | tf_op jit(solution)/shard_map/all_to_all | solution.py:156
  82.6 3.4 %convert_reduce_fusion = (f32[64]{0:T(128)S(1)}, bf16[64,1536]{1,0:T(8,128)(2,1)S(1)}) fusion(bf16[64,1536]{1,0:T(8,128)(2,1)S(1)} %bitcast.100, bf16[1536,1536]{1,0:T(8,128)(2,1)} %param.21, f32[1536]{0:T(1024)S(1)} %copy-done.7, bf16[64,1536]{1,0:T(8,128)(2,1)S(1)} %copy-done.5), kind=kOutput, calls=%fused_computation.36 | convolution fusion | flops 302579648 | bytes 5314816 | tf_op jit(solution)/shard_map/dot_general | solution.py:157
  86.8 2.5 %collective-permute-start.3 = (bf16[2,4,32,16]{3,2,1,0:T(8,128)(2,1)S(1)}, bf16[2,4,32,16]{3,2,1,0:T(8,128)(2,1)S(1)}, u32[]{:S(2)}, u32[]{:S(2)}) collective-permute-start(bf16[2,4,32,16]{3,2,1,0:T(8,128)(2,1)S(1)} %subtract_convert_fusion), channel_id=1, source_target_pairs={{0,1},{1,2},{2,3},{3,4},{4,5},{5,6},{6,7},{7,8},{8,9},{9,10},{10,1... | collective-permute-start | bytes 24584 | tf_op jit(solution)/shard_map/ppermute | solution.py:22
  89.3 7.9 %collective-permute-done.3 = bf16[2,4,32,16]{3,2,1,0:T(8,128)(2,1)S(1)} collective-permute-done((bf16[2,4,32,16]{3,2,1,0:T(8,128)(2,1)S(1)}, bf16[2,4,32,16]{3,2,1,0:T(8,128)(2,1)S(1)}, u32[]{:S(2)}, u32[]{:S(2)}) %collective-permute-start.3) | collective-permute-done | bytes 8224 | tf_op jit(solution)/shard_map/ppermute | solution.py:22
  99.1 2.1 %collective-permute-start.4 = (bf16[2,4,32,384]{3,1,2,0:T(4,128)(2,1)S(1)}, bf16[2,4,32,384]{3,1,2,0:T(4,128)(2,1)S(1)}, u32[]{:S(2)}, u32[]{:S(2)}) collective-permute-start(bf16[2,4,32,384]{3,1,2,0:T(4,128)(2,1)S(1)} %fusion.47), channel_id=1, source_target_pairs={{0,1},{1,2},{2,3},{3,4},{4,5},{5,6},{6,7},{7,8},{8,9},{9,10},{10,1... | collective-permute-start | bytes 589832 | tf_op jit(solution)/shard_map/ppermute | solution.py:22
  101.2 9.7 %collective-permute-done.4 = bf16[2,4,32,384]{3,1,2,0:T(4,128)(2,1)S(1)} collective-permute-done((bf16[2,4,32,384]{3,1,2,0:T(4,128)(2,1)S(1)}, bf16[2,4,32,384]{3,1,2,0:T(4,128)(2,1)S(1)}, u32[]{:S(2)}, u32[]{:S(2)}) %collective-permute-start.4) | collective-permute-done | bytes 196640 | tf_op jit(solution)/shard_map/ppermute | solution.py:22
  111.5 7.0 %convolution_select_fusion.2 = f32[2,4,8,5,384]{4,2,3,1,0:T(8,128)S(1)} fusion(bf16[3,3,3,384,384]{4,3,2,1,0:T(8,128)(2,1)} %param.29, bf16[4,4,1,7,2,384]{5,3,4,1,0,2:T(8,128)(2,1)S(1)} %slice.18, bf16[4,4,1,8,5,384]{5,3,4,1,0,2:T(8,128)(2,1)S(1)} %copy.74, pred[8,5]{0,1:T(8,128)(4,1)S(1)} %copy-done.13), kind=kOutput, calls=%fused_computation.15 | convolution fusion | flops 2125553664 | bytes 9117736 | tf_op jit(solution)/shard_map/conv_general_dilated | solution.py:74
  119.2 1.9 %collective-permute-start.5 = (bf16[2,4,32,384]{3,1,2,0:T(4,128)(2,1)S(1)}, bf16[2,4,32,384]{3,1,2,0:T(4,128)(2,1)S(1)}, u32[]{:S(2)}, u32[]{:S(2)}) collective-permute-start(bf16[2,4,32,384]{3,1,2,0:T(4,128)(2,1)S(1)} %fusion.49), channel_id=1, source_target_pairs={{0,1},{1,2},{2,3},{3,4},{4,5},{5,6},{6,7},{7,8},{8,9},{9,10},{10,1... | collective-permute-start | bytes 589832 | tf_op jit(solution)/shard_map/ppermute | solution.py:22
  121.1 9.9 %collective-permute-done.5 = bf16[2,4,32,384]{3,1,2,0:T(4,128)(2,1)S(1)} collective-permute-done((bf16[2,4,32,384]{3,1,2,0:T(4,128)(2,1)S(1)}, bf16[2,4,32,384]{3,1,2,0:T(4,128)(2,1)S(1)}, u32[]{:S(2)}, u32[]{:S(2)}) %collective-permute-start.5) | collective-permute-done | bytes 196640 | tf_op jit(solution)/shard_map/ppermute | solution.py:22
  131.5 3.7 %convolution_select_fusion.1 = f32[2,4,8,5,384]{4,2,3,1,0:T(8,128)S(1)} fusion(bf16[3,3,3,384,384]{4,3,2,1,0:T(8,128)(2,1)S(1)} %bitcast.106, bf16[4,4,1,7,2,384]{5,3,4,1,0,2:T(8,128)(2,1)S(1)} %slice.20, bf16[4,4,1,8,5,384]{5,3,4,1,0,2:T(8,128)(2,1)S(1)} %copy.77, pred[8,5]{0,1:T(8,128)(4,1)S(1)} %copy-done.13), kind=kOutput, calls=%fused_computation.14 | convolution fusion | flops 2125553664 | bytes 9117736 | tf_op jit(solution)/shard_map/conv_general_dilated | solution.py:74
  (93 shorter events, 23.0 us)
Async XLA Ops:
  0.6 96.8 %copy-start = (bf16[3,3,3,16,384]{4,3,2,1,0:T(8,128)(2,1)S(1)}, bf16[3,3,3,16,384]{4,3,2,1,0:T(8,128)(2,1)}, u32[]{:S(2)}) copy-start(bf16[3,3,3,16,384]{4,3,2,1,0:T(8,128)(2,1)} %param.27) | copy-start | bytes 995332
  5.2 18.9 %copy-start.6 = (f32[2,4,512]{2,1,0:T(4,128)S(1)}, f32[2,4,512]{2,1,0:T(4,128)}, u32[]{:S(2)}) copy-start(f32[2,4,512]{2,1,0:T(4,128)} %param.26) | copy-start | bytes 49156
  5.2 58.7 %all-to-all-start = ((bf16[32,64,2,384]{3,1,2,0:T(8,128)(2,1)}), bf16[32,64,2,384]{3,1,2,0:T(8,128)(2,1)S(1)}, u32[]{:S(2)}, u32[]{:S(2)}) async-start(bf16[32,64,2,384]{3,1,2,0:T(8,128)(2,1)} %bitcast.87), calls=%async_computation | async-start | bytes 6291456 | tf_op jit(solution)/shard_map/all_to_all | solution.py:131
  17.2 6.3 %copy-start.2 = (bf16[64,1,384]{2,1,0:T(2,128)(2,1)}, bf16[64,1,384]{2,1,0:T(2,128)(2,1)S(1)}, u32[]{:S(2)}) copy-start(bf16[64,1,384]{2,1,0:T(2,128)(2,1)S(1)} %get-tuple-element.13) | copy-start | bytes 147460
  17.8 33.1 %collective-permute-start = (bf16[64,384]{1,0:T(8,128)(2,1)}, bf16[64,384]{1,0:T(8,128)(2,1)S(1)}, u32[]{:S(2)}, u32[]{:S(2)}) collective-permute-start(bf16[64,384]{1,0:T(8,128)(2,1)} %bitcast.85), channel_id=1, source_target_pairs={{0,3},{1,0},{2,1},{3,2},{4,7},{5,4},{6,5},{7,6},{8,11},{9,8},{10,9... | collective-permute-start | bytes 147464 | tf_op jit(solution)/shard_map/ppermute | solution.py:141
  21.1 31.6 %collective-permute-start.1 = (bf16[64,384]{1,0:T(8,128)(2,1)}, bf16[64,384]{1,0:T(8,128)(2,1)}, u32[]{:S(2)}, u32[]{:S(2)}) collective-permute-start(bf16[64,384]{1,0:T(8,128)(2,1)} %bitcast.84), channel_id=1, source_target_pairs={{0,2},{1,3},{2,0},{3,1},{4,6},{5,7},{6,4},{7,5},{8,10},{9,11},{10,... | collective-permute-start | bytes 147464 | tf_op jit(solution)/shard_map/ppermute | solution.py:141
  22.6 31.5 %collective-permute-start.2 = (bf16[64,384]{1,0:T(8,128)(2,1)}, bf16[64,384]{1,0:T(8,128)(2,1)}, u32[]{:S(2)}, u32[]{:S(2)}) collective-permute-start(bf16[64,384]{1,0:T(8,128)(2,1)} %bitcast.83), channel_id=1, source_target_pairs={{0,1},{1,2},{2,3},{3,0},{4,5},{5,6},{6,7},{7,4},{8,9},{9,10},{10,1... | collective-permute-start | bytes 147464 | tf_op jit(solution)/shard_map/ppermute | solution.py:141
  69.0 1.4 %copy-start.1 = (bf16[2048,1,384]{0,2,1:T(8,128)(2,1)S(1)}, bf16[2048,1,384]{0,2,1:T(8,128)(2,1)}, u32[]{:S(2)}) copy-start(bf16[2048,1,384]{0,2,1:T(8,128)(2,1)} %copy.65) | copy-start | bytes 4718596
  70.4 5.9 %copy-start.8 = (f32[1536]{0:T(1024)S(1)}, f32[1536]{0:T(1024)}, u32[]{:S(2)}) copy-start(f32[1536]{0:T(1024)} %param.22) | copy-start | bytes 18436
  70.4 12.2 %copy-start.5 = (bf16[64,1536]{1,0:T(8,128)(2,1)S(1)}, bf16[64,1536]{1,0:T(8,128)(2,1)}, u32[]{:S(2)}) copy-start(bf16[64,1536]{1,0:T(8,128)(2,1)} %param.16) | copy-start | bytes 589828
  70.4 12.2 %copy-start.7 = (f32[1536]{0:T(1024)S(1)}, f32[1536]{0:T(1024)}, u32[]{:S(2)}) copy-start(f32[1536]{0:T(1024)} %param.20) | copy-start | bytes 18436
  71.8 14.4 %copy-start.11 = (bf16[1536,64]{0,1:T(8,128)(2,1)S(1)}, bf16[1536,64]{0,1:T(8,128)(2,1)}, u32[]{:S(2)}) copy-start(bf16[1536,64]{0,1:T(8,128)(2,1)} %param.24) | copy-start | bytes 589828
  71.8 14.4 %copy-start.12 = (f32[1536]{0:T(1024)S(1)}, f32[1536]{0:T(1024)}, u32[]{:S(2)}) copy-start(f32[1536]{0:T(1024)} %param.23) | copy-start | bytes 18436
  71.9 14.9 %copy-start.4 = (f32[2,4,32,16]{3,2,1,0:T(8,128)S(1)}, f32[2,4,32,16]{3,2,1,0:T(8,128)}, u32[]{:S(2)}) copy-start(f32[2,4,32,16]{3,2,1,0:T(8,128)} %reshape.82) | copy-start | bytes 49156
  72.1 25.4 %copy-start.13 = (pred[8,5]{0,1:T(8,128)(4,1)S(1)}, pred[8,5]{0,1:T(8,128)(4,1)}, u32[]{:S(2)}) copy-start(pred[8,5]{0,1:T(8,128)(4,1)} %constant.85) | copy-start | bytes 124
  72.9 9.7 %all-to-all-start.1 = ((bf16[4,64,384]{2,1,0:T(8,128)(2,1)}), bf16[4,64,384]{2,1,0:T(8,128)(2,1)S(1)}, u32[]{:S(2)}, u32[]{:S(2)}) async-start(bf16[4,64,384]{2,1,0:T(8,128)(2,1)} %convert_element_type.48), calls=%async_computation.1 | async-start | bytes 393216 | tf_op jit(solution)/shard_map/all_to_all | solution.py:156
  86.0 25.4 %copy-start.3 = (bf16[64,1536]{1,0:T(8,128)(2,1)}, bf16[64,1536]{1,0:T(8,128)(2,1)S(1)}, u32[]{:S(2)}) copy-start(bf16[64,1536]{1,0:T(8,128)(2,1)S(1)} %get-tuple-element.19) | copy-start | bytes 589828
  86.0 12.7 %copy-start.9 = (f32[384]{0:T(512)S(1)}, f32[384]{0:T(512)}, u32[]{:S(2)}) copy-start(f32[384]{0:T(512)} %param.28) | copy-start | bytes 4612
  86.8 10.4 %collective-permute-start.3 = (bf16[2,4,32,16]{3,2,1,0:T(8,128)(2,1)S(1)}, bf16[2,4,32,16]{3,2,1,0:T(8,128)(2,1)S(1)}, u32[]{:S(2)}, u32[]{:S(2)}) collective-permute-start(bf16[2,4,32,16]{3,2,1,0:T(8,128)(2,1)S(1)} %subtract_convert_fusion), channel_id=1, source_target_pairs={{0,1},{1,2},{2,3},{3,4},{4,5},{5,6},{6,7},{7,8},{8,9},{9,10},{10,1... | collective-permute-start | bytes 24584 | tf_op jit(solution)/shard_map/ppermute | solution.py:22
  99.1 11.8 %collective-permute-start.4 = (bf16[2,4,32,384]{3,1,2,0:T(4,128)(2,1)S(1)}, bf16[2,4,32,384]{3,1,2,0:T(4,128)(2,1)S(1)}, u32[]{:S(2)}, u32[]{:S(2)}) collective-permute-start(bf16[2,4,32,384]{3,1,2,0:T(4,128)(2,1)S(1)} %fusion.47), channel_id=1, source_target_pairs={{0,1},{1,2},{2,3},{3,4},{4,5},{5,6},{6,7},{7,8},{8,9},{9,10},{10,1... | collective-permute-start | bytes 589832 | tf_op jit(solution)/shard_map/ppermute | solution.py:22
  111.3 20.2 %slice-start = ((s8[7962624]{0:T(1024)(128)(4,1)}), s8[4194304]{0:T(1024)(128)(4,1)S(1)}, s32[]{:S(2)}) async-start(s8[7962624]{0:T(1024)(128)(4,1)} %bitcast.105), calls=%async_computation.2 | async-start | bytes 8388608
  111.5 7.4 %copy-start.10 = (f32[384]{0:T(512)S(1)}, f32[384]{0:T(512)}, u32[]{:S(2)}) copy-start(f32[384]{0:T(512)} %param.30) | copy-start | bytes 4612
  111.5 20.0 %slice-start.1 = ((s8[7962624]{0:T(1024)(128)(4,1)}), s8[3768320]{0:T(1024)(128)(4,1)S(1)}, s32[]{:S(2)}) async-start(s8[7962624]{0:T(1024)(128)(4,1)} %bitcast.105), calls=%async_computation.3 | async-start | bytes 7536640
  119.2 11.8 %collective-permute-start.5 = (bf16[2,4,32,384]{3,1,2,0:T(4,128)(2,1)S(1)}, bf16[2,4,32,384]{3,1,2,0:T(4,128)(2,1)S(1)}, u32[]{:S(2)}, u32[]{:S(2)}) collective-permute-start(bf16[2,4,32,384]{3,1,2,0:T(4,128)(2,1)S(1)} %fusion.49), channel_id=1, source_target_pairs={{0,1},{1,2},{2,3},{3,4},{4,5},{5,6},{6,7},{7,8},{8,9},{9,10},{10,1... | collective-permute-start | bytes 589832 | tf_op jit(solution)/shard_map/ppermute | solution.py:22

commit v5 on v2

--- a/solution.py
+++ b/solution.py
@@ -148,11 +148,14 @@
     normed = layer_norm(layer_output, head_scale, head_shift)
     velocity = jnp.dot(normed, head_weight, preferred_element_type=jnp.float32)
     clean = to_latent(velocity, noisy_latent, noise_level)
-    feature = causal_conv(clean, input_kernel).astype(jnp.bfloat16)
-    first_act = norm_silu(feature, first_gain)
-    middle = causal_conv(first_act, middle_kernel)
+    earlier = [shifted(clean, FRAMES, by) for by in (3, 2, 1)]
+    clean_ext = jnp.concatenate(earlier + [clean], axis=0)
+    feature_ext = spatial_conv(clean_ext, input_kernel).astype(jnp.bfloat16)
+    first_act = norm_silu(feature_ext, first_gain)
+    middle = spatial_conv(first_act, middle_kernel)
     second_act = norm_silu(middle, second_gain)
-    decoded = (feature.astype(jnp.float32) + causal_conv(second_act, final_kernel)).astype(
+    feature = feature_ext[-clean.shape[0]:]
+    decoded = (feature.astype(jnp.float32) + spatial_conv(second_act, final_kernel)).astype(
         jnp.bfloat16
     )
     return (layer_output, decoded)

time: 133 us -> 118 us (0.89)
  waiting for transfers between devices: 72.2 us -> 51.6 us
  starting transfers between devices: 22.3 us -> 25 us
  local copies, waits for them, and re-layouts: 14.8 us -> 16.2 us
    ppermute x3, waiting for transfers between devices: 27.4 us -> 6.83 us  [shifted(): return lax.ppermute(x, axis, pairs)]
    ppermute x3, starting transfers between devices: 6.49 us -> 9.04 us  [shifted(): return lax.ppermute(x, axis, pairs)]
where the time goes in v5:
time: 118 us
  waiting for transfers between devices  51.6 us (44%)
  starting transfers between devices  25 us (21%)
  matrix products  19.7 us (17%)
  local copies, waits for them, and re-layouts  16.2 us (14%)
  other arithmetic  3.39 us (3%)
  between operations  1.87 us (2%)
    all_to_all x1, waiting for transfers between devices, gather_group(): got = lax.all_to_all(sent, FRAMES, 0, 0, tiled=True)  34.4 us
    conv_general_dilated x3, matrix products, spatial_conv(): lax.conv_general_dilated(extended[None], kernel, (1, 1, 1), ((0, 0), (1,...  12.8 us
    ppermute x3, starting transfers between devices, shifted(): return lax.ppermute(x, axis, pairs)  9.04 us
    ppermute x3, waiting for transfers between devices, shifted(): return lax.ppermute(x, axis, pairs)  6.83 us
    all_to_all x1, starting transfers between devices, gather_group(): got = lax.all_to_all(sent, FRAMES, 0, 0, tiled=True)  6.83 us
    all_to_all x1, waiting for transfers between devices, body(): attended = lax.all_to_all(group_out, 'hg', 0, 1, tiled=True)  6.32 us
    all_to_all x1, starting transfers between devices, body(): attended = lax.all_to_all(group_out, 'hg', 0, 1, tiled=True)  4.79 us
    all_to_all x1, starting transfers between devices, to_group(): lax.all_to_all(parts, 'hg', 1, 0, tiled=True).reshape(-1, group_width)  4.29 us
  transfers between devices with their start and end apart: 6, of which 6 were waited for; matrix products, arithmetic and copies ran while one was open for 4% of the time, Pallas kernels for 0%

profile of v5, /device:TPU:96, one launch (start us, length us, event | category | flops | bytes accessed | tf_op | source)
XLA Modules:
  0.0 117.7 jit_solution(3161938445971990061)
XLA Ops:
  0.6 1.7 %copy.77 = bf16[8,4,8,384]{3,2,0,1:T(8,128)(2,1)} copy(bf16[8,4,8,384]{3,2,1,0:T(8,128)(2,1)} %bitcast.127) | data formatting | bytes 393216 | tf_op jit(solution)/shard_map/reshape | solution.py:122
  2.3 4.3 %all-to-all-start.1 = ((bf16[64,4,384]{2,0,1:T(8,128)(2,1)}), bf16[64,4,384]{2,0,1:T(8,128)(2,1)S(1)}, u32[]{:S(2)}, u32[]{:S(2)}) async-start(bf16[64,4,384]{2,0,1:T(8,128)(2,1)} %bitcast.109), calls=%async_computation.1 | async-start | bytes 393216 | tf_op jit(solution)/shard_map/all_to_all | solution.py:123
  7.6 1.0 stack.9
  8.9 4.0 %all-to-all-done.1 = bf16[64,4,384]{2,0,1:T(8,128)(2,1)S(1)} async-done(((bf16[64,4,384]{2,0,1:T(8,128)(2,1)}), bf16[64,4,384]{2,0,1:T(8,128)(2,1)S(1)}, u32[]{:S(2)}, u32[]{:S(2)}) %all-to-all-start.1) | async-done | bytes 196640 | tf_op jit(solution)/shard_map/all_to_all | solution.py:123
  12.9 2.2 %broadcast_in_dim.9 = bf16[8,4,64,2,384]{4,2,3,1,0:T(8,128)(2,1)} broadcast(bf16[4,64,2,384]{3,1,2,0:T(8,128)(2,1)S(1)} %copy.43), dimensions={1,2,3,4} | broadcast | bytes 3538944 | tf_op jit(solution)/shard_map/broadcast_in_dim | solution.py:129
  15.1 6.8 %all-to-all-start = ((bf16[32,64,2,384]{3,1,2,0:T(8,128)(2,1)}), bf16[32,64,2,384]{3,1,2,0:T(8,128)(2,1)S(1)}, u32[]{:S(2)}, u32[]{:S(2)}) async-start(bf16[32,64,2,384]{3,1,2,0:T(8,128)(2,1)} %bitcast.111), calls=%async_computation | async-start | bytes 6291456 | tf_op jit(solution)/shard_map/all_to_all | solution.py:131
  23.4 1.7 %reshape_reshape.3 = bf16[256,3,128]{2,1,0:T(4,128)(2,1)} reshape(bf16[4,64,1,384]{3,1,0,2:T(8,128)(2,1)} %bitcast.124) | data formatting | bytes 393216 | tf_op jit(solution)/shard_map/reshape;reshape | solution.py:26
  25.1 34.4 %all-to-all-done = bf16[32,64,2,384]{3,1,2,0:T(8,128)(2,1)S(1)} async-done(((bf16[32,64,2,384]{3,1,2,0:T(8,128)(2,1)}), bf16[32,64,2,384]{3,1,2,0:T(8,128)(2,1)S(1)}, u32[]{:S(2)}, u32[]{:S(2)}) %all-to-all-start) | async-done | bytes 3145760 | tf_op jit(solution)/shard_map/all_to_all | solution.py:131
  60.2 1.6 %copy.49 = bf16[2048,1,384]{0,2,1:T(8,128)(2,1)} copy(bf16[2048,1,384]{2,0,1:T(8,128)(2,1)S(1)} %get-tuple-element.7) | data formatting | bytes 3145728 | tf_op jit(solution)/shard_map/slice | solution.py:137
  62.6 2.0 %bitcast_reduce_fusion = (f32[3,256]{1,0:T(4,128)S(1)}, f32[3,2048,256]{2,1,0:T(8,128)S(1)}) fusion(bf16[2048,3,128]{0,2,1:T(8,128)(2,1)S(1)} %bitcast.113, bf16[256,3,128]{2,1,0:T(4,128)(2,1)} %reshape_reshape.3), kind=kOutput, calls=%fused_computation.1 | convolution fusion | flops 405798144 | bytes 8064000 | tf_op jit(solution)/shard_map/qhd,khd->hqk/dot_general | solution.py:39
  64.6 1.0 fusion.1
  66.0 1.2 %fusion.25 = bf16[256,3,128]{0,2,1:T(8,128)(2,1)S(1)} fusion(bf16[2048,3,128]{0,2,1:T(8,128)(2,1)S(1)} %bitcast.120, f32[3,2048,256]{2,1,0:T(8,128)S(1)} %get-tuple-element.11, f32[3,256]{1,0:T(4,128)S(1)} %get-tuple-element.9, f32[256,3]{0,1:T(4,128)S(1)} %bitcast.128, f32[256,3]{0,1:T(4,128)S(1)} %get-tuple-element.8), kind=kOutput, calls=%fused_computation.30 | convolution fusion | flops 407666688 | bytes 8070144 | tf_op jit(solution)/shard_map/hqk,khd->qhd/dot_general | solution.py:46
  68.2 4.8 %all-to-all-start.2 = ((bf16[4,64,384]{2,1,0:T(8,128)(2,1)}), bf16[4,64,384]{2,1,0:T(8,128)(2,1)S(1)}, u32[]{:S(2)}, u32[]{:S(2)}) async-start(bf16[4,64,384]{2,1,0:T(8,128)(2,1)} %convert_element_type.56), calls=%async_computation.2 | async-start | bytes 393216 | tf_op jit(solution)/shard_map/all_to_all | solution.py:145
  73.0 6.3 %all-to-all-done.2 = bf16[4,64,384]{2,1,0:T(8,128)(2,1)S(1)} async-done(((bf16[4,64,384]{2,1,0:T(8,128)(2,1)}), bf16[4,64,384]{2,1,0:T(8,128)(2,1)S(1)}, u32[]{:S(2)}, u32[]{:S(2)}) %all-to-all-start.2) | async-done | bytes 196640 | tf_op jit(solution)/shard_map/all_to_all | solution.py:145
  79.4 3.4 %convert_reduce_fusion = (f32[64]{0:T(128)S(1)}, bf16[64,1536]{1,0:T(8,128)(2,1)S(1)}) fusion(bf16[64,1536]{1,0:T(8,128)(2,1)S(1)} %bitcast.123, bf16[1536,1536]{1,0:T(8,128)(2,1)} %param.21, f32[1536]{0:T(1024)S(1)} %copy-done.7, bf16[64,1536]{1,0:T(8,128)(2,1)S(1)} %copy-done.5), kind=kOutput, calls=%fused_computation.52 | convolution fusion | flops 302579648 | bytes 5314816 | tf_op jit(solution)/shard_map/dot_general | solution.py:146
  83.7 2.7 %collective-permute-start.2 = (bf16[2,4,32,16]{3,2,1,0:T(8,128)(2,1)S(1)}, bf16[2,4,32,16]{3,2,1,0:T(8,128)(2,1)S(1)}, u32[]{:S(2)}, u32[]{:S(2)}) collective-permute-start(bf16[2,4,32,16]{3,2,1,0:T(8,128)(2,1)S(1)} %subtract_convert_fusion), channel_id=1, source_target_pairs={{0,1},{1,2},{2,3},{3,4},{4,5},{5,6},{6,7},{7,8},{8,9},{9,10},{10,1... | collective-permute-start | bytes 24584 | tf_op jit(solution)/shard_map/ppermute | solution.py:22
  86.4 4.0 %collective-permute-start.1 = (bf16[2,4,32,16]{3,2,1,0:T(8,128)(2,1)S(1)}, bf16[2,4,32,16]{3,2,1,0:T(8,128)(2,1)S(1)}, u32[]{:S(2)}, u32[]{:S(2)}) collective-permute-start(bf16[2,4,32,16]{3,2,1,0:T(8,128)(2,1)S(1)} %subtract_convert_fusion), channel_id=1, source_target_pairs={{0,2},{1,3},{2,4},{3,5},{4,6},{5,7},{6,8},{7,9},{8,10},{9,11},{10,... | collective-permute-start | bytes 24584 | tf_op jit(solution)/shard_map/ppermute | solution.py:22
  90.4 2.3 %collective-permute-start = (bf16[2,4,32,16]{3,2,1,0:T(8,128)(2,1)S(1)}, bf16[2,4,32,16]{3,2,1,0:T(8,128)(2,1)S(1)}, u32[]{:S(2)}, u32[]{:S(2)}) collective-permute-start(bf16[2,4,32,16]{3,2,1,0:T(8,128)(2,1)S(1)} %subtract_convert_fusion), channel_id=1, source_target_pairs={{0,3},{1,4},{2,5},{3,6},{4,7},{5,8},{6,9},{7,10},{8,11},{9,12},{10... | collective-permute-start | bytes 24584 | tf_op jit(solution)/shard_map/ppermute | solution.py:22
  92.8 1.6 %collective-permute-done.2 = bf16[2,4,32,16]{3,2,1,0:T(8,128)(2,1)S(1)} collective-permute-done((bf16[2,4,32,16]{3,2,1,0:T(8,128)(2,1)S(1)}, bf16[2,4,32,16]{3,2,1,0:T(8,128)(2,1)S(1)}, u32[]{:S(2)}, u32[]{:S(2)}) %collective-permute-start.2) | collective-permute-done | bytes 8224 | tf_op jit(solution)/shard_map/ppermute | solution.py:22
  94.3 2.8 %collective-permute-done.1 = bf16[2,4,32,16]{3,2,1,0:T(8,128)(2,1)S(1)} collective-permute-done((bf16[2,4,32,16]{3,2,1,0:T(8,128)(2,1)S(1)}, bf16[2,4,32,16]{3,2,1,0:T(8,128)(2,1)S(1)}, u32[]{:S(2)}, u32[]{:S(2)}) %collective-permute-start.1) | collective-permute-done | bytes 8224 | tf_op jit(solution)/shard_map/ppermute | solution.py:22
  97.1 2.5 %collective-permute-done = bf16[2,4,32,16]{3,2,1,0:T(8,128)(2,1)S(1)} collective-permute-done((bf16[2,4,32,16]{3,2,1,0:T(8,128)(2,1)S(1)}, bf16[2,4,32,16]{3,2,1,0:T(8,128)(2,1)S(1)}, u32[]{:S(2)}, u32[]{:S(2)}) %collective-permute-start) | collective-permute-done | bytes 8224 | tf_op jit(solution)/shard_map/ppermute | solution.py:22
  100.1 1.8 %convert_multiply_fusion = (f32[6,4,8,5,384]{4,2,3,1,0:T(8,128)S(1)}, bf16[6,4,8,5,384]{4,2,3,1,0:T(8,128)(2,1)S(1)}) fusion(bf16[3,3,3,16,384]{4,3,2,1,0:T(8,128)(2,1)S(1)} %copy-done, bf16[8,4,1,7,2,16]{5,3,4,1,0,2:T(8,128)(2,1)S(1)} %slice.24, bf16[8,4,1,8,5,16]{5,3,4,1,0,2:T(8,128)(2,1)S(1)} %copy.56, pred[8,5]{0,1:T(8,128)(4,1)S(1)} %copy-done.13), kind=kOutput, calls=%fused_computation.66 | convolution fusion | flops 267067392 | bytes 2598952 | tf_op jit(solution)/shard_map/conv_general_dilated | solution.py:74
  104.2 7.1 %fusion.79 = (f32[4,4,8,5,384]{4,2,3,1,0:T(8,128)S(1)}, f32[4,4,8,5,384]{4,2,3,1,0:T(8,128)S(1)}) fusion(bf16[3,3,3,384,384]{4,3,2,1,0:T(8,128)(2,1)S(1)} %bitcast.130, bf16[6,4,1,7,2,384]{5,3,4,1,0,2:T(8,128)(2,1)S(1)} %slice.28, bf16[6,4,1,8,5,384]{5,3,4,1,0,2:T(8,128)(2,1)S(1)} %copy.60, pred[8,5]{0,1:T(8,128)(4,1)S(1)} %copy-done.13), kind=kOutput, calls=%fused_computation.97 | convolution fusion | flops 4250320896 | bytes 10924072 | tf_op jit(solution)/shard_map/conv_general_dilated | solution.py:74
  112.9 3.9 %fusion.15 = bf16[2,4,8,5,384]{4,2,3,1,0:T(8,128)(2,1)S(1)} fusion(bf16[3,3,3,384,384]{4,3,2,1,0:T(8,128)(2,1)S(1)} %bitcast.132, bf16[4,4,1,7,2,384]{5,3,4,1,0,2:T(8,128)(2,1)S(1)} %slice.31, bf16[4,4,1,8,5,384]{5,3,4,1,0,2:T(8,128)(2,1)S(1)} %copy.64, bf16[6,4,8,5,384]{4,2,3,1,0:T(8,128)(2,1)S(1)} %get-tuple-element.15, pred[8,5]{0,1:T(8,128)(4,1)S(1)} %copy-done.13), kind=kOutput, calls=%fused_computation.20 | convolution fusion | flops 2125922304 | bytes 9117736 | tf_op jit(solution)/shard_map/conv_general_dilated | solution.py:74
  (81 shorter events, 10.7 us)
Async XLA Ops:
  0.6 99.4 %copy-start = (bf16[3,3,3,16,384]{4,3,2,1,0:T(8,128)(2,1)S(1)}, bf16[3,3,3,16,384]{4,3,2,1,0:T(8,128)(2,1)}, u32[]{:S(2)}) copy-start(bf16[3,3,3,16,384]{4,3,2,1,0:T(8,128)(2,1)} %param.27) | copy-start | bytes 995332
  2.3 10.6 %all-to-all-start.1 = ((bf16[64,4,384]{2,0,1:T(8,128)(2,1)}), bf16[64,4,384]{2,0,1:T(8,128)(2,1)S(1)}, u32[]{:S(2)}, u32[]{:S(2)}) async-start(bf16[64,4,384]{2,0,1:T(8,128)(2,1)} %bitcast.109), calls=%async_computation.1 | async-start | bytes 393216 | tf_op jit(solution)/shard_map/all_to_all | solution.py:123
  12.9 2.2 %copy-start.3 = (bf16[64,4,384]{2,0,1:T(8,128)(2,1)}, bf16[64,4,384]{2,0,1:T(8,128)(2,1)S(1)}, u32[]{:S(2)}) copy-start(bf16[64,4,384]{2,0,1:T(8,128)(2,1)S(1)} %all-to-all-done.1) | copy-start | bytes 589828
  15.1 6.8 %copy-start.6 = (f32[2,4,512]{2,1,0:T(4,128)S(1)}, f32[2,4,512]{2,1,0:T(4,128)}, u32[]{:S(2)}) copy-start(f32[2,4,512]{2,1,0:T(4,128)} %param.26) | copy-start | bytes 49156
  15.1 44.4 %all-to-all-start = ((bf16[32,64,2,384]{3,1,2,0:T(8,128)(2,1)}), bf16[32,64,2,384]{3,1,2,0:T(8,128)(2,1)S(1)}, u32[]{:S(2)}, u32[]{:S(2)}) async-start(bf16[32,64,2,384]{3,1,2,0:T(8,128)(2,1)} %bitcast.111), calls=%async_computation | async-start | bytes 6291456 | tf_op jit(solution)/shard_map/all_to_all | solution.py:131
  64.6 1.4 %copy-start.1 = (bf16[2048,1,384]{0,2,1:T(8,128)(2,1)S(1)}, bf16[2048,1,384]{0,2,1:T(8,128)(2,1)}, u32[]{:S(2)}) copy-start(bf16[2048,1,384]{0,2,1:T(8,128)(2,1)} %copy.49) | copy-start | bytes 4718596
  66.0 7.0 %copy-start.8 = (f32[1536]{0:T(1024)S(1)}, f32[1536]{0:T(1024)}, u32[]{:S(2)}) copy-start(f32[1536]{0:T(1024)} %param.22) | copy-start | bytes 18436
  66.0 13.4 %copy-start.5 = (bf16[64,1536]{1,0:T(8,128)(2,1)S(1)}, bf16[64,1536]{1,0:T(8,128)(2,1)}, u32[]{:S(2)}) copy-start(bf16[64,1536]{1,0:T(8,128)(2,1)} %param.16) | copy-start | bytes 589828
  66.0 13.4 %copy-start.7 = (f32[1536]{0:T(1024)S(1)}, f32[1536]{0:T(1024)}, u32[]{:S(2)}) copy-start(f32[1536]{0:T(1024)} %param.20) | copy-start | bytes 18436
  68.2 11.1 %all-to-all-start.2 = ((bf16[4,64,384]{2,1,0:T(8,128)(2,1)}), bf16[4,64,384]{2,1,0:T(8,128)(2,1)S(1)}, u32[]{:S(2)}, u32[]{:S(2)}) async-start(bf16[4,64,384]{2,1,0:T(8,128)(2,1)} %convert_element_type.56), calls=%async_computation.2 | async-start | bytes 393216 | tf_op jit(solution)/shard_map/all_to_all | solution.py:145
  79.4 3.7 %copy-start.11 = (bf16[1536,64]{0,1:T(8,128)(2,1)S(1)}, bf16[1536,64]{0,1:T(8,128)(2,1)}, u32[]{:S(2)}) copy-start(bf16[1536,64]{0,1:T(8,128)(2,1)} %param.24) | copy-start | bytes 589828
  79.4 3.7 %copy-start.12 = (f32[1536]{0:T(1024)S(1)}, f32[1536]{0:T(1024)}, u32[]{:S(2)}) copy-start(f32[1536]{0:T(1024)} %param.23) | copy-start | bytes 18436
  79.4 4.2 %copy-start.4 = (f32[2,4,32,16]{3,2,1,0:T(8,128)S(1)}, f32[2,4,32,16]{3,2,1,0:T(8,128)}, u32[]{:S(2)}) copy-start(f32[2,4,32,16]{3,2,1,0:T(8,128)} %reshape.84) | copy-start | bytes 49156
  82.9 17.1 %copy-start.2 = (bf16[64,1536]{1,0:T(8,128)(2,1)}, bf16[64,1536]{1,0:T(8,128)(2,1)S(1)}, u32[]{:S(2)}) copy-start(bf16[64,1536]{1,0:T(8,128)(2,1)S(1)} %get-tuple-element.13) | copy-start | bytes 589828
  83.1 16.9 %copy-start.13 = (pred[8,5]{0,1:T(8,128)(4,1)S(1)}, pred[8,5]{0,1:T(8,128)(4,1)}, u32[]{:S(2)}) copy-start(pred[8,5]{0,1:T(8,128)(4,1)} %constant.46) | copy-start | bytes 124
  83.6 20.5 %slice-start = ((s8[7962624]{0:T(1024)(128)(4,1)}), s8[4194304]{0:T(1024)(128)(4,1)S(1)}, s32[]{:S(2)}) async-start(s8[7962624]{0:T(1024)(128)(4,1)} %bitcast.129), calls=%async_computation.3 | async-start | bytes 8388608
  83.7 10.6 %collective-permute-start.2 = (bf16[2,4,32,16]{3,2,1,0:T(8,128)(2,1)S(1)}, bf16[2,4,32,16]{3,2,1,0:T(8,128)(2,1)S(1)}, u32[]{:S(2)}, u32[]{:S(2)}) collective-permute-start(bf16[2,4,32,16]{3,2,1,0:T(8,128)(2,1)S(1)} %subtract_convert_fusion), channel_id=1, source_target_pairs={{0,1},{1,2},{2,3},{3,4},{4,5},{5,6},{6,7},{7,8},{8,9},{9,10},{10,1... | collective-permute-start | bytes 24584 | tf_op jit(solution)/shard_map/ppermute | solution.py:22
  86.4 10.7 %collective-permute-start.1 = (bf16[2,4,32,16]{3,2,1,0:T(8,128)(2,1)S(1)}, bf16[2,4,32,16]{3,2,1,0:T(8,128)(2,1)S(1)}, u32[]{:S(2)}, u32[]{:S(2)}) collective-permute-start(bf16[2,4,32,16]{3,2,1,0:T(8,128)(2,1)S(1)} %subtract_convert_fusion), channel_id=1, source_target_pairs={{0,2},{1,3},{2,4},{3,5},{4,6},{5,7},{6,8},{7,9},{8,10},{9,11},{10,... | collective-permute-start | bytes 24584 | tf_op jit(solution)/shard_map/ppermute | solution.py:22
  90.4 9.2 %collective-permute-start = (bf16[2,4,32,16]{3,2,1,0:T(8,128)(2,1)S(1)}, bf16[2,4,32,16]{3,2,1,0:T(8,128)(2,1)S(1)}, u32[]{:S(2)}, u32[]{:S(2)}) collective-permute-start(bf16[2,4,32,16]{3,2,1,0:T(8,128)(2,1)S(1)} %subtract_convert_fusion), channel_id=1, source_target_pairs={{0,3},{1,4},{2,5},{3,6},{4,7},{5,8},{6,9},{7,10},{8,11},{9,12},{10... | collective-permute-start | bytes 24584 | tf_op jit(solution)/shard_map/ppermute | solution.py:22
  100.0 4.1 %slice-start.1 = ((s8[7962624]{0:T(1024)(128)(4,1)}), s8[3768320]{0:T(1024)(128)(4,1)S(1)}, s32[]{:S(2)}) async-start(s8[7962624]{0:T(1024)(128)(4,1)} %bitcast.129), calls=%async_computation.4 | async-start | bytes 7536640
  102.3 0.7 copy-start.10
  103.9 8.9 %slice-start.2 = ((s8[7962624]{0:T(1024)(128)(4,1)}), s8[4194304]{0:T(1024)(128)(4,1)S(1)}, s32[]{:S(2)}) async-start(s8[7962624]{0:T(1024)(128)(4,1)} %bitcast.131), calls=%async_computation.5 | async-start | bytes 8388608
  104.2 8.7 %slice-start.3 = ((s8[7962624]{0:T(1024)(128)(4,1)}), s8[3768320]{0:T(1024)(128)(4,1)S(1)}, s32[]{:S(2)}) async-start(s8[7962624]{0:T(1024)(128)(4,1)} %bitcast.131), calls=%async_computation.6 | async-start | bytes 7536640
  111.3 0.8 copy-start.9

commit v6 on v5

--- a/solution.py
+++ b/solution.py
@@ -142,8 +142,20 @@
     group_out = (
         (summed / row_total.T[:, :, None]).reshape(group_rows, group_width).astype(jnp.bfloat16)
     )
-    attended = lax.all_to_all(group_out, "hg", 0, 1, tiled=True)
-    projected = jnp.dot(attended, output_weight, preferred_element_type=jnp.float32)
+    me = lax.axis_index("hg")
+    pieces = group_out.reshape(HEAD_GROUPS, rows_here, group_width)
+    weight_groups = output_weight.reshape(HEAD_GROUPS, group_width, -1)
+
+    def project(piece, source):
+        rows_of = lax.dynamic_index_in_dim(weight_groups, source, 0, keepdims=False)
+        return jnp.dot(piece, rows_of, preferred_element_type=jnp.float32)
+
+    projected = project(lax.dynamic_index_in_dim(pieces, me, 0, keepdims=False), me)
+    for k in range(1, HEAD_GROUPS):
+        target = lax.rem(me + k, HEAD_GROUPS)
+        pairs = [(i, (i + k) % HEAD_GROUPS) for i in range(HEAD_GROUPS)]
+        piece = lax.ppermute(lax.dynamic_index_in_dim(pieces, target, 0, False), "hg", pairs)
+        projected = projected + project(piece, lax.rem(me + HEAD_GROUPS - k, HEAD_GROUPS))
     layer_output = (tokens.astype(jnp.float32) + branch_gate * projected).astype(jnp.bfloat16)
     normed = layer_norm(layer_output, head_scale, head_shift)
     velocity = jnp.dot(normed, head_weight, preferred_element_type=jnp.float32)

time: 118 us -> 116 us (0.983)
  waiting for transfers between devices: 51.6 us -> 43 us
  matrix products: 19.7 us -> 23 us
  starting transfers between devices: 25 us -> 27.7 us
    all_to_all x1 -> x0, waiting for transfers between devices: 6.32 us -> none  [body(): attended = lax.all_to_all(group_out, 'hg', 0, 1, tiled=True)]
    ppermute x0 -> x3, starting transfers between devices: none -> 5.63 us  [body(): lax.ppermute(lax.dynamic_index_in_dim(pieces, target, 0, False), 'hg', pa...]
    all_to_all x1 -> x0, starting transfers between devices: 4.79 us -> none  [body(): attended = lax.all_to_all(group_out, 'hg', 0, 1, tiled=True)]
    dot_general x1 -> x4, matrix products: 3.42 us -> 6.66 us  [project(): return jnp.dot(piece, rows_of, preferred_element_type=jnp.float32)]
    ppermute x3, waiting for transfers between devices: 6.83 us -> 4.64 us  [shifted(): return lax.ppermute(x, axis, pairs)]
    ppermute x3, starting transfers between devices: 9.04 us -> 11 us  [shifted(): return lax.ppermute(x, axis, pairs)]
  transfers between devices with their start and end apart: 6 -> 8, of which waited for: 6 -> 4; matrix products, arithmetic and copies ran while one was open for 4% -> 8% of each run, Pallas kernels for 0% -> 0%
where the time goes in v6:
time: 116 us; the launch traced here: 115 us
  waiting for transfers between devices  43 us (37%)
  starting transfers between devices  27.7 us (24%)
  matrix products  23 us (20%)
  local copies, waits for them, and re-layouts  15.7 us (14%)
  other arithmetic  3.39 us (3%)
  between operations  1.99 us (2%)
    all_to_all x1, waiting for transfers between devices, gather_group(): got = lax.all_to_all(sent, FRAMES, 0, 0, tiled=True)  34.4 us
    conv_general_dilated x3, matrix products, spatial_conv(): lax.conv_general_dilated(extended[None], kernel, (1, 1, 1), ((0, 0), (1,...  12.8 us
    ppermute x3, starting transfers between devices, shifted(): return lax.ppermute(x, axis, pairs)  11 us
    all_to_all x1, starting transfers between devices, gather_group(): got = lax.all_to_all(sent, FRAMES, 0, 0, tiled=True)  6.83 us
    dot_general x4, matrix products, project(): return jnp.dot(piece, rows_of, preferred_element_type=jnp.float32)  6.66 us
    ppermute x3, starting transfers between devices, body(): lax.ppermute(lax.dynamic_index_in_dim(pieces, target, 0, False), 'hg', pa...  5.63 us
    ppermute x3, waiting for transfers between devices, shifted(): return lax.ppermute(x, axis, pairs)  4.64 us
    all_to_all x1, starting transfers between devices, to_group(): lax.all_to_all(parts, 'hg', 1, 0, tiled=True).reshape(-1, group_width)  4.29 us
  transfers between devices with their start and end apart: 8, of which 4 were waited for; matrix products, arithmetic and copies ran while one was open for 8% of the time, Pallas kernels for 0%

profile of v6, /device:TPU:96, one launch (start us, length us, event | category | flops | bytes accessed | tf_op | source)
XLA Modules:
  0.0 114.8 jit_solution(18184707658549900918)
XLA Ops:
  0.6 1.7 %copy.74 = bf16[8,4,8,384]{3,2,0,1:T(8,128)(2,1)} copy(bf16[8,4,8,384]{3,2,1,0:T(8,128)(2,1)} %bitcast.151) | data formatting | bytes 393216 | tf_op jit(solution)/shard_map/reshape | solution.py:122
  2.3 4.3 %all-to-all-start.1 = ((bf16[64,4,384]{2,0,1:T(8,128)(2,1)}), bf16[64,4,384]{2,0,1:T(8,128)(2,1)S(1)}, u32[]{:S(2)}, u32[]{:S(2)}) async-start(bf16[64,4,384]{2,0,1:T(8,128)(2,1)} %bitcast.131), calls=%async_computation.1 | async-start | bytes 393216 | tf_op jit(solution)/shard_map/all_to_all | solution.py:123
  8.9 4.0 %all-to-all-done.1 = bf16[64,4,384]{2,0,1:T(8,128)(2,1)S(1)} async-done(((bf16[64,4,384]{2,0,1:T(8,128)(2,1)}), bf16[64,4,384]{2,0,1:T(8,128)(2,1)S(1)}, u32[]{:S(2)}, u32[]{:S(2)}) %all-to-all-start.1) | async-done | bytes 196640 | tf_op jit(solution)/shard_map/all_to_all | solution.py:123
  12.9 2.2 %broadcast_in_dim.9 = bf16[8,4,64,2,384]{4,2,3,1,0:T(8,128)(2,1)} broadcast(bf16[4,64,2,384]{3,1,2,0:T(8,128)(2,1)S(1)} %copy.42), dimensions={1,2,3,4} | broadcast | bytes 3538944 | tf_op jit(solution)/shard_map/broadcast_in_dim | solution.py:129
  15.1 6.8 %all-to-all-start = ((bf16[32,64,2,384]{3,1,2,0:T(8,128)(2,1)}), bf16[32,64,2,384]{3,1,2,0:T(8,128)(2,1)S(1)}, u32[]{:S(2)}, u32[]{:S(2)}) async-start(bf16[32,64,2,384]{3,1,2,0:T(8,128)(2,1)} %bitcast.133), calls=%async_computation | async-start | bytes 6291456 | tf_op jit(solution)/shard_map/all_to_all | solution.py:131
  23.4 1.7 %reshape_reshape.3 = bf16[256,3,128]{2,1,0:T(4,128)(2,1)} reshape(bf16[4,64,1,384]{3,1,0,2:T(8,128)(2,1)} %bitcast.149) | data formatting | bytes 393216 | tf_op jit(solution)/shard_map/reshape;reshape | solution.py:26
  25.1 34.4 %all-to-all-done = bf16[32,64,2,384]{3,1,2,0:T(8,128)(2,1)S(1)} async-done(((bf16[32,64,2,384]{3,1,2,0:T(8,128)(2,1)}), bf16[32,64,2,384]{3,1,2,0:T(8,128)(2,1)S(1)}, u32[]{:S(2)}, u32[]{:S(2)}) %all-to-all-start) | async-done | bytes 3145760 | tf_op jit(solution)/shard_map/all_to_all | solution.py:131
  60.2 1.6 %copy.48 = bf16[2048,1,384]{0,2,1:T(8,128)(2,1)} copy(bf16[2048,1,384]{2,0,1:T(8,128)(2,1)S(1)} %get-tuple-element.7) | data formatting | bytes 3145728 | tf_op jit(solution)/shard_map/slice | solution.py:137
  62.6 2.0 %bitcast_reduce_fusion = (f32[3,256]{1,0:T(4,128)S(1)}, f32[3,2048,256]{2,1,0:T(8,128)S(1)}) fusion(bf16[2048,3,128]{0,2,1:T(8,128)(2,1)S(1)} %bitcast.135, bf16[256,3,128]{2,1,0:T(4,128)(2,1)} %reshape_reshape.3), kind=kOutput, calls=%fused_computation.1 | convolution fusion | flops 405798144 | bytes 8064000 | tf_op jit(solution)/shard_map/qhd,khd->hqk/dot_general | solution.py:39
  66.0 1.2 %fusion.37 = bf16[256,3,128]{0,2,1:T(8,128)(2,1)S(1)} fusion(bf16[2048,3,128]{0,2,1:T(8,128)(2,1)S(1)} %bitcast.146, f32[3,2048,256]{2,1,0:T(8,128)S(1)} %get-tuple-element.14, f32[3,256]{1,0:T(4,128)S(1)} %get-tuple-element.12, f32[256,3]{0,1:T(4,128)S(1)} %bitcast.152, f32[256,3]{0,1:T(4,128)S(1)} %get-tuple-element.11), kind=kOutput, calls=%fused_computation.43 | convolution fusion | flops 407666688 | bytes 8070144 | tf_op jit(solution)/shard_map/hqk,khd->qhd/dot_general | solution.py:46
  67.6 2.0 %collective-permute-start.2 = (bf16[64,384]{1,0:T(8,128)(2,1)S(1)}, bf16[64,384]{1,0:T(8,128)(2,1)S(1)}, u32[]{:S(2)}, u32[]{:S(2)}) collective-permute-start(bf16[64,384]{1,0:T(8,128)(2,1)S(1)} %get-tuple-element.9), channel_id=1, source_target_pairs={{0,3},{1,0},{2,1},{3,2},{4,7},{5,4},{6,5},{7,6},{8,11},{9,8},{10,9... | collective-permute-start | bytes 147464 | tf_op jit(solution)/shard_map/ppermute | solution.py:157
  69.7 3.5 %collective-permute-start.1 = (bf16[64,384]{1,0:T(8,128)(2,1)S(1)}, bf16[64,384]{1,0:T(8,128)(2,1)S(1)}, u32[]{:S(2)}, u32[]{:S(2)}) collective-permute-start(bf16[64,384]{1,0:T(8,128)(2,1)S(1)} %get-tuple-element.8), channel_id=1, source_target_pairs={{0,2},{1,3},{2,0},{3,1},{4,6},{5,7},{6,4},{7,5},{8,10},{9,11},{10,... | collective-permute-start | bytes 147464 | tf_op jit(solution)/shard_map/ppermute | solution.py:157
  73.2 1.6 %fusion.27 = f32[64,1536]{1,0:T(8,128)S(1)} fusion(bf16[4,384,1536]{2,1,0:T(8,128)(2,1)} %bitcast.138, s32[]{:T(128)S(6)} %select_n.19, bf16[4,64,384]{2,1,0:T(8,128)(2,1)S(1)} %convert_element_type.56), kind=kOutput, calls=%fused_computation.34 | convolution fusion | flops 75497472 | bytes 1623040 | tf_op jit(solution)/shard_map/dot_general | solution.py:151
  74.9 1.7 %convolution_add_fusion.1 = f32[64,1536]{1,0:T(8,128)S(1)} fusion(f32[64,1536]{1,0:T(8,128)S(1)} %fusion.27, bf16[64,384]{1,0:T(8,128)(2,1)S(1)} %collective-permute-done, bf16[4,384,1536]{2,1,0:T(8,128)(2,1)} %bitcast.139, s32[]{:T(128)S(6)} %select_n.21), kind=kOutput, calls=%fused_computation.10 | convolution fusion | flops 75595776 | bytes 2015236 | tf_op jit(solution)/shard_map/dot_general | solution.py:151
  76.5 1.6 %fusion.23 = f32[64,1536]{1,0:T(8,128)S(1)} fusion(bf16[64,384]{1,0:T(8,128)(2,1)S(1)} %collective-permute-done.2, bf16[4,384,1536]{2,1,0:T(8,128)(2,1)} %bitcast.140, s32[]{:T(128)S(6)} %select_n.20), kind=kOutput, calls=%fused_computation.30 | convolution fusion | flops 75497472 | bytes 1622020 | tf_op jit(solution)/shard_map/dot_general | solution.py:151
  78.2 1.8 %convert_reduce_fusion = (f32[64]{0:T(128)S(1)}, bf16[64,1536]{1,0:T(8,128)(2,1)S(1)}) fusion(f32[64,1536]{1,0:T(8,128)S(1)} %fusion.23, f32[64,1536]{1,0:T(8,128)S(1)} %convolution_add_fusion.1, bf16[64,384]{1,0:T(8,128)(2,1)S(1)} %collective-permute-done.1, bf16[4,384,1536]{2,1,0:T(8,128)(2,1)} %bitcast.141, s32[]{:T(128)S(6)} %select_n.22, ...), kind=kOutput, calls=%fused_computation.65 | convolution fusion | flops 76283840 | bytes 2414852 | tf_op jit(solution)/shard_map/dot_general | solution.py:151
  80.8 2.6 %collective-permute-start.5 = (bf16[2,4,32,16]{3,2,1,0:T(8,128)(2,1)S(1)}, bf16[2,4,32,16]{3,2,1,0:T(8,128)(2,1)S(1)}, u32[]{:S(2)}, u32[]{:S(2)}) collective-permute-start(bf16[2,4,32,16]{3,2,1,0:T(8,128)(2,1)S(1)} %subtract_convert_fusion), channel_id=1, source_target_pairs={{0,1},{1,2},{2,3},{3,4},{4,5},{5,6},{6,7},{7,8},{8,9},{9,10},{10,1... | collective-permute-start | bytes 24584 | tf_op jit(solution)/shard_map/ppermute | solution.py:22
  83.5 3.9 %collective-permute-start.4 = (bf16[2,4,32,16]{3,2,1,0:T(8,128)(2,1)S(1)}, bf16[2,4,32,16]{3,2,1,0:T(8,128)(2,1)S(1)}, u32[]{:S(2)}, u32[]{:S(2)}) collective-permute-start(bf16[2,4,32,16]{3,2,1,0:T(8,128)(2,1)S(1)} %subtract_convert_fusion), channel_id=1, source_target_pairs={{0,2},{1,3},{2,4},{3,5},{4,6},{5,7},{6,8},{7,9},{8,10},{9,11},{10,... | collective-permute-start | bytes 24584 | tf_op jit(solution)/shard_map/ppermute | solution.py:22
  87.3 4.5 %collective-permute-start.3 = (bf16[2,4,32,16]{3,2,1,0:T(8,128)(2,1)S(1)}, bf16[2,4,32,16]{3,2,1,0:T(8,128)(2,1)S(1)}, u32[]{:S(2)}, u32[]{:S(2)}) collective-permute-start(bf16[2,4,32,16]{3,2,1,0:T(8,128)(2,1)S(1)} %subtract_convert_fusion), channel_id=1, source_target_pairs={{0,3},{1,4},{2,5},{3,6},{4,7},{5,8},{6,9},{7,10},{8,11},{9,12},{10... | collective-permute-start | bytes 24584 | tf_op jit(solution)/shard_map/ppermute | solution.py:22
  91.9 2.3 %collective-permute-done.4 = bf16[2,4,32,16]{3,2,1,0:T(8,128)(2,1)S(1)} collective-permute-done((bf16[2,4,32,16]{3,2,1,0:T(8,128)(2,1)S(1)}, bf16[2,4,32,16]{3,2,1,0:T(8,128)(2,1)S(1)}, u32[]{:S(2)}, u32[]{:S(2)}) %collective-permute-start.4) | collective-permute-done | bytes 8224 | tf_op jit(solution)/shard_map/ppermute | solution.py:22
  94.1 2.4 %collective-permute-done.3 = bf16[2,4,32,16]{3,2,1,0:T(8,128)(2,1)S(1)} collective-permute-done((bf16[2,4,32,16]{3,2,1,0:T(8,128)(2,1)S(1)}, bf16[2,4,32,16]{3,2,1,0:T(8,128)(2,1)S(1)}, u32[]{:S(2)}, u32[]{:S(2)}) %collective-permute-start.3) | collective-permute-done | bytes 8224 | tf_op jit(solution)/shard_map/ppermute | solution.py:22
  97.0 1.8 %convert_multiply_fusion = (f32[6,4,8,5,384]{4,2,3,1,0:T(8,128)S(1)}, bf16[6,4,8,5,384]{4,2,3,1,0:T(8,128)(2,1)S(1)}) fusion(bf16[3,3,3,16,384]{4,3,2,1,0:T(8,128)(2,1)S(1)} %copy-done, bf16[8,4,1,7,2,16]{5,3,4,1,0,2:T(8,128)(2,1)S(1)} %slice.24, bf16[8,4,1,8,5,16]{5,3,4,1,0,2:T(8,128)(2,1)S(1)} %copy.54, pred[8,5]{0,1:T(8,128)(4,1)S(1)} %copy-done.13), kind=kOutput, calls=%fused_computation.79 | convolution fusion | flops 267067392 | bytes 2598952 | tf_op jit(solution)/shard_map/conv_general_dilated | solution.py:74
  101.1 7.1 %fusion.97 = (f32[4,4,8,5,384]{4,2,3,1,0:T(8,128)S(1)}, f32[4,4,8,5,384]{4,2,3,1,0:T(8,128)S(1)}) fusion(bf16[3,3,3,384,384]{4,3,2,1,0:T(8,128)(2,1)S(1)} %bitcast.154, bf16[6,4,1,7,2,384]{5,3,4,1,0,2:T(8,128)(2,1)S(1)} %slice.28, bf16[6,4,1,8,5,384]{5,3,4,1,0,2:T(8,128)(2,1)S(1)} %copy.58, pred[8,5]{0,1:T(8,128)(4,1)S(1)} %copy-done.13), kind=kOutput, calls=%fused_computation.119 | convolution fusion | flops 4250320896 | bytes 10924072 | tf_op jit(solution)/shard_map/conv_general_dilated | solution.py:74
  110.0 3.9 %fusion.17 = bf16[2,4,8,5,384]{4,2,3,1,0:T(8,128)(2,1)S(1)} fusion(bf16[3,3,3,384,384]{4,3,2,1,0:T(8,128)(2,1)S(1)} %bitcast.156, bf16[4,4,1,7,2,384]{5,3,4,1,0,2:T(8,128)(2,1)S(1)} %slice.31, bf16[4,4,1,8,5,384]{5,3,4,1,0,2:T(8,128)(2,1)S(1)} %copy.62, bf16[6,4,8,5,384]{4,2,3,1,0:T(8,128)(2,1)S(1)} %get-tuple-element.18, pred[8,5]{0,1:T(8,128)(4,1)S(1)} %copy-done.13), kind=kOutput, calls=%fused_computation.23 | convolution fusion | flops 2125922304 | bytes 9117736 | tf_op jit(solution)/shard_map/conv_general_dilated | solution.py:74
  (88 shorter events, 12.3 us)
Async XLA Ops:
  0.6 96.3 %copy-start = (bf16[3,3,3,16,384]{4,3,2,1,0:T(8,128)(2,1)S(1)}, bf16[3,3,3,16,384]{4,3,2,1,0:T(8,128)(2,1)}, u32[]{:S(2)}) copy-start(bf16[3,3,3,16,384]{4,3,2,1,0:T(8,128)(2,1)} %param.27) | copy-start | bytes 995332
  2.3 10.6 %all-to-all-start.1 = ((bf16[64,4,384]{2,0,1:T(8,128)(2,1)}), bf16[64,4,384]{2,0,1:T(8,128)(2,1)S(1)}, u32[]{:S(2)}, u32[]{:S(2)}) async-start(bf16[64,4,384]{2,0,1:T(8,128)(2,1)} %bitcast.131), calls=%async_computation.1 | async-start | bytes 393216 | tf_op jit(solution)/shard_map/all_to_all | solution.py:123
  12.9 2.2 %copy-start.3 = (bf16[64,4,384]{2,0,1:T(8,128)(2,1)}, bf16[64,4,384]{2,0,1:T(8,128)(2,1)S(1)}, u32[]{:S(2)}) copy-start(bf16[64,4,384]{2,0,1:T(8,128)(2,1)S(1)} %all-to-all-done.1) | copy-start | bytes 589828
  15.1 6.9 %copy-start.6 = (f32[2,4,512]{2,1,0:T(4,128)S(1)}, f32[2,4,512]{2,1,0:T(4,128)}, u32[]{:S(2)}) copy-start(f32[2,4,512]{2,1,0:T(4,128)} %param.26) | copy-start | bytes 49156
  15.1 8.3 %copy-start.8 = (f32[1536]{0:T(1024)S(1)}, f32[1536]{0:T(1024)}, u32[]{:S(2)}) copy-start(f32[1536]{0:T(1024)} %param.22) | copy-start | bytes 18436
  15.1 44.4 %all-to-all-start = ((bf16[32,64,2,384]{3,1,2,0:T(8,128)(2,1)}), bf16[32,64,2,384]{3,1,2,0:T(8,128)(2,1)S(1)}, u32[]{:S(2)}, u32[]{:S(2)}) async-start(bf16[32,64,2,384]{3,1,2,0:T(8,128)(2,1)} %bitcast.133), calls=%async_computation | async-start | bytes 6291456 | tf_op jit(solution)/shard_map/all_to_all | solution.py:131
  64.6 1.4 %copy-start.1 = (bf16[2048,1,384]{0,2,1:T(8,128)(2,1)S(1)}, bf16[2048,1,384]{0,2,1:T(8,128)(2,1)}, u32[]{:S(2)}) copy-start(bf16[2048,1,384]{0,2,1:T(8,128)(2,1)} %copy.48) | copy-start | bytes 4718596
  67.6 8.9 %collective-permute-start.2 = (bf16[64,384]{1,0:T(8,128)(2,1)S(1)}, bf16[64,384]{1,0:T(8,128)(2,1)S(1)}, u32[]{:S(2)}, u32[]{:S(2)}) collective-permute-start(bf16[64,384]{1,0:T(8,128)(2,1)S(1)} %get-tuple-element.9), channel_id=1, source_target_pairs={{0,3},{1,0},{2,1},{3,2},{4,7},{5,4},{6,5},{7,6},{8,11},{9,8},{10,9... | collective-permute-start | bytes 147464 | tf_op jit(solution)/shard_map/ppermute | solution.py:157
  69.6 5.3 %collective-permute-start = (bf16[64,384]{1,0:T(8,128)(2,1)S(1)}, bf16[64,384]{1,0:T(8,128)(2,1)S(1)}, u32[]{:S(2)}, u32[]{:S(2)}) collective-permute-start(bf16[64,384]{1,0:T(8,128)(2,1)S(1)} %get-tuple-element.10), channel_id=1, source_target_pairs={{0,1},{1,2},{2,3},{3,0},{4,5},{5,6},{6,7},{7,4},{8,9},{9,10},{10,1... | collective-permute-start | bytes 147464 | tf_op jit(solution)/shard_map/ppermute | solution.py:157
  69.7 8.5 %collective-permute-start.1 = (bf16[64,384]{1,0:T(8,128)(2,1)S(1)}, bf16[64,384]{1,0:T(8,128)(2,1)S(1)}, u32[]{:S(2)}, u32[]{:S(2)}) collective-permute-start(bf16[64,384]{1,0:T(8,128)(2,1)S(1)} %get-tuple-element.8), channel_id=1, source_target_pairs={{0,2},{1,3},{2,0},{3,1},{4,6},{5,7},{6,4},{7,5},{8,10},{9,11},{10,... | collective-permute-start | bytes 147464 | tf_op jit(solution)/shard_map/ppermute | solution.py:157
  74.8 3.4 %copy-start.5 = (bf16[64,1536]{1,0:T(8,128)(2,1)S(1)}, bf16[64,1536]{1,0:T(8,128)(2,1)}, u32[]{:S(2)}) copy-start(bf16[64,1536]{1,0:T(8,128)(2,1)} %param.16) | copy-start | bytes 589828
  74.8 3.4 %copy-start.7 = (f32[1536]{0:T(1024)S(1)}, f32[1536]{0:T(1024)}, u32[]{:S(2)}) copy-start(f32[1536]{0:T(1024)} %param.20) | copy-start | bytes 18436
  78.1 2.1 %copy-start.11 = (bf16[1536,64]{0,1:T(8,128)(2,1)S(1)}, bf16[1536,64]{0,1:T(8,128)(2,1)}, u32[]{:S(2)}) copy-start(bf16[1536,64]{0,1:T(8,128)(2,1)} %param.24) | copy-start | bytes 589828
  78.1 2.1 %copy-start.12 = (f32[1536]{0:T(1024)S(1)}, f32[1536]{0:T(1024)}, u32[]{:S(2)}) copy-start(f32[1536]{0:T(1024)} %param.23) | copy-start | bytes 18436
  78.2 2.7 %copy-start.4 = (f32[2,4,32,16]{3,2,1,0:T(8,128)S(1)}, f32[2,4,32,16]{3,2,1,0:T(8,128)}, u32[]{:S(2)}) copy-start(f32[2,4,32,16]{3,2,1,0:T(8,128)} %reshape.86) | copy-start | bytes 49156
  80.0 16.8 %copy-start.2 = (bf16[64,1536]{1,0:T(8,128)(2,1)}, bf16[64,1536]{1,0:T(8,128)(2,1)S(1)}, u32[]{:S(2)}) copy-start(bf16[64,1536]{1,0:T(8,128)(2,1)S(1)} %get-tuple-element.16) | copy-start | bytes 589828
  80.6 16.4 %copy-start.13 = (pred[8,5]{0,1:T(8,128)(4,1)S(1)}, pred[8,5]{0,1:T(8,128)(4,1)}, u32[]{:S(2)}) copy-start(pred[8,5]{0,1:T(8,128)(4,1)} %constant.99) | copy-start | bytes 124
  80.7 20.3 %slice-start = ((s8[7962624]{0:T(1024)(128)(4,1)}), s8[4194304]{0:T(1024)(128)(4,1)S(1)}, s32[]{:S(2)}) async-start(s8[7962624]{0:T(1024)(128)(4,1)} %bitcast.153), calls=%async_computation.2 | async-start | bytes 8388608
  80.8 11.0 %collective-permute-start.5 = (bf16[2,4,32,16]{3,2,1,0:T(8,128)(2,1)S(1)}, bf16[2,4,32,16]{3,2,1,0:T(8,128)(2,1)S(1)}, u32[]{:S(2)}, u32[]{:S(2)}) collective-permute-start(bf16[2,4,32,16]{3,2,1,0:T(8,128)(2,1)S(1)} %subtract_convert_fusion), channel_id=1, source_target_pairs={{0,1},{1,2},{2,3},{3,4},{4,5},{5,6},{6,7},{7,8},{8,9},{9,10},{10,1... | collective-permute-start | bytes 24584 | tf_op jit(solution)/shard_map/ppermute | solution.py:22
  83.5 10.7 %collective-permute-start.4 = (bf16[2,4,32,16]{3,2,1,0:T(8,128)(2,1)S(1)}, bf16[2,4,32,16]{3,2,1,0:T(8,128)(2,1)S(1)}, u32[]{:S(2)}, u32[]{:S(2)}) collective-permute-start(bf16[2,4,32,16]{3,2,1,0:T(8,128)(2,1)S(1)} %subtract_convert_fusion), channel_id=1, source_target_pairs={{0,2},{1,3},{2,4},{3,5},{4,6},{5,7},{6,8},{7,9},{8,10},{9,11},{10,... | collective-permute-start | bytes 24584 | tf_op jit(solution)/shard_map/ppermute | solution.py:22
  87.3 9.2 %collective-permute-start.3 = (bf16[2,4,32,16]{3,2,1,0:T(8,128)(2,1)S(1)}, bf16[2,4,32,16]{3,2,1,0:T(8,128)(2,1)S(1)}, u32[]{:S(2)}, u32[]{:S(2)}) collective-permute-start(bf16[2,4,32,16]{3,2,1,0:T(8,128)(2,1)S(1)} %subtract_convert_fusion), channel_id=1, source_target_pairs={{0,3},{1,4},{2,5},{3,6},{4,7},{5,8},{6,9},{7,10},{8,11},{9,12},{10... | collective-permute-start | bytes 24584 | tf_op jit(solution)/shard_map/ppermute | solution.py:22
  96.9 4.1 %slice-start.1 = ((s8[7962624]{0:T(1024)(128)(4,1)}), s8[3768320]{0:T(1024)(128)(4,1)S(1)}, s32[]{:S(2)}) async-start(s8[7962624]{0:T(1024)(128)(4,1)} %bitcast.153), calls=%async_computation.3 | async-start | bytes 7536640
  100.8 9.1 %slice-start.2 = ((s8[7962624]{0:T(1024)(128)(4,1)}), s8[4194304]{0:T(1024)(128)(4,1)S(1)}, s32[]{:S(2)}) async-start(s8[7962624]{0:T(1024)(128)(4,1)} %bitcast.155), calls=%async_computation.4 | async-start | bytes 8388608
  101.1 8.9 %slice-start.3 = ((s8[7962624]{0:T(1024)(128)(4,1)}), s8[3768320]{0:T(1024)(128)(4,1)S(1)}, s32[]{:S(2)}) async-start(s8[7962624]{0:T(1024)(128)(4,1)} %bitcast.155), calls=%async_computation.5 | async-start | bytes 7536640
  (2 other events, 1.4 us)

commit v7 on v6

--- a/solution.py
+++ b/solution.py
@@ -122,19 +122,21 @@
         parts = matrix.reshape(rows_here, HEAD_GROUPS, group_width)
         return lax.all_to_all(parts, "hg", 1, 0, tiled=True).reshape(-1, group_width)
 
-    def gather_group(matrix):
+    def gather_groups_of(*matrices):
         blocks = lax.psum(1, "blk")
-        parts = matrix.reshape(rows_here, -1, HEAD_GROUPS, group_width)
-        parts = jnp.moveaxis(parts, 2, 0)
+        parts = jnp.stack(
+            [m.reshape(rows_here, HEAD_GROUPS, group_width).transpose(1, 0, 2) for m in matrices],
+            axis=1,
+        )
         sent = jnp.broadcast_to(parts[None], (blocks,) + parts.shape)
         sent = sent.reshape((blocks * HEAD_GROUPS,) + parts.shape[1:])
         got = lax.all_to_all(sent, FRAMES, 0, 0, tiled=True)
-        return got.reshape((-1,) + got.shape[2:])
+        return [got[:, i].reshape(-1, group_width) for i in range(len(matrices))]
 
     query_heads = split_heads(to_group(queries), group_heads)
-    key_value = gather_group(jnp.stack([keys, values], axis=1))
-    key_heads = split_heads(key_value[:, 0], group_heads)
-    value_heads = split_heads(key_value[:, 1], group_heads)
+    key_rows, value_rows = gather_groups_of(keys, values)
+    key_heads = split_heads(key_rows, group_heads)
+    value_heads = split_heads(value_rows, group_heads)
     group_rows = query_heads.shape[0]
     row_peak, row_total, summed = absorb_block(
         empty_state(group_heads, group_rows), query_heads, key_heads, value_heads

time: 116 us -> 127 us (1.095)
  local copies, waits for them, and re-layouts: 15.7 us -> 22.7 us
  other arithmetic: 3.39 us -> 6.33 us
  matrix products: 23 us -> 24.8 us
    another operation x1 -> x3, local copies, waits for them, and re-layouts: 1.68 us -> 9.55 us  [split_heads(): return matrix.reshape(matrix.shape[0], head_count, HEAD_DIM)]
    reduce_sum x1, other arithmetic: 1.04 us -> 3.98 us  [absorb_block(): row_total = jnp.sum(weights, axis=-1)]
    reshape x0 -> x2, local copies, waits for them, and re-layouts: none -> 1.95 us  [gather_groups_of(): m.reshape(rows_here, HEAD_GROUPS, group_width).transpose(1, 0, 2)]
    another operation x2 -> x1, local copies, waits for them, and re-layouts: 1.95 us -> 0.05 us  [gather_groups_of(): jnp.stack([m.reshape(rows_here, HEAD_GROUPS, group_width).transpose(1, 0,...]
    dot_general x1, matrix products: 2 us -> 3.64 us  [absorb_block(): jnp.einsum('qhd,khd->hqk', query_heads, key_heads, preferred_element_type...]
    slice x3 -> x1, local copies, waits for them, and re-layouts: 2.71 us -> 2.08 us  [gather_groups_of(): return [got[:, i].reshape(-1, group_width) for i in range(len(matrices))]]
where the time goes in v7:
time: 127 us; the launch traced here: 126 us
  waiting for transfers between devices  43 us (34%)
  starting transfers between devices  27.7 us (22%)
  matrix products  24.8 us (20%)
  local copies, waits for them, and re-layouts  22.7 us (18%)
  other arithmetic  6.33 us (5%)
  between operations  1.99 us (2%)
    all_to_all x1, waiting for transfers between devices, gather_groups_of(): got = lax.all_to_all(sent, FRAMES, 0, 0, tiled=True)  34.3 us
    conv_general_dilated x3, matrix products, spatial_conv(): lax.conv_general_dilated(extended[None], kernel, (1, 1, 1), ((0, 0), (1,...  12.8 us
    ppermute x3, starting transfers between devices, shifted(): return lax.ppermute(x, axis, pairs)  11 us
    another operation x3, local copies, waits for them, and re-layouts, split_heads(): return matrix.reshape(matrix.shape[0], head_count, HEAD_DIM)  9.55 us
    all_to_all x1, starting transfers between devices, gather_groups_of(): got = lax.all_to_all(sent, FRAMES, 0, 0, tiled=True)  6.83 us
    dot_general x4, matrix products, project(): return jnp.dot(piece, rows_of, preferred_element_type=jnp.float32)  6.65 us
    ppermute x3, starting transfers between devices, body(): lax.ppermute(lax.dynamic_index_in_dim(pieces, target, 0, False), 'hg', pa...  5.62 us
    ppermute x3, waiting for transfers between devices, shifted(): return lax.ppermute(x, axis, pairs)  4.64 us
  transfers between devices with their start and end apart: 8, of which 4 were waited for; matrix products, arithmetic and copies ran while one was open for 8% of the time, Pallas kernels for 0%

profile of v7, /device:TPU:96, one launch (start us, length us, event | category | flops | bytes accessed | tf_op | source)
XLA Modules:
  0.0 126.5 jit_solution(14420826368582906846)
XLA Ops:
  0.6 1.7 %copy.84 = bf16[8,4,8,384]{3,2,0,1:T(8,128)(2,1)} copy(bf16[8,4,8,384]{3,2,1,0:T(8,128)(2,1)} %bitcast.153) | data formatting | bytes 393216 | tf_op jit(solution)/shard_map/reshape | solution.py:122
  2.3 4.3 %all-to-all-start.1 = ((bf16[64,4,384]{2,0,1:T(8,128)(2,1)}), bf16[64,4,384]{2,0,1:T(8,128)(2,1)S(1)}, u32[]{:S(2)}, u32[]{:S(2)}) async-start(bf16[64,4,384]{2,0,1:T(8,128)(2,1)} %bitcast.134), calls=%async_computation.1 | async-start | bytes 393216 | tf_op jit(solution)/shard_map/all_to_all | solution.py:123
  8.9 4.0 %all-to-all-done.1 = bf16[64,4,384]{2,0,1:T(8,128)(2,1)S(1)} async-done(((bf16[64,4,384]{2,0,1:T(8,128)(2,1)}), bf16[64,4,384]{2,0,1:T(8,128)(2,1)S(1)}, u32[]{:S(2)}, u32[]{:S(2)}) %all-to-all-start.1) | async-done | bytes 196640 | tf_op jit(solution)/shard_map/all_to_all | solution.py:123
  12.9 2.2 %broadcast_in_dim.9 = bf16[8,4,2,64,384]{4,3,2,1,0:T(8,128)(2,1)} broadcast(bf16[4,2,64,384]{3,2,1,0:T(8,128)(2,1)S(1)} %copy.41), dimensions={1,2,3,4} | broadcast | bytes 3538944 | tf_op jit(solution)/shard_map/broadcast_in_dim | solution.py:131
  15.1 6.8 %all-to-all-start = ((bf16[32,2,64,384]{3,2,1,0:T(8,128)(2,1)}), bf16[32,2,64,384]{3,2,1,0:T(8,128)(2,1)S(1)}, u32[]{:S(2)}, u32[]{:S(2)}) async-start(bf16[32,2,64,384]{3,2,1,0:T(8,128)(2,1)} %bitcast.136), calls=%async_computation | async-start | bytes 6291456 | tf_op jit(solution)/shard_map/all_to_all | solution.py:133
  23.4 1.7 %reshape_reshape.3 = bf16[256,3,128]{2,1,0:T(4,128)(2,1)} reshape(bf16[4,64,1,384]{3,1,0,2:T(8,128)(2,1)} %bitcast.149) | data formatting | bytes 393216 | tf_op jit(solution)/shard_map/reshape;reshape | solution.py:26
  25.1 34.3 %all-to-all-done = bf16[32,2,64,384]{3,2,1,0:T(8,128)(2,1)S(1)} async-done(((bf16[32,2,64,384]{3,2,1,0:T(8,128)(2,1)}), bf16[32,2,64,384]{3,2,1,0:T(8,128)(2,1)S(1)}, u32[]{:S(2)}, u32[]{:S(2)}) %all-to-all-start) | async-done | bytes 3145760 | tf_op jit(solution)/shard_map/all_to_all | solution.py:133
  59.5 2.1 %fusion.106 = (bf16[32,1,64,384]{3,2,1,0:T(8,128)(2,1)}, bf16[32,1,64,384]{3,2,1,0:T(8,128)(2,1)}) fusion(bf16[32,2,64,384]{3,2,1,0:T(8,128)(2,1)S(1)} %all-to-all-done), kind=kLoop, calls=%fused_computation.120 | loop fusion | bytes 6291456 | tf_op jit(solution)/shard_map/slice | solution.py:134
  61.5 4.0 %reshape_reshape_squeeze.6 = bf16[2048,3,128]{2,1,0:T(4,128)(2,1)S(1)} reshape(bf16[32,1,64,384]{3,2,1,0:T(8,128)(2,1)} %get-tuple-element.7) | data formatting | bytes 3145728 | tf_op jit(solution)/shard_map/reshape;reshape;squeeze | solution.py:26
  65.5 3.6 %bitcast_reduce_fusion = (f32[3,256]{1,0:T(4,128)S(1)}, f32[3,2048,256]{2,1,0:T(8,128)}) fusion(bf16[256,3,128]{2,1,0:T(4,128)(2,1)S(1)} %copy-done.2, bf16[2048,3,128]{2,1,0:T(4,128)(2,1)S(1)} %reshape_reshape_squeeze.6), kind=kOutput, calls=%fused_computation.1 | convolution fusion | flops 405798144 | bytes 8064000 | tf_op jit(solution)/shard_map/qhd,khd->hqk/dot_general | solution.py:39
  69.2 3.9 %reshape_reshape_squeeze.7 = bf16[2048,3,128]{2,1,0:T(4,128)(2,1)S(1)} reshape(bf16[32,1,64,384]{3,2,1,0:T(8,128)(2,1)} %get-tuple-element.6) | data formatting | bytes 3145728 | tf_op jit(solution)/shard_map/reshape;reshape;squeeze | solution.py:26
  73.1 4.0 %fusion.1 = f32[3,256]{1,0:T(4,128)S(1)} fusion(f32[3,2048,256]{2,1,0:T(8,128)} %get-tuple-element.14, f32[3,256]{1,0:T(4,128)S(1)} %get-tuple-element.12), kind=kLoop, calls=%fused_computation.3 | loop fusion | flops 4717824 | bytes 6297600 | tf_op jit(solution)/shard_map/reduce_sum | solution.py:45
  79.5 2.0 %collective-permute-start.2 = (bf16[64,384]{1,0:T(8,128)(2,1)S(1)}, bf16[64,384]{1,0:T(8,128)(2,1)S(1)}, u32[]{:S(2)}, u32[]{:S(2)}) collective-permute-start(bf16[64,384]{1,0:T(8,128)(2,1)S(1)} %get-tuple-element.9), channel_id=1, source_target_pairs={{0,3},{1,0},{2,1},{3,2},{4,7},{5,4},{6,5},{7,6},{8,11},{9,8},{10,9... | collective-permute-start | bytes 147464 | tf_op jit(solution)/shard_map/ppermute | solution.py:159
  81.5 3.5 %collective-permute-start.1 = (bf16[64,384]{1,0:T(8,128)(2,1)S(1)}, bf16[64,384]{1,0:T(8,128)(2,1)S(1)}, u32[]{:S(2)}, u32[]{:S(2)}) collective-permute-start(bf16[64,384]{1,0:T(8,128)(2,1)S(1)} %get-tuple-element.8), channel_id=1, source_target_pairs={{0,2},{1,3},{2,0},{3,1},{4,6},{5,7},{6,4},{7,5},{8,10},{9,11},{10,... | collective-permute-start | bytes 147464 | tf_op jit(solution)/shard_map/ppermute | solution.py:159
  86.7 1.7 %convolution_add_fusion.1 = f32[64,1536]{1,0:T(8,128)S(1)} fusion(f32[64,1536]{1,0:T(8,128)S(1)} %fusion.34, bf16[64,384]{1,0:T(8,128)(2,1)S(1)} %collective-permute-done, bf16[4,384,1536]{2,1,0:T(8,128)(2,1)} %bitcast.140, s32[]{:T(128)S(6)} %select_n.21), kind=kOutput, calls=%fused_computation.10 | convolution fusion | flops 75595776 | bytes 2015236 | tf_op jit(solution)/shard_map/dot_general | solution.py:153
  90.1 1.7 %convert_reduce_fusion = (f32[64]{0:T(128)S(1)}, bf16[64,1536]{1,0:T(8,128)(2,1)S(1)}) fusion(f32[64,1536]{1,0:T(8,128)S(1)} %fusion.30, f32[64,1536]{1,0:T(8,128)S(1)} %convolution_add_fusion.1, bf16[64,384]{1,0:T(8,128)(2,1)S(1)} %collective-permute-done.1, bf16[4,384,1536]{2,1,0:T(8,128)(2,1)} %bitcast.142, s32[]{:T(128)S(6)} %select_n.22, ...), kind=kOutput, calls=%fused_computation.68 | convolution fusion | flops 76283840 | bytes 2414852 | tf_op jit(solution)/shard_map/dot_general | solution.py:153
  92.7 2.6 %collective-permute-start.5 = (bf16[2,4,32,16]{3,2,1,0:T(8,128)(2,1)S(1)}, bf16[2,4,32,16]{3,2,1,0:T(8,128)(2,1)S(1)}, u32[]{:S(2)}, u32[]{:S(2)}) collective-permute-start(bf16[2,4,32,16]{3,2,1,0:T(8,128)(2,1)S(1)} %subtract_convert_fusion), channel_id=1, source_target_pairs={{0,1},{1,2},{2,3},{3,4},{4,5},{5,6},{6,7},{7,8},{8,9},{9,10},{10,1... | collective-permute-start | bytes 24584 | tf_op jit(solution)/shard_map/ppermute | solution.py:22
  95.3 3.9 %collective-permute-start.4 = (bf16[2,4,32,16]{3,2,1,0:T(8,128)(2,1)S(1)}, bf16[2,4,32,16]{3,2,1,0:T(8,128)(2,1)S(1)}, u32[]{:S(2)}, u32[]{:S(2)}) collective-permute-start(bf16[2,4,32,16]{3,2,1,0:T(8,128)(2,1)S(1)} %subtract_convert_fusion), channel_id=1, source_target_pairs={{0,2},{1,3},{2,4},{3,5},{4,6},{5,7},{6,8},{7,9},{8,10},{9,11},{10,... | collective-permute-start | bytes 24584 | tf_op jit(solution)/shard_map/ppermute | solution.py:22
  99.2 4.5 %collective-permute-start.3 = (bf16[2,4,32,16]{3,2,1,0:T(8,128)(2,1)S(1)}, bf16[2,4,32,16]{3,2,1,0:T(8,128)(2,1)S(1)}, u32[]{:S(2)}, u32[]{:S(2)}) collective-permute-start(bf16[2,4,32,16]{3,2,1,0:T(8,128)(2,1)S(1)} %subtract_convert_fusion), channel_id=1, source_target_pairs={{0,3},{1,4},{2,5},{3,6},{4,7},{5,8},{6,9},{7,10},{8,11},{9,12},{10... | collective-permute-start | bytes 24584 | tf_op jit(solution)/shard_map/ppermute | solution.py:22
  103.7 2.3 %collective-permute-done.4 = bf16[2,4,32,16]{3,2,1,0:T(8,128)(2,1)S(1)} collective-permute-done((bf16[2,4,32,16]{3,2,1,0:T(8,128)(2,1)S(1)}, bf16[2,4,32,16]{3,2,1,0:T(8,128)(2,1)S(1)}, u32[]{:S(2)}, u32[]{:S(2)}) %collective-permute-start.4) | collective-permute-done | bytes 8224 | tf_op jit(solution)/shard_map/ppermute | solution.py:22
  106.0 2.4 %collective-permute-done.3 = bf16[2,4,32,16]{3,2,1,0:T(8,128)(2,1)S(1)} collective-permute-done((bf16[2,4,32,16]{3,2,1,0:T(8,128)(2,1)S(1)}, bf16[2,4,32,16]{3,2,1,0:T(8,128)(2,1)S(1)}, u32[]{:S(2)}, u32[]{:S(2)}) %collective-permute-start.3) | collective-permute-done | bytes 8224 | tf_op jit(solution)/shard_map/ppermute | solution.py:22
  108.8 1.8 %convert_multiply_fusion = (f32[6,4,8,5,384]{4,2,3,1,0:T(8,128)S(1)}, bf16[6,4,8,5,384]{4,2,3,1,0:T(8,128)(2,1)S(1)}) fusion(bf16[3,3,3,16,384]{4,3,2,1,0:T(8,128)(2,1)S(1)} %copy-done, bf16[8,4,1,7,2,16]{5,3,4,1,0,2:T(8,128)(2,1)S(1)} %slice.24, bf16[8,4,1,8,5,16]{5,3,4,1,0,2:T(8,128)(2,1)S(1)} %copy.51, pred[8,5]{0,1:T(8,128)(4,1)S(1)} %copy-done.14), kind=kOutput, calls=%fused_computation.82 | convolution fusion | flops 267067392 | bytes 2598952 | tf_op jit(solution)/shard_map/conv_general_dilated | solution.py:74
  112.9 7.1 %fusion.107 = (f32[4,4,8,5,384]{4,2,3,1,0:T(8,128)S(1)}, f32[4,4,8,5,384]{4,2,3,1,0:T(8,128)S(1)}) fusion(bf16[3,3,3,384,384]{4,3,2,1,0:T(8,128)(2,1)S(1)} %bitcast.156, bf16[6,4,1,7,2,384]{5,3,4,1,0,2:T(8,128)(2,1)S(1)} %slice.28, bf16[6,4,1,8,5,384]{5,3,4,1,0,2:T(8,128)(2,1)S(1)} %copy.55, pred[8,5]{0,1:T(8,128)(4,1)S(1)} %copy-done.14), kind=kOutput, calls=%fused_computation.121 | convolution fusion | flops 4250320896 | bytes 10924072 | tf_op jit(solution)/shard_map/conv_general_dilated | solution.py:74
  121.7 3.9 %fusion.22 = bf16[2,4,8,5,384]{4,2,3,1,0:T(8,128)(2,1)S(1)} fusion(bf16[3,3,3,384,384]{4,3,2,1,0:T(8,128)(2,1)S(1)} %bitcast.158, bf16[4,4,1,7,2,384]{5,3,4,1,0,2:T(8,128)(2,1)S(1)} %slice.31, bf16[4,4,1,8,5,384]{5,3,4,1,0,2:T(8,128)(2,1)S(1)} %copy.59, bf16[6,4,8,5,384]{4,2,3,1,0:T(8,128)(2,1)S(1)} %get-tuple-element.18, pred[8,5]{0,1:T(8,128)(4,1)S(1)} %copy-done.14), kind=kOutput, calls=%fused_computation.26 | convolution fusion | flops 2125922304 | bytes 9117736 | tf_op jit(solution)/shard_map/conv_general_dilated | solution.py:74
  (89 shorter events, 14.6 us)
Async XLA Ops:
  0.6 108.1 %copy-start = (bf16[3,3,3,16,384]{4,3,2,1,0:T(8,128)(2,1)S(1)}, bf16[3,3,3,16,384]{4,3,2,1,0:T(8,128)(2,1)}, u32[]{:S(2)}) copy-start(bf16[3,3,3,16,384]{4,3,2,1,0:T(8,128)(2,1)} %param.27) | copy-start | bytes 995332
  2.3 10.6 %all-to-all-start.1 = ((bf16[64,4,384]{2,0,1:T(8,128)(2,1)}), bf16[64,4,384]{2,0,1:T(8,128)(2,1)S(1)}, u32[]{:S(2)}, u32[]{:S(2)}) async-start(bf16[64,4,384]{2,0,1:T(8,128)(2,1)} %bitcast.134), calls=%async_computation.1 | async-start | bytes 393216 | tf_op jit(solution)/shard_map/all_to_all | solution.py:123
  15.1 6.9 %copy-start.7 = (f32[2,4,512]{2,1,0:T(4,128)S(1)}, f32[2,4,512]{2,1,0:T(4,128)}, u32[]{:S(2)}) copy-start(f32[2,4,512]{2,1,0:T(4,128)} %param.26) | copy-start | bytes 49156
  15.1 8.3 %copy-start.9 = (f32[1536]{0:T(1024)S(1)}, f32[1536]{0:T(1024)}, u32[]{:S(2)}) copy-start(f32[1536]{0:T(1024)} %param.22) | copy-start | bytes 18436
  15.1 44.4 %all-to-all-start = ((bf16[32,2,64,384]{3,2,1,0:T(8,128)(2,1)}), bf16[32,2,64,384]{3,2,1,0:T(8,128)(2,1)S(1)}, u32[]{:S(2)}, u32[]{:S(2)}) async-start(bf16[32,2,64,384]{3,2,1,0:T(8,128)(2,1)} %bitcast.136), calls=%async_computation | async-start | bytes 6291456 | tf_op jit(solution)/shard_map/all_to_all | solution.py:133
  61.5 4.0 %copy-start.2 = (bf16[256,3,128]{2,1,0:T(4,128)(2,1)S(1)}, bf16[256,3,128]{2,1,0:T(4,128)(2,1)}, u32[]{:S(2)}) copy-start(bf16[256,3,128]{2,1,0:T(4,128)(2,1)} %reshape_reshape.3) | copy-start | bytes 589828
  73.1 4.6 %copy-start.1 = (f32[3,2048,256]{2,1,0:T(8,128)S(1)}, f32[3,2048,256]{2,1,0:T(8,128)}, u32[]{:S(2)}) copy-start(f32[3,2048,256]{2,1,0:T(8,128)} %get-tuple-element.14) | copy-start | bytes 18874372
  79.5 9.0 %collective-permute-start.2 = (bf16[64,384]{1,0:T(8,128)(2,1)S(1)}, bf16[64,384]{1,0:T(8,128)(2,1)S(1)}, u32[]{:S(2)}, u32[]{:S(2)}) collective-permute-start(bf16[64,384]{1,0:T(8,128)(2,1)S(1)} %get-tuple-element.9), channel_id=1, source_target_pairs={{0,3},{1,0},{2,1},{3,2},{4,7},{5,4},{6,5},{7,6},{8,11},{9,8},{10,9... | collective-permute-start | bytes 147464 | tf_op jit(solution)/shard_map/ppermute | solution.py:159
  81.4 5.3 %collective-permute-start = (bf16[64,384]{1,0:T(8,128)(2,1)S(1)}, bf16[64,384]{1,0:T(8,128)(2,1)S(1)}, u32[]{:S(2)}, u32[]{:S(2)}) collective-permute-start(bf16[64,384]{1,0:T(8,128)(2,1)S(1)} %get-tuple-element.10), channel_id=1, source_target_pairs={{0,1},{1,2},{2,3},{3,0},{4,5},{5,6},{6,7},{7,4},{8,9},{9,10},{10,1... | collective-permute-start | bytes 147464 | tf_op jit(solution)/shard_map/ppermute | solution.py:159
  81.5 8.5 %collective-permute-start.1 = (bf16[64,384]{1,0:T(8,128)(2,1)S(1)}, bf16[64,384]{1,0:T(8,128)(2,1)S(1)}, u32[]{:S(2)}, u32[]{:S(2)}) collective-permute-start(bf16[64,384]{1,0:T(8,128)(2,1)S(1)} %get-tuple-element.8), channel_id=1, source_target_pairs={{0,2},{1,3},{2,0},{3,1},{4,6},{5,7},{6,4},{7,5},{8,10},{9,11},{10,... | collective-permute-start | bytes 147464 | tf_op jit(solution)/shard_map/ppermute | solution.py:159
  86.7 3.4 %copy-start.6 = (bf16[64,1536]{1,0:T(8,128)(2,1)S(1)}, bf16[64,1536]{1,0:T(8,128)(2,1)}, u32[]{:S(2)}) copy-start(bf16[64,1536]{1,0:T(8,128)(2,1)} %param.16) | copy-start | bytes 589828
  86.7 3.4 %copy-start.8 = (f32[1536]{0:T(1024)S(1)}, f32[1536]{0:T(1024)}, u32[]{:S(2)}) copy-start(f32[1536]{0:T(1024)} %param.20) | copy-start | bytes 18436
  88.4 3.8 %copy-start.12 = (bf16[1536,64]{0,1:T(8,128)(2,1)S(1)}, bf16[1536,64]{0,1:T(8,128)(2,1)}, u32[]{:S(2)}) copy-start(bf16[1536,64]{0,1:T(8,128)(2,1)} %param.24) | copy-start | bytes 589828
  88.4 3.8 %copy-start.13 = (f32[1536]{0:T(1024)S(1)}, f32[1536]{0:T(1024)}, u32[]{:S(2)}) copy-start(f32[1536]{0:T(1024)} %param.23) | copy-start | bytes 18436
  90.1 2.6 %copy-start.5 = (f32[2,4,32,16]{3,2,1,0:T(8,128)S(1)}, f32[2,4,32,16]{3,2,1,0:T(8,128)}, u32[]{:S(2)}) copy-start(f32[2,4,32,16]{3,2,1,0:T(8,128)} %reshape.85) | copy-start | bytes 49156
  91.9 16.9 %copy-start.3 = (bf16[64,1536]{1,0:T(8,128)(2,1)}, bf16[64,1536]{1,0:T(8,128)(2,1)S(1)}, u32[]{:S(2)}) copy-start(bf16[64,1536]{1,0:T(8,128)(2,1)S(1)} %get-tuple-element.16) | copy-start | bytes 589828
  92.1 16.7 %copy-start.14 = (pred[8,5]{0,1:T(8,128)(4,1)S(1)}, pred[8,5]{0,1:T(8,128)(4,1)}, u32[]{:S(2)}) copy-start(pred[8,5]{0,1:T(8,128)(4,1)} %constant.99) | copy-start | bytes 124
  92.7 20.2 %slice-start = ((s8[7962624]{0:T(1024)(128)(4,1)}), s8[4194304]{0:T(1024)(128)(4,1)S(1)}, s32[]{:S(2)}) async-start(s8[7962624]{0:T(1024)(128)(4,1)} %bitcast.155), calls=%async_computation.2 | async-start | bytes 8388608
  92.7 11.0 %collective-permute-start.5 = (bf16[2,4,32,16]{3,2,1,0:T(8,128)(2,1)S(1)}, bf16[2,4,32,16]{3,2,1,0:T(8,128)(2,1)S(1)}, u32[]{:S(2)}, u32[]{:S(2)}) collective-permute-start(bf16[2,4,32,16]{3,2,1,0:T(8,128)(2,1)S(1)} %subtract_convert_fusion), channel_id=1, source_target_pairs={{0,1},{1,2},{2,3},{3,4},{4,5},{5,6},{6,7},{7,8},{8,9},{9,10},{10,1... | collective-permute-start | bytes 24584 | tf_op jit(solution)/shard_map/ppermute | solution.py:22
  95.3 10.7 %collective-permute-start.4 = (bf16[2,4,32,16]{3,2,1,0:T(8,128)(2,1)S(1)}, bf16[2,4,32,16]{3,2,1,0:T(8,128)(2,1)S(1)}, u32[]{:S(2)}, u32[]{:S(2)}) collective-permute-start(bf16[2,4,32,16]{3,2,1,0:T(8,128)(2,1)S(1)} %subtract_convert_fusion), channel_id=1, source_target_pairs={{0,2},{1,3},{2,4},{3,5},{4,6},{5,7},{6,8},{7,9},{8,10},{9,11},{10,... | collective-permute-start | bytes 24584 | tf_op jit(solution)/shard_map/ppermute | solution.py:22
  99.2 9.2 %collective-permute-start.3 = (bf16[2,4,32,16]{3,2,1,0:T(8,128)(2,1)S(1)}, bf16[2,4,32,16]{3,2,1,0:T(8,128)(2,1)S(1)}, u32[]{:S(2)}, u32[]{:S(2)}) collective-permute-start(bf16[2,4,32,16]{3,2,1,0:T(8,128)(2,1)S(1)} %subtract_convert_fusion), channel_id=1, source_target_pairs={{0,3},{1,4},{2,5},{3,6},{4,7},{5,8},{6,9},{7,10},{8,11},{9,12},{10... | collective-permute-start | bytes 24584 | tf_op jit(solution)/shard_map/ppermute | solution.py:22
  108.8 4.1 %slice-start.1 = ((s8[7962624]{0:T(1024)(128)(4,1)}), s8[3768320]{0:T(1024)(128)(4,1)S(1)}, s32[]{:S(2)}) async-start(s8[7962624]{0:T(1024)(128)(4,1)} %bitcast.155), calls=%async_computation.3 | async-start | bytes 7536640
  112.7 8.9 %slice-start.2 = ((s8[7962624]{0:T(1024)(128)(4,1)}), s8[4194304]{0:T(1024)(128)(4,1)S(1)}, s32[]{:S(2)}) async-start(s8[7962624]{0:T(1024)(128)(4,1)} %bitcast.157), calls=%async_computation.4 | async-start | bytes 8388608
  112.9 8.7 %slice-start.3 = ((s8[7962624]{0:T(1024)(128)(4,1)}), s8[3768320]{0:T(1024)(128)(4,1)S(1)}, s32[]{:S(2)}) async-start(s8[7962624]{0:T(1024)(128)(4,1)} %bitcast.157), calls=%async_computation.5 | async-start | bytes 7536640
  (3 other events, 3.6 us)

commit v8 on v6

--- a/solution.py
+++ b/solution.py
@@ -131,7 +131,15 @@
         got = lax.all_to_all(sent, FRAMES, 0, 0, tiled=True)
         return got.reshape((-1,) + got.shape[2:])
 
-    query_heads = split_heads(to_group(queries), group_heads)
+    me = lax.axis_index("hg")
+    query_parts = queries.reshape(rows_here, HEAD_GROUPS, group_width)
+    received = [lax.dynamic_index_in_dim(query_parts, me, 1, keepdims=False)]
+    for k in range(1, HEAD_GROUPS):
+        target = lax.rem(me + HEAD_GROUPS - k, HEAD_GROUPS)
+        pairs = [(i, (i + HEAD_GROUPS - k) % HEAD_GROUPS) for i in range(HEAD_GROUPS)]
+        piece = lax.dynamic_index_in_dim(query_parts, target, 1, keepdims=False)
+        received.append(lax.ppermute(piece, "hg", pairs))
+    query_heads = split_heads(jnp.concatenate(received, axis=0), group_heads)
     key_value = gather_group(jnp.stack([keys, values], axis=1))
     key_heads = split_heads(key_value[:, 0], group_heads)
     value_heads = split_heads(key_value[:, 1], group_heads)
@@ -142,7 +150,6 @@
     group_out = (
         (summed / row_total.T[:, :, None]).reshape(group_rows, group_width).astype(jnp.bfloat16)
     )
-    me = lax.axis_index("hg")
     pieces = group_out.reshape(HEAD_GROUPS, rows_here, group_width)
     weight_groups = output_weight.reshape(HEAD_GROUPS, group_width, -1)
 
@@ -150,11 +157,10 @@
         rows_of = lax.dynamic_index_in_dim(weight_groups, source, 0, keepdims=False)
         return jnp.dot(piece, rows_of, preferred_element_type=jnp.float32)
 
-    projected = project(lax.dynamic_index_in_dim(pieces, me, 0, keepdims=False), me)
+    projected = project(pieces[0], me)
     for k in range(1, HEAD_GROUPS):
-        target = lax.rem(me + k, HEAD_GROUPS)
         pairs = [(i, (i + k) % HEAD_GROUPS) for i in range(HEAD_GROUPS)]
-        piece = lax.ppermute(lax.dynamic_index_in_dim(pieces, target, 0, False), "hg", pairs)
+        piece = lax.ppermute(pieces[k], "hg", pairs)
         projected = projected + project(piece, lax.rem(me + HEAD_GROUPS - k, HEAD_GROUPS))
     layer_output = (tokens.astype(jnp.float32) + branch_gate * projected).astype(jnp.bfloat16)
     normed = layer_norm(layer_output, head_scale, head_shift)

time: 116 us -> 115 us (level)
  waiting for transfers between devices: 43 us -> 33.7 us
  local copies, waits for them, and re-layouts: 15.7 us -> 21.7 us
  starting transfers between devices: 27.7 us -> 29.5 us
    all_to_all x1, waiting for transfers between devices: 34.4 us -> 0.01 us  [gather_group(): got = lax.all_to_all(sent, FRAMES, 0, 0, tiled=True)]
    ppermute x3 -> x6, waiting for transfers between devices: 0.01 us -> 29.4 us  [the longest x3 25.2 us: body(): received.append(lax.ppermute(piece, 'hg', pairs))]
    conv_general_dilated x3, matrix products: 12.8 us -> 18.2 us  [spatial_conv(): lax.conv_general_dilated(extended[None], kernel, (1, 1, 1), ((0, 0), (1,...]
    dot_general x4, matrix products: 6.66 us -> 1.49 us  [project(): return jnp.dot(piece, rows_of, preferred_element_type=jnp.float32)]
    all_to_all x1 -> x0, starting transfers between devices: 4.29 us -> none  [to_group(): lax.all_to_all(parts, 'hg', 1, 0, tiled=True).reshape(-1, group_width)]
    concatenate x0 -> x4, local copies, waits for them, and re-layouts: none -> 4.27 us  [body(): query_heads = split_heads(jnp.concatenate(received, axis=0), group_heads)]
    all_to_all x1 -> x0, waiting for transfers between devices: 4.02 us -> none  [to_group(): lax.all_to_all(parts, 'hg', 1, 0, tiled=True).reshape(-1, group_width)]
    ppermute x3 -> x6, starting transfers between devices: 5.63 us -> 8.55 us  [the longest x3 5.6 us: body(): received.append(lax.ppermute(piece, 'hg', pairs))]
  transfers between devices with their start and end apart: 8 -> 10, of which waited for: 4 -> 5; matrix products, arithmetic and copies ran while one was open for 8% -> 11% of each run, Pallas kernels for 0% -> 0%
where the time goes in v8:
time: 115 us; the launch traced here: 114 us
  waiting for transfers between devices  33.7 us (29%)
  starting transfers between devices  29.5 us (26%)
  matrix products  23.3 us (20%)
  local copies, waits for them, and re-layouts  21.7 us (19%)
  other arithmetic  4.1 us (4%)
  between operations  1.91 us (2%)
    ppermute x3, waiting for transfers between devices, body(): received.append(lax.ppermute(piece, 'hg', pairs))  25.2 us
    conv_general_dilated x3, matrix products, spatial_conv(): lax.conv_general_dilated(extended[None], kernel, (1, 1, 1), ((0, 0), (1,...  18.2 us
    ppermute x3, starting transfers between devices, shifted(): return lax.ppermute(x, axis, pairs)  12.4 us
    all_to_all x1, starting transfers between devices, gather_group(): got = lax.all_to_all(sent, FRAMES, 0, 0, tiled=True)  8.55 us
    ppermute x3, starting transfers between devices, body(): received.append(lax.ppermute(piece, 'hg', pairs))  5.6 us
    ppermute x3, waiting for transfers between devices, shifted(): return lax.ppermute(x, axis, pairs)  4.33 us
    concatenate x4, local copies, waits for them, and re-layouts, body(): query_heads = split_heads(jnp.concatenate(received, axis=0), group_heads)  4.27 us
    ppermute x3, waiting for transfers between devices, body(): piece = lax.ppermute(pieces[k], 'hg', pairs)  4.14 us
  transfers between devices with their start and end apart: 10, of which 5 were waited for; matrix products, arithmetic and copies ran while one was open for 11% of the time, Pallas kernels for 0%

profile of v8, /device:TPU:96, one launch (start us, length us, event | category | flops | bytes accessed | tf_op | source)
XLA Modules:
  0.0 114.2 jit_solution(2838741559677796282)
XLA Ops:
  3.0 2.2 %broadcast_in_dim.9 = bf16[8,4,64,2,384]{4,2,3,1,0:T(8,128)(2,1)} broadcast(bf16[4,64,2,384]{3,1,2,0:T(8,128)(2,1)S(1)} %copy.67), dimensions={1,2,3,4} | broadcast | bytes 3538944 | tf_op jit(solution)/shard_map/broadcast_in_dim | solution.py:129
  5.2 8.6 %all-to-all-start = ((bf16[32,64,2,384]{3,1,2,0:T(8,128)(2,1)}), bf16[32,64,2,384]{3,1,2,0:T(8,128)(2,1)S(1)}, u32[]{:S(2)}, u32[]{:S(2)}) async-start(bf16[32,64,2,384]{3,1,2,0:T(8,128)(2,1)} %bitcast.129), calls=%async_computation | async-start | bytes 6291456 | tf_op jit(solution)/shard_map/all_to_all | solution.py:131
  13.8 1.7 %reshape.98 = bf16[64,4,384]{2,1,0:T(4,128)(2,1)} reshape(bf16[64,1536]{1,0:T(8,128)(2,1)} %param.17) | data formatting | bytes 393216 | tf_op jit(solution)/shard_map/reshape | solution.py:135
  15.4 1.8 %dynamic-slice_reduce_fusion = (bf16[64,384]{1,0:T(8,128)(2,1)S(1)}, bf16[64,1,384]{2,1,0:T(2,128)(2,1)S(1)}, bf16[64,1,384]{2,1,0:T(2,128)(2,1)S(1)}, bf16[64,1,384]{2,1,0:T(2,128)(2,1)S(1)}) fusion(bf16[64,4,384]{2,1,0:T(4,128)(2,1)} %reshape.98, s32[]{:T(128)S(6)} %select_n.18, s32[]{:T(128)S(6)} %select_n.21, s32[]{:T(128)S(6)} %select_n.20, s32[]{:T(128)S(6)} %select_n.19), kind=kLoop, calls=%fused_computation.97 | loop fusion | bytes 393232 | tf_op jit(solution)/shard_map/jit(dynamic_index_in_dim)/dynamic_slice | solution.py:136
  17.9 1.5 %collective-permute-start.2 = (bf16[64,384]{1,0:T(8,128)(2,1)}, bf16[64,384]{1,0:T(8,128)(2,1)}, u32[]{:S(2)}, u32[]{:S(2)}) collective-permute-start(bf16[64,384]{1,0:T(8,128)(2,1)} %bitcast.125), channel_id=1, source_target_pairs={{0,1},{1,2},{2,3},{3,0},{4,5},{5,6},{6,7},{7,4},{8,9},{9,10},{10,1... | collective-permute-start | bytes 147464 | tf_op jit(solution)/shard_map/ppermute | solution.py:141
  20.0 2.7 %collective-permute-start.1 = (bf16[64,384]{1,0:T(8,128)(2,1)}, bf16[64,384]{1,0:T(8,128)(2,1)}, u32[]{:S(2)}, u32[]{:S(2)}) collective-permute-start(bf16[64,384]{1,0:T(8,128)(2,1)} %bitcast.126), channel_id=1, source_target_pairs={{0,2},{1,3},{2,0},{3,1},{4,6},{5,7},{6,4},{7,5},{8,10},{9,11},{10,... | collective-permute-start | bytes 147464 | tf_op jit(solution)/shard_map/ppermute | solution.py:141
  23.3 1.5 %collective-permute-start = (bf16[64,384]{1,0:T(8,128)(2,1)}, bf16[64,384]{1,0:T(8,128)(2,1)}, u32[]{:S(2)}, u32[]{:S(2)}) collective-permute-start(bf16[64,384]{1,0:T(8,128)(2,1)} %bitcast.127), channel_id=1, source_target_pairs={{0,3},{1,0},{2,1},{3,2},{4,7},{5,4},{6,5},{7,6},{8,11},{9,8},{10,9... | collective-permute-start | bytes 147464 | tf_op jit(solution)/shard_map/ppermute | solution.py:141
  26.8 25.2 %collective-permute-done.2 = bf16[64,384]{1,0:T(8,128)(2,1)} collective-permute-done((bf16[64,384]{1,0:T(8,128)(2,1)}, bf16[64,384]{1,0:T(8,128)(2,1)}, u32[]{:S(2)}, u32[]{:S(2)}) %collective-permute-start.2) | collective-permute-done | bytes 49184 | tf_op jit(solution)/shard_map/ppermute | solution.py:141
  52.0 1.4 %copy_bitcast_fusion = bf16[64,3,128]{2,0,1:T(8,128)(2,1)} fusion(bf16[64,384]{1,0:T(8,128)(2,1)} %collective-permute-done.2), kind=kLoop, calls=%fused_computation.99 | loop fusion | bytes 98304 | tf_op jit(solution)/shard_map/concatenate | solution.py:142
  53.4 1.4 %copy_bitcast_fusion.1 = bf16[64,3,128]{2,0,1:T(8,128)(2,1)} fusion(bf16[64,384]{1,0:T(8,128)(2,1)} %collective-permute-done.1), kind=kLoop, calls=%fused_computation.100 | loop fusion | bytes 98304 | tf_op jit(solution)/shard_map/concatenate | solution.py:142
  54.9 1.4 %copy_bitcast_fusion.2 = bf16[64,3,128]{2,0,1:T(8,128)(2,1)} fusion(bf16[64,384]{1,0:T(8,128)(2,1)} %collective-permute-done), kind=kLoop, calls=%fused_computation.101 | loop fusion | bytes 98304 | tf_op jit(solution)/shard_map/concatenate | solution.py:142
  57.0 1.7 %copy.71 = bf16[2048,1,384]{0,2,1:T(8,128)(2,1)} copy(bf16[2048,1,384]{2,0,1:T(8,128)(2,1)S(1)} %get-tuple-element.9) | data formatting | bytes 3145728 | tf_op jit(solution)/shard_map/slice | solution.py:145
  59.4 1.9 %multiply_reduce_fusion = (f32[3,256]{1,0:T(4,128)S(1)}, f32[3,256,2048]{2,1,0:T(8,128)S(1)}) fusion(bf16[2048,3,128]{0,2,1:T(8,128)(2,1)S(1)} %bitcast.131, bf16[64,3,128]{2,0,1:T(8,128)(2,1)} %copy_bitcast_fusion, bf16[64,3,128]{2,0,1:T(8,128)(2,1)} %copy_bitcast_fusion.1, bf16[64,3,128]{2,0,1:T(8,128)(2,1)} %copy_bitcast_fusion.2, ...), kind=kOutput, calls=%fused_computation.1 | convolution fusion | flops 406584576 | bytes 8064000 | tf_op jit(solution)/shard_map/qhd,khd->hqk/dot_general | solution.py:39
  61.4 1.2 %fusion = f32[3,256]{1,0:T(4,128)S(1)} fusion(f32[3,256,2048]{2,1,0:T(8,128)S(1)} %get-tuple-element.21, f32[3,256]{1,0:T(4,128)S(1)} %get-tuple-element.19), kind=kLoop, calls=%fused_computation.2 | loop fusion | flops 4717824 | bytes 6297600 | tf_op jit(solution)/shard_map/reduce_sum | solution.py:45
  62.8 1.4 %fusion.36 = bf16[256,3,128]{0,2,1:T(8,128)(2,1)S(1)} fusion(bf16[2048,3,128]{0,2,1:T(8,128)(2,1)S(1)} %bitcast.144, f32[3,256,2048]{2,1,0:T(8,128)S(1)} %get-tuple-element.21, f32[3,256]{1,0:T(4,128)S(1)} %get-tuple-element.19, f32[256,3]{0,1:T(4,128)S(1)} %bitcast.152, f32[256,3]{0,1:T(4,128)S(1)} %get-tuple-element.18), kind=kOutput, calls=%fused_computation.42 | convolution fusion | flops 407666688 | bytes 8070144 | tf_op jit(solution)/shard_map/hqk,khd->qhd/dot_general | solution.py:46
  64.3 1.1 collective-permute-start.5
  67.6 3.6 %collective-permute-done.3 = bf16[64,384]{0,1:T(8,128)(2,1)S(1)} collective-permute-done((bf16[64,384]{0,1:T(8,128)(2,1)S(1)}, bf16[64,384]{0,1:T(8,128)(2,1)S(1)}, u32[]{:S(2)}, u32[]{:S(2)}) %collective-permute-start.3) | collective-permute-done | bytes 49184 | tf_op jit(solution)/shard_map/ppermute | solution.py:163
  73.8 1.9 %collective-permute-start.8 = (bf16[2,4,32,16]{3,2,1,0:T(8,128)(2,1)S(1)}, bf16[2,4,32,16]{3,2,1,0:T(8,128)(2,1)S(1)}, u32[]{:S(2)}, u32[]{:S(2)}) collective-permute-start(bf16[2,4,32,16]{3,2,1,0:T(8,128)(2,1)S(1)} %subtract_convert_fusion), channel_id=1, source_target_pairs={{0,1},{1,2},{2,3},{3,4},{4,5},{5,6},{6,7},{7,8},{8,9},{9,10},{10,1... | collective-permute-start | bytes 24584 | tf_op jit(solution)/shard_map/ppermute | solution.py:22
  75.7 5.6 %collective-permute-start.7 = (bf16[2,4,32,16]{3,2,1,0:T(8,128)(2,1)S(1)}, bf16[2,4,32,16]{3,2,1,0:T(8,128)(2,1)S(1)}, u32[]{:S(2)}, u32[]{:S(2)}) collective-permute-start(bf16[2,4,32,16]{3,2,1,0:T(8,128)(2,1)S(1)} %subtract_convert_fusion), channel_id=1, source_target_pairs={{0,2},{1,3},{2,4},{3,5},{4,6},{5,7},{6,8},{7,9},{8,10},{9,11},{10,... | collective-permute-start | bytes 24584 | tf_op jit(solution)/shard_map/ppermute | solution.py:22
  81.4 4.8 %collective-permute-start.6 = (bf16[2,4,32,16]{3,2,1,0:T(8,128)(2,1)S(1)}, bf16[2,4,32,16]{3,2,1,0:T(8,128)(2,1)S(1)}, u32[]{:S(2)}, u32[]{:S(2)}) collective-permute-start(bf16[2,4,32,16]{3,2,1,0:T(8,128)(2,1)S(1)} %subtract_convert_fusion), channel_id=1, source_target_pairs={{0,3},{1,4},{2,5},{3,6},{4,7},{5,8},{6,9},{7,10},{8,11},{9,12},{10... | collective-permute-start | bytes 24584 | tf_op jit(solution)/shard_map/ppermute | solution.py:22
  86.9 3.7 %collective-permute-done.6 = bf16[2,4,32,16]{3,2,1,0:T(8,128)(2,1)S(1)} collective-permute-done((bf16[2,4,32,16]{3,2,1,0:T(8,128)(2,1)S(1)}, bf16[2,4,32,16]{3,2,1,0:T(8,128)(2,1)S(1)}, u32[]{:S(2)}, u32[]{:S(2)}) %collective-permute-start.6) | collective-permute-done | bytes 8224 | tf_op jit(solution)/shard_map/ppermute | solution.py:22
  91.0 1.8 %convert_multiply_fusion = (f32[6,4,8,5,384]{4,2,3,1,0:T(8,128)S(1)}, bf16[6,4,8,5,384]{4,2,3,1,0:T(8,128)(2,1)S(1)}) fusion(bf16[3,3,3,16,384]{4,3,2,1,0:T(8,128)(2,1)S(1)} %copy-done, bf16[8,4,1,7,2,16]{5,3,4,1,0,2:T(8,128)(2,1)S(1)} %slice.64, bf16[8,4,1,8,5,16]{5,3,4,1,0,2:T(8,128)(2,1)S(1)} %copy.75, pred[8,5]{0,1:T(8,128)(4,1)S(1)} %copy-done.13), kind=kOutput, calls=%fused_computation.78 | convolution fusion | flops 267067392 | bytes 2598952 | tf_op jit(solution)/shard_map/conv_general_dilated | solution.py:74
  95.1 12.7 %fusion.102 = (f32[4,4,8,5,384]{4,2,3,1,0:T(8,128)S(1)}, f32[4,4,8,5,384]{4,2,3,1,0:T(8,128)S(1)}) fusion(bf16[3,3,3,384,384]{4,3,2,1,0:T(8,128)(2,1)} %param.29, bf16[6,4,1,7,2,384]{5,3,4,1,0,2:T(8,128)(2,1)S(1)} %slice.68, bf16[6,4,1,8,5,384]{5,3,4,1,0,2:T(8,128)(2,1)S(1)} %copy.79, pred[8,5]{0,1:T(8,128)(4,1)S(1)} %copy-done.13), kind=kOutput, calls=%fused_computation.131 | convolution fusion | flops 4250320896 | bytes 10924072 | tf_op jit(solution)/shard_map/conv_general_dilated | solution.py:74
  109.6 3.7 %fusion.16 = bf16[2,4,8,5,384]{4,2,3,1,0:T(8,128)(2,1)S(1)} fusion(bf16[3,3,3,384,384]{4,3,2,1,0:T(8,128)(2,1)S(1)} %bitcast.154, bf16[4,4,1,7,2,384]{5,3,4,1,0,2:T(8,128)(2,1)S(1)} %slice.71, bf16[4,4,1,8,5,384]{5,3,4,1,0,2:T(8,128)(2,1)S(1)} %copy.83, bf16[6,4,8,5,384]{4,2,3,1,0:T(8,128)(2,1)S(1)} %get-tuple-element.25, pred[8,5]{0,1:T(8,128)(4,1)S(1)} %copy-done.13), kind=kOutput, calls=%fused_computation.22 | convolution fusion | flops 2125922304 | bytes 9117736 | tf_op jit(solution)/shard_map/conv_general_dilated | solution.py:74
  (97 shorter events, 17.8 us)
Async XLA Ops:
  0.6 90.3 %copy-start = (bf16[3,3,3,16,384]{4,3,2,1,0:T(8,128)(2,1)S(1)}, bf16[3,3,3,16,384]{4,3,2,1,0:T(8,128)(2,1)}, u32[]{:S(2)}) copy-start(bf16[3,3,3,16,384]{4,3,2,1,0:T(8,128)(2,1)} %param.27) | copy-start | bytes 995332
  5.2 51.1 %all-to-all-start = ((bf16[32,64,2,384]{3,1,2,0:T(8,128)(2,1)}), bf16[32,64,2,384]{3,1,2,0:T(8,128)(2,1)S(1)}, u32[]{:S(2)}, u32[]{:S(2)}) async-start(bf16[32,64,2,384]{3,1,2,0:T(8,128)(2,1)} %bitcast.129), calls=%async_computation | async-start | bytes 6291456 | tf_op jit(solution)/shard_map/all_to_all | solution.py:131
  13.7 11.0 %copy-start.7 = (f32[1536]{0:T(1024)S(1)}, f32[1536]{0:T(1024)}, u32[]{:S(2)}) copy-start(f32[1536]{0:T(1024)} %param.22) | copy-start | bytes 18436
  13.7 11.6 %copy-start.5 = (f32[2,4,512]{2,1,0:T(4,128)S(1)}, f32[2,4,512]{2,1,0:T(4,128)}, u32[]{:S(2)}) copy-start(f32[2,4,512]{2,1,0:T(4,128)} %param.26) | copy-start | bytes 49156
  17.9 34.1 %collective-permute-start.2 = (bf16[64,384]{1,0:T(8,128)(2,1)}, bf16[64,384]{1,0:T(8,128)(2,1)}, u32[]{:S(2)}, u32[]{:S(2)}) collective-permute-start(bf16[64,384]{1,0:T(8,128)(2,1)} %bitcast.125), channel_id=1, source_target_pairs={{0,1},{1,2},{2,3},{3,0},{4,5},{5,6},{6,7},{7,4},{8,9},{9,10},{10,1... | collective-permute-start | bytes 147464 | tf_op jit(solution)/shard_map/ppermute | solution.py:141
  20.0 33.4 %collective-permute-start.1 = (bf16[64,384]{1,0:T(8,128)(2,1)}, bf16[64,384]{1,0:T(8,128)(2,1)}, u32[]{:S(2)}, u32[]{:S(2)}) collective-permute-start(bf16[64,384]{1,0:T(8,128)(2,1)} %bitcast.126), channel_id=1, source_target_pairs={{0,2},{1,3},{2,0},{3,1},{4,6},{5,7},{6,4},{7,5},{8,10},{9,11},{10,... | collective-permute-start | bytes 147464 | tf_op jit(solution)/shard_map/ppermute | solution.py:141
  23.3 31.6 %collective-permute-start = (bf16[64,384]{1,0:T(8,128)(2,1)}, bf16[64,384]{1,0:T(8,128)(2,1)}, u32[]{:S(2)}, u32[]{:S(2)}) collective-permute-start(bf16[64,384]{1,0:T(8,128)(2,1)} %bitcast.127), channel_id=1, source_target_pairs={{0,3},{1,0},{2,1},{3,2},{4,7},{5,4},{6,5},{7,6},{8,11},{9,8},{10,9... | collective-permute-start | bytes 147464 | tf_op jit(solution)/shard_map/ppermute | solution.py:141
  61.3 1.4 %copy-start.1 = (bf16[2048,1,384]{0,2,1:T(8,128)(2,1)S(1)}, bf16[2048,1,384]{0,2,1:T(8,128)(2,1)}, u32[]{:S(2)}) copy-start(bf16[2048,1,384]{0,2,1:T(8,128)(2,1)} %copy.71) | copy-start | bytes 4718596
  61.4 5.9 %slice-start = ((s8[4718592]{0:T(1024)(128)(4,1)}), s8[4194304]{0:T(1024)(128)(4,1)S(1)}, s32[]{:S(2)}) async-start(s8[4718592]{0:T(1024)(128)(4,1)} %bitcast.134), calls=%async_computation.1 | async-start | bytes 8388608
  62.8 4.5 %slice-start.1 = ((s8[4718592]{0:T(1024)(128)(4,1)}), s8[524288]{0:T(1024)(128)(4,1)S(1)}, s32[]{:S(2)}) async-start(s8[4718592]{0:T(1024)(128)(4,1)} %bitcast.134), calls=%async_computation.2 | async-start | bytes 1048576
  64.3 7.3 %collective-permute-start.5 = (bf16[64,384]{0,1:T(8,128)(2,1)S(1)}, bf16[64,384]{0,1:T(8,128)(2,1)S(1)}, u32[]{:S(2)}, u32[]{:S(2)}) collective-permute-start(bf16[64,384]{0,1:T(8,128)(2,1)S(1)} %bitcast.150), channel_id=1, source_target_pairs={{0,3},{1,0},{2,1},{3,2},{4,7},{5,4},{6,5},{7,6},{8,11},{9,8},{10,9... | collective-permute-start | bytes 147464 | tf_op jit(solution)/shard_map/ppermute | solution.py:163
  65.4 5.8 %collective-permute-start.3 = (bf16[64,384]{0,1:T(8,128)(2,1)S(1)}, bf16[64,384]{0,1:T(8,128)(2,1)S(1)}, u32[]{:S(2)}, u32[]{:S(2)}) collective-permute-start(bf16[64,384]{0,1:T(8,128)(2,1)S(1)} %bitcast.151), channel_id=1, source_target_pairs={{0,1},{1,2},{2,3},{3,0},{4,5},{5,6},{6,7},{7,4},{8,9},{9,10},{10,1... | collective-permute-start | bytes 147464 | tf_op jit(solution)/shard_map/ppermute | solution.py:163
  66.4 6.1 %collective-permute-start.4 = (bf16[64,384]{0,1:T(8,128)(2,1)S(1)}, bf16[64,384]{0,1:T(8,128)(2,1)S(1)}, u32[]{:S(2)}, u32[]{:S(2)}) collective-permute-start(bf16[64,384]{0,1:T(8,128)(2,1)S(1)} %bitcast.149), channel_id=1, source_target_pairs={{0,2},{1,3},{2,0},{3,1},{4,6},{5,7},{6,4},{7,5},{8,10},{9,11},{10,... | collective-permute-start | bytes 147464 | tf_op jit(solution)/shard_map/ppermute | solution.py:163
  67.6 4.9 %copy-start.4 = (bf16[64,1536]{1,0:T(8,128)(2,1)S(1)}, bf16[64,1536]{1,0:T(8,128)(2,1)}, u32[]{:S(2)}) copy-start(bf16[64,1536]{1,0:T(8,128)(2,1)} %param.16) | copy-start | bytes 589828
  67.6 4.9 %copy-start.6 = (f32[1536]{0:T(1024)S(1)}, f32[1536]{0:T(1024)}, u32[]{:S(2)}) copy-start(f32[1536]{0:T(1024)} %param.20) | copy-start | bytes 18436
  71.9 1.3 %copy-start.8 = (f32[1536]{0:T(1024)S(1)}, f32[1536]{0:T(1024)}, u32[]{:S(2)}) copy-start(f32[1536]{0:T(1024)} %broadcast_add_fusion) | copy-start | bytes 18436
  72.0 1.8 %copy-start.3 = (f32[2,4,32,16]{3,2,1,0:T(8,128)S(1)}, f32[2,4,32,16]{3,2,1,0:T(8,128)}, u32[]{:S(2)}) copy-start(f32[2,4,32,16]{3,2,1,0:T(8,128)} %reshape.102) | copy-start | bytes 49156
  73.0 17.9 %copy-start.2 = (bf16[64,1536]{1,0:T(8,128)(2,1)}, bf16[64,1536]{1,0:T(8,128)(2,1)S(1)}, u32[]{:S(2)}) copy-start(bf16[64,1536]{1,0:T(8,128)(2,1)S(1)} %get-tuple-element.23) | copy-start | bytes 589828
  73.7 17.3 %copy-start.13 = (pred[8,5]{0,1:T(8,128)(4,1)S(1)}, pred[8,5]{0,1:T(8,128)(4,1)}, u32[]{:S(2)}) copy-start(pred[8,5]{0,1:T(8,128)(4,1)} %constant.91) | copy-start | bytes 124
  73.8 12.4 %collective-permute-start.8 = (bf16[2,4,32,16]{3,2,1,0:T(8,128)(2,1)S(1)}, bf16[2,4,32,16]{3,2,1,0:T(8,128)(2,1)S(1)}, u32[]{:S(2)}, u32[]{:S(2)}) collective-permute-start(bf16[2,4,32,16]{3,2,1,0:T(8,128)(2,1)S(1)} %subtract_convert_fusion), channel_id=1, source_target_pairs={{0,1},{1,2},{2,3},{3,4},{4,5},{5,6},{6,7},{7,8},{8,9},{9,10},{10,1... | collective-permute-start | bytes 24584 | tf_op jit(solution)/shard_map/ppermute | solution.py:22
  75.7 11.1 %collective-permute-start.7 = (bf16[2,4,32,16]{3,2,1,0:T(8,128)(2,1)S(1)}, bf16[2,4,32,16]{3,2,1,0:T(8,128)(2,1)S(1)}, u32[]{:S(2)}, u32[]{:S(2)}) collective-permute-start(bf16[2,4,32,16]{3,2,1,0:T(8,128)(2,1)S(1)} %subtract_convert_fusion), channel_id=1, source_target_pairs={{0,2},{1,3},{2,4},{3,5},{4,6},{5,7},{6,8},{7,9},{8,10},{9,11},{10,... | collective-permute-start | bytes 24584 | tf_op jit(solution)/shard_map/ppermute | solution.py:22
  81.4 9.2 %collective-permute-start.6 = (bf16[2,4,32,16]{3,2,1,0:T(8,128)(2,1)S(1)}, bf16[2,4,32,16]{3,2,1,0:T(8,128)(2,1)S(1)}, u32[]{:S(2)}, u32[]{:S(2)}) collective-permute-start(bf16[2,4,32,16]{3,2,1,0:T(8,128)(2,1)S(1)} %subtract_convert_fusion), channel_id=1, source_target_pairs={{0,3},{1,4},{2,5},{3,6},{4,7},{5,8},{6,9},{7,10},{8,11},{9,12},{10... | collective-permute-start | bytes 24584 | tf_op jit(solution)/shard_map/ppermute | solution.py:22
  94.9 14.7 %slice-start.2 = ((s8[7962624]{0:T(1024)(128)(4,1)}), s8[4194304]{0:T(1024)(128)(4,1)S(1)}, s32[]{:S(2)}) async-start(s8[7962624]{0:T(1024)(128)(4,1)} %bitcast.153), calls=%async_computation.3 | async-start | bytes 8388608
  95.0 14.5 %slice-start.3 = ((s8[7962624]{0:T(1024)(128)(4,1)}), s8[3768320]{0:T(1024)(128)(4,1)S(1)}, s32[]{:S(2)}) async-start(s8[7962624]{0:T(1024)(128)(4,1)} %bitcast.153), calls=%async_computation.4 | async-start | bytes 7536640
  (4 other events, 4.0 us)

commit v9 on v8

--- a/solution.py
+++ b/solution.py
@@ -80,6 +80,23 @@
         preferred_element_type=jnp.float32,
     )
     return result[0]
+
+
+def tap_conv(extended, kernel):
+    taps = kernel.shape[0]
+    out_frames = extended.shape[0] - taps + 1
+    total = None
+    for dt in range(taps):
+        part = lax.conv_general_dilated(
+            extended[dt : dt + out_frames],
+            kernel[dt],
+            (1, 1),
+            ((1, 1), (1, 1)),
+            dimension_numbers=("NHWC", "HWIO", "NHWC"),
+            preferred_element_type=jnp.float32,
+        )
+        total = part if total is None else total + part
+    return total
 
 
 def causal_conv(activ, kernel):
@@ -170,7 +187,7 @@
     clean_ext = jnp.concatenate(earlier + [clean], axis=0)
     feature_ext = spatial_conv(clean_ext, input_kernel).astype(jnp.bfloat16)
     first_act = norm_silu(feature_ext, first_gain)
-    middle = spatial_conv(first_act, middle_kernel)
+    middle = tap_conv(first_act, middle_kernel)
     second_act = norm_silu(middle, second_gain)
     feature = feature_ext[-clean.shape[0]:]
     decoded = (feature.astype(jnp.float32) + spatial_conv(second_act, final_kernel)).astype(

time: 115 us -> 116 us (level)
  matrix products: 23.3 us -> 21.4 us
  local copies, waits for them, and re-layouts: 21.7 us -> 23.3 us
    conv_general_dilated x3 -> x2, matrix products: 18.2 us -> 8.7 us  [spatial_conv(): lax.conv_general_dilated(extended[None], kernel, (1, 1, 1), ((0, 0), (1,...]
    conv_general_dilated x0 -> x3, matrix products: none -> 7.58 us  [tap_conv(): lax.conv_general_dilated(extended[dt:dt + out_frames], kernel[dt], (1, 1)...]
    unnamed x41 -> x46, local copies, waits for them, and re-layouts: 3.32 us -> 4.03 us
  transfers between devices with their start and end apart: 10 -> 10, of which waited for: 5 -> 5; matrix products, arithmetic and copies ran while one was open for 11% -> 10% of each run, Pallas kernels for 0% -> 0%
where the time goes in v9:
time: 116 us; the launch traced here: 115 us
  waiting for transfers between devices  33.7 us (29%)
  starting transfers between devices  29.5 us (25%)
  local copies, waits for them, and re-layouts  23.3 us (20%)
  matrix products  21.4 us (18%)
  other arithmetic  4.93 us (4%)
  between operations  2.01 us (2%)
    ppermute x3, waiting for transfers between devices, body(): received.append(lax.ppermute(piece, 'hg', pairs))  25.2 us
    ppermute x3, starting transfers between devices, shifted(): return lax.ppermute(x, axis, pairs)  12.4 us
    conv_general_dilated x2, matrix products, spatial_conv(): lax.conv_general_dilated(extended[None], kernel, (1, 1, 1), ((0, 0), (1,...  8.7 us
    all_to_all x1, starting transfers between devices, gather_group(): got = lax.all_to_all(sent, FRAMES, 0, 0, tiled=True)  8.55 us
    conv_general_dilated x3, matrix products, tap_conv(): lax.conv_general_dilated(extended[dt:dt + out_frames], kernel[dt], (1, 1)...  7.58 us
    ppermute x3, starting transfers between devices, body(): received.append(lax.ppermute(piece, 'hg', pairs))  5.6 us
    ppermute x3, waiting for transfers between devices, shifted(): return lax.ppermute(x, axis, pairs)  4.33 us
    concatenate x4, local copies, waits for them, and re-layouts, body(): query_heads = split_heads(jnp.concatenate(received, axis=0), group_heads)  4.28 us
  transfers between devices with their start and end apart: 10, of which 5 were waited for; matrix products, arithmetic and copies ran while one was open for 10% of the time, Pallas kernels for 0%

profile of v9, /device:TPU:96, one launch (start us, length us, event | category | flops | bytes accessed | tf_op | source)
XLA Modules:
  0.0 114.7 jit_solution(8517946299347092511)
XLA Ops:
  3.0 2.2 %broadcast_in_dim.11 = bf16[8,4,64,2,384]{4,2,3,1,0:T(8,128)(2,1)} broadcast(bf16[4,64,2,384]{3,1,2,0:T(8,128)(2,1)S(1)} %copy.73), dimensions={1,2,3,4} | broadcast | bytes 3538944 | tf_op jit(solution)/shard_map/broadcast_in_dim | solution.py:146
  5.2 8.6 %all-to-all-start = ((bf16[32,64,2,384]{3,1,2,0:T(8,128)(2,1)}), bf16[32,64,2,384]{3,1,2,0:T(8,128)(2,1)S(1)}, u32[]{:S(2)}, u32[]{:S(2)}) async-start(bf16[32,64,2,384]{3,1,2,0:T(8,128)(2,1)} %bitcast.158), calls=%async_computation | async-start | bytes 6291456 | tf_op jit(solution)/shard_map/all_to_all | solution.py:148
  13.8 1.7 %reshape.97 = bf16[64,4,384]{2,1,0:T(4,128)(2,1)} reshape(bf16[64,1536]{1,0:T(8,128)(2,1)} %param.17) | data formatting | bytes 393216 | tf_op jit(solution)/shard_map/reshape | solution.py:152
  15.4 1.8 %dynamic-slice_reduce_fusion = (bf16[64,384]{1,0:T(8,128)(2,1)S(1)}, bf16[64,1,384]{2,1,0:T(2,128)(2,1)S(1)}, bf16[64,1,384]{2,1,0:T(2,128)(2,1)S(1)}, bf16[64,1,384]{2,1,0:T(2,128)(2,1)S(1)}) fusion(bf16[64,4,384]{2,1,0:T(4,128)(2,1)} %reshape.97, s32[]{:T(128)S(6)} %select_n.18, s32[]{:T(128)S(6)} %select_n.21, s32[]{:T(128)S(6)} %select_n.20, ...), kind=kLoop, calls=%fused_computation.120 | loop fusion | bytes 393232 | tf_op jit(solution)/shard_map/jit(dynamic_index_in_dim)/dynamic_slice | solution.py:153
  17.9 1.5 %collective-permute-start.2 = (bf16[64,384]{1,0:T(8,128)(2,1)}, bf16[64,384]{1,0:T(8,128)(2,1)}, u32[]{:S(2)}, u32[]{:S(2)}) collective-permute-start(bf16[64,384]{1,0:T(8,128)(2,1)} %bitcast.154), channel_id=1, source_target_pairs={{0,1},{1,2},{2,3},{3,0},{4,5},{5,6},{6,7},{7,4},{8,9},{9,10},{10,1... | collective-permute-start | bytes 147464 | tf_op jit(solution)/shard_map/ppermute | solution.py:158
  20.0 2.7 %collective-permute-start.1 = (bf16[64,384]{1,0:T(8,128)(2,1)}, bf16[64,384]{1,0:T(8,128)(2,1)}, u32[]{:S(2)}, u32[]{:S(2)}) collective-permute-start(bf16[64,384]{1,0:T(8,128)(2,1)} %bitcast.155), channel_id=1, source_target_pairs={{0,2},{1,3},{2,0},{3,1},{4,6},{5,7},{6,4},{7,5},{8,10},{9,11},{10,... | collective-permute-start | bytes 147464 | tf_op jit(solution)/shard_map/ppermute | solution.py:158
  23.3 1.5 %collective-permute-start = (bf16[64,384]{1,0:T(8,128)(2,1)}, bf16[64,384]{1,0:T(8,128)(2,1)}, u32[]{:S(2)}, u32[]{:S(2)}) collective-permute-start(bf16[64,384]{1,0:T(8,128)(2,1)} %bitcast.156), channel_id=1, source_target_pairs={{0,3},{1,0},{2,1},{3,2},{4,7},{5,4},{6,5},{7,6},{8,11},{9,8},{10,9... | collective-permute-start | bytes 147464 | tf_op jit(solution)/shard_map/ppermute | solution.py:158
  26.8 25.2 %collective-permute-done.2 = bf16[64,384]{1,0:T(8,128)(2,1)} collective-permute-done((bf16[64,384]{1,0:T(8,128)(2,1)}, bf16[64,384]{1,0:T(8,128)(2,1)}, u32[]{:S(2)}, u32[]{:S(2)}) %collective-permute-start.2) | collective-permute-done | bytes 49184 | tf_op jit(solution)/shard_map/ppermute | solution.py:158
  52.0 1.4 %copy_bitcast_fusion = bf16[64,3,128]{2,0,1:T(8,128)(2,1)} fusion(bf16[64,384]{1,0:T(8,128)(2,1)} %collective-permute-done.2), kind=kLoop, calls=%fused_computation.121 | loop fusion | bytes 98304 | tf_op jit(solution)/shard_map/concatenate | solution.py:159
  53.4 1.4 %copy_bitcast_fusion.1 = bf16[64,3,128]{2,0,1:T(8,128)(2,1)} fusion(bf16[64,384]{1,0:T(8,128)(2,1)} %collective-permute-done.1), kind=kLoop, calls=%fused_computation.122 | loop fusion | bytes 98304 | tf_op jit(solution)/shard_map/concatenate | solution.py:159
  54.9 1.4 %copy_bitcast_fusion.2 = bf16[64,3,128]{2,0,1:T(8,128)(2,1)} fusion(bf16[64,384]{1,0:T(8,128)(2,1)} %collective-permute-done), kind=kLoop, calls=%fused_computation.123 | loop fusion | bytes 98304 | tf_op jit(solution)/shard_map/concatenate | solution.py:159
  57.0 1.6 %copy.77 = bf16[2048,1,384]{0,2,1:T(8,128)(2,1)} copy(bf16[2048,1,384]{2,0,1:T(8,128)(2,1)S(1)} %get-tuple-element.9) | data formatting | bytes 3145728 | tf_op jit(solution)/shard_map/slice | solution.py:162
  59.4 1.9 %multiply_reduce_fusion = (f32[3,256]{1,0:T(4,128)S(1)}, f32[3,256,2048]{2,1,0:T(8,128)S(1)}) fusion(bf16[2048,3,128]{0,2,1:T(8,128)(2,1)S(1)} %bitcast.160, bf16[64,3,128]{2,0,1:T(8,128)(2,1)} %copy_bitcast_fusion, bf16[64,3,128]{2,0,1:T(8,128)(2,1)} %copy_bitcast_fusion.1, bf16[64,3,128]{2,0,1:T(8,128)(2,1)} %copy_bitcast_fusion.2, ...), kind=kOutput, calls=%fused_computation.1 | convolution fusion | flops 406584576 | bytes 8064000 | tf_op jit(solution)/shard_map/qhd,khd->hqk/dot_general | solution.py:39
  62.7 1.4 %fusion.65 = bf16[256,3,128]{0,2,1:T(8,128)(2,1)S(1)} fusion(bf16[2048,3,128]{0,2,1:T(8,128)(2,1)S(1)} %bitcast.177, f32[3,256,2048]{2,1,0:T(8,128)S(1)} %get-tuple-element.24, f32[3,256]{1,0:T(4,128)S(1)} %get-tuple-element.22, f32[256,3]{0,1:T(4,128)S(1)} %bitcast.185, f32[256,3]{0,1:T(4,128)S(1)} %get-tuple-element.21), kind=kOutput, calls=%fused_computation.60 | convolution fusion | flops 407666688 | bytes 8070144 | tf_op jit(solution)/shard_map/hqk,khd->qhd/dot_general | solution.py:46
  67.6 3.6 %collective-permute-done.3 = bf16[64,384]{0,1:T(8,128)(2,1)S(1)} collective-permute-done((bf16[64,384]{0,1:T(8,128)(2,1)S(1)}, bf16[64,384]{0,1:T(8,128)(2,1)S(1)}, u32[]{:S(2)}, u32[]{:S(2)}) %collective-permute-start.3) | collective-permute-done | bytes 49184 | tf_op jit(solution)/shard_map/ppermute | solution.py:180
  73.8 1.9 %collective-permute-start.8 = (bf16[2,4,32,16]{3,2,1,0:T(8,128)(2,1)S(1)}, bf16[2,4,32,16]{3,2,1,0:T(8,128)(2,1)S(1)}, u32[]{:S(2)}, u32[]{:S(2)}) collective-permute-start(bf16[2,4,32,16]{3,2,1,0:T(8,128)(2,1)S(1)} %subtract_convert_fusion), channel_id=1, source_target_pairs={{0,1},{1,2},{2,3},{3,4},{4,5},{5,6},{6,7},{7,8},{8,9},{9,10},{10,1... | collective-permute-start | bytes 24584 | tf_op jit(solution)/shard_map/ppermute | solution.py:22
  75.7 5.6 %collective-permute-start.7 = (bf16[2,4,32,16]{3,2,1,0:T(8,128)(2,1)S(1)}, bf16[2,4,32,16]{3,2,1,0:T(8,128)(2,1)S(1)}, u32[]{:S(2)}, u32[]{:S(2)}) collective-permute-start(bf16[2,4,32,16]{3,2,1,0:T(8,128)(2,1)S(1)} %subtract_convert_fusion), channel_id=1, source_target_pairs={{0,2},{1,3},{2,4},{3,5},{4,6},{5,7},{6,8},{7,9},{8,10},{9,11},{10,... | collective-permute-start | bytes 24584 | tf_op jit(solution)/shard_map/ppermute | solution.py:22
  81.3 4.8 %collective-permute-start.6 = (bf16[2,4,32,16]{3,2,1,0:T(8,128)(2,1)S(1)}, bf16[2,4,32,16]{3,2,1,0:T(8,128)(2,1)S(1)}, u32[]{:S(2)}, u32[]{:S(2)}) collective-permute-start(bf16[2,4,32,16]{3,2,1,0:T(8,128)(2,1)S(1)} %subtract_convert_fusion), channel_id=1, source_target_pairs={{0,3},{1,4},{2,5},{3,6},{4,7},{5,8},{6,9},{7,10},{8,11},{9,12},{10... | collective-permute-start | bytes 24584 | tf_op jit(solution)/shard_map/ppermute | solution.py:22
  86.8 3.7 %collective-permute-done.6 = bf16[2,4,32,16]{3,2,1,0:T(8,128)(2,1)S(1)} collective-permute-done((bf16[2,4,32,16]{3,2,1,0:T(8,128)(2,1)S(1)}, bf16[2,4,32,16]{3,2,1,0:T(8,128)(2,1)S(1)}, u32[]{:S(2)}, u32[]{:S(2)}) %collective-permute-start.6) | collective-permute-done | bytes 8224 | tf_op jit(solution)/shard_map/ppermute | solution.py:22
  91.0 1.8 %select_convert_fusion = bf16[6,4,8,5,384]{4,2,3,1,0:T(8,128)(2,1)S(1)} fusion(bf16[3,3,3,16,384]{4,3,2,1,0:T(8,128)(2,1)S(1)} %copy-done, pred[8,5]{0,1:T(8,128)(4,1)S(1)} %copy-done.13, bf16[8,4,1,7,2,16]{5,3,4,1,0,2:T(8,128)(2,1)S(1)} %slice.89, bf16[8,4,1,8,5,16]{5,3,4,1,0,2:T(8,128)(2,1)S(1)} %copy.81), kind=kOutput, calls=%fused_computation.24 | convolution fusion | flops 266330112 | bytes 1124392 | tf_op jit(solution)/shard_map/conv_general_dilated | solution.py:74
  96.4 2.5 %fusion.35 = f32[4,32,5,384]{3,1,2,0:T(8,128)S(1)} fusion(bf16[3,3,3,384,384]{4,3,2,1,0:T(8,128)(2,1)S(1)} %bitcast.187, bf16[4,4,8,7,384]{4,1,3,2,0:T(4,128)(2,1)S(1)} %fusion.77, pred[32,5]{0,1:T(8,128)(4,1)S(1)} %copy-done.14), kind=kOutput, calls=%fused_computation.35 | convolution fusion | flops 1415823360 | bytes 4326400 | tf_op jit(solution)/shard_map/conv_general_dilated | solution.py:90
  98.9 2.5 %fusion.32 = f32[4,32,5,384]{3,1,2,0:T(8,128)S(1)} fusion(bf16[3,3,3,384,384]{4,3,2,1,0:T(8,128)(2,1)S(1)} %bitcast.187, bf16[4,4,8,7,384]{4,1,3,2,0:T(4,128)(2,1)S(1)} %fusion.76, pred[32,5]{0,1:T(8,128)(4,1)S(1)} %copy-done.14), kind=kOutput, calls=%fused_computation.34 | convolution fusion | flops 1415823360 | bytes 4326400 | tf_op jit(solution)/shard_map/conv_general_dilated | solution.py:90
  102.3 2.6 %multiply_reduce_fusion.1 = (f32[4,32,5]{1,2,0:T(8,128)S(1)}, f32[4,32,5,384]{3,1,2,0:T(8,128)S(1)}) fusion(f32[4,32,5,384]{3,1,2,0:T(8,128)S(1)} %fusion.35, f32[4,32,5,384]{3,1,2,0:T(8,128)S(1)} %fusion.32, bf16[3,3,3,384,384]{4,3,2,1,0:T(8,128)(2,1)S(1)} %bitcast.187, bf16[4,4,8,7,384]{4,1,3,2,0:T(4,128)(2,1)S(1)} %fusion.75, ...), kind=kOutput, calls=%fused_computation.61 | convolution fusion | flops 1416805760 | bytes 6295040 | tf_op jit(solution)/shard_map/conv_general_dilated | solution.py:90
  106.9 6.9 %fusion.42 = bf16[2,4,8,5,384]{4,2,3,1,0:T(8,128)(2,1)S(1)} fusion(bf16[3,3,3,384,384]{4,3,2,1,0:T(8,128)(2,1)} %param.31, bf16[4,4,1,7,2,384]{5,3,4,1,0,2:T(8,128)(2,1)S(1)} %slice.100, bf16[4,4,1,8,5,384]{5,3,4,1,0,2:T(8,128)(2,1)S(1)} %copy.93, bf16[6,4,8,5,384]{4,2,3,1,0:T(8,128)(2,1)S(1)} %select_convert_fusion, pred[8,5]{0,1:T(8,128)(4,1)S(1)} %copy-done.13), kind=kOutput, calls=%fused_computation.39 | convolution fusion | flops 2125922304 | bytes 9117736 | tf_op jit(solution)/shard_map/conv_general_dilated | solution.py:74
  (112 shorter events, 22.5 us)
Async XLA Ops:
  0.6 90.3 %copy-start = (bf16[3,3,3,16,384]{4,3,2,1,0:T(8,128)(2,1)S(1)}, bf16[3,3,3,16,384]{4,3,2,1,0:T(8,128)(2,1)}, u32[]{:S(2)}) copy-start(bf16[3,3,3,16,384]{4,3,2,1,0:T(8,128)(2,1)} %param.27) | copy-start | bytes 995332
  5.2 51.1 %all-to-all-start = ((bf16[32,64,2,384]{3,1,2,0:T(8,128)(2,1)}), bf16[32,64,2,384]{3,1,2,0:T(8,128)(2,1)S(1)}, u32[]{:S(2)}, u32[]{:S(2)}) async-start(bf16[32,64,2,384]{3,1,2,0:T(8,128)(2,1)} %bitcast.158), calls=%async_computation | async-start | bytes 6291456 | tf_op jit(solution)/shard_map/all_to_all | solution.py:148
  13.7 11.0 %copy-start.7 = (f32[1536]{0:T(1024)S(1)}, f32[1536]{0:T(1024)}, u32[]{:S(2)}) copy-start(f32[1536]{0:T(1024)} %param.22) | copy-start | bytes 18436
  13.7 11.6 %copy-start.5 = (f32[2,4,512]{2,1,0:T(4,128)S(1)}, f32[2,4,512]{2,1,0:T(4,128)}, u32[]{:S(2)}) copy-start(f32[2,4,512]{2,1,0:T(4,128)} %param.26) | copy-start | bytes 49156
  17.9 34.1 %collective-permute-start.2 = (bf16[64,384]{1,0:T(8,128)(2,1)}, bf16[64,384]{1,0:T(8,128)(2,1)}, u32[]{:S(2)}, u32[]{:S(2)}) collective-permute-start(bf16[64,384]{1,0:T(8,128)(2,1)} %bitcast.154), channel_id=1, source_target_pairs={{0,1},{1,2},{2,3},{3,0},{4,5},{5,6},{6,7},{7,4},{8,9},{9,10},{10,1... | collective-permute-start | bytes 147464 | tf_op jit(solution)/shard_map/ppermute | solution.py:158
  20.0 33.4 %collective-permute-start.1 = (bf16[64,384]{1,0:T(8,128)(2,1)}, bf16[64,384]{1,0:T(8,128)(2,1)}, u32[]{:S(2)}, u32[]{:S(2)}) collective-permute-start(bf16[64,384]{1,0:T(8,128)(2,1)} %bitcast.155), channel_id=1, source_target_pairs={{0,2},{1,3},{2,0},{3,1},{4,6},{5,7},{6,4},{7,5},{8,10},{9,11},{10,... | collective-permute-start | bytes 147464 | tf_op jit(solution)/shard_map/ppermute | solution.py:158
  23.3 31.6 %collective-permute-start = (bf16[64,384]{1,0:T(8,128)(2,1)}, bf16[64,384]{1,0:T(8,128)(2,1)}, u32[]{:S(2)}, u32[]{:S(2)}) collective-permute-start(bf16[64,384]{1,0:T(8,128)(2,1)} %bitcast.156), channel_id=1, source_target_pairs={{0,3},{1,0},{2,1},{3,2},{4,7},{5,4},{6,5},{7,6},{8,11},{9,8},{10,9... | collective-permute-start | bytes 147464 | tf_op jit(solution)/shard_map/ppermute | solution.py:158
  61.3 1.4 %copy-start.1 = (bf16[2048,1,384]{0,2,1:T(8,128)(2,1)S(1)}, bf16[2048,1,384]{0,2,1:T(8,128)(2,1)}, u32[]{:S(2)}) copy-start(bf16[2048,1,384]{0,2,1:T(8,128)(2,1)} %copy.77) | copy-start | bytes 4718596
  61.3 5.9 %slice-start = ((s8[4718592]{0:T(1024)(128)(4,1)}), s8[4194304]{0:T(1024)(128)(4,1)S(1)}, s32[]{:S(2)}) async-start(s8[4718592]{0:T(1024)(128)(4,1)} %bitcast.163), calls=%async_computation.1 | async-start | bytes 8388608
  62.7 4.5 %slice-start.1 = ((s8[4718592]{0:T(1024)(128)(4,1)}), s8[524288]{0:T(1024)(128)(4,1)S(1)}, s32[]{:S(2)}) async-start(s8[4718592]{0:T(1024)(128)(4,1)} %bitcast.163), calls=%async_computation.2 | async-start | bytes 1048576
  64.3 7.3 %collective-permute-start.5 = (bf16[64,384]{0,1:T(8,128)(2,1)S(1)}, bf16[64,384]{0,1:T(8,128)(2,1)S(1)}, u32[]{:S(2)}, u32[]{:S(2)}) collective-permute-start(bf16[64,384]{0,1:T(8,128)(2,1)S(1)} %bitcast.183), channel_id=1, source_target_pairs={{0,3},{1,0},{2,1},{3,2},{4,7},{5,4},{6,5},{7,6},{8,11},{9,8},{10,9... | collective-permute-start | bytes 147464 | tf_op jit(solution)/shard_map/ppermute | solution.py:180
  65.4 5.8 %collective-permute-start.3 = (bf16[64,384]{0,1:T(8,128)(2,1)S(1)}, bf16[64,384]{0,1:T(8,128)(2,1)S(1)}, u32[]{:S(2)}, u32[]{:S(2)}) collective-permute-start(bf16[64,384]{0,1:T(8,128)(2,1)S(1)} %bitcast.184), channel_id=1, source_target_pairs={{0,1},{1,2},{2,3},{3,0},{4,5},{5,6},{6,7},{7,4},{8,9},{9,10},{10,1... | collective-permute-start | bytes 147464 | tf_op jit(solution)/shard_map/ppermute | solution.py:180
  66.4 6.1 %collective-permute-start.4 = (bf16[64,384]{0,1:T(8,128)(2,1)S(1)}, bf16[64,384]{0,1:T(8,128)(2,1)S(1)}, u32[]{:S(2)}, u32[]{:S(2)}) collective-permute-start(bf16[64,384]{0,1:T(8,128)(2,1)S(1)} %bitcast.182), channel_id=1, source_target_pairs={{0,2},{1,3},{2,0},{3,1},{4,6},{5,7},{6,4},{7,5},{8,10},{9,11},{10,... | collective-permute-start | bytes 147464 | tf_op jit(solution)/shard_map/ppermute | solution.py:180
  67.6 4.9 %copy-start.4 = (bf16[64,1536]{1,0:T(8,128)(2,1)S(1)}, bf16[64,1536]{1,0:T(8,128)(2,1)}, u32[]{:S(2)}) copy-start(bf16[64,1536]{1,0:T(8,128)(2,1)} %param.16) | copy-start | bytes 589828
  67.6 4.9 %copy-start.6 = (f32[1536]{0:T(1024)S(1)}, f32[1536]{0:T(1024)}, u32[]{:S(2)}) copy-start(f32[1536]{0:T(1024)} %param.20) | copy-start | bytes 18436
  71.9 1.3 %copy-start.8 = (f32[1536]{0:T(1024)S(1)}, f32[1536]{0:T(1024)}, u32[]{:S(2)}) copy-start(f32[1536]{0:T(1024)} %broadcast_add_fusion) | copy-start | bytes 18436
  72.0 1.8 %copy-start.3 = (f32[2,4,32,16]{3,2,1,0:T(8,128)S(1)}, f32[2,4,32,16]{3,2,1,0:T(8,128)}, u32[]{:S(2)}) copy-start(f32[2,4,32,16]{3,2,1,0:T(8,128)} %reshape.101) | copy-start | bytes 49156
  73.0 17.9 %copy-start.2 = (bf16[64,1536]{1,0:T(8,128)(2,1)}, bf16[64,1536]{1,0:T(8,128)(2,1)S(1)}, u32[]{:S(2)}) copy-start(bf16[64,1536]{1,0:T(8,128)(2,1)S(1)} %get-tuple-element.26) | copy-start | bytes 589828
  73.7 17.3 %copy-start.13 = (pred[8,5]{0,1:T(8,128)(4,1)S(1)}, pred[8,5]{0,1:T(8,128)(4,1)}, u32[]{:S(2)}) copy-start(pred[8,5]{0,1:T(8,128)(4,1)} %constant.99) | copy-start | bytes 124
  73.8 12.4 %collective-permute-start.8 = (bf16[2,4,32,16]{3,2,1,0:T(8,128)(2,1)S(1)}, bf16[2,4,32,16]{3,2,1,0:T(8,128)(2,1)S(1)}, u32[]{:S(2)}, u32[]{:S(2)}) collective-permute-start(bf16[2,4,32,16]{3,2,1,0:T(8,128)(2,1)S(1)} %subtract_convert_fusion), channel_id=1, source_target_pairs={{0,1},{1,2},{2,3},{3,4},{4,5},{5,6},{6,7},{7,8},{8,9},{9,10},{10,1... | collective-permute-start | bytes 24584 | tf_op jit(solution)/shard_map/ppermute | solution.py:22
  75.7 11.1 %collective-permute-start.7 = (bf16[2,4,32,16]{3,2,1,0:T(8,128)(2,1)S(1)}, bf16[2,4,32,16]{3,2,1,0:T(8,128)(2,1)S(1)}, u32[]{:S(2)}, u32[]{:S(2)}) collective-permute-start(bf16[2,4,32,16]{3,2,1,0:T(8,128)(2,1)S(1)} %subtract_convert_fusion), channel_id=1, source_target_pairs={{0,2},{1,3},{2,4},{3,5},{4,6},{5,7},{6,8},{7,9},{8,10},{9,11},{10,... | collective-permute-start | bytes 24584 | tf_op jit(solution)/shard_map/ppermute | solution.py:22
  81.3 9.2 %collective-permute-start.6 = (bf16[2,4,32,16]{3,2,1,0:T(8,128)(2,1)S(1)}, bf16[2,4,32,16]{3,2,1,0:T(8,128)(2,1)S(1)}, u32[]{:S(2)}, u32[]{:S(2)}) collective-permute-start(bf16[2,4,32,16]{3,2,1,0:T(8,128)(2,1)S(1)} %subtract_convert_fusion), channel_id=1, source_target_pairs={{0,3},{1,4},{2,5},{3,6},{4,7},{5,8},{6,9},{7,10},{8,11},{9,12},{10... | collective-permute-start | bytes 24584 | tf_op jit(solution)/shard_map/ppermute | solution.py:22
  91.0 5.4 %slice-start.2 = ((s8[7962624]{0:T(1024)(128)(4,1)}), s8[4194304]{0:T(1024)(128)(4,1)S(1)}, s32[]{:S(2)}) async-start(s8[7962624]{0:T(1024)(128)(4,1)} %bitcast.186), calls=%async_computation.3 | async-start | bytes 8388608
  93.1 3.3 %slice-start.3 = ((s8[7962624]{0:T(1024)(128)(4,1)}), s8[3768320]{0:T(1024)(128)(4,1)S(1)}, s32[]{:S(2)}) async-start(s8[7962624]{0:T(1024)(128)(4,1)} %bitcast.186), calls=%async_computation.4 | async-start | bytes 7536640
  (5 other events, 5.4 us)

commit v10 on v9

--- a/solution.py
+++ b/solution.py
@@ -190,7 +190,7 @@
     middle = tap_conv(first_act, middle_kernel)
     second_act = norm_silu(middle, second_gain)
     feature = feature_ext[-clean.shape[0]:]
-    decoded = (feature.astype(jnp.float32) + spatial_conv(second_act, final_kernel)).astype(
+    decoded = (feature.astype(jnp.float32) + tap_conv(second_act, final_kernel)).astype(
         jnp.bfloat16
     )
     return (layer_output, decoded)

time: 116 us -> 121 us (1.043)
  matrix products: 21.4 us -> 23.8 us
  local copies, waits for them, and re-layouts: 23.3 us -> 24.6 us
    conv_general_dilated x3 -> x6, matrix products: 7.58 us -> 16.9 us  [tap_conv(): lax.conv_general_dilated(extended[dt:dt + out_frames], kernel[dt], (1, 1)...]
    conv_general_dilated x2 -> x1, matrix products: 8.7 us -> 1.8 us  [spatial_conv(): lax.conv_general_dilated(extended[None], kernel, (1, 1, 1), ((0, 0), (1,...]
    unnamed x46 -> x55, local copies, waits for them, and re-layouts: 4.03 us -> 4.66 us
where the time goes in v10:
time: 121 us; the launch traced here: 120 us
  waiting for transfers between devices  33.7 us (28%)
  starting transfers between devices  29.6 us (24%)
  local copies, waits for them, and re-layouts  24.6 us (20%)
  matrix products  23.8 us (20%)
  other arithmetic  5.94 us (5%)
  between operations  2.13 us (2%)
    ppermute x3, waiting for transfers between devices, body(): received.append(lax.ppermute(piece, 'hg', pairs))  25.3 us
    conv_general_dilated x6, matrix products, tap_conv(): lax.conv_general_dilated(extended[dt:dt + out_frames], kernel[dt], (1, 1)...  16.9 us
    ppermute x3, starting transfers between devices, shifted(): return lax.ppermute(x, axis, pairs)  12.4 us
    all_to_all x1, starting transfers between devices, gather_group(): got = lax.all_to_all(sent, FRAMES, 0, 0, tiled=True)  8.68 us
    ppermute x3, starting transfers between devices, body(): received.append(lax.ppermute(piece, 'hg', pairs))  5.6 us
    unnamed x55, local copies, waits for them, and re-layouts  4.66 us
    ppermute x3, waiting for transfers between devices, shifted(): return lax.ppermute(x, axis, pairs)  4.33 us
    concatenate x4, local copies, waits for them, and re-layouts, body(): query_heads = split_heads(jnp.concatenate(received, axis=0), group_heads)  4.27 us
  transfers between devices with their start and end apart: 10, of which 5 were waited for; matrix products, arithmetic and copies ran while one was open for 10% of the time, Pallas kernels for 0%

profile of v10, /device:TPU:96, one launch (start us, length us, event | category | flops | bytes accessed | tf_op | source)
XLA Modules:
  0.0 119.8 jit_solution(12639184283586649511)
XLA Ops:
  3.0 2.1 %broadcast_in_dim.9 = bf16[8,4,64,2,384]{4,2,3,1,0:T(8,128)(2,1)} broadcast(bf16[4,64,2,384]{3,1,2,0:T(8,128)(2,1)S(1)} %copy.83), dimensions={1,2,3,4} | broadcast | bytes 3538944 | tf_op jit(solution)/shard_map/broadcast_in_dim | solution.py:146
  5.1 8.7 %all-to-all-start = ((bf16[32,64,2,384]{3,1,2,0:T(8,128)(2,1)}), bf16[32,64,2,384]{3,1,2,0:T(8,128)(2,1)S(1)}, u32[]{:S(2)}, u32[]{:S(2)}) async-start(bf16[32,64,2,384]{3,1,2,0:T(8,128)(2,1)} %bitcast.196), calls=%async_computation | async-start | bytes 6291456 | tf_op jit(solution)/shard_map/all_to_all | solution.py:148
  13.9 1.7 %reshape.96 = bf16[64,4,384]{2,1,0:T(4,128)(2,1)} reshape(bf16[64,1536]{1,0:T(8,128)(2,1)} %param.17) | data formatting | bytes 393216 | tf_op jit(solution)/shard_map/reshape | solution.py:152
  15.5 1.8 %dynamic-slice_reduce_fusion = (bf16[64,384]{1,0:T(8,128)(2,1)S(1)}, bf16[64,1,384]{2,1,0:T(2,128)(2,1)S(1)}, bf16[64,1,384]{2,1,0:T(2,128)(2,1)S(1)}, bf16[64,1,384]{2,1,0:T(2,128)(2,1)S(1)}) fusion(bf16[64,4,384]{2,1,0:T(4,128)(2,1)} %reshape.96, s32[]{:T(128)S(6)} %select_n.18, s32[]{:T(128)S(6)} %select_n.21, s32[]{:T(128)S(6)} %select_n.20, ...), kind=kLoop, calls=%fused_computation.141 | loop fusion | bytes 393232 | tf_op jit(solution)/shard_map/jit(dynamic_index_in_dim)/dynamic_slice | solution.py:153
  18.0 1.5 %collective-permute-start.2 = (bf16[64,384]{1,0:T(8,128)(2,1)}, bf16[64,384]{1,0:T(8,128)(2,1)}, u32[]{:S(2)}, u32[]{:S(2)}) collective-permute-start(bf16[64,384]{1,0:T(8,128)(2,1)} %bitcast.192), channel_id=1, source_target_pairs={{0,1},{1,2},{2,3},{3,0},{4,5},{5,6},{6,7},{7,4},{8,9},{9,10},{10,1... | collective-permute-start | bytes 147464 | tf_op jit(solution)/shard_map/ppermute | solution.py:158
  20.1 2.7 %collective-permute-start.1 = (bf16[64,384]{1,0:T(8,128)(2,1)}, bf16[64,384]{1,0:T(8,128)(2,1)}, u32[]{:S(2)}, u32[]{:S(2)}) collective-permute-start(bf16[64,384]{1,0:T(8,128)(2,1)} %bitcast.193), channel_id=1, source_target_pairs={{0,2},{1,3},{2,0},{3,1},{4,6},{5,7},{6,4},{7,5},{8,10},{9,11},{10,... | collective-permute-start | bytes 147464 | tf_op jit(solution)/shard_map/ppermute | solution.py:158
  23.4 1.5 %collective-permute-start = (bf16[64,384]{1,0:T(8,128)(2,1)}, bf16[64,384]{1,0:T(8,128)(2,1)}, u32[]{:S(2)}, u32[]{:S(2)}) collective-permute-start(bf16[64,384]{1,0:T(8,128)(2,1)} %bitcast.194), channel_id=1, source_target_pairs={{0,3},{1,0},{2,1},{3,2},{4,7},{5,4},{6,5},{7,6},{8,11},{9,8},{10,9... | collective-permute-start | bytes 147464 | tf_op jit(solution)/shard_map/ppermute | solution.py:158
  26.9 25.2 %collective-permute-done.2 = bf16[64,384]{1,0:T(8,128)(2,1)} collective-permute-done((bf16[64,384]{1,0:T(8,128)(2,1)}, bf16[64,384]{1,0:T(8,128)(2,1)}, u32[]{:S(2)}, u32[]{:S(2)}) %collective-permute-start.2) | collective-permute-done | bytes 49184 | tf_op jit(solution)/shard_map/ppermute | solution.py:158
  52.1 1.4 %copy_bitcast_fusion = bf16[64,3,128]{2,0,1:T(8,128)(2,1)} fusion(bf16[64,384]{1,0:T(8,128)(2,1)} %collective-permute-done.2), kind=kLoop, calls=%fused_computation.142 | loop fusion | bytes 98304 | tf_op jit(solution)/shard_map/concatenate | solution.py:159
  55.0 1.4 %copy_bitcast_fusion.2 = bf16[64,3,128]{2,0,1:T(8,128)(2,1)} fusion(bf16[64,384]{1,0:T(8,128)(2,1)} %collective-permute-done), kind=kLoop, calls=%fused_computation.144 | loop fusion | bytes 98304 | tf_op jit(solution)/shard_map/concatenate | solution.py:159
  57.1 1.7 %copy.87 = bf16[2048,1,384]{0,2,1:T(8,128)(2,1)} copy(bf16[2048,1,384]{2,0,1:T(8,128)(2,1)S(1)} %get-tuple-element.9) | data formatting | bytes 3145728 | tf_op jit(solution)/shard_map/slice | solution.py:162
  59.5 1.9 %multiply_reduce_fusion = (f32[3,256]{1,0:T(4,128)S(1)}, f32[3,256,2048]{2,1,0:T(8,128)S(1)}) fusion(bf16[2048,3,128]{0,2,1:T(8,128)(2,1)S(1)} %bitcast.198, bf16[64,3,128]{2,0,1:T(8,128)(2,1)} %copy_bitcast_fusion, bf16[64,3,128]{2,0,1:T(8,128)(2,1)} %copy_bitcast_fusion.1, bf16[64,3,128]{2,0,1:T(8,128)(2,1)} %copy_bitcast_fusion.2, ...), kind=kOutput, calls=%fused_computation.1 | convolution fusion | flops 406584576 | bytes 8064000 | tf_op jit(solution)/shard_map/qhd,khd->hqk/dot_general | solution.py:39
  67.7 3.6 %collective-permute-done.3 = bf16[64,384]{0,1:T(8,128)(2,1)S(1)} collective-permute-done((bf16[64,384]{0,1:T(8,128)(2,1)S(1)}, bf16[64,384]{0,1:T(8,128)(2,1)S(1)}, u32[]{:S(2)}, u32[]{:S(2)}) %collective-permute-start.3) | collective-permute-done | bytes 49184 | tf_op jit(solution)/shard_map/ppermute | solution.py:180
  73.9 1.9 %collective-permute-start.8 = (bf16[2,4,32,16]{3,2,1,0:T(8,128)(2,1)S(1)}, bf16[2,4,32,16]{3,2,1,0:T(8,128)(2,1)S(1)}, u32[]{:S(2)}, u32[]{:S(2)}) collective-permute-start(bf16[2,4,32,16]{3,2,1,0:T(8,128)(2,1)S(1)} %subtract_convert_fusion), channel_id=1, source_target_pairs={{0,1},{1,2},{2,3},{3,4},{4,5},{5,6},{6,7},{7,8},{8,9},{9,10},{10,1... | collective-permute-start | bytes 24584 | tf_op jit(solution)/shard_map/ppermute | solution.py:22
  75.8 5.6 %collective-permute-start.7 = (bf16[2,4,32,16]{3,2,1,0:T(8,128)(2,1)S(1)}, bf16[2,4,32,16]{3,2,1,0:T(8,128)(2,1)S(1)}, u32[]{:S(2)}, u32[]{:S(2)}) collective-permute-start(bf16[2,4,32,16]{3,2,1,0:T(8,128)(2,1)S(1)} %subtract_convert_fusion), channel_id=1, source_target_pairs={{0,2},{1,3},{2,4},{3,5},{4,6},{5,7},{6,8},{7,9},{8,10},{9,11},{10,... | collective-permute-start | bytes 24584 | tf_op jit(solution)/shard_map/ppermute | solution.py:22
  81.5 4.8 %collective-permute-start.6 = (bf16[2,4,32,16]{3,2,1,0:T(8,128)(2,1)S(1)}, bf16[2,4,32,16]{3,2,1,0:T(8,128)(2,1)S(1)}, u32[]{:S(2)}, u32[]{:S(2)}) collective-permute-start(bf16[2,4,32,16]{3,2,1,0:T(8,128)(2,1)S(1)} %subtract_convert_fusion), channel_id=1, source_target_pairs={{0,3},{1,4},{2,5},{3,6},{4,7},{5,8},{6,9},{7,10},{8,11},{9,12},{10... | collective-permute-start | bytes 24584 | tf_op jit(solution)/shard_map/ppermute | solution.py:22
  87.0 3.7 %collective-permute-done.6 = bf16[2,4,32,16]{3,2,1,0:T(8,128)(2,1)S(1)} collective-permute-done((bf16[2,4,32,16]{3,2,1,0:T(8,128)(2,1)S(1)}, bf16[2,4,32,16]{3,2,1,0:T(8,128)(2,1)S(1)}, u32[]{:S(2)}, u32[]{:S(2)}) %collective-permute-start.6) | collective-permute-done | bytes 8224 | tf_op jit(solution)/shard_map/ppermute | solution.py:22
  91.1 1.8 %select_convert_fusion = bf16[6,4,8,5,384]{4,2,3,1,0:T(8,128)(2,1)S(1)} fusion(bf16[3,3,3,16,384]{4,3,2,1,0:T(8,128)(2,1)S(1)} %copy-done, pred[8,5]{0,1:T(8,128)(4,1)S(1)} %copy-done.17, bf16[8,4,1,7,2,16]{5,3,4,1,0,2:T(8,128)(2,1)S(1)} %slice.116, bf16[8,4,1,8,5,16]{5,3,4,1,0,2:T(8,128)(2,1)S(1)} %copy.91), kind=kOutput, calls=%fused_computation.33 | convolution fusion | flops 266330112 | bytes 1124392 | tf_op jit(solution)/shard_map/conv_general_dilated | solution.py:74
  96.6 2.5 %fusion.43 = f32[4,32,5,384]{3,1,2,0:T(8,128)S(1)} fusion(bf16[3,3,3,384,384]{4,3,2,1,0:T(8,128)(2,1)S(1)} %bitcast.231, bf16[4,4,8,7,384]{4,1,3,2,0:T(4,128)(2,1)S(1)} %fusion.95, pred[32,5]{0,1:T(8,128)(4,1)S(1)} %copy-done.16), kind=kOutput, calls=%fused_computation.42 | convolution fusion | flops 1415823360 | bytes 4326400 | tf_op jit(solution)/shard_map/conv_general_dilated | solution.py:90
  99.0 2.5 %fusion.40 = f32[4,32,5,384]{3,1,2,0:T(8,128)S(1)} fusion(bf16[3,3,3,384,384]{4,3,2,1,0:T(8,128)(2,1)S(1)} %bitcast.231, bf16[4,4,8,7,384]{4,1,3,2,0:T(4,128)(2,1)S(1)} %fusion.94, pred[32,5]{0,1:T(8,128)(4,1)S(1)} %copy-done.16), kind=kOutput, calls=%fused_computation.41 | convolution fusion | flops 1415823360 | bytes 4326400 | tf_op jit(solution)/shard_map/conv_general_dilated | solution.py:90
  102.4 2.6 %multiply_reduce_fusion.1 = (f32[4,32,5]{1,2,0:T(8,128)S(1)}, f32[4,32,5,384]{3,1,2,0:T(8,128)S(1)}) fusion(f32[4,32,5,384]{3,1,2,0:T(8,128)S(1)} %fusion.43, f32[4,32,5,384]{3,1,2,0:T(8,128)S(1)} %fusion.40, bf16[3,3,3,384,384]{4,3,2,1,0:T(8,128)(2,1)S(1)} %bitcast.231, bf16[4,4,8,7,384]{4,1,3,2,0:T(4,128)(2,1)S(1)} %fusion.93, ...), kind=kOutput, calls=%fused_computation.70 | convolution fusion | flops 1416805760 | bytes 6295040 | tf_op jit(solution)/shard_map/conv_general_dilated | solution.py:90
  108.5 3.1 %fusion.58 = f32[4,16,5,384]{3,1,2,0:T(8,128)S(1)} fusion(bf16[3,3,3,384,384]{4,3,2,1,0:T(8,128)(2,1)} %param.31, bf16[4,2,8,7,384]{4,1,3,2,0:T(2,128)(2,1)S(1)} %fusion.121, pred[16,5]{0,1:T(8,128)(4,1)S(1)} %copy-done.15), kind=kOutput, calls=%fused_computation.47 | convolution fusion | flops 707911680 | bytes 3489872 | tf_op jit(solution)/shard_map/conv_general_dilated | solution.py:90
  111.6 3.1 %fusion.55 = f32[4,16,5,384]{3,1,2,0:T(8,128)S(1)} fusion(bf16[3,3,3,384,384]{4,3,2,1,0:T(8,128)(2,1)} %param.31, bf16[4,2,8,7,384]{4,1,3,2,0:T(2,128)(2,1)S(1)} %fusion.120, pred[16,5]{0,1:T(8,128)(4,1)S(1)} %copy-done.15), kind=kOutput, calls=%fused_computation.46 | convolution fusion | flops 707911680 | bytes 3489872 | tf_op jit(solution)/shard_map/conv_general_dilated | solution.py:90
  115.5 3.2 %fusion.52 = f32[4,16,5,384]{3,1,2,0:T(8,128)S(1)} fusion(f32[4,16,5,384]{3,1,2,0:T(8,128)S(1)} %fusion.58, f32[4,16,5,384]{3,1,2,0:T(8,128)S(1)} %fusion.55, bf16[3,3,3,384,384]{4,3,2,1,0:T(8,128)(2,1)} %param.31, bf16[4,2,8,7,384]{4,1,3,2,0:T(2,128)(2,1)S(1)} %fusion.119, pred[16,5]{0,1:T(8,128)(4,1)S(1)} %copy-done.15), kind=kOutput, calls=%fused_computation.45 | convolution fusion | flops 708157440 | bytes 4472912 | tf_op jit(solution)/shard_map/conv_general_dilated | solution.py:90
  (133 shorter events, 27.7 us)
Async XLA Ops:
  0.6 90.4 %copy-start = (bf16[3,3,3,16,384]{4,3,2,1,0:T(8,128)(2,1)S(1)}, bf16[3,3,3,16,384]{4,3,2,1,0:T(8,128)(2,1)}, u32[]{:S(2)}) copy-start(bf16[3,3,3,16,384]{4,3,2,1,0:T(8,128)(2,1)} %param.27) | copy-start | bytes 995332
  5.1 19.7 %copy-start.9 = (f32[1536]{0:T(1024)S(1)}, f32[1536]{0:T(1024)}, u32[]{:S(2)}) copy-start(f32[1536]{0:T(1024)} %param.22) | copy-start | bytes 18436
  5.1 20.3 %copy-start.7 = (f32[2,4,512]{2,1,0:T(4,128)S(1)}, f32[2,4,512]{2,1,0:T(4,128)}, u32[]{:S(2)}) copy-start(f32[2,4,512]{2,1,0:T(4,128)} %param.26) | copy-start | bytes 49156
  5.1 51.2 %all-to-all-start = ((bf16[32,64,2,384]{3,1,2,0:T(8,128)(2,1)}), bf16[32,64,2,384]{3,1,2,0:T(8,128)(2,1)S(1)}, u32[]{:S(2)}, u32[]{:S(2)}) async-start(bf16[32,64,2,384]{3,1,2,0:T(8,128)(2,1)} %bitcast.196), calls=%async_computation | async-start | bytes 6291456 | tf_op jit(solution)/shard_map/all_to_all | solution.py:148
  18.0 34.1 %collective-permute-start.2 = (bf16[64,384]{1,0:T(8,128)(2,1)}, bf16[64,384]{1,0:T(8,128)(2,1)}, u32[]{:S(2)}, u32[]{:S(2)}) collective-permute-start(bf16[64,384]{1,0:T(8,128)(2,1)} %bitcast.192), channel_id=1, source_target_pairs={{0,1},{1,2},{2,3},{3,0},{4,5},{5,6},{6,7},{7,4},{8,9},{9,10},{10,1... | collective-permute-start | bytes 147464 | tf_op jit(solution)/shard_map/ppermute | solution.py:158
  20.1 33.5 %collective-permute-start.1 = (bf16[64,384]{1,0:T(8,128)(2,1)}, bf16[64,384]{1,0:T(8,128)(2,1)}, u32[]{:S(2)}, u32[]{:S(2)}) collective-permute-start(bf16[64,384]{1,0:T(8,128)(2,1)} %bitcast.193), channel_id=1, source_target_pairs={{0,2},{1,3},{2,0},{3,1},{4,6},{5,7},{6,4},{7,5},{8,10},{9,11},{10,... | collective-permute-start | bytes 147464 | tf_op jit(solution)/shard_map/ppermute | solution.py:158
  23.4 31.6 %collective-permute-start = (bf16[64,384]{1,0:T(8,128)(2,1)}, bf16[64,384]{1,0:T(8,128)(2,1)}, u32[]{:S(2)}, u32[]{:S(2)}) collective-permute-start(bf16[64,384]{1,0:T(8,128)(2,1)} %bitcast.194), channel_id=1, source_target_pairs={{0,3},{1,0},{2,1},{3,2},{4,7},{5,4},{6,5},{7,6},{8,11},{9,8},{10,9... | collective-permute-start | bytes 147464 | tf_op jit(solution)/shard_map/ppermute | solution.py:158
  61.5 5.9 %slice-start = ((s8[4718592]{0:T(1024)(128)(4,1)}), s8[4194304]{0:T(1024)(128)(4,1)S(1)}, s32[]{:S(2)}) async-start(s8[4718592]{0:T(1024)(128)(4,1)} %bitcast.201), calls=%async_computation.1 | async-start | bytes 8388608
  62.9 4.5 %slice-start.1 = ((s8[4718592]{0:T(1024)(128)(4,1)}), s8[524288]{0:T(1024)(128)(4,1)S(1)}, s32[]{:S(2)}) async-start(s8[4718592]{0:T(1024)(128)(4,1)} %bitcast.201), calls=%async_computation.2 | async-start | bytes 1048576
  64.4 7.3 %collective-permute-start.5 = (bf16[64,384]{0,1:T(8,128)(2,1)S(1)}, bf16[64,384]{0,1:T(8,128)(2,1)S(1)}, u32[]{:S(2)}, u32[]{:S(2)}) collective-permute-start(bf16[64,384]{0,1:T(8,128)(2,1)S(1)} %bitcast.227), channel_id=1, source_target_pairs={{0,3},{1,0},{2,1},{3,2},{4,7},{5,4},{6,5},{7,6},{8,11},{9,8},{10,9... | collective-permute-start | bytes 147464 | tf_op jit(solution)/shard_map/ppermute | solution.py:180
  65.5 5.8 %collective-permute-start.3 = (bf16[64,384]{0,1:T(8,128)(2,1)S(1)}, bf16[64,384]{0,1:T(8,128)(2,1)S(1)}, u32[]{:S(2)}, u32[]{:S(2)}) collective-permute-start(bf16[64,384]{0,1:T(8,128)(2,1)S(1)} %bitcast.228), channel_id=1, source_target_pairs={{0,1},{1,2},{2,3},{3,0},{4,5},{5,6},{6,7},{7,4},{8,9},{9,10},{10,1... | collective-permute-start | bytes 147464 | tf_op jit(solution)/shard_map/ppermute | solution.py:180
  66.5 6.1 %collective-permute-start.4 = (bf16[64,384]{0,1:T(8,128)(2,1)S(1)}, bf16[64,384]{0,1:T(8,128)(2,1)S(1)}, u32[]{:S(2)}, u32[]{:S(2)}) collective-permute-start(bf16[64,384]{0,1:T(8,128)(2,1)S(1)} %bitcast.226), channel_id=1, source_target_pairs={{0,2},{1,3},{2,0},{3,1},{4,6},{5,7},{6,4},{7,5},{8,10},{9,11},{10,... | collective-permute-start | bytes 147464 | tf_op jit(solution)/shard_map/ppermute | solution.py:180
  67.4 5.3 %copy-start.6 = (bf16[64,1536]{1,0:T(8,128)(2,1)S(1)}, bf16[64,1536]{1,0:T(8,128)(2,1)}, u32[]{:S(2)}) copy-start(bf16[64,1536]{1,0:T(8,128)(2,1)} %param.16) | copy-start | bytes 589828
  67.4 5.3 %copy-start.8 = (f32[1536]{0:T(1024)S(1)}, f32[1536]{0:T(1024)}, u32[]{:S(2)}) copy-start(f32[1536]{0:T(1024)} %param.20) | copy-start | bytes 18436
  73.1 19.8 %copy-start.4 = (bf16[64,1536]{1,0:T(8,128)(2,1)}, bf16[64,1536]{1,0:T(8,128)(2,1)S(1)}, u32[]{:S(2)}) copy-start(bf16[64,1536]{1,0:T(8,128)(2,1)S(1)} %get-tuple-element.29) | copy-start | bytes 589828
  73.1 18.0 %copy-start.17 = (pred[8,5]{0,1:T(8,128)(4,1)S(1)}, pred[8,5]{0,1:T(8,128)(4,1)}, u32[]{:S(2)}) copy-start(pred[8,5]{0,1:T(8,128)(4,1)} %constant.107) | copy-start | bytes 124
  73.9 12.4 %collective-permute-start.8 = (bf16[2,4,32,16]{3,2,1,0:T(8,128)(2,1)S(1)}, bf16[2,4,32,16]{3,2,1,0:T(8,128)(2,1)S(1)}, u32[]{:S(2)}, u32[]{:S(2)}) collective-permute-start(bf16[2,4,32,16]{3,2,1,0:T(8,128)(2,1)S(1)} %subtract_convert_fusion), channel_id=1, source_target_pairs={{0,1},{1,2},{2,3},{3,4},{4,5},{5,6},{6,7},{7,8},{8,9},{9,10},{10,1... | collective-permute-start | bytes 24584 | tf_op jit(solution)/shard_map/ppermute | solution.py:22
  75.8 11.1 %collective-permute-start.7 = (bf16[2,4,32,16]{3,2,1,0:T(8,128)(2,1)S(1)}, bf16[2,4,32,16]{3,2,1,0:T(8,128)(2,1)S(1)}, u32[]{:S(2)}, u32[]{:S(2)}) collective-permute-start(bf16[2,4,32,16]{3,2,1,0:T(8,128)(2,1)S(1)} %subtract_convert_fusion), channel_id=1, source_target_pairs={{0,2},{1,3},{2,4},{3,5},{4,6},{5,7},{6,8},{7,9},{8,10},{9,11},{10,... | collective-permute-start | bytes 24584 | tf_op jit(solution)/shard_map/ppermute | solution.py:22
  81.5 9.2 %collective-permute-start.6 = (bf16[2,4,32,16]{3,2,1,0:T(8,128)(2,1)S(1)}, bf16[2,4,32,16]{3,2,1,0:T(8,128)(2,1)S(1)}, u32[]{:S(2)}, u32[]{:S(2)}) collective-permute-start(bf16[2,4,32,16]{3,2,1,0:T(8,128)(2,1)S(1)} %subtract_convert_fusion), channel_id=1, source_target_pairs={{0,3},{1,4},{2,5},{3,6},{4,7},{5,8},{6,9},{7,10},{8,11},{9,12},{10... | collective-permute-start | bytes 24584 | tf_op jit(solution)/shard_map/ppermute | solution.py:22
  91.1 5.5 %slice-start.3 = ((s8[7962624]{0:T(1024)(128)(4,1)}), s8[4194304]{0:T(1024)(128)(4,1)S(1)}, s32[]{:S(2)}) async-start(s8[7962624]{0:T(1024)(128)(4,1)} %bitcast.230), calls=%async_computation.4 | async-start | bytes 8388608
  93.2 3.3 %slice-start.4 = ((s8[7962624]{0:T(1024)(128)(4,1)}), s8[3768320]{0:T(1024)(128)(4,1)S(1)}, s32[]{:S(2)}) async-start(s8[7962624]{0:T(1024)(128)(4,1)} %bitcast.230), calls=%async_computation.5 | async-start | bytes 7536640
  102.4 3.8 %copy-start.12 = (f32[384]{0:T(512)S(1)}, f32[384]{0:T(512)}, u32[]{:S(2)}) copy-start(f32[384]{0:T(512)} %param.30) | copy-start | bytes 4612
  115.5 3.4 %slice-start.2 = ((bf16[6,4,8,5,384]{4,2,3,1,0:T(8,128)(2,1)}), bf16[2,4,8,5,384]{4,2,3,1,0:T(8,128)(2,1)S(1)}, s32[]{:S(2)}) async-start(bf16[6,4,8,5,384]{4,2,3,1,0:T(8,128)(2,1)} %copy-done.3), calls=%async_computation.3 | async-start | bytes 491520 | tf_op jit(solution)/shard_map/convert_element_type | solution.py:188
  115.5 4.3 %copy-start.1 = (bf16[3,3,3,16,384]{4,3,2,1,0:T(8,128)(2,1)S(1)}, bf16[3,3,3,16,384]{4,3,2,1,0:T(8,128)(2,1)}, u32[]{:S(2)}) copy-start(bf16[3,3,3,16,384]{4,3,2,1,0:T(8,128)(2,1)} %param.27) | copy-start | bytes 995332
  (9 other events, 14.7 us)

commit v11 on v8

--- a/solution.py
+++ b/solution.py
@@ -133,13 +133,17 @@
 
     me = lax.axis_index("hg")
     query_parts = queries.reshape(rows_here, HEAD_GROUPS, group_width)
-    received = [lax.dynamic_index_in_dim(query_parts, me, 1, keepdims=False)]
+
+    def head_major(piece):
+        return split_heads(piece, group_heads).transpose(1, 0, 2)
+
+    received = [head_major(lax.dynamic_index_in_dim(query_parts, me, 1, keepdims=False))]
     for k in range(1, HEAD_GROUPS):
         target = lax.rem(me + HEAD_GROUPS - k, HEAD_GROUPS)
         pairs = [(i, (i + HEAD_GROUPS - k) % HEAD_GROUPS) for i in range(HEAD_GROUPS)]
-        piece = lax.dynamic_index_in_dim(query_parts, target, 1, keepdims=False)
+        piece = head_major(lax.dynamic_index_in_dim(query_parts, target, 1, keepdims=False))
         received.append(lax.ppermute(piece, "hg", pairs))
-    query_heads = split_heads(jnp.concatenate(received, axis=0), group_heads)
+    query_heads = jnp.concatenate(received, axis=1).transpose(1, 0, 2)
     key_value = gather_group(jnp.stack([keys, values], axis=1))
     key_heads = split_heads(key_value[:, 0], group_heads)
     value_heads = split_heads(key_value[:, 1], group_heads)

time: 115 us -> 113 us (0.983)
  starting transfers between devices: 29.5 us -> 32.1 us
  local copies, waits for them, and re-layouts: 21.7 us -> 19.4 us
  waiting for transfers between devices: 33.7 us -> 31.8 us
    all_to_all x1, waiting for transfers between devices: 0.01 us -> 25.7 us  [gather_group(): got = lax.all_to_all(sent, FRAMES, 0, 0, tiled=True)]
    ppermute x3, waiting for transfers between devices: 25.2 us -> 0.01 us  [body(): received.append(lax.ppermute(piece, 'hg', pairs))]
    concatenate x4 -> x0, local copies, waits for them, and re-layouts: 4.27 us -> none  [body(): query_heads = split_heads(jnp.concatenate(received, axis=0), group_heads)]
    transpose x0 -> x4, local copies, waits for them, and re-layouts: none -> 2.68 us  [head_major(): return split_heads(piece, group_heads).transpose(1, 0, 2)]
    ppermute x3, starting transfers between devices: 2.95 us -> 5.22 us  [body(): piece = lax.ppermute(pieces[k], 'hg', pairs)]
    unnamed x41 -> x36, local copies, waits for them, and re-layouts: 3.32 us -> 1.44 us
    ppermute x3, waiting for transfers between devices: 4.14 us -> 2.53 us  [body(): piece = lax.ppermute(pieces[k], 'hg', pairs)]
    dynamic_slice x1, local copies, waits for them, and re-layouts: 1.84 us -> 3.01 us  [body(): lax.dynamic_index_in_dim(query_parts, me, 1, keepdims=False)]
where the time goes in v11:
time: 113 us; the launch traced here: 112 us
  starting transfers between devices  32.1 us (28%)
  waiting for transfers between devices  31.8 us (28%)
  matrix products  23.3 us (21%)
  local copies, waits for them, and re-layouts  19.4 us (17%)
  other arithmetic  3.5 us (3%)
  between operations  1.9 us (2%)
    all_to_all x1, waiting for transfers between devices, gather_group(): got = lax.all_to_all(sent, FRAMES, 0, 0, tiled=True)  25.7 us
    conv_general_dilated x3, matrix products, spatial_conv(): lax.conv_general_dilated(extended[None], kernel, (1, 1, 1), ((0, 0), (1,...  18.2 us
    ppermute x3, starting transfers between devices, shifted(): return lax.ppermute(x, axis, pairs)  12.6 us
    all_to_all x1, starting transfers between devices, gather_group(): got = lax.all_to_all(sent, FRAMES, 0, 0, tiled=True)  8.69 us
    ppermute x3, starting transfers between devices, body(): received.append(lax.ppermute(piece, 'hg', pairs))  5.6 us
    ppermute x3, starting transfers between devices, body(): piece = lax.ppermute(pieces[k], 'hg', pairs)  5.22 us
    ppermute x3, waiting for transfers between devices, shifted(): return lax.ppermute(x, axis, pairs)  3.59 us
    dynamic_slice x1, local copies, waits for them, and re-layouts, body(): lax.dynamic_index_in_dim(query_parts, me, 1, keepdims=False)  3.01 us
  transfers between devices with their start and end apart: 10, of which 5 were waited for; matrix products, arithmetic and copies ran while one was open for 11% of the time, Pallas kernels for 0%

profile of v11, /device:TPU:96, one launch (start us, length us, event | category | flops | bytes accessed | tf_op | source)
XLA Modules:
  0.0 112.0 jit_solution(13762607410158863875)
XLA Ops:
  0.6 1.0 stack.10
  3.0 2.1 %broadcast_in_dim.9 = bf16[8,4,64,2,384]{4,2,3,1,0:T(8,128)(2,1)} broadcast(bf16[4,64,2,384]{3,1,2,0:T(8,128)(2,1)S(1)} %copy.53), dimensions={1,2,3,4} | broadcast | bytes 3538944 | tf_op jit(solution)/shard_map/broadcast_in_dim | solution.py:129
  5.1 8.7 %all-to-all-start = ((bf16[32,64,2,384]{3,1,2,0:T(8,128)(2,1)}), bf16[32,64,2,384]{3,1,2,0:T(8,128)(2,1)S(1)}, u32[]{:S(2)}, u32[]{:S(2)}) async-start(bf16[32,64,2,384]{3,1,2,0:T(8,128)(2,1)} %bitcast.133), calls=%async_computation | async-start | bytes 6291456 | tf_op jit(solution)/shard_map/all_to_all | solution.py:131
  13.9 1.7 %reshape.108 = bf16[64,4,384]{2,1,0:T(4,128)(2,1)} reshape(bf16[64,1536]{1,0:T(8,128)(2,1)} %param.17) | data formatting | bytes 393216 | tf_op jit(solution)/shard_map/reshape | solution.py:135
  15.5 3.0 %dynamic-slice_reduce_fusion.3 = (bf16[64,384]{1,0:T(8,128)(2,1)}, bf16[64,384]{1,0:T(8,128)(2,1)S(1)}, bf16[64,384]{1,0:T(8,128)(2,1)S(1)}, bf16[64,384]{1,0:T(8,128)(2,1)S(1)}) fusion(bf16[64,4,384]{2,1,0:T(4,128)(2,1)} %reshape.108, s32[]{:T(128)S(6)} %select_n.18, s32[]{:T(128)S(6)} %select_n.20, s32[]{:T(128)S(6)} %select_n.19, s32[]{:T(128)S(6)} %select_n.21), kind=kLoop, calls=%fused_computation.100 | loop fusion | bytes 393232 | tf_op jit(solution)/shard_map/jit(dynamic_index_in_dim)/dynamic_slice | solution.py:140
  19.2 1.5 %collective-permute-start.2 = (bf16[3,64,128]{2,1,0:T(8,128)(2,1)}, bf16[3,64,128]{2,1,0:T(8,128)(2,1)}, u32[]{:S(2)}, u32[]{:S(2)}) collective-permute-start(bf16[3,64,128]{2,1,0:T(8,128)(2,1)} %bitcast_bitcast_fusion), channel_id=1, source_target_pairs={{0,1},{1,2},{2,3},{3,0},{4,5},{5,6},{6,7},{7,4},{8,9},{9,10},{10,1... | collective-permute-start | bytes 147464 | tf_op jit(solution)/shard_map/ppermute | solution.py:145
  21.2 2.7 %collective-permute-start.1 = (bf16[3,64,128]{2,1,0:T(8,128)(2,1)}, bf16[3,64,128]{2,1,0:T(8,128)(2,1)}, u32[]{:S(2)}, u32[]{:S(2)}) collective-permute-start(bf16[3,64,128]{2,1,0:T(8,128)(2,1)} %bitcast_bitcast_fusion.1), channel_id=1, source_target_pairs={{0,2},{1,3},{2,0},{3,1},{4,6},{5,7},{6,4},{7,5},{8,10},{9,11},{10,... | collective-permute-start | bytes 147464 | tf_op jit(solution)/shard_map/ppermute | solution.py:145
  24.5 1.5 %collective-permute-start = (bf16[3,64,128]{2,1,0:T(8,128)(2,1)}, bf16[3,64,128]{2,1,0:T(8,128)(2,1)}, u32[]{:S(2)}, u32[]{:S(2)}) collective-permute-start(bf16[3,64,128]{2,1,0:T(8,128)(2,1)} %bitcast_bitcast_fusion.2), channel_id=1, source_target_pairs={{0,3},{1,0},{2,1},{3,2},{4,7},{5,4},{6,5},{7,6},{8,11},{9,8},{10,9... | collective-permute-start | bytes 147464 | tf_op jit(solution)/shard_map/ppermute | solution.py:145
  28.2 25.7 %all-to-all-done = bf16[32,64,2,384]{3,1,2,0:T(8,128)(2,1)S(1)} async-done(((bf16[32,64,2,384]{3,1,2,0:T(8,128)(2,1)}), bf16[32,64,2,384]{3,1,2,0:T(8,128)(2,1)S(1)}, u32[]{:S(2)}, u32[]{:S(2)}) %all-to-all-start) | async-done | bytes 3145760 | tf_op jit(solution)/shard_map/all_to_all | solution.py:131
  54.6 1.7 %copy.57 = bf16[2048,1,384]{0,2,1:T(8,128)(2,1)} copy(bf16[2048,1,384]{2,0,1:T(8,128)(2,1)S(1)} %get-tuple-element.11) | data formatting | bytes 3145728 | tf_op jit(solution)/shard_map/slice | solution.py:149
  57.1 1.9 %multiply_reduce_fusion = (f32[3,256]{1,0:T(4,128)S(1)}, f32[3,256,2048]{2,1,0:T(8,128)S(1)}) fusion(bf16[2048,3,128]{0,2,1:T(8,128)(2,1)S(1)} %bitcast.135, bf16[3,64,128]{2,1,0:T(8,128)(2,1)} %collective-permute-done.2, bf16[3,64,128]{2,1,0:T(8,128)(2,1)} %collective-permute-done.1, bf16[3,64,128]{2,1,0:T(8,128)(2,1)} %collective-permute-done, ...), kind=kOutput, calls=%fused_computation.1 | convolution fusion | flops 406584576 | bytes 8064000 | tf_op jit(solution)/shard_map/qhd,khd->hqk/dot_general | solution.py:39
  59.1 1.2 %fusion = f32[3,256]{1,0:T(4,128)S(1)} fusion(f32[3,256,2048]{2,1,0:T(8,128)S(1)} %get-tuple-element.19, f32[3,256]{1,0:T(4,128)S(1)} %get-tuple-element.17), kind=kLoop, calls=%fused_computation.2 | loop fusion | flops 4717824 | bytes 6297600 | tf_op jit(solution)/shard_map/reduce_sum | solution.py:45
  60.5 1.4 %fusion.36 = bf16[256,3,128]{0,2,1:T(8,128)(2,1)S(1)} fusion(bf16[2048,3,128]{0,2,1:T(8,128)(2,1)S(1)} %bitcast.148, f32[3,256,2048]{2,1,0:T(8,128)S(1)} %get-tuple-element.19, f32[3,256]{1,0:T(4,128)S(1)} %get-tuple-element.17, f32[256,3]{0,1:T(4,128)S(1)} %bitcast.156, f32[256,3]{0,1:T(4,128)S(1)} %get-tuple-element.16), kind=kOutput, calls=%fused_computation.42 | convolution fusion | flops 407666688 | bytes 8070144 | tf_op jit(solution)/shard_map/hqk,khd->qhd/dot_general | solution.py:46
  62.0 1.3 %collective-permute-start.5 = (bf16[64,384]{0,1:T(8,128)(2,1)S(1)}, bf16[64,384]{0,1:T(8,128)(2,1)S(1)}, u32[]{:S(2)}, u32[]{:S(2)}) collective-permute-start(bf16[64,384]{0,1:T(8,128)(2,1)S(1)} %bitcast.154), channel_id=1, source_target_pairs={{0,3},{1,0},{2,1},{3,2},{4,7},{5,4},{6,5},{7,6},{8,11},{9,8},{10,9... | collective-permute-start | bytes 147464 | tf_op jit(solution)/shard_map/ppermute | solution.py:167
  64.1 3.1 %collective-permute-start.4 = (bf16[64,384]{0,1:T(8,128)(2,1)S(1)}, bf16[64,384]{0,1:T(8,128)(2,1)S(1)}, u32[]{:S(2)}, u32[]{:S(2)}) collective-permute-start(bf16[64,384]{0,1:T(8,128)(2,1)S(1)} %bitcast.153), channel_id=1, source_target_pairs={{0,2},{1,3},{2,0},{3,1},{4,6},{5,7},{6,4},{7,5},{8,10},{9,11},{10,... | collective-permute-start | bytes 147464 | tf_op jit(solution)/shard_map/ppermute | solution.py:167
  67.6 1.5 %collective-permute-done.3 = bf16[64,384]{0,1:T(8,128)(2,1)S(1)} collective-permute-done((bf16[64,384]{0,1:T(8,128)(2,1)S(1)}, bf16[64,384]{0,1:T(8,128)(2,1)S(1)}, u32[]{:S(2)}, u32[]{:S(2)}) %collective-permute-start.3) | collective-permute-done | bytes 49184 | tf_op jit(solution)/shard_map/ppermute | solution.py:167
  69.8 1.0 collective-permute-done.4
  72.2 2.4 %collective-permute-start.8 = (bf16[2,4,32,16]{3,2,1,0:T(8,128)(2,1)S(1)}, bf16[2,4,32,16]{3,2,1,0:T(8,128)(2,1)S(1)}, u32[]{:S(2)}, u32[]{:S(2)}) collective-permute-start(bf16[2,4,32,16]{3,2,1,0:T(8,128)(2,1)S(1)} %subtract_convert_fusion), channel_id=1, source_target_pairs={{0,1},{1,2},{2,3},{3,4},{4,5},{5,6},{6,7},{7,8},{8,9},{9,10},{10,1... | collective-permute-start | bytes 24584 | tf_op jit(solution)/shard_map/ppermute | solution.py:22
  74.6 4.7 %collective-permute-start.7 = (bf16[2,4,32,16]{3,2,1,0:T(8,128)(2,1)S(1)}, bf16[2,4,32,16]{3,2,1,0:T(8,128)(2,1)S(1)}, u32[]{:S(2)}, u32[]{:S(2)}) collective-permute-start(bf16[2,4,32,16]{3,2,1,0:T(8,128)(2,1)S(1)} %subtract_convert_fusion), channel_id=1, source_target_pairs={{0,2},{1,3},{2,4},{3,5},{4,6},{5,7},{6,8},{7,9},{8,10},{9,11},{10,... | collective-permute-start | bytes 24584 | tf_op jit(solution)/shard_map/ppermute | solution.py:22
  79.2 5.6 %collective-permute-start.6 = (bf16[2,4,32,16]{3,2,1,0:T(8,128)(2,1)S(1)}, bf16[2,4,32,16]{3,2,1,0:T(8,128)(2,1)S(1)}, u32[]{:S(2)}, u32[]{:S(2)}) collective-permute-start(bf16[2,4,32,16]{3,2,1,0:T(8,128)(2,1)S(1)} %subtract_convert_fusion), channel_id=1, source_target_pairs={{0,3},{1,4},{2,5},{3,6},{4,7},{5,8},{6,9},{7,10},{8,11},{9,12},{10... | collective-permute-start | bytes 24584 | tf_op jit(solution)/shard_map/ppermute | solution.py:22
  85.2 3.2 %collective-permute-done.6 = bf16[2,4,32,16]{3,2,1,0:T(8,128)(2,1)S(1)} collective-permute-done((bf16[2,4,32,16]{3,2,1,0:T(8,128)(2,1)S(1)}, bf16[2,4,32,16]{3,2,1,0:T(8,128)(2,1)S(1)}, u32[]{:S(2)}, u32[]{:S(2)}) %collective-permute-start.6) | collective-permute-done | bytes 8224 | tf_op jit(solution)/shard_map/ppermute | solution.py:22
  88.8 1.8 %convert_multiply_fusion = (f32[6,4,8,5,384]{4,2,3,1,0:T(8,128)S(1)}, bf16[6,4,8,5,384]{4,2,3,1,0:T(8,128)(2,1)S(1)}) fusion(bf16[3,3,3,16,384]{4,3,2,1,0:T(8,128)(2,1)S(1)} %copy-done, bf16[8,4,1,7,2,16]{5,3,4,1,0,2:T(8,128)(2,1)S(1)} %slice.64, bf16[8,4,1,8,5,16]{5,3,4,1,0,2:T(8,128)(2,1)S(1)} %copy.61, pred[8,5]{0,1:T(8,128)(4,1)S(1)} %copy-done.12), kind=kOutput, calls=%fused_computation.78 | convolution fusion | flops 267067392 | bytes 2598952 | tf_op jit(solution)/shard_map/conv_general_dilated | solution.py:74
  92.9 12.7 %fusion.101 = (f32[4,4,8,5,384]{4,2,3,1,0:T(8,128)S(1)}, f32[4,4,8,5,384]{4,2,3,1,0:T(8,128)S(1)}) fusion(bf16[3,3,3,384,384]{4,3,2,1,0:T(8,128)(2,1)} %param.29, bf16[6,4,1,7,2,384]{5,3,4,1,0,2:T(8,128)(2,1)S(1)} %slice.68, bf16[6,4,1,8,5,384]{5,3,4,1,0,2:T(8,128)(2,1)S(1)} %copy.65, pred[8,5]{0,1:T(8,128)(4,1)S(1)} %copy-done.12), kind=kOutput, calls=%fused_computation.128 | convolution fusion | flops 4250320896 | bytes 10924072 | tf_op jit(solution)/shard_map/conv_general_dilated | solution.py:74
  107.5 3.7 %fusion.16 = bf16[2,4,8,5,384]{4,2,3,1,0:T(8,128)(2,1)S(1)} fusion(bf16[3,3,3,384,384]{4,3,2,1,0:T(8,128)(2,1)S(1)} %bitcast.158, bf16[4,4,1,7,2,384]{5,3,4,1,0,2:T(8,128)(2,1)S(1)} %slice.71, bf16[4,4,1,8,5,384]{5,3,4,1,0,2:T(8,128)(2,1)S(1)} %copy.69, bf16[6,4,8,5,384]{4,2,3,1,0:T(8,128)(2,1)S(1)} %get-tuple-element.23, pred[8,5]{0,1:T(8,128)(4,1)S(1)} %copy-done.12), kind=kOutput, calls=%fused_computation.22 | convolution fusion | flops 2125922304 | bytes 9117736 | tf_op jit(solution)/shard_map/conv_general_dilated | solution.py:74
  (92 shorter events, 15.2 us)
Async XLA Ops:
  0.6 88.2 %copy-start = (bf16[3,3,3,16,384]{4,3,2,1,0:T(8,128)(2,1)S(1)}, bf16[3,3,3,16,384]{4,3,2,1,0:T(8,128)(2,1)}, u32[]{:S(2)}) copy-start(bf16[3,3,3,16,384]{4,3,2,1,0:T(8,128)(2,1)} %param.27) | copy-start | bytes 995332
  5.1 20.9 %copy-start.5 = (f32[2,4,512]{2,1,0:T(4,128)S(1)}, f32[2,4,512]{2,1,0:T(4,128)}, u32[]{:S(2)}) copy-start(f32[2,4,512]{2,1,0:T(4,128)} %param.26) | copy-start | bytes 49156
  5.1 22.3 %copy-start.7 = (f32[1536]{0:T(1024)S(1)}, f32[1536]{0:T(1024)}, u32[]{:S(2)}) copy-start(f32[1536]{0:T(1024)} %param.22) | copy-start | bytes 18436
  5.1 48.8 %all-to-all-start = ((bf16[32,64,2,384]{3,1,2,0:T(8,128)(2,1)}), bf16[32,64,2,384]{3,1,2,0:T(8,128)(2,1)S(1)}, u32[]{:S(2)}, u32[]{:S(2)}) async-start(bf16[32,64,2,384]{3,1,2,0:T(8,128)(2,1)} %bitcast.133), calls=%async_computation | async-start | bytes 6291456 | tf_op jit(solution)/shard_map/all_to_all | solution.py:131
  19.2 37.9 %collective-permute-start.2 = (bf16[3,64,128]{2,1,0:T(8,128)(2,1)}, bf16[3,64,128]{2,1,0:T(8,128)(2,1)}, u32[]{:S(2)}, u32[]{:S(2)}) collective-permute-start(bf16[3,64,128]{2,1,0:T(8,128)(2,1)} %bitcast_bitcast_fusion), channel_id=1, source_target_pairs={{0,1},{1,2},{2,3},{3,0},{4,5},{5,6},{6,7},{7,4},{8,9},{9,10},{10,1... | collective-permute-start | bytes 147464 | tf_op jit(solution)/shard_map/ppermute | solution.py:145
  21.2 35.9 %collective-permute-start.1 = (bf16[3,64,128]{2,1,0:T(8,128)(2,1)}, bf16[3,64,128]{2,1,0:T(8,128)(2,1)}, u32[]{:S(2)}, u32[]{:S(2)}) collective-permute-start(bf16[3,64,128]{2,1,0:T(8,128)(2,1)} %bitcast_bitcast_fusion.1), channel_id=1, source_target_pairs={{0,2},{1,3},{2,0},{3,1},{4,6},{5,7},{6,4},{7,5},{8,10},{9,11},{10,... | collective-permute-start | bytes 147464 | tf_op jit(solution)/shard_map/ppermute | solution.py:145
  24.5 32.6 %collective-permute-start = (bf16[3,64,128]{2,1,0:T(8,128)(2,1)}, bf16[3,64,128]{2,1,0:T(8,128)(2,1)}, u32[]{:S(2)}, u32[]{:S(2)}) collective-permute-start(bf16[3,64,128]{2,1,0:T(8,128)(2,1)} %bitcast_bitcast_fusion.2), channel_id=1, source_target_pairs={{0,3},{1,0},{2,1},{3,2},{4,7},{5,4},{6,5},{7,6},{8,11},{9,8},{10,9... | collective-permute-start | bytes 147464 | tf_op jit(solution)/shard_map/ppermute | solution.py:145
  59.1 8.2 %slice-start = ((s8[4718592]{0:T(1024)(128)(4,1)}), s8[4194304]{0:T(1024)(128)(4,1)S(1)}, s32[]{:S(2)}) async-start(s8[4718592]{0:T(1024)(128)(4,1)} %bitcast.138), calls=%async_computation.1 | async-start | bytes 8388608
  60.5 6.8 %slice-start.1 = ((s8[4718592]{0:T(1024)(128)(4,1)}), s8[524288]{0:T(1024)(128)(4,1)S(1)}, s32[]{:S(2)}) async-start(s8[4718592]{0:T(1024)(128)(4,1)} %bitcast.138), calls=%async_computation.2 | async-start | bytes 1048576
  62.0 7.5 %collective-permute-start.5 = (bf16[64,384]{0,1:T(8,128)(2,1)S(1)}, bf16[64,384]{0,1:T(8,128)(2,1)S(1)}, u32[]{:S(2)}, u32[]{:S(2)}) collective-permute-start(bf16[64,384]{0,1:T(8,128)(2,1)S(1)} %bitcast.154), channel_id=1, source_target_pairs={{0,3},{1,0},{2,1},{3,2},{4,7},{5,4},{6,5},{7,6},{8,11},{9,8},{10,9... | collective-permute-start | bytes 147464 | tf_op jit(solution)/shard_map/ppermute | solution.py:167
  63.3 5.8 %collective-permute-start.3 = (bf16[64,384]{0,1:T(8,128)(2,1)S(1)}, bf16[64,384]{0,1:T(8,128)(2,1)S(1)}, u32[]{:S(2)}, u32[]{:S(2)}) collective-permute-start(bf16[64,384]{0,1:T(8,128)(2,1)S(1)} %bitcast.155), channel_id=1, source_target_pairs={{0,1},{1,2},{2,3},{3,0},{4,5},{5,6},{6,7},{7,4},{8,9},{9,10},{10,1... | collective-permute-start | bytes 147464 | tf_op jit(solution)/shard_map/ppermute | solution.py:167
  64.1 6.8 %collective-permute-start.4 = (bf16[64,384]{0,1:T(8,128)(2,1)S(1)}, bf16[64,384]{0,1:T(8,128)(2,1)S(1)}, u32[]{:S(2)}, u32[]{:S(2)}) collective-permute-start(bf16[64,384]{0,1:T(8,128)(2,1)S(1)} %bitcast.153), channel_id=1, source_target_pairs={{0,2},{1,3},{2,0},{3,1},{4,6},{5,7},{6,4},{7,5},{8,10},{9,11},{10,... | collective-permute-start | bytes 147464 | tf_op jit(solution)/shard_map/ppermute | solution.py:167
  67.6 3.3 %copy-start.4 = (bf16[64,1536]{1,0:T(8,128)(2,1)S(1)}, bf16[64,1536]{1,0:T(8,128)(2,1)}, u32[]{:S(2)}) copy-start(bf16[64,1536]{1,0:T(8,128)(2,1)} %param.16) | copy-start | bytes 589828
  67.6 3.3 %copy-start.6 = (f32[1536]{0:T(1024)S(1)}, f32[1536]{0:T(1024)}, u32[]{:S(2)}) copy-start(f32[1536]{0:T(1024)} %param.20) | copy-start | bytes 18436
  69.8 1.8 %copy-start.10 = (bf16[1536,64]{0,1:T(8,128)(2,1)S(1)}, bf16[1536,64]{0,1:T(8,128)(2,1)}, u32[]{:S(2)}) copy-start(bf16[1536,64]{0,1:T(8,128)(2,1)} %param.24) | copy-start | bytes 589828
  69.8 1.8 %copy-start.11 = (f32[1536]{0:T(1024)S(1)}, f32[1536]{0:T(1024)}, u32[]{:S(2)}) copy-start(f32[1536]{0:T(1024)} %param.23) | copy-start | bytes 18436
  69.8 2.3 %copy-start.3 = (f32[2,4,32,16]{3,2,1,0:T(8,128)S(1)}, f32[2,4,32,16]{3,2,1,0:T(8,128)}, u32[]{:S(2)}) copy-start(f32[2,4,32,16]{3,2,1,0:T(8,128)} %reshape.116) | copy-start | bytes 49156
  71.3 17.4 %copy-start.2 = (bf16[64,1536]{1,0:T(8,128)(2,1)}, bf16[64,1536]{1,0:T(8,128)(2,1)S(1)}, u32[]{:S(2)}) copy-start(bf16[64,1536]{1,0:T(8,128)(2,1)S(1)} %get-tuple-element.21) | copy-start | bytes 589828
  72.1 16.8 %copy-start.12 = (pred[8,5]{0,1:T(8,128)(4,1)S(1)}, pred[8,5]{0,1:T(8,128)(4,1)}, u32[]{:S(2)}) copy-start(pred[8,5]{0,1:T(8,128)(4,1)} %constant.91) | copy-start | bytes 124
  72.2 12.6 %collective-permute-start.8 = (bf16[2,4,32,16]{3,2,1,0:T(8,128)(2,1)S(1)}, bf16[2,4,32,16]{3,2,1,0:T(8,128)(2,1)S(1)}, u32[]{:S(2)}, u32[]{:S(2)}) collective-permute-start(bf16[2,4,32,16]{3,2,1,0:T(8,128)(2,1)S(1)} %subtract_convert_fusion), channel_id=1, source_target_pairs={{0,1},{1,2},{2,3},{3,4},{4,5},{5,6},{6,7},{7,8},{8,9},{9,10},{10,1... | collective-permute-start | bytes 24584 | tf_op jit(solution)/shard_map/ppermute | solution.py:22
  74.6 10.7 %collective-permute-start.7 = (bf16[2,4,32,16]{3,2,1,0:T(8,128)(2,1)S(1)}, bf16[2,4,32,16]{3,2,1,0:T(8,128)(2,1)S(1)}, u32[]{:S(2)}, u32[]{:S(2)}) collective-permute-start(bf16[2,4,32,16]{3,2,1,0:T(8,128)(2,1)S(1)} %subtract_convert_fusion), channel_id=1, source_target_pairs={{0,2},{1,3},{2,4},{3,5},{4,6},{5,7},{6,8},{7,9},{8,10},{9,11},{10,... | collective-permute-start | bytes 24584 | tf_op jit(solution)/shard_map/ppermute | solution.py:22
  79.2 9.2 %collective-permute-start.6 = (bf16[2,4,32,16]{3,2,1,0:T(8,128)(2,1)S(1)}, bf16[2,4,32,16]{3,2,1,0:T(8,128)(2,1)S(1)}, u32[]{:S(2)}, u32[]{:S(2)}) collective-permute-start(bf16[2,4,32,16]{3,2,1,0:T(8,128)(2,1)S(1)} %subtract_convert_fusion), channel_id=1, source_target_pairs={{0,3},{1,4},{2,5},{3,6},{4,7},{5,8},{6,9},{7,10},{8,11},{9,12},{10... | collective-permute-start | bytes 24584 | tf_op jit(solution)/shard_map/ppermute | solution.py:22
  92.7 14.7 %slice-start.2 = ((s8[7962624]{0:T(1024)(128)(4,1)}), s8[4194304]{0:T(1024)(128)(4,1)S(1)}, s32[]{:S(2)}) async-start(s8[7962624]{0:T(1024)(128)(4,1)} %bitcast.157), calls=%async_computation.3 | async-start | bytes 8388608
  92.9 14.5 %slice-start.3 = ((s8[7962624]{0:T(1024)(128)(4,1)}), s8[3768320]{0:T(1024)(128)(4,1)S(1)}, s32[]{:S(2)}) async-start(s8[7962624]{0:T(1024)(128)(4,1)} %bitcast.157), calls=%async_computation.4 | async-start | bytes 7536640
  (3 other events, 2.8 us)

commit v12 on v11

--- a/solution.py
+++ b/solution.py
@@ -122,14 +122,17 @@
         parts = matrix.reshape(rows_here, HEAD_GROUPS, group_width)
         return lax.all_to_all(parts, "hg", 1, 0, tiled=True).reshape(-1, group_width)
 
-    def gather_group(matrix):
+    def gather_heads(*matrices):
         blocks = lax.psum(1, "blk")
-        parts = matrix.reshape(rows_here, -1, HEAD_GROUPS, group_width)
-        parts = jnp.moveaxis(parts, 2, 0)
+        parts = jnp.stack(
+            [m.reshape(rows_here, HEAD_GROUPS, group_heads, HEAD_DIM) for m in matrices], axis=0
+        )
+        parts = parts.transpose(2, 0, 3, 1, 4)
         sent = jnp.broadcast_to(parts[None], (blocks,) + parts.shape)
         sent = sent.reshape((blocks * HEAD_GROUPS,) + parts.shape[1:])
         got = lax.all_to_all(sent, FRAMES, 0, 0, tiled=True)
-        return got.reshape((-1,) + got.shape[2:])
+        got = got.transpose(1, 2, 0, 3, 4)
+        return [got[i].reshape(group_heads, -1, HEAD_DIM).transpose(1, 0, 2) for i in range(len(matrices))]
 
     me = lax.axis_index("hg")
     query_parts = queries.reshape(rows_here, HEAD_GROUPS, group_width)
@@ -144,9 +147,7 @@
         piece = head_major(lax.dynamic_index_in_dim(query_parts, target, 1, keepdims=False))
         received.append(lax.ppermute(piece, "hg", pairs))
     query_heads = jnp.concatenate(received, axis=1).transpose(1, 0, 2)
-    key_value = gather_group(jnp.stack([keys, values], axis=1))
-    key_heads = split_heads(key_value[:, 0], group_heads)
-    value_heads = split_heads(key_value[:, 1], group_heads)
+    key_heads, value_heads = gather_heads(keys, values)
     group_rows = query_heads.shape[0]
     row_peak, row_total, summed = absorb_block(
         empty_state(group_heads, group_rows), query_heads, key_heads, value_heads

time: 113 us -> 116 us (1.027)
  waiting for transfers between devices: 31.8 us -> 38.2 us
  starting transfers between devices: 32.1 us -> 28.5 us
  other arithmetic: 3.5 us -> 6.53 us
  matrix products: 23.3 us -> 20.5 us
    conv_general_dilated x3, matrix products: 18.2 us -> 12.8 us  [spatial_conv(): lax.conv_general_dilated(extended[None], kernel, (1, 1, 1), ((0, 0), (1,...]
    ppermute x3, waiting for transfers between devices: 3.59 us -> 8.26 us  [shifted(): return lax.ppermute(x, axis, pairs)]
    reduce_sum x1, other arithmetic: 1.16 us -> 4.09 us  [absorb_block(): row_total = jnp.sum(weights, axis=-1)]
    dot_general x1, matrix products: 1.92 us -> 4.48 us  [absorb_block(): jnp.einsum('qhd,khd->hqk', query_heads, key_heads, preferred_element_type...]
    ppermute x3, starting transfers between devices: 12.6 us -> 10.2 us  [shifted(): return lax.ppermute(x, axis, pairs)]
    slice x3 -> x1, local copies, waits for them, and re-layouts: 2.76 us -> 0.69 us  [gather_heads(): got[i].reshape(group_heads, -1, HEAD_DIM).transpose(1, 0, 2)]
    ppermute x3, starting transfers between devices: 5.6 us -> 4.39 us  [body(): received.append(lax.ppermute(piece, 'hg', pairs))]
    another operation x2 -> x3, local copies, waits for them, and re-layouts: 2 us -> 2.87 us  [the longest x2 2.17 us: gather_heads(): jnp.stack([m.reshape(rows_here, HEAD_GROUPS, group_heads, HEAD_DIM) for m...]
  transfers between devices with their start and end apart: 10 -> 10, of which waited for: 5 -> 5; matrix products, arithmetic and copies ran while one was open for 11% -> 9% of each run, Pallas kernels for 0% -> 0%
where the time goes in v12:
time: 116 us; the launch traced here: 115 us
  waiting for transfers between devices  38.2 us (33%)
  starting transfers between devices  28.5 us (25%)
  matrix products  20.5 us (18%)
  local copies, waits for them, and re-layouts  19.5 us (17%)
  other arithmetic  6.53 us (6%)
  between operations  1.93 us (2%)
    all_to_all x1, waiting for transfers between devices, gather_heads(): got = lax.all_to_all(sent, FRAMES, 0, 0, tiled=True)  26.8 us
    conv_general_dilated x3, matrix products, spatial_conv(): lax.conv_general_dilated(extended[None], kernel, (1, 1, 1), ((0, 0), (1,...  12.8 us
    ppermute x3, starting transfers between devices, shifted(): return lax.ppermute(x, axis, pairs)  10.2 us
    all_to_all x1, starting transfers between devices, gather_heads(): got = lax.all_to_all(sent, FRAMES, 0, 0, tiled=True)  8.69 us
    ppermute x3, waiting for transfers between devices, shifted(): return lax.ppermute(x, axis, pairs)  8.26 us
    ppermute x3, starting transfers between devices, body(): piece = lax.ppermute(pieces[k], 'hg', pairs)  5.18 us
    dot_general x1, matrix products, absorb_block(): jnp.einsum('qhd,khd->hqk', query_heads, key_heads, preferred_element_type...  4.48 us
    ppermute x3, starting transfers between devices, body(): received.append(lax.ppermute(piece, 'hg', pairs))  4.39 us
  transfers between devices with their start and end apart: 10, of which 5 were waited for; matrix products, arithmetic and copies ran while one was open for 9% of the time, Pallas kernels for 0%

profile of v12, /device:TPU:96, one launch (start us, length us, event | category | flops | bytes accessed | tf_op | source)
XLA Modules:
  0.0 115.1 jit_solution(13681540810015942907)
XLA Ops:
  0.6 1.1 stack_reshape.6
  1.8 1.1 stack_reshape.7
  3.3 2.4 %broadcast_in_dim.9 = bf16[8,4,2,3,64,128]{5,4,3,2,1,0:T(8,128)(2,1)} broadcast(bf16[4,2,3,64,128]{4,3,2,1,0:T(8,128)(2,1)S(1)} %copy.52), dimensions={1,2,3,4,5} | broadcast | bytes 3538944 | tf_op jit(solution)/shard_map/broadcast_in_dim | solution.py:131
  5.8 8.7 %all-to-all-start = ((bf16[32,2,3,64,128]{4,3,2,1,0:T(8,128)(2,1)}), bf16[32,2,3,64,128]{4,3,2,1,0:T(8,128)(2,1)S(1)}, u32[]{:S(2)}, u32[]{:S(2)}) async-start(bf16[32,2,3,64,128]{4,3,2,1,0:T(8,128)(2,1)} %bitcast.147), calls=%async_computation | async-start | bytes 6291456 | tf_op jit(solution)/shard_map/all_to_all | solution.py:133
  14.5 1.7 %reshape.100 = bf16[64,4,384]{2,1,0:T(4,128)(2,1)} reshape(bf16[64,1536]{1,0:T(8,128)(2,1)} %param.17) | data formatting | bytes 393216 | tf_op jit(solution)/shard_map/reshape | solution.py:138
  16.1 3.2 %dynamic-slice_reduce_fusion.3 = (bf16[64,384]{1,0:T(8,128)(2,1)}, bf16[64,384]{1,0:T(8,128)(2,1)S(1)}, bf16[64,384]{1,0:T(8,128)(2,1)S(1)}, bf16[64,384]{1,0:T(8,128)(2,1)S(1)}) fusion(bf16[64,4,384]{2,1,0:T(4,128)(2,1)} %reshape.100, s32[]{:T(128)S(6)} %select_n.18, s32[]{:T(128)S(6)} %select_n.20, s32[]{:T(128)S(6)} %select_n.19, s32[]{:T(128)S(6)} %select_n.21), kind=kLoop, calls=%fused_computation.102 | loop fusion | bytes 393232 | tf_op jit(solution)/shard_map/jit(dynamic_index_in_dim)/dynamic_slice | solution.py:143
  19.9 2.7 %collective-permute-start = (bf16[3,64,128]{2,1,0:T(8,128)(2,1)}, bf16[3,64,128]{2,1,0:T(8,128)(2,1)}, u32[]{:S(2)}, u32[]{:S(2)}) collective-permute-start(bf16[3,64,128]{2,1,0:T(8,128)(2,1)} %bitcast_bitcast_fusion.2), channel_id=1, source_target_pairs={{0,3},{1,0},{2,1},{3,2},{4,7},{5,4},{6,5},{7,6},{8,11},{9,8},{10,9... | collective-permute-start | bytes 147464 | tf_op jit(solution)/shard_map/ppermute | solution.py:148
  24.7 0.9 collective-permute-start.2
  27.8 26.8 %all-to-all-done = bf16[32,2,3,64,128]{4,3,2,1,0:T(8,128)(2,1)S(1)} async-done(((bf16[32,2,3,64,128]{4,3,2,1,0:T(8,128)(2,1)}), bf16[32,2,3,64,128]{4,3,2,1,0:T(8,128)(2,1)S(1)}, u32[]{:S(2)}, u32[]{:S(2)}) %all-to-all-start) | async-done | bytes 3145760 | tf_op jit(solution)/shard_map/all_to_all | solution.py:133
  54.6 0.9 copy.83
  56.2 4.5 %multiply_reduce_fusion = (f32[3,256]{1,0:T(4,128)S(1)}, f32[3,256,2048]{2,1,0:T(8,128)}) fusion(bf16[2048,3,128]{2,0,1:T(8,128)(2,1)S(1)} %bitcast.149, bf16[3,64,128]{2,1,0:T(8,128)(2,1)} %collective-permute-done.2, bf16[3,64,128]{2,1,0:T(8,128)(2,1)} %collective-permute-done.1, bf16[3,64,128]{2,1,0:T(8,128)(2,1)} %collective-permute-done, ...), kind=kOutput, calls=%fused_computation.1 | convolution fusion | flops 406584576 | bytes 8064000 | tf_op jit(solution)/shard_map/qhd,khd->hqk/dot_general | solution.py:39
  61.5 4.1 %fusion = f32[3,256]{1,0:T(4,128)S(1)} fusion(f32[3,256,2048]{2,1,0:T(8,128)} %get-tuple-element.19, f32[3,256]{1,0:T(4,128)S(1)} %get-tuple-element.17), kind=kLoop, calls=%fused_computation.2 | loop fusion | flops 4717824 | bytes 6297600 | tf_op jit(solution)/shard_map/reduce_sum | solution.py:45
  66.1 1.4 %fusion.43 = bf16[256,3,128]{0,2,1:T(8,128)(2,1)S(1)} fusion(f32[3,256,2048]{2,1,0:T(8,128)S(1)} %copy-done.1, f32[3,256]{1,0:T(4,128)S(1)} %get-tuple-element.17, bf16[3,2048,128]{1,2,0:T(8,128)(2,1)S(1)} %copy.54, f32[256,3]{0,1:T(4,128)S(1)} %bitcast.170, f32[256,3]{0,1:T(4,128)S(1)} %get-tuple-element.16), kind=kOutput, calls=%fused_computation.44 | convolution fusion | flops 407666688 | bytes 8070144 | tf_op jit(solution)/shard_map/hqk,khd->qhd/dot_general | solution.py:46
  67.7 3.2 %collective-permute-start.5 = (bf16[64,384]{0,1:T(8,128)(2,1)S(1)}, bf16[64,384]{0,1:T(8,128)(2,1)S(1)}, u32[]{:S(2)}, u32[]{:S(2)}) collective-permute-start(bf16[64,384]{0,1:T(8,128)(2,1)S(1)} %bitcast.168), channel_id=1, source_target_pairs={{0,3},{1,0},{2,1},{3,2},{4,7},{5,4},{6,5},{7,6},{8,11},{9,8},{10,9... | collective-permute-start | bytes 147464 | tf_op jit(solution)/shard_map/ppermute | solution.py:168
  70.9 1.9 %collective-permute-start.4 = (bf16[64,384]{0,1:T(8,128)(2,1)S(1)}, bf16[64,384]{0,1:T(8,128)(2,1)S(1)}, u32[]{:S(2)}, u32[]{:S(2)}) collective-permute-start(bf16[64,384]{0,1:T(8,128)(2,1)S(1)} %bitcast.167), channel_id=1, source_target_pairs={{0,2},{1,3},{2,0},{3,1},{4,6},{5,7},{6,4},{7,5},{8,10},{9,11},{10,... | collective-permute-start | bytes 147464 | tf_op jit(solution)/shard_map/ppermute | solution.py:168
  74.2 2.8 %collective-permute-done.4 = bf16[64,384]{0,1:T(8,128)(2,1)S(1)} collective-permute-done((bf16[64,384]{0,1:T(8,128)(2,1)S(1)}, bf16[64,384]{0,1:T(8,128)(2,1)S(1)}, u32[]{:S(2)}, u32[]{:S(2)}) %collective-permute-start.4) | collective-permute-done | bytes 49184 | tf_op jit(solution)/shard_map/ppermute | solution.py:168
  78.3 3.5 %collective-permute-start.6 = (bf16[2,4,32,16]{3,2,1,0:T(8,128)(2,1)S(1)}, bf16[2,4,32,16]{3,2,1,0:T(8,128)(2,1)S(1)}, u32[]{:S(2)}, u32[]{:S(2)}) collective-permute-start(bf16[2,4,32,16]{3,2,1,0:T(8,128)(2,1)S(1)} %subtract_convert_fusion), channel_id=1, source_target_pairs={{0,3},{1,4},{2,5},{3,6},{4,7},{5,8},{6,9},{7,10},{8,11},{9,12},{10... | collective-permute-start | bytes 24584 | tf_op jit(solution)/shard_map/ppermute | solution.py:22
  81.8 4.6 %collective-permute-start.7 = (bf16[2,4,32,16]{3,2,1,0:T(8,128)(2,1)S(1)}, bf16[2,4,32,16]{3,2,1,0:T(8,128)(2,1)S(1)}, u32[]{:S(2)}, u32[]{:S(2)}) collective-permute-start(bf16[2,4,32,16]{3,2,1,0:T(8,128)(2,1)S(1)} %subtract_convert_fusion), channel_id=1, source_target_pairs={{0,2},{1,3},{2,4},{3,5},{4,6},{5,7},{6,8},{7,9},{8,10},{9,11},{10,... | collective-permute-start | bytes 24584 | tf_op jit(solution)/shard_map/ppermute | solution.py:22
  86.5 2.1 %collective-permute-start.8 = (bf16[2,4,32,16]{3,2,1,0:T(8,128)(2,1)S(1)}, bf16[2,4,32,16]{3,2,1,0:T(8,128)(2,1)S(1)}, u32[]{:S(2)}, u32[]{:S(2)}) collective-permute-start(bf16[2,4,32,16]{3,2,1,0:T(8,128)(2,1)S(1)} %subtract_convert_fusion), channel_id=1, source_target_pairs={{0,1},{1,2},{2,3},{3,4},{4,5},{5,6},{6,7},{7,8},{8,9},{9,10},{10,1... | collective-permute-start | bytes 24584 | tf_op jit(solution)/shard_map/ppermute | solution.py:22
  88.6 4.4 %collective-permute-done.7 = bf16[2,4,32,16]{3,2,1,0:T(8,128)(2,1)S(1)} collective-permute-done((bf16[2,4,32,16]{3,2,1,0:T(8,128)(2,1)S(1)}, bf16[2,4,32,16]{3,2,1,0:T(8,128)(2,1)S(1)}, u32[]{:S(2)}, u32[]{:S(2)}) %collective-permute-start.7) | collective-permute-done | bytes 8224 | tf_op jit(solution)/shard_map/ppermute | solution.py:22
  92.9 3.9 %collective-permute-done.8 = bf16[2,4,32,16]{3,2,1,0:T(8,128)(2,1)S(1)} collective-permute-done((bf16[2,4,32,16]{3,2,1,0:T(8,128)(2,1)S(1)}, bf16[2,4,32,16]{3,2,1,0:T(8,128)(2,1)S(1)}, u32[]{:S(2)}, u32[]{:S(2)}) %collective-permute-start.8) | collective-permute-done | bytes 8224 | tf_op jit(solution)/shard_map/ppermute | solution.py:22
  97.3 1.8 %convert_multiply_fusion = (f32[6,4,8,5,384]{4,2,3,1,0:T(8,128)S(1)}, bf16[6,4,8,5,384]{4,2,3,1,0:T(8,128)(2,1)S(1)}) fusion(bf16[3,3,3,16,384]{4,3,2,1,0:T(8,128)(2,1)S(1)} %copy-done, bf16[8,4,1,7,2,16]{5,3,4,1,0,2:T(8,128)(2,1)S(1)} %slice.64, bf16[8,4,1,8,5,16]{5,3,4,1,0,2:T(8,128)(2,1)S(1)} %copy.58, pred[8,5]{0,1:T(8,128)(4,1)S(1)} %copy-done.12), kind=kOutput, calls=%fused_computation.80 | convolution fusion | flops 267067392 | bytes 2598952 | tf_op jit(solution)/shard_map/conv_general_dilated | solution.py:74
  101.4 7.1 %fusion.110 = (f32[4,4,8,5,384]{4,2,3,1,0:T(8,128)S(1)}, f32[4,4,8,5,384]{4,2,3,1,0:T(8,128)S(1)}) fusion(bf16[3,3,3,384,384]{4,3,2,1,0:T(8,128)(2,1)S(1)} %bitcast.172, bf16[6,4,1,7,2,384]{5,3,4,1,0,2:T(8,128)(2,1)S(1)} %slice.68, bf16[6,4,1,8,5,384]{5,3,4,1,0,2:T(8,128)(2,1)S(1)} %copy.62, pred[8,5]{0,1:T(8,128)(4,1)S(1)} %copy-done.12), kind=kOutput, calls=%fused_computation.130 | convolution fusion | flops 4250320896 | bytes 10924072 | tf_op jit(solution)/shard_map/conv_general_dilated | solution.py:74
  110.3 3.9 %fusion.19 = bf16[2,4,8,5,384]{4,2,3,1,0:T(8,128)(2,1)S(1)} fusion(bf16[3,3,3,384,384]{4,3,2,1,0:T(8,128)(2,1)S(1)} %bitcast.174, bf16[4,4,1,7,2,384]{5,3,4,1,0,2:T(8,128)(2,1)S(1)} %slice.71, bf16[4,4,1,8,5,384]{5,3,4,1,0,2:T(8,128)(2,1)S(1)} %copy.66, bf16[6,4,8,5,384]{4,2,3,1,0:T(8,128)(2,1)S(1)} %get-tuple-element.23, pred[8,5]{0,1:T(8,128)(4,1)S(1)} %copy-done.12), kind=kOutput, calls=%fused_computation.24 | convolution fusion | flops 2125922304 | bytes 9117736 | tf_op jit(solution)/shard_map/conv_general_dilated | solution.py:74
  (96 shorter events, 14.7 us)
Async XLA Ops:
  0.6 96.6 %copy-start = (bf16[3,3,3,16,384]{4,3,2,1,0:T(8,128)(2,1)S(1)}, bf16[3,3,3,16,384]{4,3,2,1,0:T(8,128)(2,1)}, u32[]{:S(2)}) copy-start(bf16[3,3,3,16,384]{4,3,2,1,0:T(8,128)(2,1)} %param.27) | copy-start | bytes 995332
  5.7 20.5 %copy-start.5 = (f32[2,4,512]{2,1,0:T(4,128)S(1)}, f32[2,4,512]{2,1,0:T(4,128)}, u32[]{:S(2)}) copy-start(f32[2,4,512]{2,1,0:T(4,128)} %param.26) | copy-start | bytes 49156
  5.8 21.2 %copy-start.7 = (f32[1536]{0:T(1024)S(1)}, f32[1536]{0:T(1024)}, u32[]{:S(2)}) copy-start(f32[1536]{0:T(1024)} %param.22) | copy-start | bytes 18436
  5.8 48.8 %all-to-all-start = ((bf16[32,2,3,64,128]{4,3,2,1,0:T(8,128)(2,1)}), bf16[32,2,3,64,128]{4,3,2,1,0:T(8,128)(2,1)S(1)}, u32[]{:S(2)}, u32[]{:S(2)}) async-start(bf16[32,2,3,64,128]{4,3,2,1,0:T(8,128)(2,1)} %bitcast.147), calls=%async_computation | async-start | bytes 6291456 | tf_op jit(solution)/shard_map/all_to_all | solution.py:133
  19.9 36.3 %collective-permute-start = (bf16[3,64,128]{2,1,0:T(8,128)(2,1)}, bf16[3,64,128]{2,1,0:T(8,128)(2,1)}, u32[]{:S(2)}, u32[]{:S(2)}) collective-permute-start(bf16[3,64,128]{2,1,0:T(8,128)(2,1)} %bitcast_bitcast_fusion.2), channel_id=1, source_target_pairs={{0,3},{1,0},{2,1},{3,2},{4,7},{5,4},{6,5},{7,6},{8,11},{9,8},{10,9... | collective-permute-start | bytes 147464 | tf_op jit(solution)/shard_map/ppermute | solution.py:148
  23.2 33.0 %collective-permute-start.1 = (bf16[3,64,128]{2,1,0:T(8,128)(2,1)}, bf16[3,64,128]{2,1,0:T(8,128)(2,1)}, u32[]{:S(2)}, u32[]{:S(2)}) collective-permute-start(bf16[3,64,128]{2,1,0:T(8,128)(2,1)} %bitcast_bitcast_fusion.1), channel_id=1, source_target_pairs={{0,2},{1,3},{2,0},{3,1},{4,6},{5,7},{6,4},{7,5},{8,10},{9,11},{10,... | collective-permute-start | bytes 147464 | tf_op jit(solution)/shard_map/ppermute | solution.py:148
  24.7 31.6 %collective-permute-start.2 = (bf16[3,64,128]{2,1,0:T(8,128)(2,1)}, bf16[3,64,128]{2,1,0:T(8,128)(2,1)}, u32[]{:S(2)}, u32[]{:S(2)}) collective-permute-start(bf16[3,64,128]{2,1,0:T(8,128)(2,1)} %bitcast_bitcast_fusion), channel_id=1, source_target_pairs={{0,1},{1,2},{2,3},{3,0},{4,5},{5,6},{6,7},{7,4},{8,9},{9,10},{10,1... | collective-permute-start | bytes 147464 | tf_op jit(solution)/shard_map/ppermute | solution.py:148
  61.4 4.6 %copy-start.1 = (f32[3,256,2048]{2,1,0:T(8,128)S(1)}, f32[3,256,2048]{2,1,0:T(8,128)}, u32[]{:S(2)}) copy-start(f32[3,256,2048]{2,1,0:T(8,128)} %get-tuple-element.19) | copy-start | bytes 18874372
  61.5 11.3 %slice-start = ((s8[4718592]{0:T(1024)(128)(4,1)}), s8[4194304]{0:T(1024)(128)(4,1)S(1)}, s32[]{:S(2)}) async-start(s8[4718592]{0:T(1024)(128)(4,1)} %bitcast.153), calls=%async_computation.1 | async-start | bytes 8388608
  66.0 6.8 %slice-start.1 = ((s8[4718592]{0:T(1024)(128)(4,1)}), s8[524288]{0:T(1024)(128)(4,1)S(1)}, s32[]{:S(2)}) async-start(s8[4718592]{0:T(1024)(128)(4,1)} %bitcast.153), calls=%async_computation.2 | async-start | bytes 1048576
  67.6 5.9 %collective-permute-start.3 = (bf16[64,384]{0,1:T(8,128)(2,1)S(1)}, bf16[64,384]{0,1:T(8,128)(2,1)S(1)}, u32[]{:S(2)}, u32[]{:S(2)}) collective-permute-start(bf16[64,384]{0,1:T(8,128)(2,1)S(1)} %bitcast.169), channel_id=1, source_target_pairs={{0,1},{1,2},{2,3},{3,0},{4,5},{5,6},{6,7},{7,4},{8,9},{9,10},{10,1... | collective-permute-start | bytes 147464 | tf_op jit(solution)/shard_map/ppermute | solution.py:168
  67.7 6.2 %collective-permute-start.5 = (bf16[64,384]{0,1:T(8,128)(2,1)S(1)}, bf16[64,384]{0,1:T(8,128)(2,1)S(1)}, u32[]{:S(2)}, u32[]{:S(2)}) collective-permute-start(bf16[64,384]{0,1:T(8,128)(2,1)S(1)} %bitcast.168), channel_id=1, source_target_pairs={{0,3},{1,0},{2,1},{3,2},{4,7},{5,4},{6,5},{7,6},{8,11},{9,8},{10,9... | collective-permute-start | bytes 147464 | tf_op jit(solution)/shard_map/ppermute | solution.py:168
  70.9 6.1 %collective-permute-start.4 = (bf16[64,384]{0,1:T(8,128)(2,1)S(1)}, bf16[64,384]{0,1:T(8,128)(2,1)S(1)}, u32[]{:S(2)}, u32[]{:S(2)}) collective-permute-start(bf16[64,384]{0,1:T(8,128)(2,1)S(1)} %bitcast.167), channel_id=1, source_target_pairs={{0,2},{1,3},{2,0},{3,1},{4,6},{5,7},{6,4},{7,5},{8,10},{9,11},{10,... | collective-permute-start | bytes 147464 | tf_op jit(solution)/shard_map/ppermute | solution.py:168
  73.1 3.9 %copy-start.4 = (bf16[64,1536]{1,0:T(8,128)(2,1)S(1)}, bf16[64,1536]{1,0:T(8,128)(2,1)}, u32[]{:S(2)}) copy-start(bf16[64,1536]{1,0:T(8,128)(2,1)} %param.16) | copy-start | bytes 589828
  74.2 4.1 %copy-start.3 = (f32[2,4,32,16]{3,2,1,0:T(8,128)S(1)}, f32[2,4,32,16]{3,2,1,0:T(8,128)}, u32[]{:S(2)}) copy-start(f32[2,4,32,16]{3,2,1,0:T(8,128)} %reshape.107) | copy-start | bytes 49156
  77.5 19.6 %copy-start.2 = (bf16[64,1536]{1,0:T(8,128)(2,1)}, bf16[64,1536]{1,0:T(8,128)(2,1)S(1)}, u32[]{:S(2)}) copy-start(bf16[64,1536]{1,0:T(8,128)(2,1)S(1)} %get-tuple-element.21) | copy-start | bytes 589828
  78.1 19.2 %copy-start.12 = (pred[8,5]{0,1:T(8,128)(4,1)S(1)}, pred[8,5]{0,1:T(8,128)(4,1)}, u32[]{:S(2)}) copy-start(pred[8,5]{0,1:T(8,128)(4,1)} %constant.91) | copy-start | bytes 124
  78.2 23.1 %slice-start.2 = ((s8[7962624]{0:T(1024)(128)(4,1)}), s8[4194304]{0:T(1024)(128)(4,1)S(1)}, s32[]{:S(2)}) async-start(s8[7962624]{0:T(1024)(128)(4,1)} %bitcast.171), calls=%async_computation.3 | async-start | bytes 8388608
  78.3 10.2 %collective-permute-start.6 = (bf16[2,4,32,16]{3,2,1,0:T(8,128)(2,1)S(1)}, bf16[2,4,32,16]{3,2,1,0:T(8,128)(2,1)S(1)}, u32[]{:S(2)}, u32[]{:S(2)}) collective-permute-start(bf16[2,4,32,16]{3,2,1,0:T(8,128)(2,1)S(1)} %subtract_convert_fusion), channel_id=1, source_target_pairs={{0,3},{1,4},{2,5},{3,6},{4,7},{5,8},{6,9},{7,10},{8,11},{9,12},{10... | collective-permute-start | bytes 24584 | tf_op jit(solution)/shard_map/ppermute | solution.py:22
  81.8 11.1 %collective-permute-start.7 = (bf16[2,4,32,16]{3,2,1,0:T(8,128)(2,1)S(1)}, bf16[2,4,32,16]{3,2,1,0:T(8,128)(2,1)S(1)}, u32[]{:S(2)}, u32[]{:S(2)}) collective-permute-start(bf16[2,4,32,16]{3,2,1,0:T(8,128)(2,1)S(1)} %subtract_convert_fusion), channel_id=1, source_target_pairs={{0,2},{1,3},{2,4},{3,5},{4,6},{5,7},{6,8},{7,9},{8,10},{9,11},{10,... | collective-permute-start | bytes 24584 | tf_op jit(solution)/shard_map/ppermute | solution.py:22
  86.5 10.4 %collective-permute-start.8 = (bf16[2,4,32,16]{3,2,1,0:T(8,128)(2,1)S(1)}, bf16[2,4,32,16]{3,2,1,0:T(8,128)(2,1)S(1)}, u32[]{:S(2)}, u32[]{:S(2)}) collective-permute-start(bf16[2,4,32,16]{3,2,1,0:T(8,128)(2,1)S(1)} %subtract_convert_fusion), channel_id=1, source_target_pairs={{0,1},{1,2},{2,3},{3,4},{4,5},{5,6},{6,7},{7,8},{8,9},{9,10},{10,1... | collective-permute-start | bytes 24584 | tf_op jit(solution)/shard_map/ppermute | solution.py:22
  97.3 4.1 %slice-start.3 = ((s8[7962624]{0:T(1024)(128)(4,1)}), s8[3768320]{0:T(1024)(128)(4,1)S(1)}, s32[]{:S(2)}) async-start(s8[7962624]{0:T(1024)(128)(4,1)} %bitcast.171), calls=%async_computation.4 | async-start | bytes 7536640
  101.2 9.1 %slice-start.4 = ((s8[7962624]{0:T(1024)(128)(4,1)}), s8[4194304]{0:T(1024)(128)(4,1)S(1)}, s32[]{:S(2)}) async-start(s8[7962624]{0:T(1024)(128)(4,1)} %bitcast.173), calls=%async_computation.5 | async-start | bytes 8388608
  101.4 8.9 %slice-start.5 = ((s8[7962624]{0:T(1024)(128)(4,1)}), s8[3768320]{0:T(1024)(128)(4,1)S(1)}, s32[]{:S(2)}) async-start(s8[7962624]{0:T(1024)(128)(4,1)} %bitcast.173), calls=%async_computation.6 | async-start | bytes 7536640
  (5 other events, 12.4 us)

commit v13 on v11

--- a/solution.py
+++ b/solution.py
@@ -80,6 +80,24 @@
         preferred_element_type=jnp.float32,
     )
     return result[0]
+
+
+def patch_conv(extended, kernel):
+    taps, rows, cols = kernel.shape[:3]
+    frames = extended.shape[0] - taps + 1
+    height, width = extended.shape[1], extended.shape[2]
+    padded = jnp.pad(extended, ((0, 0), (rows // 2, rows // 2), (cols // 2, cols // 2), (0, 0)))
+    windows = [
+        padded[dt : dt + frames, dy : dy + height, dx : dx + width]
+        for dt in range(taps)
+        for dy in range(rows)
+        for dx in range(cols)
+    ]
+    patches = jnp.stack(windows, axis=3).reshape(frames * height * width, -1)
+    result = jnp.dot(
+        patches, kernel.reshape(-1, kernel.shape[-1]), preferred_element_type=jnp.float32
+    )
+    return result.reshape(frames, height, width, kernel.shape[-1])
 
 
 def causal_conv(activ, kernel):
@@ -174,7 +192,7 @@
     clean_ext = jnp.concatenate(earlier + [clean], axis=0)
     feature_ext = spatial_conv(clean_ext, input_kernel).astype(jnp.bfloat16)
     first_act = norm_silu(feature_ext, first_gain)
-    middle = spatial_conv(first_act, middle_kernel)
+    middle = patch_conv(first_act, middle_kernel)
     second_act = norm_silu(middle, second_gain)
     feature = feature_ext[-clean.shape[0]:]
     decoded = (feature.astype(jnp.float32) + spatial_conv(second_act, final_kernel)).astype(

time: 113 us -> 153 us (1.35)
  the two profiles are of different devices: /device:TPU:96 before, /device:TPU:34 now
where the time goes in v13:
time: 153 us; the launch traced here: 152 us
  local copies, waits for them, and re-layouts  55.4 us (36%)
  waiting for transfers between devices  36.6 us (24%)
  starting transfers between devices  29.4 us (19%)
  matrix products  25.2 us (16%)
  other arithmetic  3.24 us (2%)
  between operations  2 us (1%)
    all_to_all x1, waiting for transfers between devices, gather_group(): got = lax.all_to_all(sent, FRAMES, 0, 0, tiled=True)  25.4 us
    dot_general x1, local copies, waits for them, and re-layouts, patch_conv(): jnp.dot(patches, kernel.reshape(-1, kernel.shape[-1]), preferred_element_...  18.2 us
    ppermute x3, starting transfers between devices, shifted(): return lax.ppermute(x, axis, pairs)  11.9 us
    dot_general x1, matrix products, patch_conv(): jnp.dot(patches, kernel.reshape(-1, kernel.shape[-1]), preferred_element_...  11.3 us
    another operation x2, local copies, waits for them, and re-layouts, patch_conv(): patches = jnp.stack(windows, axis=3).reshape(frames * height * width, -1)  9.8 us
    conv_general_dilated x2, matrix products, spatial_conv(): lax.conv_general_dilated(extended[None], kernel, (1, 1, 1), ((0, 0), (1,...  8.74 us
    all_to_all x1, starting transfers between devices, gather_group(): got = lax.all_to_all(sent, FRAMES, 0, 0, tiled=True)  8.53 us
    unnamed x61, local copies, waits for them, and re-layouts  8.35 us
  transfers between devices with their start and end apart: 10, of which 4 were waited for; matrix products, arithmetic and copies ran while one was open for 10% of the time, Pallas kernels for 0%

profile of v13, /device:TPU:34, one launch (start us, length us, event | category | flops | bytes accessed | tf_op | source)
XLA Modules:
  0.0 151.9 jit_solution(5967383127846937953)
XLA Ops:
  3.0 2.2 %broadcast_in_dim.11 = bf16[8,4,64,2,384]{4,2,3,1,0:T(8,128)(2,1)} broadcast(bf16[4,64,2,384]{3,1,2,0:T(8,128)(2,1)S(1)} %copy.80), dimensions={1,2,3,4} | broadcast | bytes 3538944 | tf_op jit(solution)/shard_map/broadcast_in_dim | solution.py:147
  5.2 8.5 %all-to-all-start = ((bf16[32,64,2,384]{3,1,2,0:T(8,128)(2,1)}), bf16[32,64,2,384]{3,1,2,0:T(8,128)(2,1)S(1)}, u32[]{:S(2)}, u32[]{:S(2)}) async-start(bf16[32,64,2,384]{3,1,2,0:T(8,128)(2,1)} %bitcast.221), calls=%async_computation | async-start | bytes 6291456 | tf_op jit(solution)/shard_map/all_to_all | solution.py:149
  13.7 1.7 %reshape.114 = bf16[64,4,384]{2,1,0:T(4,128)(2,1)} reshape(bf16[64,1536]{1,0:T(8,128)(2,1)} %param.17) | data formatting | bytes 393216 | tf_op jit(solution)/shard_map/reshape | solution.py:153
  15.4 3.2 %dynamic-slice_reduce_fusion.3 = (bf16[64,384]{1,0:T(8,128)(2,1)}, bf16[64,384]{1,0:T(8,128)(2,1)S(1)}, bf16[64,384]{1,0:T(8,128)(2,1)S(1)}, bf16[64,384]{1,0:T(8,128)(2,1)S(1)}) fusion(bf16[64,4,384]{2,1,0:T(4,128)(2,1)} %reshape.114, s32[]{:T(128)S(6)} %select_n.18, s32[]{:T(128)S(6)} %select_n.20, s32[]{:T(128)S(6)} %select_n.19, s32[]{:T(128)S(6)} %select_n.21), kind=kLoop, calls=%fused_computation.167 | loop fusion | bytes 393232 | tf_op jit(solution)/shard_map/jit(dynamic_index_in_dim)/dynamic_slice | solution.py:158
  19.3 1.5 collective-permute-start.2
  22.6 2.1 %collective-permute-start.1 = (bf16[3,64,128]{2,1,0:T(8,128)(2,1)}, bf16[3,64,128]{2,1,0:T(8,128)(2,1)}, u32[]{:S(2)}, u32[]{:S(2)}) collective-permute-start(bf16[3,64,128]{2,1,0:T(8,128)(2,1)} %bitcast_bitcast_fusion.1), channel_id=1, source_target_pairs={{0,2},{1,3},{2,0},{3,1},{4,6},{5,7},{6,4},{7,5},{8,10},{9,11},{10,... | collective-permute-start | bytes 147464 | tf_op jit(solution)/shard_map/ppermute | solution.py:163
  26.9 25.4 %all-to-all-done = bf16[32,64,2,384]{3,1,2,0:T(8,128)(2,1)S(1)} async-done(((bf16[32,64,2,384]{3,1,2,0:T(8,128)(2,1)}), bf16[32,64,2,384]{3,1,2,0:T(8,128)(2,1)S(1)}, u32[]{:S(2)}, u32[]{:S(2)}) %all-to-all-start) | async-done | bytes 3145760 | tf_op jit(solution)/shard_map/all_to_all | solution.py:149
  52.6 1.5 fusion.138
  54.1 1.7 %copy.82 = bf16[2048,1,384]{0,2,1:T(8,128)(2,1)S(1)} copy(bf16[2048,1,384]{2,0,1:T(8,128)(2,1)} %get-tuple-element.10) | data formatting | bytes 3145728 | tf_op jit(solution)/shard_map/slice | solution.py:166
  55.8 1.7 %copy.84 = bf16[2048,1,384]{0,2,1:T(8,128)(2,1)} copy(bf16[2048,1,384]{2,0,1:T(8,128)(2,1)S(1)} %get-tuple-element.11) | data formatting | bytes 3145728 | tf_op jit(solution)/shard_map/slice | solution.py:167
  57.5 2.0 %multiply_reduce_fusion = (f32[3,256]{1,0:T(4,128)S(1)}, f32[3,256,2048]{2,1,0:T(8,128)S(1)}) fusion(bf16[2048,3,128]{0,2,1:T(8,128)(2,1)S(1)} %bitcast.223, bf16[3,64,128]{2,1,0:T(8,128)(2,1)} %collective-permute-done.2, bf16[3,64,128]{2,1,0:T(8,128)(2,1)} %collective-permute-done.1, bf16[3,64,128]{2,1,0:T(8,128)(2,1)} %collective-permute-done, ...), kind=kOutput, calls=%fused_computation.1 | convolution fusion | flops 406584576 | bytes 8064000 | tf_op jit(solution)/shard_map/qhd,khd->hqk/dot_general | solution.py:39
  62.4 2.2 %collective-permute-start.5 = (bf16[64,384]{0,1:T(8,128)(2,1)S(1)}, bf16[64,384]{0,1:T(8,128)(2,1)S(1)}, u32[]{:S(2)}, u32[]{:S(2)}) collective-permute-start(bf16[64,384]{0,1:T(8,128)(2,1)S(1)} %bitcast.239), channel_id=1, source_target_pairs={{0,3},{1,0},{2,1},{3,2},{4,7},{5,4},{6,5},{7,6},{8,11},{9,8},{10,9... | collective-permute-start | bytes 147464 | tf_op jit(solution)/shard_map/ppermute | solution.py:185
  64.6 2.5 %collective-permute-start.4 = (bf16[64,384]{0,1:T(8,128)(2,1)S(1)}, bf16[64,384]{0,1:T(8,128)(2,1)S(1)}, u32[]{:S(2)}, u32[]{:S(2)}) collective-permute-start(bf16[64,384]{0,1:T(8,128)(2,1)S(1)} %bitcast.238), channel_id=1, source_target_pairs={{0,2},{1,3},{2,0},{3,1},{4,6},{5,7},{6,4},{7,5},{8,10},{9,11},{10,... | collective-permute-start | bytes 147464 | tf_op jit(solution)/shard_map/ppermute | solution.py:185
  67.6 4.1 %collective-permute-done.3 = bf16[64,384]{0,1:T(8,128)(2,1)S(1)} collective-permute-done((bf16[64,384]{0,1:T(8,128)(2,1)S(1)}, bf16[64,384]{0,1:T(8,128)(2,1)S(1)}, u32[]{:S(2)}, u32[]{:S(2)}) %collective-permute-start.3) | collective-permute-done | bytes 49184 | tf_op jit(solution)/shard_map/ppermute | solution.py:185
  73.7 3.1 %collective-permute-start.8 = (bf16[2,4,32,16]{3,2,1,0:T(8,128)(2,1)S(1)}, bf16[2,4,32,16]{3,2,1,0:T(8,128)(2,1)S(1)}, u32[]{:S(2)}, u32[]{:S(2)}) collective-permute-start(bf16[2,4,32,16]{3,2,1,0:T(8,128)(2,1)S(1)} %subtract_convert_fusion), channel_id=1, source_target_pairs={{0,1},{1,2},{2,3},{3,4},{4,5},{5,6},{6,7},{7,8},{8,9},{9,10},{10,1... | collective-permute-start | bytes 24584 | tf_op jit(solution)/shard_map/ppermute | solution.py:22
  76.8 6.7 %collective-permute-start.7 = (bf16[2,4,32,16]{3,2,1,0:T(8,128)(2,1)S(1)}, bf16[2,4,32,16]{3,2,1,0:T(8,128)(2,1)S(1)}, u32[]{:S(2)}, u32[]{:S(2)}) collective-permute-start(bf16[2,4,32,16]{3,2,1,0:T(8,128)(2,1)S(1)} %subtract_convert_fusion), channel_id=1, source_target_pairs={{0,2},{1,3},{2,4},{3,5},{4,6},{5,7},{6,8},{7,9},{8,10},{9,11},{10,... | collective-permute-start | bytes 24584 | tf_op jit(solution)/shard_map/ppermute | solution.py:22
  83.6 2.1 %collective-permute-start.6 = (bf16[2,4,32,16]{3,2,1,0:T(8,128)(2,1)S(1)}, bf16[2,4,32,16]{3,2,1,0:T(8,128)(2,1)S(1)}, u32[]{:S(2)}, u32[]{:S(2)}) collective-permute-start(bf16[2,4,32,16]{3,2,1,0:T(8,128)(2,1)S(1)} %subtract_convert_fusion), channel_id=1, source_target_pairs={{0,3},{1,4},{2,5},{3,6},{4,7},{5,8},{6,9},{7,10},{8,11},{9,12},{10... | collective-permute-start | bytes 24584 | tf_op jit(solution)/shard_map/ppermute | solution.py:22
  85.7 1.8 %collective-permute-done.7 = bf16[2,4,32,16]{3,2,1,0:T(8,128)(2,1)S(1)} collective-permute-done((bf16[2,4,32,16]{3,2,1,0:T(8,128)(2,1)S(1)}, bf16[2,4,32,16]{3,2,1,0:T(8,128)(2,1)S(1)}, u32[]{:S(2)}, u32[]{:S(2)}) %collective-permute-start.7) | collective-permute-done | bytes 8224 | tf_op jit(solution)/shard_map/ppermute | solution.py:22
  87.5 5.2 %collective-permute-done.6 = bf16[2,4,32,16]{3,2,1,0:T(8,128)(2,1)S(1)} collective-permute-done((bf16[2,4,32,16]{3,2,1,0:T(8,128)(2,1)S(1)}, bf16[2,4,32,16]{3,2,1,0:T(8,128)(2,1)S(1)}, u32[]{:S(2)}, u32[]{:S(2)}) %collective-permute-start.6) | collective-permute-done | bytes 8224 | tf_op jit(solution)/shard_map/ppermute | solution.py:22
  93.2 1.8 %select_convert_fusion = bf16[6,4,8,5,384]{4,2,3,1,0:T(8,128)(2,1)S(1)} fusion(bf16[3,3,3,16,384]{4,3,2,1,0:T(8,128)(2,1)S(1)} %copy-done, pred[8,5]{0,1:T(8,128)(4,1)S(1)} %copy-done.13, bf16[8,4,1,7,2,16]{5,3,4,1,0,2:T(8,128)(2,1)S(1)} %slice.171, bf16[8,4,1,8,5,16]{5,3,4,1,0,2:T(8,128)(2,1)S(1)} %copy.88), kind=kOutput, calls=%fused_computation.39 | convolution fusion | flops 266330112 | bytes 1124392 | tf_op jit(solution)/shard_map/conv_general_dilated | solution.py:74
  104.2 9.5 %copy.92 = bf16[4,4,32,27,384]{4,3,2,1,0:T(8,128)(2,1)} copy(bf16[4,4,32,27,384]{4,1,2,0,3:T(4,128)(2,1)S(1)} %fusion.107) | data formatting | bytes 21233664 | tf_op jit(solution)/shard_map/stack | solution.py:96
  113.6 18.2 %dot_general.33 = bf16[4,4,32,10368]{3,2,1,0:T(8,128)(2,1)} reshape(bf16[4,4,32,27,384]{4,3,2,1,0:T(8,128)(2,1)} %copy.92) | data formatting | bytes 21233664 | tf_op jit(solution)/shard_map/dot_general | solution.py:97
  131.9 11.3 %multiply_reduce_fusion.1 = (f32[4,4,32]{2,1,0:T(4,128)S(1)}, f32[4,4,32,384]{3,2,1,0:T(8,128)S(1)}) fusion(bf16[4,4,32,10368]{3,2,1,0:T(8,128)(2,1)} %dot_general.33, bf16[10368,384,1,1]{1,0,3,2:T(8,128)(2,1)} %bitcast.242), kind=kOutput, calls=%fused_computation.70 | convolution fusion | flops 4077256192 | bytes 19367936 | tf_op jit(solution)/shard_map/dot_general | solution.py:97
  144.0 6.9 %fusion.15 = bf16[2,4,8,5,384]{4,2,3,1,0:T(8,128)(2,1)S(1)} fusion(bf16[3,3,3,384,384]{4,3,2,1,0:T(8,128)(2,1)} %param.31, bf16[4,4,1,7,2,384]{5,3,4,1,0,2:T(8,128)(2,1)S(1)} %slice.177, bf16[4,4,1,8,5,384]{5,3,4,1,0,2:T(8,128)(2,1)S(1)} %copy.95, bf16[6,4,8,5,384]{4,2,3,1,0:T(8,128)(2,1)S(1)} %select_convert_fusion, pred[8,5]{0,1:T(8,128)(4,1)S(1)} %copy-done.13), kind=kOutput, calls=%fused_computation.45 | convolution fusion | flops 2125922304 | bytes 9117736 | tf_op jit(solution)/shard_map/conv_general_dilated | solution.py:74
  (112 shorter events, 22.9 us)
Async XLA Ops:
  0.6 92.6 %copy-start = (bf16[3,3,3,16,384]{4,3,2,1,0:T(8,128)(2,1)S(1)}, bf16[3,3,3,16,384]{4,3,2,1,0:T(8,128)(2,1)}, u32[]{:S(2)}) copy-start(bf16[3,3,3,16,384]{4,3,2,1,0:T(8,128)(2,1)} %param.27) | copy-start | bytes 995332
  2.7 22.6 %copy-start.6 = (f32[2,4,512]{2,1,0:T(4,128)S(1)}, f32[2,4,512]{2,1,0:T(4,128)}, u32[]{:S(2)}) copy-start(f32[2,4,512]{2,1,0:T(4,128)} %param.26) | copy-start | bytes 49156
  2.7 23.4 %copy-start.8 = (f32[1536]{0:T(1024)S(1)}, f32[1536]{0:T(1024)}, u32[]{:S(2)}) copy-start(f32[1536]{0:T(1024)} %param.22) | copy-start | bytes 18436
  5.2 47.1 %all-to-all-start = ((bf16[32,64,2,384]{3,1,2,0:T(8,128)(2,1)}), bf16[32,64,2,384]{3,1,2,0:T(8,128)(2,1)S(1)}, u32[]{:S(2)}, u32[]{:S(2)}) async-start(bf16[32,64,2,384]{3,1,2,0:T(8,128)(2,1)} %bitcast.221), calls=%async_computation | async-start | bytes 6291456 | tf_op jit(solution)/shard_map/all_to_all | solution.py:149
  19.3 38.3 %collective-permute-start.2 = (bf16[3,64,128]{2,1,0:T(8,128)(2,1)}, bf16[3,64,128]{2,1,0:T(8,128)(2,1)}, u32[]{:S(2)}, u32[]{:S(2)}) collective-permute-start(bf16[3,64,128]{2,1,0:T(8,128)(2,1)} %bitcast_bitcast_fusion), channel_id=1, source_target_pairs={{0,1},{1,2},{2,3},{3,0},{4,5},{5,6},{6,7},{7,4},{8,9},{9,10},{10,1... | collective-permute-start | bytes 147464 | tf_op jit(solution)/shard_map/ppermute | solution.py:163
  21.4 36.2 %collective-permute-start = (bf16[3,64,128]{2,1,0:T(8,128)(2,1)}, bf16[3,64,128]{2,1,0:T(8,128)(2,1)}, u32[]{:S(2)}, u32[]{:S(2)}) collective-permute-start(bf16[3,64,128]{2,1,0:T(8,128)(2,1)} %bitcast_bitcast_fusion.2), channel_id=1, source_target_pairs={{0,3},{1,0},{2,1},{3,2},{4,7},{5,4},{6,5},{7,6},{8,11},{9,8},{10,9... | collective-permute-start | bytes 147464 | tf_op jit(solution)/shard_map/ppermute | solution.py:163
  22.6 35.0 %collective-permute-start.1 = (bf16[3,64,128]{2,1,0:T(8,128)(2,1)}, bf16[3,64,128]{2,1,0:T(8,128)(2,1)}, u32[]{:S(2)}, u32[]{:S(2)}) collective-permute-start(bf16[3,64,128]{2,1,0:T(8,128)(2,1)} %bitcast_bitcast_fusion.1), channel_id=1, source_target_pairs={{0,2},{1,3},{2,0},{3,1},{4,6},{5,7},{6,4},{7,5},{8,10},{9,11},{10,... | collective-permute-start | bytes 147464 | tf_op jit(solution)/shard_map/ppermute | solution.py:163
  60.7 6.5 %slice-start = ((s8[4718592]{0:T(1024)(128)(4,1)}), s8[4194304]{0:T(1024)(128)(4,1)S(1)}, s32[]{:S(2)}) async-start(s8[4718592]{0:T(1024)(128)(4,1)} %bitcast.226), calls=%async_computation.1 | async-start | bytes 8388608
  60.8 6.5 %slice-start.1 = ((s8[4718592]{0:T(1024)(128)(4,1)}), s8[524288]{0:T(1024)(128)(4,1)S(1)}, s32[]{:S(2)}) async-start(s8[4718592]{0:T(1024)(128)(4,1)} %bitcast.226), calls=%async_computation.2 | async-start | bytes 1048576
  60.8 11.7 %copy-start.5 = (bf16[64,1536]{1,0:T(8,128)(2,1)S(1)}, bf16[64,1536]{1,0:T(8,128)(2,1)}, u32[]{:S(2)}) copy-start(bf16[64,1536]{1,0:T(8,128)(2,1)} %param.16) | copy-start | bytes 589828
  60.8 11.7 %copy-start.7 = (f32[1536]{0:T(1024)S(1)}, f32[1536]{0:T(1024)}, u32[]{:S(2)}) copy-start(f32[1536]{0:T(1024)} %param.20) | copy-start | bytes 18436
  62.2 11.0 %copy-start.11 = (bf16[1536,64]{0,1:T(8,128)(2,1)S(1)}, bf16[1536,64]{0,1:T(8,128)(2,1)}, u32[]{:S(2)}) copy-start(bf16[1536,64]{0,1:T(8,128)(2,1)} %param.24) | copy-start | bytes 589828
  62.2 11.0 %copy-start.12 = (f32[1536]{0:T(1024)S(1)}, f32[1536]{0:T(1024)}, u32[]{:S(2)}) copy-start(f32[1536]{0:T(1024)} %param.23) | copy-start | bytes 18436
  62.2 11.5 %copy-start.4 = (f32[2,4,32,16]{3,2,1,0:T(8,128)S(1)}, f32[2,4,32,16]{3,2,1,0:T(8,128)}, u32[]{:S(2)}) copy-start(f32[2,4,32,16]{3,2,1,0:T(8,128)} %reshape.122) | copy-start | bytes 49156
  62.2 31.0 %copy-start.13 = (pred[8,5]{0,1:T(8,128)(4,1)S(1)}, pred[8,5]{0,1:T(8,128)(4,1)}, u32[]{:S(2)}) copy-start(pred[8,5]{0,1:T(8,128)(4,1)} %constant.92) | copy-start | bytes 124
  62.4 9.7 %collective-permute-start.5 = (bf16[64,384]{0,1:T(8,128)(2,1)S(1)}, bf16[64,384]{0,1:T(8,128)(2,1)S(1)}, u32[]{:S(2)}, u32[]{:S(2)}) collective-permute-start(bf16[64,384]{0,1:T(8,128)(2,1)S(1)} %bitcast.239), channel_id=1, source_target_pairs={{0,3},{1,0},{2,1},{3,2},{4,7},{5,4},{6,5},{7,6},{8,11},{9,8},{10,9... | collective-permute-start | bytes 147464 | tf_op jit(solution)/shard_map/ppermute | solution.py:185
  64.6 7.8 %collective-permute-start.4 = (bf16[64,384]{0,1:T(8,128)(2,1)S(1)}, bf16[64,384]{0,1:T(8,128)(2,1)S(1)}, u32[]{:S(2)}, u32[]{:S(2)}) collective-permute-start(bf16[64,384]{0,1:T(8,128)(2,1)S(1)} %bitcast.238), channel_id=1, source_target_pairs={{0,2},{1,3},{2,0},{3,1},{4,6},{5,7},{6,4},{7,5},{8,10},{9,11},{10,... | collective-permute-start | bytes 147464 | tf_op jit(solution)/shard_map/ppermute | solution.py:185
  67.1 4.6 %collective-permute-start.3 = (bf16[64,384]{0,1:T(8,128)(2,1)S(1)}, bf16[64,384]{0,1:T(8,128)(2,1)S(1)}, u32[]{:S(2)}, u32[]{:S(2)}) collective-permute-start(bf16[64,384]{0,1:T(8,128)(2,1)S(1)} %bitcast.240), channel_id=1, source_target_pairs={{0,1},{1,2},{2,3},{3,0},{4,5},{5,6},{6,7},{7,4},{8,9},{9,10},{10,1... | collective-permute-start | bytes 147464 | tf_op jit(solution)/shard_map/ppermute | solution.py:185
  72.9 22.1 %copy-start.3 = (bf16[64,1536]{1,0:T(8,128)(2,1)}, bf16[64,1536]{1,0:T(8,128)(2,1)S(1)}, u32[]{:S(2)}) copy-start(bf16[64,1536]{1,0:T(8,128)(2,1)S(1)} %get-tuple-element.21) | copy-start | bytes 589828
  73.7 12.0 %collective-permute-start.8 = (bf16[2,4,32,16]{3,2,1,0:T(8,128)(2,1)S(1)}, bf16[2,4,32,16]{3,2,1,0:T(8,128)(2,1)S(1)}, u32[]{:S(2)}, u32[]{:S(2)}) collective-permute-start(bf16[2,4,32,16]{3,2,1,0:T(8,128)(2,1)S(1)} %subtract_convert_fusion), channel_id=1, source_target_pairs={{0,1},{1,2},{2,3},{3,4},{4,5},{5,6},{6,7},{7,8},{8,9},{9,10},{10,1... | collective-permute-start | bytes 24584 | tf_op jit(solution)/shard_map/ppermute | solution.py:22
  76.8 10.7 %collective-permute-start.7 = (bf16[2,4,32,16]{3,2,1,0:T(8,128)(2,1)S(1)}, bf16[2,4,32,16]{3,2,1,0:T(8,128)(2,1)S(1)}, u32[]{:S(2)}, u32[]{:S(2)}) collective-permute-start(bf16[2,4,32,16]{3,2,1,0:T(8,128)(2,1)S(1)} %subtract_convert_fusion), channel_id=1, source_target_pairs={{0,2},{1,3},{2,4},{3,5},{4,6},{5,7},{6,8},{7,9},{8,10},{9,11},{10,... | collective-permute-start | bytes 24584 | tf_op jit(solution)/shard_map/ppermute | solution.py:22
  83.6 9.2 %collective-permute-start.6 = (bf16[2,4,32,16]{3,2,1,0:T(8,128)(2,1)S(1)}, bf16[2,4,32,16]{3,2,1,0:T(8,128)(2,1)S(1)}, u32[]{:S(2)}, u32[]{:S(2)}) collective-permute-start(bf16[2,4,32,16]{3,2,1,0:T(8,128)(2,1)S(1)} %subtract_convert_fusion), channel_id=1, source_target_pairs={{0,3},{1,4},{2,5},{3,6},{4,7},{5,8},{6,9},{7,10},{8,11},{9,12},{10... | collective-permute-start | bytes 24584 | tf_op jit(solution)/shard_map/ppermute | solution.py:22
  131.9 11.3 %copy-start.10 = (f32[384]{0:T(512)S(1)}, f32[384]{0:T(512)}, u32[]{:S(2)}) copy-start(f32[384]{0:T(512)} %param.30) | copy-start | bytes 4612
  144.0 7.9 %copy-start.1 = (bf16[3,3,3,16,384]{4,3,2,1,0:T(8,128)(2,1)S(1)}, bf16[3,3,3,16,384]{4,3,2,1,0:T(8,128)(2,1)}, u32[]{:S(2)}) copy-start(bf16[3,3,3,16,384]{4,3,2,1,0:T(8,128)(2,1)} %param.27) | copy-start | bytes 995332
  (2 other events, 5.9 us)

commit v14 on v11

--- a/solution.py
+++ b/solution.py
@@ -174,7 +174,14 @@
     clean_ext = jnp.concatenate(earlier + [clean], axis=0)
     feature_ext = spatial_conv(clean_ext, input_kernel).astype(jnp.bfloat16)
     first_act = norm_silu(feature_ext, first_gain)
-    middle = spatial_conv(first_act, middle_kernel)
+    half = (first_act.shape[0] - 2) // 2
+    middle = jnp.concatenate(
+        [
+            spatial_conv(first_act[: half + 2], middle_kernel),
+            spatial_conv(first_act[half:], middle_kernel),
+        ],
+        axis=0,
+    )
     second_act = norm_silu(middle, second_gain)
     feature = feature_ext[-clean.shape[0]:]
     decoded = (feature.astype(jnp.float32) + spatial_conv(second_act, final_kernel)).astype(

time: 113 us -> 109 us (0.965)
  matrix products: 23.3 us -> 17.9 us
    conv_general_dilated x3 -> x4, matrix products: 18.2 us -> 12.8 us  [spatial_conv(): lax.conv_general_dilated(extended[None], kernel, (1, 1, 1), ((0, 0), (1,...]
where the time goes in v14:
time: 109 us; the launch traced here: 107 us
  starting transfers between devices  32.4 us (30%)
  waiting for transfers between devices  31.8 us (29%)
  local copies, waits for them, and re-layouts  19.3 us (18%)
  matrix products  17.9 us (16%)
  other arithmetic  4 us (4%)
  between operations  1.99 us (2%)
    all_to_all x1, waiting for transfers between devices, gather_group(): got = lax.all_to_all(sent, FRAMES, 0, 0, tiled=True)  25.7 us
    ppermute x3, starting transfers between devices, shifted(): return lax.ppermute(x, axis, pairs)  12.9 us
    conv_general_dilated x4, matrix products, spatial_conv(): lax.conv_general_dilated(extended[None], kernel, (1, 1, 1), ((0, 0), (1,...  12.8 us
    all_to_all x1, starting transfers between devices, gather_group(): got = lax.all_to_all(sent, FRAMES, 0, 0, tiled=True)  8.69 us
    ppermute x3, starting transfers between devices, body(): received.append(lax.ppermute(piece, 'hg', pairs))  5.6 us
    ppermute x3, starting transfers between devices, body(): piece = lax.ppermute(pieces[k], 'hg', pairs)  5.21 us
    ppermute x3, waiting for transfers between devices, shifted(): return lax.ppermute(x, axis, pairs)  3.59 us
    dynamic_slice x1, local copies, waits for them, and re-layouts, body(): lax.dynamic_index_in_dim(query_parts, me, 1, keepdims=False)  3.01 us
  transfers between devices with their start and end apart: 10, of which 5 were waited for; matrix products, arithmetic and copies ran while one was open for 11% of the time, Pallas kernels for 0%

profile of v14, /device:TPU:96, one launch (start us, length us, event | category | flops | bytes accessed | tf_op | source)
XLA Modules:
  0.0 107.4 jit_solution(15923377602754552621)
XLA Ops:
  0.6 1.0 stack.10
  3.0 2.1 %broadcast_in_dim.13 = bf16[8,4,64,2,384]{4,2,3,1,0:T(8,128)(2,1)} broadcast(bf16[4,64,2,384]{3,1,2,0:T(8,128)(2,1)S(1)} %copy.55), dimensions={1,2,3,4} | broadcast | bytes 3538944 | tf_op jit(solution)/shard_map/broadcast_in_dim | solution.py:129
  5.1 8.7 %all-to-all-start = ((bf16[32,64,2,384]{3,1,2,0:T(8,128)(2,1)}), bf16[32,64,2,384]{3,1,2,0:T(8,128)(2,1)S(1)}, u32[]{:S(2)}, u32[]{:S(2)}) async-start(bf16[32,64,2,384]{3,1,2,0:T(8,128)(2,1)} %bitcast.137), calls=%async_computation | async-start | bytes 6291456 | tf_op jit(solution)/shard_map/all_to_all | solution.py:131
  13.9 1.7 %reshape.153 = bf16[64,4,384]{2,1,0:T(4,128)(2,1)} reshape(bf16[64,1536]{1,0:T(8,128)(2,1)} %param.17) | data formatting | bytes 393216 | tf_op jit(solution)/shard_map/reshape | solution.py:135
  15.5 3.0 %dynamic-slice_reduce_fusion.3 = (bf16[64,384]{1,0:T(8,128)(2,1)}, bf16[64,384]{1,0:T(8,128)(2,1)S(1)}, bf16[64,384]{1,0:T(8,128)(2,1)S(1)}, bf16[64,384]{1,0:T(8,128)(2,1)S(1)}) fusion(bf16[64,4,384]{2,1,0:T(4,128)(2,1)} %reshape.153, s32[]{:T(128)S(6)} %select_n.18, s32[]{:T(128)S(6)} %select_n.20, s32[]{:T(128)S(6)} %select_n.19, s32[]{:T(128)S(6)} %select_n.21), kind=kLoop, calls=%fused_computation.115 | loop fusion | bytes 393232 | tf_op jit(solution)/shard_map/jit(dynamic_index_in_dim)/dynamic_slice | solution.py:140
  19.1 1.5 %collective-permute-start.2 = (bf16[3,64,128]{2,1,0:T(8,128)(2,1)}, bf16[3,64,128]{2,1,0:T(8,128)(2,1)}, u32[]{:S(2)}, u32[]{:S(2)}) collective-permute-start(bf16[3,64,128]{2,1,0:T(8,128)(2,1)} %bitcast_bitcast_fusion), channel_id=1, source_target_pairs={{0,1},{1,2},{2,3},{3,0},{4,5},{5,6},{6,7},{7,4},{8,9},{9,10},{10,1... | collective-permute-start | bytes 147464 | tf_op jit(solution)/shard_map/ppermute | solution.py:145
  21.2 2.7 %collective-permute-start.1 = (bf16[3,64,128]{2,1,0:T(8,128)(2,1)}, bf16[3,64,128]{2,1,0:T(8,128)(2,1)}, u32[]{:S(2)}, u32[]{:S(2)}) collective-permute-start(bf16[3,64,128]{2,1,0:T(8,128)(2,1)} %bitcast_bitcast_fusion.1), channel_id=1, source_target_pairs={{0,2},{1,3},{2,0},{3,1},{4,6},{5,7},{6,4},{7,5},{8,10},{9,11},{10,... | collective-permute-start | bytes 147464 | tf_op jit(solution)/shard_map/ppermute | solution.py:145
  24.5 1.5 %collective-permute-start = (bf16[3,64,128]{2,1,0:T(8,128)(2,1)}, bf16[3,64,128]{2,1,0:T(8,128)(2,1)}, u32[]{:S(2)}, u32[]{:S(2)}) collective-permute-start(bf16[3,64,128]{2,1,0:T(8,128)(2,1)} %bitcast_bitcast_fusion.2), channel_id=1, source_target_pairs={{0,3},{1,0},{2,1},{3,2},{4,7},{5,4},{6,5},{7,6},{8,11},{9,8},{10,9... | collective-permute-start | bytes 147464 | tf_op jit(solution)/shard_map/ppermute | solution.py:145
  28.2 25.7 %all-to-all-done = bf16[32,64,2,384]{3,1,2,0:T(8,128)(2,1)S(1)} async-done(((bf16[32,64,2,384]{3,1,2,0:T(8,128)(2,1)}), bf16[32,64,2,384]{3,1,2,0:T(8,128)(2,1)S(1)}, u32[]{:S(2)}, u32[]{:S(2)}) %all-to-all-start) | async-done | bytes 3145760 | tf_op jit(solution)/shard_map/all_to_all | solution.py:131
  54.6 1.7 %copy.59 = bf16[2048,1,384]{0,2,1:T(8,128)(2,1)} copy(bf16[2048,1,384]{2,0,1:T(8,128)(2,1)S(1)} %get-tuple-element.11) | data formatting | bytes 3145728 | tf_op jit(solution)/shard_map/slice | solution.py:149
  57.1 1.9 %multiply_reduce_fusion = (f32[3,256]{1,0:T(4,128)S(1)}, f32[3,256,2048]{2,1,0:T(8,128)S(1)}) fusion(bf16[2048,3,128]{0,2,1:T(8,128)(2,1)S(1)} %bitcast.139, bf16[3,64,128]{2,1,0:T(8,128)(2,1)} %collective-permute-done.2, bf16[3,64,128]{2,1,0:T(8,128)(2,1)} %collective-permute-done.1, bf16[3,64,128]{2,1,0:T(8,128)(2,1)} %collective-permute-done, ...), kind=kOutput, calls=%fused_computation.1 | convolution fusion | flops 406584576 | bytes 8064000 | tf_op jit(solution)/shard_map/qhd,khd->hqk/dot_general | solution.py:39
  59.1 1.2 %fusion = f32[3,256]{1,0:T(4,128)S(1)} fusion(f32[3,256,2048]{2,1,0:T(8,128)S(1)} %get-tuple-element.21, f32[3,256]{1,0:T(4,128)S(1)} %get-tuple-element.19), kind=kLoop, calls=%fused_computation.2 | loop fusion | flops 4717824 | bytes 6297600 | tf_op jit(solution)/shard_map/reduce_sum | solution.py:45
  60.5 1.4 %fusion.40 = bf16[256,3,128]{0,2,1:T(8,128)(2,1)S(1)} fusion(bf16[2048,3,128]{0,2,1:T(8,128)(2,1)S(1)} %bitcast.154, f32[3,256,2048]{2,1,0:T(8,128)S(1)} %get-tuple-element.21, f32[3,256]{1,0:T(4,128)S(1)} %get-tuple-element.19, f32[256,3]{0,1:T(4,128)S(1)} %bitcast.162, f32[256,3]{0,1:T(4,128)S(1)} %get-tuple-element.18), kind=kOutput, calls=%fused_computation.46 | convolution fusion | flops 407666688 | bytes 8070144 | tf_op jit(solution)/shard_map/hqk,khd->qhd/dot_general | solution.py:46
  62.0 1.3 %collective-permute-start.5 = (bf16[64,384]{0,1:T(8,128)(2,1)S(1)}, bf16[64,384]{0,1:T(8,128)(2,1)S(1)}, u32[]{:S(2)}, u32[]{:S(2)}) collective-permute-start(bf16[64,384]{0,1:T(8,128)(2,1)S(1)} %bitcast.160), channel_id=1, source_target_pairs={{0,3},{1,0},{2,1},{3,2},{4,7},{5,4},{6,5},{7,6},{8,11},{9,8},{10,9... | collective-permute-start | bytes 147464 | tf_op jit(solution)/shard_map/ppermute | solution.py:167
  64.1 3.1 %collective-permute-start.4 = (bf16[64,384]{0,1:T(8,128)(2,1)S(1)}, bf16[64,384]{0,1:T(8,128)(2,1)S(1)}, u32[]{:S(2)}, u32[]{:S(2)}) collective-permute-start(bf16[64,384]{0,1:T(8,128)(2,1)S(1)} %bitcast.159), channel_id=1, source_target_pairs={{0,2},{1,3},{2,0},{3,1},{4,6},{5,7},{6,4},{7,5},{8,10},{9,11},{10,... | collective-permute-start | bytes 147464 | tf_op jit(solution)/shard_map/ppermute | solution.py:167
  67.6 1.5 %collective-permute-done.3 = bf16[64,384]{0,1:T(8,128)(2,1)S(1)} collective-permute-done((bf16[64,384]{0,1:T(8,128)(2,1)S(1)}, bf16[64,384]{0,1:T(8,128)(2,1)S(1)}, u32[]{:S(2)}, u32[]{:S(2)}) %collective-permute-start.3) | collective-permute-done | bytes 49184 | tf_op jit(solution)/shard_map/ppermute | solution.py:167
  72.1 2.7 %collective-permute-start.8 = (bf16[2,4,32,16]{3,2,1,0:T(8,128)(2,1)S(1)}, bf16[2,4,32,16]{3,2,1,0:T(8,128)(2,1)S(1)}, u32[]{:S(2)}, u32[]{:S(2)}) collective-permute-start(bf16[2,4,32,16]{3,2,1,0:T(8,128)(2,1)S(1)} %subtract_convert_fusion), channel_id=1, source_target_pairs={{0,1},{1,2},{2,3},{3,4},{4,5},{5,6},{6,7},{7,8},{8,9},{9,10},{10,1... | collective-permute-start | bytes 24584 | tf_op jit(solution)/shard_map/ppermute | solution.py:22
  74.8 4.7 %collective-permute-start.7 = (bf16[2,4,32,16]{3,2,1,0:T(8,128)(2,1)S(1)}, bf16[2,4,32,16]{3,2,1,0:T(8,128)(2,1)S(1)}, u32[]{:S(2)}, u32[]{:S(2)}) collective-permute-start(bf16[2,4,32,16]{3,2,1,0:T(8,128)(2,1)S(1)} %subtract_convert_fusion), channel_id=1, source_target_pairs={{0,2},{1,3},{2,4},{3,5},{4,6},{5,7},{6,8},{7,9},{8,10},{9,11},{10,... | collective-permute-start | bytes 24584 | tf_op jit(solution)/shard_map/ppermute | solution.py:22
  79.5 5.6 %collective-permute-start.6 = (bf16[2,4,32,16]{3,2,1,0:T(8,128)(2,1)S(1)}, bf16[2,4,32,16]{3,2,1,0:T(8,128)(2,1)S(1)}, u32[]{:S(2)}, u32[]{:S(2)}) collective-permute-start(bf16[2,4,32,16]{3,2,1,0:T(8,128)(2,1)S(1)} %subtract_convert_fusion), channel_id=1, source_target_pairs={{0,3},{1,4},{2,5},{3,6},{4,7},{5,8},{6,9},{7,10},{8,11},{9,12},{10... | collective-permute-start | bytes 24584 | tf_op jit(solution)/shard_map/ppermute | solution.py:22
  85.5 3.2 %collective-permute-done.6 = bf16[2,4,32,16]{3,2,1,0:T(8,128)(2,1)S(1)} collective-permute-done((bf16[2,4,32,16]{3,2,1,0:T(8,128)(2,1)S(1)}, bf16[2,4,32,16]{3,2,1,0:T(8,128)(2,1)S(1)}, u32[]{:S(2)}, u32[]{:S(2)}) %collective-permute-start.6) | collective-permute-done | bytes 8224 | tf_op jit(solution)/shard_map/ppermute | solution.py:22
  89.1 1.8 %select_convert_fusion = bf16[6,4,8,5,384]{4,2,3,1,0:T(8,128)(2,1)S(1)} fusion(bf16[3,3,3,16,384]{4,3,2,1,0:T(8,128)(2,1)S(1)} %copy-done, pred[8,5]{0,1:T(8,128)(4,1)S(1)} %copy-done.12, bf16[8,4,1,7,2,16]{5,3,4,1,0,2:T(8,128)(2,1)S(1)} %slice.73, bf16[8,4,1,8,5,16]{5,3,4,1,0,2:T(8,128)(2,1)S(1)} %copy.63), kind=kOutput, calls=%fused_computation.15 | convolution fusion | flops 266330112 | bytes 1124392 | tf_op jit(solution)/shard_map/conv_general_dilated | solution.py:74
  93.0 3.7 %convolution_select_fusion.1 = f32[2,4,8,5,384]{4,2,3,1,0:T(8,128)S(1)} fusion(bf16[3,3,3,384,384]{4,3,2,1,0:T(8,128)(2,1)S(1)} %bitcast.164, bf16[4,4,1,7,2,384]{5,3,4,1,0,2:T(8,128)(2,1)S(1)} %slice.79, bf16[4,4,1,8,5,384]{5,3,4,1,0,2:T(8,128)(2,1)S(1)} %copy.68, pred[8,5]{0,1:T(8,128)(4,1)S(1)} %copy-done.12), kind=kOutput, calls=%fused_computation.21 | convolution fusion | flops 2125553664 | bytes 9117736 | tf_op jit(solution)/shard_map/conv_general_dilated | solution.py:74
  97.1 3.7 %convolution_select_fusion.2 = f32[2,4,8,5,384]{4,2,3,1,0:T(8,128)S(1)} fusion(bf16[3,3,3,384,384]{4,3,2,1,0:T(8,128)(2,1)S(1)} %bitcast.164, bf16[4,4,1,7,2,384]{5,3,4,1,0,2:T(8,128)(2,1)S(1)} %slice.77, bf16[4,4,1,8,5,384]{5,3,4,1,0,2:T(8,128)(2,1)S(1)} %copy.66, pred[8,5]{0,1:T(8,128)(4,1)S(1)} %copy-done.12), kind=kOutput, calls=%fused_computation.22 | convolution fusion | flops 2125553664 | bytes 9117736 | tf_op jit(solution)/shard_map/conv_general_dilated | solution.py:74
  102.9 3.7 %fusion.17 = bf16[2,4,8,5,384]{4,2,3,1,0:T(8,128)(2,1)S(1)} fusion(bf16[3,3,3,384,384]{4,3,2,1,0:T(8,128)(2,1)S(1)} %bitcast.166, bf16[4,4,1,7,2,384]{5,3,4,1,0,2:T(8,128)(2,1)S(1)} %slice.83, bf16[4,4,1,8,5,384]{5,3,4,1,0,2:T(8,128)(2,1)S(1)} %copy.73, bf16[6,4,8,5,384]{4,2,3,1,0:T(8,128)(2,1)S(1)} %select_convert_fusion, pred[8,5]{0,1:T(8,128)(4,1)S(1)} %copy-done.12), kind=kOutput, calls=%fused_computation.25 | convolution fusion | flops 2125922304 | bytes 9117736 | tf_op jit(solution)/shard_map/conv_general_dilated | solution.py:74
  (104 shorter events, 16.7 us)
Async XLA Ops:
  0.6 88.4 %copy-start = (bf16[3,3,3,16,384]{4,3,2,1,0:T(8,128)(2,1)S(1)}, bf16[3,3,3,16,384]{4,3,2,1,0:T(8,128)(2,1)}, u32[]{:S(2)}) copy-start(bf16[3,3,3,16,384]{4,3,2,1,0:T(8,128)(2,1)} %param.27) | copy-start | bytes 995332
  5.1 20.9 %copy-start.5 = (f32[2,4,512]{2,1,0:T(4,128)S(1)}, f32[2,4,512]{2,1,0:T(4,128)}, u32[]{:S(2)}) copy-start(f32[2,4,512]{2,1,0:T(4,128)} %param.26) | copy-start | bytes 49156
  5.1 22.3 %copy-start.7 = (f32[1536]{0:T(1024)S(1)}, f32[1536]{0:T(1024)}, u32[]{:S(2)}) copy-start(f32[1536]{0:T(1024)} %param.22) | copy-start | bytes 18436
  5.1 48.8 %all-to-all-start = ((bf16[32,64,2,384]{3,1,2,0:T(8,128)(2,1)}), bf16[32,64,2,384]{3,1,2,0:T(8,128)(2,1)S(1)}, u32[]{:S(2)}, u32[]{:S(2)}) async-start(bf16[32,64,2,384]{3,1,2,0:T(8,128)(2,1)} %bitcast.137), calls=%async_computation | async-start | bytes 6291456 | tf_op jit(solution)/shard_map/all_to_all | solution.py:131
  19.1 37.9 %collective-permute-start.2 = (bf16[3,64,128]{2,1,0:T(8,128)(2,1)}, bf16[3,64,128]{2,1,0:T(8,128)(2,1)}, u32[]{:S(2)}, u32[]{:S(2)}) collective-permute-start(bf16[3,64,128]{2,1,0:T(8,128)(2,1)} %bitcast_bitcast_fusion), channel_id=1, source_target_pairs={{0,1},{1,2},{2,3},{3,0},{4,5},{5,6},{6,7},{7,4},{8,9},{9,10},{10,1... | collective-permute-start | bytes 147464 | tf_op jit(solution)/shard_map/ppermute | solution.py:145
  21.2 35.9 %collective-permute-start.1 = (bf16[3,64,128]{2,1,0:T(8,128)(2,1)}, bf16[3,64,128]{2,1,0:T(8,128)(2,1)}, u32[]{:S(2)}, u32[]{:S(2)}) collective-permute-start(bf16[3,64,128]{2,1,0:T(8,128)(2,1)} %bitcast_bitcast_fusion.1), channel_id=1, source_target_pairs={{0,2},{1,3},{2,0},{3,1},{4,6},{5,7},{6,4},{7,5},{8,10},{9,11},{10,... | collective-permute-start | bytes 147464 | tf_op jit(solution)/shard_map/ppermute | solution.py:145
  24.5 32.6 %collective-permute-start = (bf16[3,64,128]{2,1,0:T(8,128)(2,1)}, bf16[3,64,128]{2,1,0:T(8,128)(2,1)}, u32[]{:S(2)}, u32[]{:S(2)}) collective-permute-start(bf16[3,64,128]{2,1,0:T(8,128)(2,1)} %bitcast_bitcast_fusion.2), channel_id=1, source_target_pairs={{0,3},{1,0},{2,1},{3,2},{4,7},{5,4},{6,5},{7,6},{8,11},{9,8},{10,9... | collective-permute-start | bytes 147464 | tf_op jit(solution)/shard_map/ppermute | solution.py:145
  59.0 8.2 %slice-start = ((s8[4718592]{0:T(1024)(128)(4,1)}), s8[4194304]{0:T(1024)(128)(4,1)S(1)}, s32[]{:S(2)}) async-start(s8[4718592]{0:T(1024)(128)(4,1)} %bitcast.142), calls=%async_computation.1 | async-start | bytes 8388608
  60.4 6.8 %slice-start.1 = ((s8[4718592]{0:T(1024)(128)(4,1)}), s8[524288]{0:T(1024)(128)(4,1)S(1)}, s32[]{:S(2)}) async-start(s8[4718592]{0:T(1024)(128)(4,1)} %bitcast.142), calls=%async_computation.2 | async-start | bytes 1048576
  62.0 7.5 %collective-permute-start.5 = (bf16[64,384]{0,1:T(8,128)(2,1)S(1)}, bf16[64,384]{0,1:T(8,128)(2,1)S(1)}, u32[]{:S(2)}, u32[]{:S(2)}) collective-permute-start(bf16[64,384]{0,1:T(8,128)(2,1)S(1)} %bitcast.160), channel_id=1, source_target_pairs={{0,3},{1,0},{2,1},{3,2},{4,7},{5,4},{6,5},{7,6},{8,11},{9,8},{10,9... | collective-permute-start | bytes 147464 | tf_op jit(solution)/shard_map/ppermute | solution.py:167
  63.3 5.8 %collective-permute-start.3 = (bf16[64,384]{0,1:T(8,128)(2,1)S(1)}, bf16[64,384]{0,1:T(8,128)(2,1)S(1)}, u32[]{:S(2)}, u32[]{:S(2)}) collective-permute-start(bf16[64,384]{0,1:T(8,128)(2,1)S(1)} %bitcast.161), channel_id=1, source_target_pairs={{0,1},{1,2},{2,3},{3,0},{4,5},{5,6},{6,7},{7,4},{8,9},{9,10},{10,1... | collective-permute-start | bytes 147464 | tf_op jit(solution)/shard_map/ppermute | solution.py:167
  64.1 6.8 %collective-permute-start.4 = (bf16[64,384]{0,1:T(8,128)(2,1)S(1)}, bf16[64,384]{0,1:T(8,128)(2,1)S(1)}, u32[]{:S(2)}, u32[]{:S(2)}) collective-permute-start(bf16[64,384]{0,1:T(8,128)(2,1)S(1)} %bitcast.159), channel_id=1, source_target_pairs={{0,2},{1,3},{2,0},{3,1},{4,6},{5,7},{6,4},{7,5},{8,10},{9,11},{10,... | collective-permute-start | bytes 147464 | tf_op jit(solution)/shard_map/ppermute | solution.py:167
  67.5 3.3 %copy-start.4 = (bf16[64,1536]{1,0:T(8,128)(2,1)S(1)}, bf16[64,1536]{1,0:T(8,128)(2,1)}, u32[]{:S(2)}) copy-start(bf16[64,1536]{1,0:T(8,128)(2,1)} %param.16) | copy-start | bytes 589828
  67.6 3.3 %copy-start.6 = (f32[1536]{0:T(1024)S(1)}, f32[1536]{0:T(1024)}, u32[]{:S(2)}) copy-start(f32[1536]{0:T(1024)} %param.20) | copy-start | bytes 18436
  69.8 2.3 %copy-start.3 = (f32[2,4,32,16]{3,2,1,0:T(8,128)S(1)}, f32[2,4,32,16]{3,2,1,0:T(8,128)}, u32[]{:S(2)}) copy-start(f32[2,4,32,16]{3,2,1,0:T(8,128)} %reshape.161) | copy-start | bytes 49156
  71.3 17.6 %copy-start.2 = (bf16[64,1536]{1,0:T(8,128)(2,1)}, bf16[64,1536]{1,0:T(8,128)(2,1)S(1)}, u32[]{:S(2)}) copy-start(bf16[64,1536]{1,0:T(8,128)(2,1)S(1)} %get-tuple-element.23) | copy-start | bytes 589828
  71.9 17.2 %copy-start.12 = (pred[8,5]{0,1:T(8,128)(4,1)S(1)}, pred[8,5]{0,1:T(8,128)(4,1)}, u32[]{:S(2)}) copy-start(pred[8,5]{0,1:T(8,128)(4,1)} %constant.95) | copy-start | bytes 124
  72.0 20.9 %slice-start.2 = ((s8[7962624]{0:T(1024)(128)(4,1)}), s8[4194304]{0:T(1024)(128)(4,1)S(1)}, s32[]{:S(2)}) async-start(s8[7962624]{0:T(1024)(128)(4,1)} %bitcast.163), calls=%async_computation.3 | async-start | bytes 8388608
  72.1 12.9 %collective-permute-start.8 = (bf16[2,4,32,16]{3,2,1,0:T(8,128)(2,1)S(1)}, bf16[2,4,32,16]{3,2,1,0:T(8,128)(2,1)S(1)}, u32[]{:S(2)}, u32[]{:S(2)}) collective-permute-start(bf16[2,4,32,16]{3,2,1,0:T(8,128)(2,1)S(1)} %subtract_convert_fusion), channel_id=1, source_target_pairs={{0,1},{1,2},{2,3},{3,4},{4,5},{5,6},{6,7},{7,8},{8,9},{9,10},{10,1... | collective-permute-start | bytes 24584 | tf_op jit(solution)/shard_map/ppermute | solution.py:22
  74.8 10.7 %collective-permute-start.7 = (bf16[2,4,32,16]{3,2,1,0:T(8,128)(2,1)S(1)}, bf16[2,4,32,16]{3,2,1,0:T(8,128)(2,1)S(1)}, u32[]{:S(2)}, u32[]{:S(2)}) collective-permute-start(bf16[2,4,32,16]{3,2,1,0:T(8,128)(2,1)S(1)} %subtract_convert_fusion), channel_id=1, source_target_pairs={{0,2},{1,3},{2,4},{3,5},{4,6},{5,7},{6,8},{7,9},{8,10},{9,11},{10,... | collective-permute-start | bytes 24584 | tf_op jit(solution)/shard_map/ppermute | solution.py:22
  79.5 9.2 %collective-permute-start.6 = (bf16[2,4,32,16]{3,2,1,0:T(8,128)(2,1)S(1)}, bf16[2,4,32,16]{3,2,1,0:T(8,128)(2,1)S(1)}, u32[]{:S(2)}, u32[]{:S(2)}) collective-permute-start(bf16[2,4,32,16]{3,2,1,0:T(8,128)(2,1)S(1)} %subtract_convert_fusion), channel_id=1, source_target_pairs={{0,3},{1,4},{2,5},{3,6},{4,7},{5,8},{6,9},{7,10},{8,11},{9,12},{10... | collective-permute-start | bytes 24584 | tf_op jit(solution)/shard_map/ppermute | solution.py:22
  89.1 3.9 %slice-start.3 = ((s8[7962624]{0:T(1024)(128)(4,1)}), s8[3768320]{0:T(1024)(128)(4,1)S(1)}, s32[]{:S(2)}) async-start(s8[7962624]{0:T(1024)(128)(4,1)} %bitcast.163), calls=%async_computation.4 | async-start | bytes 7536640
  97.0 5.9 %slice-start.4 = ((s8[7962624]{0:T(1024)(128)(4,1)}), s8[4194304]{0:T(1024)(128)(4,1)S(1)}, s32[]{:S(2)}) async-start(s8[7962624]{0:T(1024)(128)(4,1)} %bitcast.165), calls=%async_computation.5 | async-start | bytes 8388608
  97.1 5.7 %slice-start.5 = ((s8[7962624]{0:T(1024)(128)(4,1)}), s8[3768320]{0:T(1024)(128)(4,1)S(1)}, s32[]{:S(2)}) async-start(s8[7962624]{0:T(1024)(128)(4,1)} %bitcast.165), calls=%async_computation.6 | async-start | bytes 7536640
  (5 other events, 6.4 us)

commit v15 on v14

--- a/solution.py
+++ b/solution.py
@@ -170,8 +170,9 @@
     normed = layer_norm(layer_output, head_scale, head_shift)
     velocity = jnp.dot(normed, head_weight, preferred_element_type=jnp.float32)
     clean = to_latent(velocity, noisy_latent, noise_level)
-    earlier = [shifted(clean, FRAMES, by) for by in (3, 2, 1)]
-    clean_ext = jnp.concatenate(earlier + [clean], axis=0)
+    previous = shifted(clean, FRAMES, 1)
+    two_before = shifted(jnp.concatenate([previous, clean], axis=0), FRAMES, 2)
+    clean_ext = jnp.concatenate([two_before, previous, clean], axis=0)
     feature_ext = spatial_conv(clean_ext, input_kernel).astype(jnp.bfloat16)
     first_act = norm_silu(feature_ext, first_gain)
     half = (first_act.shape[0] - 2) // 2

time: 109 us -> 113 us (1.037); the launches traced: 107 us -> 113 us
  waiting for transfers between devices: 31.8 us -> 45.5 us
  starting transfers between devices: 32.4 us -> 24.3 us
    ppermute x3 -> x2, waiting for transfers between devices: 3.59 us -> 17.2 us  [shifted(): return lax.ppermute(x, axis, pairs)]
    ppermute x3 -> x2, starting transfers between devices: 12.9 us -> 4.76 us  [shifted(): return lax.ppermute(x, axis, pairs)]
  transfers between devices with their start and end apart: 10 -> 9, of which waited for: 5 -> 5; matrix products, arithmetic and copies ran while one was open for 11% -> 11% of each run, Pallas kernels for 0% -> 0%
where the time goes in v15:
time: 113 us
  waiting for transfers between devices  45.5 us (40%)
  starting transfers between devices  24.3 us (22%)
  local copies, waits for them, and re-layouts  19.3 us (17%)
  matrix products  17.9 us (16%)
  other arithmetic  4.03 us (4%)
  between operations  1.98 us (2%)
    all_to_all x1, waiting for transfers between devices, gather_group(): got = lax.all_to_all(sent, FRAMES, 0, 0, tiled=True)  25.7 us
    ppermute x2, waiting for transfers between devices, shifted(): return lax.ppermute(x, axis, pairs)  17.2 us
    conv_general_dilated x4, matrix products, spatial_conv(): lax.conv_general_dilated(extended[None], kernel, (1, 1, 1), ((0, 0), (1,...  12.8 us
    all_to_all x1, starting transfers between devices, gather_group(): got = lax.all_to_all(sent, FRAMES, 0, 0, tiled=True)  8.69 us
    ppermute x3, starting transfers between devices, body(): received.append(lax.ppermute(piece, 'hg', pairs))  5.6 us
    ppermute x3, starting transfers between devices, body(): piece = lax.ppermute(pieces[k], 'hg', pairs)  5.22 us
    ppermute x2, starting transfers between devices, shifted(): return lax.ppermute(x, axis, pairs)  4.76 us
    dynamic_slice x1, local copies, waits for them, and re-layouts, body(): lax.dynamic_index_in_dim(query_parts, me, 1, keepdims=False)  3.01 us
  transfers between devices with their start and end apart: 9, of which 5 were waited for; matrix products, arithmetic and copies ran while one was open for 11% of the time, Pallas kernels for 0%

profile of v15, /device:TPU:96, one launch (start us, length us, event | category | flops | bytes accessed | tf_op | source)
XLA Modules:
  0.0 113.0 jit_solution(7649267485092325583)
XLA Ops:
  0.6 1.0 stack.10
  3.0 2.1 %broadcast_in_dim.13 = bf16[8,4,64,2,384]{4,2,3,1,0:T(8,128)(2,1)} broadcast(bf16[4,64,2,384]{3,1,2,0:T(8,128)(2,1)S(1)} %copy.55), dimensions={1,2,3,4} | broadcast | bytes 3538944 | tf_op jit(solution)/shard_map/broadcast_in_dim | solution.py:129
  5.1 8.7 %all-to-all-start = ((bf16[32,64,2,384]{3,1,2,0:T(8,128)(2,1)}), bf16[32,64,2,384]{3,1,2,0:T(8,128)(2,1)S(1)}, u32[]{:S(2)}, u32[]{:S(2)}) async-start(bf16[32,64,2,384]{3,1,2,0:T(8,128)(2,1)} %bitcast.137), calls=%async_computation | async-start | bytes 6291456 | tf_op jit(solution)/shard_map/all_to_all | solution.py:131
  13.9 1.7 %reshape.153 = bf16[64,4,384]{2,1,0:T(4,128)(2,1)} reshape(bf16[64,1536]{1,0:T(8,128)(2,1)} %param.17) | data formatting | bytes 393216 | tf_op jit(solution)/shard_map/reshape | solution.py:135
  15.5 3.0 %dynamic-slice_reduce_fusion.3 = (bf16[64,384]{1,0:T(8,128)(2,1)}, bf16[64,384]{1,0:T(8,128)(2,1)S(1)}, bf16[64,384]{1,0:T(8,128)(2,1)S(1)}, bf16[64,384]{1,0:T(8,128)(2,1)S(1)}) fusion(bf16[64,4,384]{2,1,0:T(4,128)(2,1)} %reshape.153, s32[]{:T(128)S(6)} %select_n.18, s32[]{:T(128)S(6)} %select_n.20, s32[]{:T(128)S(6)} %select_n.19, s32[]{:T(128)S(6)} %select_n.21), kind=kLoop, calls=%fused_computation.116 | loop fusion | bytes 393232 | tf_op jit(solution)/shard_map/jit(dynamic_index_in_dim)/dynamic_slice | solution.py:140
  19.2 1.5 %collective-permute-start.2 = (bf16[3,64,128]{2,1,0:T(8,128)(2,1)}, bf16[3,64,128]{2,1,0:T(8,128)(2,1)}, u32[]{:S(2)}, u32[]{:S(2)}) collective-permute-start(bf16[3,64,128]{2,1,0:T(8,128)(2,1)} %bitcast_bitcast_fusion), channel_id=1, source_target_pairs={{0,1},{1,2},{2,3},{3,0},{4,5},{5,6},{6,7},{7,4},{8,9},{9,10},{10,1... | collective-permute-start | bytes 147464 | tf_op jit(solution)/shard_map/ppermute | solution.py:145
  21.2 2.7 %collective-permute-start.1 = (bf16[3,64,128]{2,1,0:T(8,128)(2,1)}, bf16[3,64,128]{2,1,0:T(8,128)(2,1)}, u32[]{:S(2)}, u32[]{:S(2)}) collective-permute-start(bf16[3,64,128]{2,1,0:T(8,128)(2,1)} %bitcast_bitcast_fusion.1), channel_id=1, source_target_pairs={{0,2},{1,3},{2,0},{3,1},{4,6},{5,7},{6,4},{7,5},{8,10},{9,11},{10,... | collective-permute-start | bytes 147464 | tf_op jit(solution)/shard_map/ppermute | solution.py:145
  24.5 1.5 %collective-permute-start = (bf16[3,64,128]{2,1,0:T(8,128)(2,1)}, bf16[3,64,128]{2,1,0:T(8,128)(2,1)}, u32[]{:S(2)}, u32[]{:S(2)}) collective-permute-start(bf16[3,64,128]{2,1,0:T(8,128)(2,1)} %bitcast_bitcast_fusion.2), channel_id=1, source_target_pairs={{0,3},{1,0},{2,1},{3,2},{4,7},{5,4},{6,5},{7,6},{8,11},{9,8},{10,9... | collective-permute-start | bytes 147464 | tf_op jit(solution)/shard_map/ppermute | solution.py:145
  28.2 25.7 %all-to-all-done = bf16[32,64,2,384]{3,1,2,0:T(8,128)(2,1)S(1)} async-done(((bf16[32,64,2,384]{3,1,2,0:T(8,128)(2,1)}), bf16[32,64,2,384]{3,1,2,0:T(8,128)(2,1)S(1)}, u32[]{:S(2)}, u32[]{:S(2)}) %all-to-all-start) | async-done | bytes 3145760 | tf_op jit(solution)/shard_map/all_to_all | solution.py:131
  54.6 1.6 %copy.59 = bf16[2048,1,384]{0,2,1:T(8,128)(2,1)} copy(bf16[2048,1,384]{2,0,1:T(8,128)(2,1)S(1)} %get-tuple-element.11) | data formatting | bytes 3145728 | tf_op jit(solution)/shard_map/slice | solution.py:149
  57.1 1.9 %multiply_reduce_fusion = (f32[3,256]{1,0:T(4,128)S(1)}, f32[3,256,2048]{2,1,0:T(8,128)S(1)}) fusion(bf16[2048,3,128]{0,2,1:T(8,128)(2,1)S(1)} %bitcast.139, bf16[3,64,128]{2,1,0:T(8,128)(2,1)} %collective-permute-done.2, bf16[3,64,128]{2,1,0:T(8,128)(2,1)} %collective-permute-done.1, bf16[3,64,128]{2,1,0:T(8,128)(2,1)} %collective-permute-done, ...), kind=kOutput, calls=%fused_computation.1 | convolution fusion | flops 406584576 | bytes 8064000 | tf_op jit(solution)/shard_map/qhd,khd->hqk/dot_general | solution.py:39
  59.0 1.2 %fusion = f32[3,256]{1,0:T(4,128)S(1)} fusion(f32[3,256,2048]{2,1,0:T(8,128)S(1)} %get-tuple-element.21, f32[3,256]{1,0:T(4,128)S(1)} %get-tuple-element.19), kind=kLoop, calls=%fused_computation.2 | loop fusion | flops 4717824 | bytes 6297600 | tf_op jit(solution)/shard_map/reduce_sum | solution.py:45
  60.4 1.4 %fusion.40 = bf16[256,3,128]{0,2,1:T(8,128)(2,1)S(1)} fusion(bf16[2048,3,128]{0,2,1:T(8,128)(2,1)S(1)} %bitcast.154, f32[3,256,2048]{2,1,0:T(8,128)S(1)} %get-tuple-element.21, f32[3,256]{1,0:T(4,128)S(1)} %get-tuple-element.19, f32[256,3]{0,1:T(4,128)S(1)} %bitcast.162, f32[256,3]{0,1:T(4,128)S(1)} %get-tuple-element.18), kind=kOutput, calls=%fused_computation.46 | convolution fusion | flops 407666688 | bytes 8070144 | tf_op jit(solution)/shard_map/hqk,khd->qhd/dot_general | solution.py:46
  61.9 1.3 %collective-permute-start.5 = (bf16[64,384]{0,1:T(8,128)(2,1)S(1)}, bf16[64,384]{0,1:T(8,128)(2,1)S(1)}, u32[]{:S(2)}, u32[]{:S(2)}) collective-permute-start(bf16[64,384]{0,1:T(8,128)(2,1)S(1)} %bitcast.160), channel_id=1, source_target_pairs={{0,3},{1,0},{2,1},{3,2},{4,7},{5,4},{6,5},{7,6},{8,11},{9,8},{10,9... | collective-permute-start | bytes 147464 | tf_op jit(solution)/shard_map/ppermute | solution.py:167
  64.0 3.1 %collective-permute-start.4 = (bf16[64,384]{0,1:T(8,128)(2,1)S(1)}, bf16[64,384]{0,1:T(8,128)(2,1)S(1)}, u32[]{:S(2)}, u32[]{:S(2)}) collective-permute-start(bf16[64,384]{0,1:T(8,128)(2,1)S(1)} %bitcast.159), channel_id=1, source_target_pairs={{0,2},{1,3},{2,0},{3,1},{4,6},{5,7},{6,4},{7,5},{8,10},{9,11},{10,... | collective-permute-start | bytes 147464 | tf_op jit(solution)/shard_map/ppermute | solution.py:167
  67.5 1.5 %collective-permute-done.3 = bf16[64,384]{0,1:T(8,128)(2,1)S(1)} collective-permute-done((bf16[64,384]{0,1:T(8,128)(2,1)S(1)}, bf16[64,384]{0,1:T(8,128)(2,1)S(1)}, u32[]{:S(2)}, u32[]{:S(2)}) %collective-permute-start.3) | collective-permute-done | bytes 49184 | tf_op jit(solution)/shard_map/ppermute | solution.py:167
  72.1 2.7 %collective-permute-start.6 = (bf16[2,4,32,16]{3,2,1,0:T(8,128)(2,1)S(1)}, bf16[2,4,32,16]{3,2,1,0:T(8,128)(2,1)S(1)}, u32[]{:S(2)}, u32[]{:S(2)}) collective-permute-start(bf16[2,4,32,16]{3,2,1,0:T(8,128)(2,1)S(1)} %subtract_convert_fusion), channel_id=1, source_target_pairs={{0,1},{1,2},{2,3},{3,4},{4,5},{5,6},{6,7},{7,8},{8,9},{9,10},{10,1... | collective-permute-start | bytes 24584 | tf_op jit(solution)/shard_map/ppermute | solution.py:22
  74.8 8.0 %collective-permute-done.6 = bf16[2,4,32,16]{3,2,1,0:T(8,128)(2,1)S(1)} collective-permute-done((bf16[2,4,32,16]{3,2,1,0:T(8,128)(2,1)S(1)}, bf16[2,4,32,16]{3,2,1,0:T(8,128)(2,1)S(1)}, u32[]{:S(2)}, u32[]{:S(2)}) %collective-permute-start.6) | collective-permute-done | bytes 8224 | tf_op jit(solution)/shard_map/ppermute | solution.py:22
  82.8 2.1 %collective-permute-start.7 = (bf16[4,4,32,16]{3,2,1,0:T(8,128)(2,1)S(1)}, bf16[4,4,32,16]{3,2,1,0:T(8,128)(2,1)S(1)}, u32[]{:S(2)}, u32[]{:S(2)}) collective-permute-start(bf16[4,4,32,16]{3,2,1,0:T(8,128)(2,1)S(1)} %pad_maximum_fusion.1), channel_id=1, source_target_pairs={{0,2},{1,3},{2,4},{3,5},{4,6},{5,7},{6,8},{7,9},{8,10},{9,11},{10,... | collective-permute-start | bytes 49160 | tf_op jit(solution)/shard_map/ppermute | solution.py:22
  84.9 9.3 %collective-permute-done.7 = bf16[4,4,32,16]{3,2,1,0:T(8,128)(2,1)S(1)} collective-permute-done((bf16[4,4,32,16]{3,2,1,0:T(8,128)(2,1)S(1)}, bf16[4,4,32,16]{3,2,1,0:T(8,128)(2,1)S(1)}, u32[]{:S(2)}, u32[]{:S(2)}) %collective-permute-start.7) | collective-permute-done | bytes 16416 | tf_op jit(solution)/shard_map/ppermute | solution.py:22
  94.6 1.8 %select_convert_fusion = bf16[6,4,8,5,384]{4,2,3,1,0:T(8,128)(2,1)S(1)} fusion(bf16[3,3,3,16,384]{4,3,2,1,0:T(8,128)(2,1)S(1)} %copy-done, pred[8,5]{0,1:T(8,128)(4,1)S(1)} %copy-done.12, bf16[8,4,1,7,2,16]{5,3,4,1,0,2:T(8,128)(2,1)S(1)} %slice.73, bf16[8,4,1,8,5,16]{5,3,4,1,0,2:T(8,128)(2,1)S(1)} %copy.63), kind=kOutput, calls=%fused_computation.15 | convolution fusion | flops 266330112 | bytes 1124392 | tf_op jit(solution)/shard_map/conv_general_dilated | solution.py:74
  98.5 3.7 %convolution_select_fusion.1 = f32[2,4,8,5,384]{4,2,3,1,0:T(8,128)S(1)} fusion(bf16[3,3,3,384,384]{4,3,2,1,0:T(8,128)(2,1)S(1)} %bitcast.164, bf16[4,4,1,7,2,384]{5,3,4,1,0,2:T(8,128)(2,1)S(1)} %slice.79, bf16[4,4,1,8,5,384]{5,3,4,1,0,2:T(8,128)(2,1)S(1)} %copy.68, pred[8,5]{0,1:T(8,128)(4,1)S(1)} %copy-done.12), kind=kOutput, calls=%fused_computation.21 | convolution fusion | flops 2125553664 | bytes 9117736 | tf_op jit(solution)/shard_map/conv_general_dilated | solution.py:74
  102.7 3.7 %convolution_select_fusion.2 = f32[2,4,8,5,384]{4,2,3,1,0:T(8,128)S(1)} fusion(bf16[3,3,3,384,384]{4,3,2,1,0:T(8,128)(2,1)S(1)} %bitcast.164, bf16[4,4,1,7,2,384]{5,3,4,1,0,2:T(8,128)(2,1)S(1)} %slice.77, bf16[4,4,1,8,5,384]{5,3,4,1,0,2:T(8,128)(2,1)S(1)} %copy.66, pred[8,5]{0,1:T(8,128)(4,1)S(1)} %copy-done.12), kind=kOutput, calls=%fused_computation.22 | convolution fusion | flops 2125553664 | bytes 9117736 | tf_op jit(solution)/shard_map/conv_general_dilated | solution.py:74
  108.4 3.7 %fusion.17 = bf16[2,4,8,5,384]{4,2,3,1,0:T(8,128)(2,1)S(1)} fusion(bf16[3,3,3,384,384]{4,3,2,1,0:T(8,128)(2,1)S(1)} %bitcast.166, bf16[4,4,1,7,2,384]{5,3,4,1,0,2:T(8,128)(2,1)S(1)} %slice.83, bf16[4,4,1,8,5,384]{5,3,4,1,0,2:T(8,128)(2,1)S(1)} %copy.73, bf16[6,4,8,5,384]{4,2,3,1,0:T(8,128)(2,1)S(1)} %select_convert_fusion, pred[8,5]{0,1:T(8,128)(4,1)S(1)} %copy-done.12), kind=kOutput, calls=%fused_computation.25 | convolution fusion | flops 2125922304 | bytes 9117736 | tf_op jit(solution)/shard_map/conv_general_dilated | solution.py:74
  (103 shorter events, 16.3 us)
Async XLA Ops:
  0.6 94.0 %copy-start = (bf16[3,3,3,16,384]{4,3,2,1,0:T(8,128)(2,1)S(1)}, bf16[3,3,3,16,384]{4,3,2,1,0:T(8,128)(2,1)}, u32[]{:S(2)}) copy-start(bf16[3,3,3,16,384]{4,3,2,1,0:T(8,128)(2,1)} %param.27) | copy-start | bytes 995332
  5.1 20.9 %copy-start.5 = (f32[2,4,512]{2,1,0:T(4,128)S(1)}, f32[2,4,512]{2,1,0:T(4,128)}, u32[]{:S(2)}) copy-start(f32[2,4,512]{2,1,0:T(4,128)} %param.26) | copy-start | bytes 49156
  5.1 22.3 %copy-start.7 = (f32[1536]{0:T(1024)S(1)}, f32[1536]{0:T(1024)}, u32[]{:S(2)}) copy-start(f32[1536]{0:T(1024)} %param.22) | copy-start | bytes 18436
  5.1 48.8 %all-to-all-start = ((bf16[32,64,2,384]{3,1,2,0:T(8,128)(2,1)}), bf16[32,64,2,384]{3,1,2,0:T(8,128)(2,1)S(1)}, u32[]{:S(2)}, u32[]{:S(2)}) async-start(bf16[32,64,2,384]{3,1,2,0:T(8,128)(2,1)} %bitcast.137), calls=%async_computation | async-start | bytes 6291456 | tf_op jit(solution)/shard_map/all_to_all | solution.py:131
  19.2 37.9 %collective-permute-start.2 = (bf16[3,64,128]{2,1,0:T(8,128)(2,1)}, bf16[3,64,128]{2,1,0:T(8,128)(2,1)}, u32[]{:S(2)}, u32[]{:S(2)}) collective-permute-start(bf16[3,64,128]{2,1,0:T(8,128)(2,1)} %bitcast_bitcast_fusion), channel_id=1, source_target_pairs={{0,1},{1,2},{2,3},{3,0},{4,5},{5,6},{6,7},{7,4},{8,9},{9,10},{10,1... | collective-permute-start | bytes 147464 | tf_op jit(solution)/shard_map/ppermute | solution.py:145
  21.2 35.8 %collective-permute-start.1 = (bf16[3,64,128]{2,1,0:T(8,128)(2,1)}, bf16[3,64,128]{2,1,0:T(8,128)(2,1)}, u32[]{:S(2)}, u32[]{:S(2)}) collective-permute-start(bf16[3,64,128]{2,1,0:T(8,128)(2,1)} %bitcast_bitcast_fusion.1), channel_id=1, source_target_pairs={{0,2},{1,3},{2,0},{3,1},{4,6},{5,7},{6,4},{7,5},{8,10},{9,11},{10,... | collective-permute-start | bytes 147464 | tf_op jit(solution)/shard_map/ppermute | solution.py:145
  24.5 32.5 %collective-permute-start = (bf16[3,64,128]{2,1,0:T(8,128)(2,1)}, bf16[3,64,128]{2,1,0:T(8,128)(2,1)}, u32[]{:S(2)}, u32[]{:S(2)}) collective-permute-start(bf16[3,64,128]{2,1,0:T(8,128)(2,1)} %bitcast_bitcast_fusion.2), channel_id=1, source_target_pairs={{0,3},{1,0},{2,1},{3,2},{4,7},{5,4},{6,5},{7,6},{8,11},{9,8},{10,9... | collective-permute-start | bytes 147464 | tf_op jit(solution)/shard_map/ppermute | solution.py:145
  59.0 8.2 %slice-start = ((s8[4718592]{0:T(1024)(128)(4,1)}), s8[4194304]{0:T(1024)(128)(4,1)S(1)}, s32[]{:S(2)}) async-start(s8[4718592]{0:T(1024)(128)(4,1)} %bitcast.142), calls=%async_computation.1 | async-start | bytes 8388608
  60.4 6.8 %slice-start.1 = ((s8[4718592]{0:T(1024)(128)(4,1)}), s8[524288]{0:T(1024)(128)(4,1)S(1)}, s32[]{:S(2)}) async-start(s8[4718592]{0:T(1024)(128)(4,1)} %bitcast.142), calls=%async_computation.2 | async-start | bytes 1048576
  61.9 7.5 %collective-permute-start.5 = (bf16[64,384]{0,1:T(8,128)(2,1)S(1)}, bf16[64,384]{0,1:T(8,128)(2,1)S(1)}, u32[]{:S(2)}, u32[]{:S(2)}) collective-permute-start(bf16[64,384]{0,1:T(8,128)(2,1)S(1)} %bitcast.160), channel_id=1, source_target_pairs={{0,3},{1,0},{2,1},{3,2},{4,7},{5,4},{6,5},{7,6},{8,11},{9,8},{10,9... | collective-permute-start | bytes 147464 | tf_op jit(solution)/shard_map/ppermute | solution.py:167
  63.2 5.8 %collective-permute-start.3 = (bf16[64,384]{0,1:T(8,128)(2,1)S(1)}, bf16[64,384]{0,1:T(8,128)(2,1)S(1)}, u32[]{:S(2)}, u32[]{:S(2)}) collective-permute-start(bf16[64,384]{0,1:T(8,128)(2,1)S(1)} %bitcast.161), channel_id=1, source_target_pairs={{0,1},{1,2},{2,3},{3,0},{4,5},{5,6},{6,7},{7,4},{8,9},{9,10},{10,1... | collective-permute-start | bytes 147464 | tf_op jit(solution)/shard_map/ppermute | solution.py:167
  64.0 6.8 %collective-permute-start.4 = (bf16[64,384]{0,1:T(8,128)(2,1)S(1)}, bf16[64,384]{0,1:T(8,128)(2,1)S(1)}, u32[]{:S(2)}, u32[]{:S(2)}) collective-permute-start(bf16[64,384]{0,1:T(8,128)(2,1)S(1)} %bitcast.159), channel_id=1, source_target_pairs={{0,2},{1,3},{2,0},{3,1},{4,6},{5,7},{6,4},{7,5},{8,10},{9,11},{10,... | collective-permute-start | bytes 147464 | tf_op jit(solution)/shard_map/ppermute | solution.py:167
  67.5 3.3 %copy-start.4 = (bf16[64,1536]{1,0:T(8,128)(2,1)S(1)}, bf16[64,1536]{1,0:T(8,128)(2,1)}, u32[]{:S(2)}) copy-start(bf16[64,1536]{1,0:T(8,128)(2,1)} %param.16) | copy-start | bytes 589828
  67.5 3.3 %copy-start.6 = (f32[1536]{0:T(1024)S(1)}, f32[1536]{0:T(1024)}, u32[]{:S(2)}) copy-start(f32[1536]{0:T(1024)} %param.20) | copy-start | bytes 18436
  69.8 1.8 %copy-start.10 = (bf16[1536,64]{0,1:T(8,128)(2,1)S(1)}, bf16[1536,64]{0,1:T(8,128)(2,1)}, u32[]{:S(2)}) copy-start(bf16[1536,64]{0,1:T(8,128)(2,1)} %param.24) | copy-start | bytes 589828
  69.8 2.3 %copy-start.3 = (f32[2,4,32,16]{3,2,1,0:T(8,128)S(1)}, f32[2,4,32,16]{3,2,1,0:T(8,128)}, u32[]{:S(2)}) copy-start(f32[2,4,32,16]{3,2,1,0:T(8,128)} %reshape.161) | copy-start | bytes 49156
  71.3 23.2 %copy-start.2 = (bf16[64,1536]{1,0:T(8,128)(2,1)}, bf16[64,1536]{1,0:T(8,128)(2,1)S(1)}, u32[]{:S(2)}) copy-start(bf16[64,1536]{1,0:T(8,128)(2,1)S(1)} %get-tuple-element.23) | copy-start | bytes 589828
  72.1 22.5 %copy-start.12 = (pred[8,5]{0,1:T(8,128)(4,1)S(1)}, pred[8,5]{0,1:T(8,128)(4,1)}, u32[]{:S(2)}) copy-start(pred[8,5]{0,1:T(8,128)(4,1)} %constant.95) | copy-start | bytes 124
  72.1 26.4 %slice-start.2 = ((s8[7962624]{0:T(1024)(128)(4,1)}), s8[4194304]{0:T(1024)(128)(4,1)S(1)}, s32[]{:S(2)}) async-start(s8[7962624]{0:T(1024)(128)(4,1)} %bitcast.163), calls=%async_computation.3 | async-start | bytes 8388608
  72.1 10.6 %collective-permute-start.6 = (bf16[2,4,32,16]{3,2,1,0:T(8,128)(2,1)S(1)}, bf16[2,4,32,16]{3,2,1,0:T(8,128)(2,1)S(1)}, u32[]{:S(2)}, u32[]{:S(2)}) collective-permute-start(bf16[2,4,32,16]{3,2,1,0:T(8,128)(2,1)S(1)} %subtract_convert_fusion), channel_id=1, source_target_pairs={{0,1},{1,2},{2,3},{3,4},{4,5},{5,6},{6,7},{7,8},{8,9},{9,10},{10,1... | collective-permute-start | bytes 24584 | tf_op jit(solution)/shard_map/ppermute | solution.py:22
  82.8 11.4 %collective-permute-start.7 = (bf16[4,4,32,16]{3,2,1,0:T(8,128)(2,1)S(1)}, bf16[4,4,32,16]{3,2,1,0:T(8,128)(2,1)S(1)}, u32[]{:S(2)}, u32[]{:S(2)}) collective-permute-start(bf16[4,4,32,16]{3,2,1,0:T(8,128)(2,1)S(1)} %pad_maximum_fusion.1), channel_id=1, source_target_pairs={{0,2},{1,3},{2,4},{3,5},{4,6},{5,7},{6,8},{7,9},{8,10},{9,11},{10,... | collective-permute-start | bytes 49160 | tf_op jit(solution)/shard_map/ppermute | solution.py:22
  94.6 3.9 %slice-start.3 = ((s8[7962624]{0:T(1024)(128)(4,1)}), s8[3768320]{0:T(1024)(128)(4,1)S(1)}, s32[]{:S(2)}) async-start(s8[7962624]{0:T(1024)(128)(4,1)} %bitcast.163), calls=%async_computation.4 | async-start | bytes 7536640
  102.5 5.9 %slice-start.4 = ((s8[7962624]{0:T(1024)(128)(4,1)}), s8[4194304]{0:T(1024)(128)(4,1)S(1)}, s32[]{:S(2)}) async-start(s8[7962624]{0:T(1024)(128)(4,1)} %bitcast.165), calls=%async_computation.5 | async-start | bytes 8388608
  102.7 5.7 %slice-start.5 = ((s8[7962624]{0:T(1024)(128)(4,1)}), s8[3768320]{0:T(1024)(128)(4,1)S(1)}, s32[]{:S(2)}) async-start(s8[7962624]{0:T(1024)(128)(4,1)} %bitcast.165), calls=%async_computation.6 | async-start | bytes 7536640
  (4 other events, 4.6 us)
